TPU v7x, 32 devices: a whole 2x2x4 slice. The times are simulated.
32 devices in a mesh: row: 8 (over z, x), col: 4 (over y, core).
Axes of the slice: x: 2, y: 2, z: 4, core: 2. Of those that a mesh axis runs over, the one named last changes fastest.
Arguments:
- hamiltonian: bfloat16 [2, 2048, 2048], P(None, 'row', 'col'), may hold values from -0.25 to 0.25
- basis_metric: bfloat16 [2048, 2048], P('row', 'col'), may hold values from -0.25 to 0.25
- density: bfloat16 [2, 2048, 2048], P(None, 'row', 'col'), may hold values from -6 to 6
- hamiltonian_keep: int32 [16, 16], P('row', 'col'), may hold values from 0 to 1, as said below
- metric_keep: int32 [16, 16], P('row', 'col'), may hold values from 0 to 1, as said below
- density_keep: int32 [16, 16], P('row', 'col'), may hold values from 0 to 1, as said below
- gradient_keep: int32 [16, 16], P('row', 'col'), may hold values 0 or 1
Outputs:
- gradient: float32 [2, 2048, 2048], P(None, 'row', 'col')
Inputs may be any that keep to these rules, and one draw needn't show every extreme that they name: `hamiltonian_keep`: each block row has at most 4 blocks in the pattern, and some rows have exactly 4. `metric_keep`: each block row has at most 4 blocks in the pattern, and some rows have exactly 4. `density_keep`: each block row keeps at most 7 blocks, and some rows keep exactly 7.
All inputs are finite; a program needn't handle non-finite values. No bound on the sum of `gradient_keep` on one device may be relied on, other than what follows from the above.
Results may differ from a plain program's by a relative error of at most 0.0029.
Values may be sent and summed in bfloat16 or wider, within the bound.
No kernel may reach another device: no remote copies, remote signals or barrier semaphores. Data moves between devices by JAX's collectives and lax.ppermute only.
A program may use at most 64 MiB of HBM per device.

v0:
```python
import jax
import jax.numpy as jnp
from jax import lax
from jax.sharding import PartitionSpec as P

BLOCK = 128


def widen(keep):
    return jnp.repeat(jnp.repeat(keep, BLOCK, axis=0), BLOCK, axis=1) > 0


def first_terms(rows_part, cols_part):
    hterm = jnp.einsum("srl,slc->src", rows_part[:2], cols_part, preferred_element_type=jnp.float32)
    sterm = jnp.einsum("rl,slc->src", rows_part[2], cols_part, preferred_element_type=jnp.float32)
    return jnp.concatenate([hterm, sterm], axis=0)


def second_terms(rows_part, cols_part):
    left = jnp.einsum(
        "srl,lc->src", rows_part[:2], cols_part[2], preferred_element_type=jnp.float32
    )
    right = jnp.einsum(
        "srl,slc->src", rows_part[2:], cols_part[:2], preferred_element_type=jnp.float32
    )
    return left - right


def body(
    hamiltonian, basis_metric, density, hamiltonian_keep, metric_keep, density_keep, gradient_keep
):
    kohn_sham = jnp.where(widen(hamiltonian_keep)[None], hamiltonian, jnp.zeros_like(hamiltonian))
    smat = jnp.where(widen(metric_keep), basis_metric, jnp.zeros_like(basis_metric))
    filtered = jnp.where(widen(density_keep)[None], density, jnp.zeros_like(density))
    operators = jnp.concatenate([kohn_sham, smat[None]], axis=0)
    density_cols = lax.all_gather(filtered, "row", axis=1, tiled=True)
    cols_part = density_cols
    products = first_terms(lax.all_gather(operators, "col", axis=2, tiled=True), cols_part)
    products = products.astype(jnp.bfloat16)
    operator_cols = lax.all_gather(operators, "row", axis=1, tiled=True)
    cols_part = operator_cols
    commut = second_terms(lax.all_gather(products, "col", axis=2, tiled=True), cols_part)
    grad_mask = widen(gradient_keep)[None]
    return jnp.where(grad_mask, commut, jnp.zeros_like(commut))


def solution(mesh):
    in_specs = (
        P(None, "row", "col"),
        P("row", "col"),
        P(None, "row", "col"),
        P("row", "col"),
        P("row", "col"),
        P("row", "col"),
        P("row", "col"),
    )
    out_specs = P(None, "row", "col")
    return jax.shard_map(body, mesh=mesh, in_specs=in_specs, out_specs=out_specs, check_vma=False)
```

profile of v0, /device:TPU:1, one launch (start us, length us, event | category | flops | bytes accessed | tf_op | source)
XLA Modules:
  0.0 266.9 jit_solution(11964594302407016854)
XLA Ops:
  6.5 0.0 all-gather.5.cloned.1.call-start
  6.5 0.7 broadcast_compare_fusion.2
  7.3 0.3 broadcast_in_dim.61
  7.6 0.1 copy.23
  7.7 0.7 broadcast_compare_fusion.1
  8.4 1.1 broadcast_select_fusion.1
  9.5 0.3 broadcast_in_dim.64
  9.9 1.0 fusion.6
  10.9 1.0 pad_maximum_fusion.1
  11.9 0.0 all-gather.5.cloned.1.call-update
  11.9 0.0 all-gather.7.cloned.1.call-start
  12.0 0.3 broadcast_in_dim.68
  12.3 0.1 copy.22
  12.4 0.9 broadcast_select_fusion
  13.2 0.0 all-gather.7.cloned.1.call-update
  13.3 0.0 all-gather.11.cloned.1.call-start
  13.3 0.7 all-gather.11.cloned.1.call-update
  14.0 0.0 all-gather.9.cloned.1.call-start
  14.1 29.0 %all-gather.5.cloned.1.call-done = bf16[3,256,2048]{2,1,0:T(8,128)(2,1)} async-done(((bf16[3,256,512]{2,1,0:T(8,128)(2,1)}), bf16[3,256,2048]{2,1,0:T(8,128)(2,1)}) %all-gather.5.cloned.1.call-update) | async-done | bytes 3145744 | tf_op jit(solution)/shard_map/all_gather | solution.py:38
  43.1 74.0 %all-gather.7.cloned.1.call-done = bf16[2,2048,512]{2,1,0:T(8,128)(2,1)} async-done(((bf16[2,256,512]{2,1,0:T(8,128)(2,1)}), bf16[2,2048,512]{2,1,0:T(8,128)(2,1)}) %all-gather.7.cloned.1.call-update) | async-done | bytes 4194320 | tf_op jit(solution)/shard_map/all_gather | solution.py:36
  117.1 3.9 %fusion.5 = bf16[2,256,512]{2,1,0:T(8,128)(2,1)S(1)} fusion(bf16[2,2048,512]{2,1,0:T(8,128)(2,1)} %all-gather.7.cloned.1.call-done, bf16[3,256,2048]{2,1,0:T(8,128)(2,1)} %all-gather.5.cloned.1.call-done), kind=kOutput, calls=%fused_computation.8 | convolution fusion | flops 1074003968 | bytes 5767168 | tf_op jit(solution)/shard_map/rl,slc->src/dot_general | solution.py:15
  121.0 0.0 copy-start.5
  121.0 1.3 convolution_convert_fusion
  122.3 1.1 pad_maximum_fusion
  123.4 0.0 all-gather.9.cloned.1.call-update
  123.4 0.0 copy-done.5
  123.4 0.3 broadcast_in_dim.58
  123.8 0.1 copy.24
  123.8 93.4 %all-gather.11.cloned.1.call-done = bf16[3,2048,512]{2,1,0:T(8,128)(2,1)} async-done(((bf16[3,256,512]{2,1,0:T(8,128)(2,1)}), bf16[3,2048,512]{2,1,0:T(8,128)(2,1)}) %all-gather.11.cloned.1.call-update) | async-done | bytes 6291472 | tf_op jit(solution)/shard_map/all_gather | solution.py:40
  217.3 35.0 %all-gather.9.cloned.1.call-done = bf16[4,256,2048]{2,1,0:T(8,128)(2,1)} async-done(((bf16[4,256,512]{2,1,0:T(8,128)(2,1)}), bf16[4,256,2048]{2,1,0:T(8,128)(2,1)}) %all-gather.9.cloned.1.call-update) | async-done | bytes 4194320 | tf_op jit(solution)/shard_map/all_gather | solution.py:42
  252.3 4.2 %fusion = f32[2,256,512]{2,1,0:T(8,128)S(1)} fusion(bf16[4,256,2048]{2,1,0:T(8,128)(2,1)} %all-gather.9.cloned.1.call-done, bf16[3,2048,512]{2,1,0:T(8,128)(2,1)} %all-gather.11.cloned.1.call-done), kind=kOutput, calls=%fused_computation | convolution fusion | flops 1073741824 | bytes 9437184 | tf_op jit(solution)/shard_map/srl,slc->src/dot_general | solution.py:23
  256.5 3.8 %fusion.4 = f32[2,256,512]{2,1,0:T(8,128)} fusion(f32[2,256,512]{2,1,0:T(8,128)S(1)} %fusion, bf16[4,256,2048]{2,1,0:T(8,128)(2,1)S(1)} %copy-done.2, bf16[3,2048,512]{2,1,0:T(8,128)(2,1)} %all-gather.11.cloned.1.call-done, pred[256,512]{1,0:T(8,128)(4,1)S(1)} %bitcast.52), kind=kOutput, calls=%fused_computation.5 | convolution fusion | flops 1074266112 | bytes 8519680 | tf_op jit(solution)/shard_map/srl,lc->src/dot_general | solution.py:20
  (16 shorter events, 0.1 us)
Async XLA Ops:
  6.5 5.4 %copy-start.4 = (s32[2,4]{1,0:T(2,128)S(1)}, s32[2,4]{1,0:T(2,128)}, u32[]{:S(2)}) copy-start(s32[2,4]{1,0:T(2,128)} %param.12) | copy-start | bytes 100
  6.5 5.9 %copy-start = (bf16[2,256,512]{2,1,0:T(8,128)(2,1)S(1)}, bf16[2,256,512]{2,1,0:T(8,128)(2,1)}, u32[]{:S(2)}) copy-start(bf16[2,256,512]{2,1,0:T(8,128)(2,1)} %param.9) | copy-start | bytes 1572868
  6.5 36.5 %all-gather.5.cloned.1.call-start = ((), (), s32[]{:S(2)}) async-start(), calls=%async_computation | async-start | bytes 3932160 | tf_op jit(solution)/shard_map/all_gather | solution.py:38
  11.9 105.2 %all-gather.7.cloned.1.call-start = ((), (), s32[]{:S(2)}) async-start(), calls=%async_computation.1 | async-start | bytes 4718592 | tf_op jit(solution)/shard_map/all_gather | solution.py:36
  13.3 204.0 %all-gather.11.cloned.1.call-start = ((), (), s32[]{:S(2)}) async-start(), calls=%async_computation.3 | async-start | bytes 7077888 | tf_op jit(solution)/shard_map/all_gather | solution.py:40
  14.0 238.3 %all-gather.9.cloned.1.call-start = ((), (), s32[]{:S(2)}) async-start(), calls=%async_computation.2 | async-start | bytes 5242880 | tf_op jit(solution)/shard_map/all_gather | solution.py:42
  43.1 77.9 %copy-start.3 = (bf16[3,256,2048]{2,1,0:T(8,128)(2,1)S(1)}, bf16[3,256,2048]{2,1,0:T(8,128)(2,1)}, u32[]{:S(2)}) copy-start(bf16[3,256,2048]{2,1,0:T(8,128)(2,1)} %all-gather.5.cloned.1.call-done) | copy-start | bytes 9437188
  117.1 3.9 %copy-start.1 = (bf16[2,2048,512]{2,1,0:T(8,128)(2,1)S(1)}, bf16[2,2048,512]{2,1,0:T(8,128)(2,1)}, u32[]{:S(2)}) copy-start(bf16[2,2048,512]{2,1,0:T(8,128)(2,1)} %all-gather.7.cloned.1.call-done) | copy-start | bytes 12582916
  121.0 2.4 copy-start.5
  252.3 4.2 %copy-start.2 = (bf16[4,256,2048]{2,1,0:T(8,128)(2,1)S(1)}, bf16[4,256,2048]{2,1,0:T(8,128)(2,1)}, u32[]{:S(2)}) copy-start(bf16[4,256,2048]{2,1,0:T(8,128)(2,1)} %all-gather.9.cloned.1.call-done) | copy-start | bytes 12582916
Sparse Core Ops, SparseCore 0:
  12.0 31.0 all-gather.4
  45.2 71.7 all-gather.6
  119.2 97.9 all-gather.10
  218.7 33.5 all-gather.8
where the time goes:
time: 267 us
  waiting for transfers between devices  232 us (87%)
  matrix products  13.3 us (5%)
  between operations  13.3 us (5%)
  other arithmetic  6.44 us (2%)
    all_gather x1, waiting for transfers between devices, body(): operator_cols = lax.all_gather(operators, 'row', axis=1, tiled=True)  93.4 us
    all_gather x1, waiting for transfers between devices, body(): density_cols = lax.all_gather(filtered, 'row', axis=1, tiled=True)  74 us
    all_gather x1, waiting for transfers between devices, body(): lax.all_gather(products, 'col', axis=2, tiled=True)  35 us
    all_gather x1, waiting for transfers between devices, body(): lax.all_gather(operators, 'col', axis=2, tiled=True)  29 us
  transfers between devices with their start and end apart: 4, of which 4 were waited for; matrix products, arithmetic and copies ran while one was open for 3% of the time, Pallas kernels for 0%

commit v1 on v0

v1 whole, which is shorter than its diff:
```python
import functools

import jax
import jax.numpy as jnp
from jax import lax
from jax.experimental import pallas as pl
from jax.experimental.pallas import tpu as pltpu
from jax.sharding import PartitionSpec as P

BLOCK = 128
OPERATOR_SLOTS = 4
DENSITY_SLOTS = 7

ANY = pl.BlockSpec(memory_space=pl.ANY)
VMEM = pl.BlockSpec(memory_space=pltpu.VMEM)
SMEM = pl.BlockSpec(memory_space=pltpu.SMEM)


def estimate(flops, nbytes):
    return pl.CostEstimate(flops=flops, bytes_accessed=nbytes, transcendentals=0)


def split_kernel(place, density, hamiltonian, metric, *rest):
    outs, sems = rest[:4], rest[4]
    spin, row = place[0], place[1]
    copies = []
    for v in (2, 3, 1, 0):
        other_spin = spin if v < 2 else 1 - spin
        other_row = row if v % 2 == 0 else 1 - row
        rows = pl.ds(pl.multiple_of(other_row * BLOCK, BLOCK), BLOCK)
        sources = (density.at[other_spin, rows], hamiltonian.at[other_spin, rows], metric.at[rows])
        for n, source in enumerate(sources):
            copies.append(pltpu.make_async_copy(source, outs[v].at[n], sems.at[v * 3 + n]))
    for copy in copies:
        copy.start()
    for copy in copies:
        copy.wait()


def pack_kernel(sources, col, keep, *refs):
    ins, dens_out, oper_out = refs[:sources], refs[sources], refs[sources + 1]
    per = ins[0].shape[2] // BLOCK
    dens_out[...] = jnp.zeros_like(dens_out)
    oper_out[...] = jnp.zeros_like(oper_out)
    here = col[0]
    for mat, (out, first) in enumerate(((dens_out, 0), (oper_out, 0), (oper_out, OPERATOR_SLOTS))):
        flags = [[keep[m, mat, b] for b in range(per)] for m in range(sources)]
        counts = [functools.reduce(lambda p, q: p + q, f) for f in flags]
        for m in range(sources):
            slot = jnp.int32(first)
            for n in range(sources):
                if n != m:
                    slot += jnp.where((here ^ n) < (here ^ m), counts[n], 0)
            for b in range(per):

                @pl.when(flags[m][b] > 0)
                def _(slot=slot, m=m, b=b):
                    out[slot] = ins[m][mat, :, b * BLOCK : (b + 1) * BLOCK]

                slot += flags[m][b]


def row_of(place, key, layers):
    shift, flip, other = key
    layer = place[0] - shift
    layer = jnp.where(layer < 0, layer + layers, layer)
    side = place[1] if flip == 0 else 1 - place[1]
    half = place[2] if other == 0 else 1 - place[2]
    return (layer * 2 + side) * 2 + half


def fetch(place, keys, layers, bufs, held, sems):
    copies = [
        pltpu.make_async_copy(buf, held.at[row_of(place, key, layers)], sems.at[n])
        for n, (key, buf) in enumerate(zip(keys, bufs, strict=True))
    ]
    for copy in copies:
        copy.start()
    return copies


def first_kernel(keys, layers, place, mine, cols, own, *refs):
    count = len(keys)
    bufs, out, held, acc, sems = refs[:count], *refs[count:]
    copies = fetch(place, keys, layers, bufs, held, sems)
    acc[...] = jnp.zeros_like(acc)
    for copy in copies:
        copy.wait()
    nblk = held.shape[0]
    for u in range(2 * OPERATOR_SLOTS):
        k = mine[u]
        left = own[u]
        base = (u // OPERATOR_SLOTS) * nblk
        for t in range(DENSITY_SLOTS):
            acc[base + cols[k, t]] += jnp.dot(left, held[k, t], preferred_element_type=jnp.float32)
    out[...] = acc[...].astype(out.dtype)


def second_kernel(keys, layers, place, cols, prods, *refs):
    count = len(keys)
    bufs, outs, (held, acc, sems) = refs[:count], refs[count : count + 4], refs[count + 4 :]
    copies = fetch(place, keys, layers, bufs, held, sems)
    acc[...] = jnp.zeros_like(acc)
    for copy in copies:
        copy.wait()
    nblk = held.shape[0]

    def step(k, carry):
        hp, sp = prods[k], prods[nblk + k]
        for t in range(OPERATOR_SLOTS):
            u = OPERATOR_SLOTS + t
            acc[cols[k, u]] += jnp.dot(hp, held[k, u], preferred_element_type=jnp.float32)
            acc[cols[k, t]] -= jnp.dot(sp, held[k, t], preferred_element_type=jnp.float32)
        return carry

    lax.fori_loop(0, nblk, step, 0)
    per = outs[0].shape[0]
    for v in range(4):
        for b in range(per):
            outs[v][b] = acc[place[3 + v] * per + b]


def join_kernel(place, keep, *refs):
    ins, out = refs[:4], refs[4]
    per = ins[0].shape[0]
    for v in range(4):
        spin = place[0] if v < 2 else 1 - place[0]
        row = place[1] if v % 2 == 0 else 1 - place[1]
        rows = pl.ds(pl.multiple_of(row * BLOCK, BLOCK), BLOCK)
        for b in range(per):
            value = ins[v][b]
            out[spin, rows, b * BLOCK : (b + 1) * BLOCK] = jnp.where(
                keep[row, b] > 0, value, jnp.zeros_like(value)
            )


def columns_of(keep, slots):
    n = keep.shape[1]
    index = jnp.arange(n, dtype=jnp.int32)
    before = (index[:, None] < index[None, :]).astype(jnp.int32)
    rank = jnp.sum(keep[:, :, None] * before[None], axis=1)
    hit = (rank[:, None, :] == jnp.arange(slots, dtype=jnp.int32)[None, :, None]) & (keep > 0)[:, None, :]
    return jnp.sum(jnp.where(hit, index[None, None, :], 0), axis=2)


def body(nrow, ncol, hamiltonian, metric, density, ham_keep, met_keep, dens_keep, grad_keep):
    layers, half = nrow // 2, ncol // 2
    per = ham_keep.shape[1]
    nblk = ham_keep.shape[0] * nrow
    width = per * BLOCK
    bf16, f32, i32 = jnp.bfloat16, jnp.float32, jnp.int32

    def by_row(pairs):
        return lambda a: lax.ppermute(a, "row", pairs)

    def by_mask(mask):
        return lambda a: lax.ppermute(a, "col", [(c, c ^ mask) for c in range(ncol)])

    def variant(mask):
        return (2 if mask >= half else 0) + (mask & 1)

    up = by_row([(r, (r + 2) % nrow) for r in range(nrow)])
    across = by_row([(r, r ^ 1) for r in range(nrow)])
    twin = by_mask(1)

    row, col = lax.axis_index("row").astype(i32), lax.axis_index("col").astype(i32)
    spin, part = col // half, col % 2
    z, x = row // 2, row % 2
    masks = (0, 1, half, half + 1)

    keeps = (jnp.stack([dens_keep, ham_keep, met_keep]) > 0).astype(i32)
    spread = lax.all_gather(keeps, ("row", "col"))

    split = pl.pallas_call(
        split_kernel,
        out_shape=[jax.ShapeDtypeStruct((3, BLOCK, width), bf16)] * 4,
        in_specs=[SMEM, ANY, ANY, ANY],
        out_specs=[ANY] * 4,
        scratch_shapes=[pltpu.SemaphoreType.DMA((12,))],
        cost_estimate=estimate(0, 24 * BLOCK * width * 2),
        name="split",
    )(jnp.stack([spin, part]), density, hamiltonian, metric)
    got = {m: by_mask(m)(split[variant(m)]) for m in reversed(range(1, ncol))}
    got[0] = split[0]
    keep_rows = [lax.dynamic_index_in_dim(keeps, part ^ d, 1, keepdims=False) for d in (0, 1)]
    keep_got = jnp.stack(
        [keep_rows[0]] + [by_mask(m)(keep_rows[m & 1]) for m in range(1, ncol)]
    )

    dens, oper = pl.pallas_call(
        functools.partial(pack_kernel, ncol),
        out_shape=[
            jax.ShapeDtypeStruct((DENSITY_SLOTS, BLOCK, BLOCK), bf16),
            jax.ShapeDtypeStruct((2 * OPERATOR_SLOTS, BLOCK, BLOCK), bf16),
        ],
        in_specs=[SMEM, SMEM] + [VMEM] * ncol,
        out_specs=[VMEM, VMEM],
        cost_estimate=estimate(0, ncol * 3 * BLOCK * width * 2),
        name="pack",
    )(col[None], keep_got, *[got[m] for m in range(ncol)])

    dens_bufs, oper_bufs = {}, {}
    curs = [dens, oper]
    for t in range(layers):
        nexts = []
        for bufs, cur in zip((dens_bufs, oper_bufs), curs, strict=True):
            side = across(cur)
            if t < layers - 1:
                new, side = lax.optimization_barrier((up(cur), side))
                nexts.append(new)
            bufs[t, 0, 0], bufs[t, 1, 0] = cur, side
            bufs[t, 0, 1], bufs[t, 1, 1] = twin(cur), twin(side)
        curs = nexts
    keys = list(dens_bufs)

    tables = spread.reshape(nrow, ncol, 3, 2, per).transpose(2, 0, 3, 1, 4).reshape(3, nblk, nblk)
    dens_cols = columns_of(tables[0], DENSITY_SLOTS)
    oper_cols = jnp.concatenate(
        [columns_of(tables[1], OPERATOR_SLOTS), columns_of(tables[2], OPERATOR_SLOTS)], axis=1
    )
    mine = lax.dynamic_index_in_dim(oper_cols, 2 * row + part, 0, keepdims=False)
    place = jnp.stack([z, x, part] + [col ^ m for m in masks])

    prods = pl.pallas_call(
        functools.partial(first_kernel, keys, layers),
        out_shape=jax.ShapeDtypeStruct((2 * nblk, BLOCK, BLOCK), bf16),
        in_specs=[SMEM, SMEM, SMEM, VMEM] + [ANY] * len(keys),
        out_specs=VMEM,
        scratch_shapes=[
            pltpu.VMEM((nblk, DENSITY_SLOTS, BLOCK, BLOCK), bf16),
            pltpu.VMEM((2 * nblk, BLOCK, BLOCK), f32),
            pltpu.SemaphoreType.DMA((len(keys),)),
        ],
        cost_estimate=estimate(56 * 2 * BLOCK**3, nblk * 9 * BLOCK * BLOCK * 2),
        name="first",
    )(place, mine, dens_cols, oper, *[dens_bufs[k] for k in keys])

    outs = pl.pallas_call(
        functools.partial(second_kernel, keys, layers),
        out_shape=[jax.ShapeDtypeStruct((per, BLOCK, BLOCK), f32)] * 4,
        in_specs=[SMEM, SMEM, VMEM] + [ANY] * len(keys),
        out_specs=[VMEM] * 4,
        scratch_shapes=[
            pltpu.VMEM((nblk, 2 * OPERATOR_SLOTS, BLOCK, BLOCK), bf16),
            pltpu.VMEM((nblk, BLOCK, BLOCK), f32),
            pltpu.SemaphoreType.DMA((len(keys),)),
        ],
        cost_estimate=estimate(nblk * 16 * BLOCK**3, nblk * 12 * BLOCK * BLOCK * 2),
        name="second",
    )(place, oper_cols, prods, *[oper_bufs[k] for k in keys])

    back = [outs[0]] + [by_mask(m)(o) for m, o in zip(masks[1:], outs[1:], strict=True)]
    return pl.pallas_call(
        join_kernel,
        out_shape=jax.ShapeDtypeStruct((2, 2 * BLOCK, width), f32),
        in_specs=[SMEM, SMEM] + [VMEM] * 4,
        out_specs=VMEM,
        cost_estimate=estimate(0, 8 * BLOCK * width * 4),
        name="join",
    )(jnp.stack([spin, part]), grad_keep, *back)


def solution(mesh):
    grid = P("row", "col")
    spins = P(None, "row", "col")
    return jax.shard_map(
        functools.partial(body, mesh.shape["row"], mesh.shape["col"]),
        mesh=mesh,
        in_specs=(spins, grid, spins, grid, grid, grid, grid),
        out_specs=spins,
        check_vma=False,
    )
```

time: 267 us -> 203 us (0.76)
  waiting for transfers between devices: 232 us -> 52.4 us
  Pallas kernels: 0 us -> 67.6 us
  blocking collectives: 0 us -> 45.1 us
  starting transfers between devices: 0.12 us -> 25.7 us
  matrix products: 13.3 us -> 0 us
  between operations: 13.3 us -> 0.48 us
  local copies, waits for them, and re-layouts: 1.63 us -> 7.81 us
  other arithmetic: 6.44 us -> 3.72 us
    all_gather x4 -> x0, waiting for transfers between devices: 231 us -> none  [the longest x1 93.4 us: body(): operator_cols = lax.all_gather(operators, 'row', axis=1, tiled=True)]
    pallas_call x0 -> x5, Pallas kernels: none -> 67.6 us  [the longest x1 49.5 us: body(): pl.pallas_call(split_kernel, out_shape=[jax.ShapeDtypeStruct((3, BLOCK, w...]
    ppermute x0 -> x39, waiting for transfers between devices: none -> 52.4 us  [the longest x25 27.8 us: by_mask(): lax.ppermute(a, 'col', [(c, c ^ mask) for c in range(ncol)])]
    all_gather x0 -> x1, blocking collectives: none -> 45.1 us  [body(): spread = lax.all_gather(keeps, ('row', 'col'))]
    ppermute x0 -> x39, starting transfers between devices: none -> 25.7 us  [the longest x25 19.2 us: by_mask(): lax.ppermute(a, 'col', [(c, c ^ mask) for c in range(ncol)])]
    dot_general x4 -> x0, matrix products: 13.3 us -> none  [the longest x1 4.21 us: second_terms(): jnp.einsum('srl,slc->src', rows_part[2:], cols_part[:2], preferred_elemen...]
    unnamed x15 -> x80, local copies, waits for them, and re-layouts: 0.23 us -> 4.64 us
  transfers between devices with their start and end apart: 4 -> 39, of which waited for: 4 -> 14; matrix products, arithmetic and copies ran while one was open for 3% -> 3% of each run, Pallas kernels for 0% -> 2%
where the time goes in v1:
time: 203 us
  Pallas kernels  67.6 us (33%)
  waiting for transfers between devices  52.4 us (26%)
  blocking collectives  45.1 us (22%)
  starting transfers between devices  25.7 us (13%)
  local copies, waits for them, and re-layouts  7.81 us (4%)
  other arithmetic  3.72 us (2%)
    pallas_call x1, Pallas kernels, body(): pl.pallas_call(split_kernel, out_shape=[jax.ShapeDtypeStruct((3, BLOCK, w...  49.5 us
    all_gather x1, blocking collectives, body(): spread = lax.all_gather(keeps, ('row', 'col'))  45.1 us
    ppermute x25, waiting for transfers between devices, by_mask(): lax.ppermute(a, 'col', [(c, c ^ mask) for c in range(ncol)])  27.8 us
    ppermute x14, waiting for transfers between devices, by_row(): return lambda a: lax.ppermute(a, 'row', pairs)  24.6 us
    ppermute x25, starting transfers between devices, by_mask(): lax.ppermute(a, 'col', [(c, c ^ mask) for c in range(ncol)])  19.2 us
    pallas_call x1, Pallas kernels, body(): pl.pallas_call(functools.partial(second_kernel, keys, layers), out_shape=...  8.27 us
    ppermute x14, starting transfers between devices, by_row(): return lambda a: lax.ppermute(a, 'row', pairs)  6.54 us
    pallas_call x1, Pallas kernels, body(): pl.pallas_call(functools.partial(first_kernel, keys, layers), out_shape=j...  4.97 us
  transfers between devices with their start and end apart: 39, of which 14 were waited for; matrix products, arithmetic and copies ran while one was open for 3% of the time, Pallas kernels for 2%

profile of v1, /device:TPU:1, one launch (start us, length us, event | category | flops | bytes accessed | tf_op | source)
XLA Modules:
  0.0 202.9 jit_solution(16918352518990090106)
XLA Ops:
  0.6 49.5 %split.1 = (bf16[3,128,512]{2,1,0:T(8,128)(2,1)}, bf16[3,128,512]{2,1,0:T(8,128)(2,1)}, bf16[3,128,512]{2,1,0:T(8,128)(2,1)}, bf16[3,128,512]{2,1,0:T(8,128)(2,1)}) custom-call(s32[2]{0:T(128)} %pad_add_fusion.2.place, bf16[2,256,512]{2,1,0:T(8,128)(2,1)} %density.1, bf16[2,256,512]{2,1,0:T(8,128)(2,1)} %hamiltonian.1, bf16[256,512]{1,0:T(8,128)(2,1)} %metric.1), custom_call_target="tpu_custom_call" | custom-call | bytes 3145728 | tf_op jit(solution)/shard_map/split/pallas_call | solution.py:174
  50.2 2.7 %collective-permute-start.4 = (bf16[3,128,512]{2,1,0:T(8,128)(2,1)}, bf16[3,128,512]{2,1,0:T(8,128)(2,1)S(1)}, u32[]{:S(2)}, u32[]{:S(2)}) collective-permute-start(bf16[3,128,512]{2,1,0:T(8,128)(2,1)} %get-tuple-element.29), channel_id=1, source_target_pairs={{0,2},{1,3},{2,0},{3,1},{4,6},{5,7},{6,4},{7,5},{8,10},{9,11},{10,... | collective-permute-start | bytes 1179656 | tf_op jit(solution)/shard_map/ppermute | solution.py:157
  53.7 1.7 collective-permute-start.1
  55.8 15.2 %collective-permute-done.1 = s32[3,4]{1,0:T(4,128)S(1)} collective-permute-done((s32[3,4]{1,0:T(4,128)S(1)}, s32[3,4]{1,0:T(4,128)S(1)}, u32[]{:S(2)}, u32[]{:S(2)}) %collective-permute-start.1) | collective-permute-done | bytes 80 | tf_op jit(solution)/shard_map/ppermute | solution.py:157
  70.9 0.7 collective-permute-start
  71.7 0.8 collective-permute-done
  73.1 0.7 copy-done.1
  74.1 2.6 %pack.1 = (bf16[7,128,128]{2,1,0:T(8,128)(2,1)}, bf16[8,128,128]{2,1,0:T(8,128)(2,1)}) custom-call(s32[1]{0:T(128)} %bitcast.4.col, s32[4,3,4]{2,1,0:T(4,128)} %pad_add_fusion.keep, bf16[3,128,512]{2,1,0:T(8,128)(2,1)} %get-tuple-element.27.refs_0_, bf16[3,128,512]{2,1,0:T(8,128)(2,1)} %copy-done.1, bf16[3,128,512]{2,1,0:T(8,128)(2,1)} %copy-done.2, ...), custom_call_target="tpu_custom_call" | custom-call | bytes 1572864 | tf_op jit(solution)/shard_map/pack/pallas_call | solution.py:190
  76.7 1.5 collective-permute-start.7
  78.1 1.3 collective-permute-start.6
  79.7 1.3 collective-permute-start.21
  81.0 2.8 %collective-permute-done.7.refs_1_ = bf16[7,128,128]{2,1,0:T(8,128)(2,1)S(1)} collective-permute-done((bf16[7,128,128]{2,1,0:T(8,128)(2,1)}, bf16[7,128,128]{2,1,0:T(8,128)(2,1)S(1)}, u32[]{:S(2)}, u32[]{:S(2)}) %collective-permute-start.7) | collective-permute-done | bytes 229408 | tf_op jit(solution)/shard_map/ppermute | solution.py:154
  83.8 3.1 %collective-permute-done.6.refs_4_ = bf16[7,128,128]{2,1,0:T(8,128)(2,1)S(1)} collective-permute-done((bf16[7,128,128]{2,1,0:T(8,128)(2,1)}, bf16[7,128,128]{2,1,0:T(8,128)(2,1)S(1)}, u32[]{:S(2)}, u32[]{:S(2)}) %collective-permute-start.6) | collective-permute-done | bytes 229408 | tf_op jit(solution)/shard_map/ppermute | solution.py:154
  87.4 2.0 collective-permute-done.22.refs_1_
  89.4 3.1 %collective-permute-done.21.refs_4_ = bf16[8,128,128]{2,1,0:T(8,128)(2,1)S(1)} collective-permute-done((bf16[8,128,128]{2,1,0:T(8,128)(2,1)}, bf16[8,128,128]{2,1,0:T(8,128)(2,1)S(1)}, u32[]{:S(2)}, u32[]{:S(2)}) %collective-permute-start.21) | collective-permute-done | bytes 262176 | tf_op jit(solution)/shard_map/ppermute | solution.py:154
  93.4 3.9 %collective-permute-done.10.refs_8_ = bf16[7,128,128]{2,1,0:T(8,128)(2,1)S(1)} collective-permute-done((bf16[7,128,128]{2,1,0:T(8,128)(2,1)S(1)}, bf16[7,128,128]{2,1,0:T(8,128)(2,1)S(1)}, u32[]{:S(2)}, u32[]{:S(2)}) %collective-permute-start.10) | collective-permute-done | bytes 229408 | tf_op jit(solution)/shard_map/ppermute | solution.py:154
  97.3 45.1 %all_gather.4 = s32[32,3,2,4]{3,2,1,0:T(2,128)S(1)} all-gather(s32[1,3,2,4]{3,2,1,0:T(2,128)S(1)} %compare_convert_fusion.1), channel_id=1, replica_groups=mesh['row'=8,'col'=4] {'row','col'}, dimensions={0}, use_global_device_ids=true | all-gather | bytes 3168 | tf_op jit(solution)/shard_map/all_gather | solution.py:172
  144.5 0.8 mul.48
  146.6 4.8 %collective-permute-done.30.refs_9_ = bf16[8,128,128]{2,1,0:T(8,128)(2,1)S(1)} collective-permute-done((bf16[8,128,128]{2,1,0:T(8,128)(2,1)S(1)}, bf16[8,128,128]{2,1,0:T(8,128)(2,1)S(1)}, u32[]{:S(2)}, u32[]{:S(2)}) %collective-permute-start.30) | collective-permute-done | bytes 262176 | tf_op jit(solution)/shard_map/ppermute | solution.py:154
  151.4 1.2 collective-permute-start.13
  153.3 1.1 collective-permute-start.18
  154.6 1.8 collective-permute-start.16
  157.0 2.4 %collective-permute-done.18.refs_13_ = bf16[7,128,128]{2,1,0:T(8,128)(2,1)S(1)} collective-permute-done((bf16[7,128,128]{2,1,0:T(8,128)(2,1)}, bf16[7,128,128]{2,1,0:T(8,128)(2,1)S(1)}, u32[]{:S(2)}, u32[]{:S(2)}) %collective-permute-start.18) | collective-permute-done | bytes 229408 | tf_op jit(solution)/shard_map/ppermute | solution.py:154
  159.4 3.5 %collective-permute-start.20 = (bf16[7,128,128]{2,1,0:T(8,128)(2,1)S(1)}, bf16[7,128,128]{2,1,0:T(8,128)(2,1)S(1)}, u32[]{:S(2)}, u32[]{:S(2)}) collective-permute-start(bf16[7,128,128]{2,1,0:T(8,128)(2,1)S(1)} %collective-permute-done.18.refs_13_), channel_id=1, source_target_pairs={{0,1},{1,0},{2,3},{3,2},{4,5},{5,4},{6,7},{7,6},{8,9},{9,8},{10,11... | collective-permute-start | bytes 688136 | tf_op jit(solution)/shard_map/ppermute | solution.py:157
  163.9 1.5 collective-permute-done.33.refs_13_
  165.3 1.8 collective-permute-start.32
  170.9 5.0 %first.1.prods = bf16[32,128,128]{2,1,0:T(8,128)(2,1)} custom-call(s32[7]{0:T(128)} %stack.78.place, s32[8]{0:T(128)} %fusion.5.mine, s32[16,7]{1,0:T(8,128)} %copy.17.cols, bf16[8,128,128]{2,1,0:T(8,128)(2,1)} %get-tuple-element.31.own.refs_0_, bf16[7,128,128]{2,1,0:T(8,128)(2,1)} %get-tuple-element.32.refs_0_, bf16[7,128,128]{2,1,0:T(8,128)(2,1)} %copy-done.23, ...), custom_call_target="tpu_custom_call" | custom-call | flops 234881024 | bytes 4718592 | tf_op jit(solution)/shard_map/first/pallas_call | solution.py:224
  177.6 8.3 %second.1 = (f32[4,128,128]{2,1,0:T(8,128)}, f32[4,128,128]{2,1,0:T(8,128)}, f32[4,128,128]{2,1,0:T(8,128)}, f32[4,128,128]{2,1,0:T(8,128)}) custom-call(s32[7]{0:T(128)} %stack.78.place, s32[16,8]{1,0:T(8,128)} %pad_add_fusion.1.cols, bf16[32,128,128]{2,1,0:T(8,128)(2,1)} %first.1.prods, bf16[8,128,128]{2,1,0:T(8,128)(2,1)} %get-tuple-element.31.own.refs_0_, ...), custom_call_target="tpu_custom_call" | custom-call | flops 536870912 | bytes 6291456 | tf_op jit(solution)/shard_map/second/pallas_call | solution.py:238
  186.1 2.0 %collective-permute-start.38 = (f32[4,128,128]{2,1,0:T(8,128)}, f32[4,128,128]{2,1,0:T(8,128)S(1)}, u32[]{:S(2)}, u32[]{:S(2)}) collective-permute-start(f32[4,128,128]{2,1,0:T(8,128)} %get-tuple-element.48), channel_id=1, source_target_pairs={{0,3},{1,2},{2,1},{3,0},{4,7},{5,6},{6,5},{7,4},{8,11},{9,10},{10,... | collective-permute-start | bytes 786440 | tf_op jit(solution)/shard_map/ppermute | solution.py:157
  188.1 5.6 %collective-permute-done.37.refs_2_ = f32[4,128,128]{2,1,0:T(8,128)S(1)} collective-permute-done((f32[4,128,128]{2,1,0:T(8,128)}, f32[4,128,128]{2,1,0:T(8,128)S(1)}, u32[]{:S(2)}, u32[]{:S(2)}) %collective-permute-start.37) | collective-permute-done | bytes 262176 | tf_op jit(solution)/shard_map/ppermute | solution.py:157
  193.7 6.2 %collective-permute-done.38.refs_3_ = f32[4,128,128]{2,1,0:T(8,128)S(1)} collective-permute-done((f32[4,128,128]{2,1,0:T(8,128)}, f32[4,128,128]{2,1,0:T(8,128)S(1)}, u32[]{:S(2)}, u32[]{:S(2)}) %collective-permute-start.38) | collective-permute-done | bytes 262176 | tf_op jit(solution)/shard_map/ppermute | solution.py:157
  200.6 2.3 %join.1 = f32[2,256,512]{2,1,0:T(8,128)} custom-call(s32[2]{0:T(128)} %pad_add_fusion.2.place, s32[2,4]{1,0:T(2,128)} %keep.1, f32[4,128,128]{2,1,0:T(8,128)} %get-tuple-element.45.refs_0_, f32[4,128,128]{2,1,0:T(8,128)} %copy-done.4, f32[4,128,128]{2,1,0:T(8,128)} %copy-done.5, f32[4,128,128]{2,1,0:T(8,128)} %copy-done.6), custom_call_target="tpu_custom_call" | custom-call | bytes 2097152 | tf_op jit(solution)/shard_map/join/pallas_call | solution.py:253
  (156 shorter events, 16.3 us)
Async XLA Ops:
  50.1 23.0 %collective-permute-start.3 = (bf16[3,128,512]{2,1,0:T(8,128)(2,1)}, bf16[3,128,512]{2,1,0:T(8,128)(2,1)S(1)}, u32[]{:S(2)}, u32[]{:S(2)}) collective-permute-start(bf16[3,128,512]{2,1,0:T(8,128)(2,1)} %get-tuple-element.28), channel_id=1, source_target_pairs={{0,1},{1,0},{2,3},{3,2},{4,5},{5,4},{6,7},{7,6},{8,9},{9,8},{10,11... | collective-permute-start | bytes 1179656 | tf_op jit(solution)/shard_map/ppermute | solution.py:157
  50.2 22.9 %collective-permute-start.4 = (bf16[3,128,512]{2,1,0:T(8,128)(2,1)}, bf16[3,128,512]{2,1,0:T(8,128)(2,1)S(1)}, u32[]{:S(2)}, u32[]{:S(2)}) collective-permute-start(bf16[3,128,512]{2,1,0:T(8,128)(2,1)} %get-tuple-element.29), channel_id=1, source_target_pairs={{0,2},{1,3},{2,0},{3,1},{4,6},{5,7},{6,4},{7,5},{8,10},{9,11},{10,... | collective-permute-start | bytes 1179656 | tf_op jit(solution)/shard_map/ppermute | solution.py:157
  52.9 20.2 %collective-permute-start.5 = (bf16[3,128,512]{2,1,0:T(8,128)(2,1)}, bf16[3,128,512]{2,1,0:T(8,128)(2,1)S(1)}, u32[]{:S(2)}, u32[]{:S(2)}) collective-permute-start(bf16[3,128,512]{2,1,0:T(8,128)(2,1)} %get-tuple-element.30), channel_id=1, source_target_pairs={{0,3},{1,2},{2,1},{3,0},{4,7},{5,6},{6,5},{7,4},{8,11},{9,10},{10,... | collective-permute-start | bytes 1179656 | tf_op jit(solution)/shard_map/ppermute | solution.py:157
  53.7 17.3 %collective-permute-start.1 = (s32[3,4]{1,0:T(4,128)S(1)}, s32[3,4]{1,0:T(4,128)S(1)}, u32[]{:S(2)}, u32[]{:S(2)}) collective-permute-start(s32[3,4]{1,0:T(4,128)S(1)} %bitcast.41), channel_id=1, source_target_pairs={{0,2},{1,3},{2,0},{3,1},{4,6},{5,7},{6,4},{7,5},{8,10},{9,11},{10,... | collective-permute-start | bytes 152 | tf_op jit(solution)/shard_map/ppermute | solution.py:157
  55.4 16.3 %collective-permute-start.2 = (s32[3,4]{1,0:T(4,128)S(1)}, s32[3,4]{1,0:T(4,128)S(1)}, u32[]{:S(2)}, u32[]{:S(2)}) collective-permute-start(s32[3,4]{1,0:T(4,128)S(1)} %bitcast.39), channel_id=1, source_target_pairs={{0,3},{1,2},{2,1},{3,0},{4,7},{5,6},{6,5},{7,4},{8,11},{9,10},{10,... | collective-permute-start | bytes 152 | tf_op jit(solution)/shard_map/ppermute | solution.py:157
  76.7 7.1 %collective-permute-start.7 = (bf16[7,128,128]{2,1,0:T(8,128)(2,1)}, bf16[7,128,128]{2,1,0:T(8,128)(2,1)S(1)}, u32[]{:S(2)}, u32[]{:S(2)}) collective-permute-start(bf16[7,128,128]{2,1,0:T(8,128)(2,1)} %get-tuple-element.32.refs_0_), channel_id=1, source_target_pairs={{0,4},{4,0},{8,12},{12,8},{16,20},{20,16},{24,28},{28,24},{1,5},{5... | collective-permute-start | bytes 688136 | tf_op jit(solution)/shard_map/ppermute | solution.py:154
  78.1 8.7 %collective-permute-start.6 = (bf16[7,128,128]{2,1,0:T(8,128)(2,1)}, bf16[7,128,128]{2,1,0:T(8,128)(2,1)S(1)}, u32[]{:S(2)}, u32[]{:S(2)}) collective-permute-start(bf16[7,128,128]{2,1,0:T(8,128)(2,1)} %get-tuple-element.32.refs_0_), channel_id=1, source_target_pairs={{0,8},{4,12},{8,16},{12,20},{16,24},{20,28},{24,0},{28,4},{1,9},{5... | collective-permute-start | bytes 688136 | tf_op jit(solution)/shard_map/ppermute | solution.py:154
  79.4 9.9 %collective-permute-start.22 = (bf16[8,128,128]{2,1,0:T(8,128)(2,1)}, bf16[8,128,128]{2,1,0:T(8,128)(2,1)S(1)}, u32[]{:S(2)}, u32[]{:S(2)}) collective-permute-start(bf16[8,128,128]{2,1,0:T(8,128)(2,1)} %get-tuple-element.31.own.refs_0_), channel_id=1, source_target_pairs={{0,4},{4,0},{8,12},{12,8},{16,20},{20,16},{24,28},{28,24},{1,5},{5... | collective-permute-start | bytes 786440 | tf_op jit(solution)/shard_map/ppermute | solution.py:154
  79.7 12.8 %collective-permute-start.21 = (bf16[8,128,128]{2,1,0:T(8,128)(2,1)}, bf16[8,128,128]{2,1,0:T(8,128)(2,1)S(1)}, u32[]{:S(2)}, u32[]{:S(2)}) collective-permute-start(bf16[8,128,128]{2,1,0:T(8,128)(2,1)} %get-tuple-element.31.own.refs_0_), channel_id=1, source_target_pairs={{0,8},{4,12},{8,16},{12,20},{16,24},{20,28},{24,0},{28,4},{1,9},{5... | collective-permute-start | bytes 786440 | tf_op jit(solution)/shard_map/ppermute | solution.py:154
  86.8 6.5 %collective-permute-start.11 = (bf16[7,128,128]{2,1,0:T(8,128)(2,1)S(1)}, bf16[7,128,128]{2,1,0:T(8,128)(2,1)S(1)}, u32[]{:S(2)}, u32[]{:S(2)}) collective-permute-start(bf16[7,128,128]{2,1,0:T(8,128)(2,1)S(1)} %collective-permute-done.6.refs_4_), channel_id=1, source_target_pairs={{0,4},{4,0},{8,12},{12,8},{16,20},{20,16},{24,28},{28,24},{1,5},{5... | collective-permute-start | bytes 688136 | tf_op jit(solution)/shard_map/ppermute | solution.py:154
  87.4 9.9 %collective-permute-start.10 = (bf16[7,128,128]{2,1,0:T(8,128)(2,1)S(1)}, bf16[7,128,128]{2,1,0:T(8,128)(2,1)S(1)}, u32[]{:S(2)}, u32[]{:S(2)}) collective-permute-start(bf16[7,128,128]{2,1,0:T(8,128)(2,1)S(1)} %collective-permute-done.6.refs_4_), channel_id=1, source_target_pairs={{0,8},{4,12},{8,16},{12,20},{16,24},{20,28},{24,0},{28,4},{1,9},{5... | collective-permute-start | bytes 688136 | tf_op jit(solution)/shard_map/ppermute | solution.py:154
  92.5 50.8 %collective-permute-start.26 = (bf16[8,128,128]{2,1,0:T(8,128)(2,1)S(1)}, bf16[8,128,128]{2,1,0:T(8,128)(2,1)S(1)}, u32[]{:S(2)}, u32[]{:S(2)}) collective-permute-start(bf16[8,128,128]{2,1,0:T(8,128)(2,1)S(1)} %collective-permute-done.21.refs_4_), channel_id=1, source_target_pairs={{0,4},{4,0},{8,12},{12,8},{16,20},{20,16},{24,28},{28,24},{1,5},{5... | collective-permute-start | bytes 786440 | tf_op jit(solution)/shard_map/ppermute | solution.py:154
  93.0 50.7 %collective-permute-start.25 = (bf16[8,128,128]{2,1,0:T(8,128)(2,1)S(1)}, bf16[8,128,128]{2,1,0:T(8,128)(2,1)S(1)}, u32[]{:S(2)}, u32[]{:S(2)}) collective-permute-start(bf16[8,128,128]{2,1,0:T(8,128)(2,1)S(1)} %collective-permute-done.21.refs_4_), channel_id=1, source_target_pairs={{0,8},{4,12},{8,16},{12,20},{16,24},{20,28},{24,0},{28,4},{1,9},{5... | collective-permute-start | bytes 786440 | tf_op jit(solution)/shard_map/ppermute | solution.py:154
  97.3 46.6 %collective-permute-start.15 = (bf16[7,128,128]{2,1,0:T(8,128)(2,1)S(1)}, bf16[7,128,128]{2,1,0:T(8,128)(2,1)S(1)}, u32[]{:S(2)}, u32[]{:S(2)}) collective-permute-start(bf16[7,128,128]{2,1,0:T(8,128)(2,1)S(1)} %collective-permute-done.10.refs_8_), channel_id=1, source_target_pairs={{0,4},{4,0},{8,12},{12,8},{16,20},{20,16},{24,28},{28,24},{1,5},{5... | collective-permute-start | bytes 688136 | tf_op jit(solution)/shard_map/ppermute | solution.py:154
  97.3 46.6 %collective-permute-start.14 = (bf16[7,128,128]{2,1,0:T(8,128)(2,1)S(1)}, bf16[7,128,128]{2,1,0:T(8,128)(2,1)}, u32[]{:S(2)}, u32[]{:S(2)}) collective-permute-start(bf16[7,128,128]{2,1,0:T(8,128)(2,1)S(1)} %collective-permute-done.10.refs_8_), channel_id=1, source_target_pairs={{0,8},{4,12},{8,16},{12,20},{16,24},{20,28},{24,0},{28,4},{1,9},{5... | collective-permute-start | bytes 688136 | tf_op jit(solution)/shard_map/ppermute | solution.py:154
  143.8 7.5 %collective-permute-start.30 = (bf16[8,128,128]{2,1,0:T(8,128)(2,1)S(1)}, bf16[8,128,128]{2,1,0:T(8,128)(2,1)S(1)}, u32[]{:S(2)}, u32[]{:S(2)}) collective-permute-start(bf16[8,128,128]{2,1,0:T(8,128)(2,1)S(1)} %collective-permute-done.25.refs_8_), channel_id=1, source_target_pairs={{0,4},{4,0},{8,12},{12,8},{16,20},{20,16},{24,28},{28,24},{1,5},{5... | collective-permute-start | bytes 786440 | tf_op jit(solution)/shard_map/ppermute | solution.py:154
  143.9 9.4 %collective-permute-start.29 = (bf16[8,128,128]{2,1,0:T(8,128)(2,1)S(1)}, bf16[8,128,128]{2,1,0:T(8,128)(2,1)S(1)}, u32[]{:S(2)}, u32[]{:S(2)}) collective-permute-start(bf16[8,128,128]{2,1,0:T(8,128)(2,1)S(1)} %collective-permute-done.25.refs_8_), channel_id=1, source_target_pairs={{0,8},{4,12},{8,16},{12,20},{16,24},{20,28},{24,0},{28,4},{1,9},{5... | collective-permute-start | bytes 786440 | tf_op jit(solution)/shard_map/ppermute | solution.py:154
  145.6 9.0 %collective-permute-start.12 = (bf16[7,128,128]{2,1,0:T(8,128)(2,1)S(1)}, bf16[7,128,128]{2,1,0:T(8,128)(2,1)S(1)}, u32[]{:S(2)}, u32[]{:S(2)}) collective-permute-start(bf16[7,128,128]{2,1,0:T(8,128)(2,1)S(1)} %collective-permute-done.6.refs_4_), channel_id=1, source_target_pairs={{0,1},{1,0},{2,3},{3,2},{4,5},{5,4},{6,7},{7,6},{8,9},{9,8},{10,11... | collective-permute-start | bytes 688136 | tf_op jit(solution)/shard_map/ppermute | solution.py:157
  146.0 10.5 %collective-permute-start.27 = (bf16[8,128,128]{2,1,0:T(8,128)(2,1)S(1)}, bf16[8,128,128]{2,1,0:T(8,128)(2,1)S(1)}, u32[]{:S(2)}, u32[]{:S(2)}) collective-permute-start(bf16[8,128,128]{2,1,0:T(8,128)(2,1)S(1)} %collective-permute-done.21.refs_4_), channel_id=1, source_target_pairs={{0,1},{1,0},{2,3},{3,2},{4,5},{5,4},{6,7},{7,6},{8,9},{9,8},{10,11... | collective-permute-start | bytes 786440 | tf_op jit(solution)/shard_map/ppermute | solution.py:157
  146.2 10.2 %collective-permute-start.24 = (bf16[8,128,128]{2,1,0:T(8,128)(2,1)S(1)}, bf16[8,128,128]{2,1,0:T(8,128)(2,1)S(1)}, u32[]{:S(2)}, u32[]{:S(2)}) collective-permute-start(bf16[8,128,128]{2,1,0:T(8,128)(2,1)S(1)} %collective-permute-done.22.refs_1_), channel_id=1, source_target_pairs={{0,1},{1,0},{2,3},{3,2},{4,5},{5,4},{6,7},{7,6},{8,9},{9,8},{10,11... | collective-permute-start | bytes 786440 | tf_op jit(solution)/shard_map/ppermute | solution.py:157
  154.6 8.5 %collective-permute-start.16 = (bf16[7,128,128]{2,1,0:T(8,128)(2,1)S(1)}, bf16[7,128,128]{2,1,0:T(8,128)(2,1)S(1)}, u32[]{:S(2)}, u32[]{:S(2)}) collective-permute-start(bf16[7,128,128]{2,1,0:T(8,128)(2,1)S(1)} %collective-permute-done.10.refs_8_), channel_id=1, source_target_pairs={{0,1},{1,0},{2,3},{3,2},{4,5},{5,4},{6,7},{7,6},{8,9},{9,8},{10,11... | collective-permute-start | bytes 688136 | tf_op jit(solution)/shard_map/ppermute | solution.py:157
  156.4 7.3 %collective-permute-start.19 = (bf16[7,128,128]{2,1,0:T(8,128)(2,1)}, bf16[7,128,128]{2,1,0:T(8,128)(2,1)S(1)}, u32[]{:S(2)}, u32[]{:S(2)}) collective-permute-start(bf16[7,128,128]{2,1,0:T(8,128)(2,1)} %collective-permute-done.14.refs_12_), channel_id=1, source_target_pairs={{0,1},{1,0},{2,3},{3,2},{4,5},{5,4},{6,7},{7,6},{8,9},{9,8},{10,11... | collective-permute-start | bytes 688136 | tf_op jit(solution)/shard_map/ppermute | solution.py:157
  156.5 6.7 %collective-permute-start.17 = (bf16[7,128,128]{2,1,0:T(8,128)(2,1)S(1)}, bf16[7,128,128]{2,1,0:T(8,128)(2,1)S(1)}, u32[]{:S(2)}, u32[]{:S(2)}) collective-permute-start(bf16[7,128,128]{2,1,0:T(8,128)(2,1)S(1)} %collective-permute-done.15.refs_9_), channel_id=1, source_target_pairs={{0,1},{1,0},{2,3},{3,2},{4,5},{5,4},{6,7},{7,6},{8,9},{9,8},{10,11... | collective-permute-start | bytes 688136 | tf_op jit(solution)/shard_map/ppermute | solution.py:157
  156.9 8.4 %collective-permute-start.33 = (bf16[8,128,128]{2,1,0:T(8,128)(2,1)S(1)}, bf16[8,128,128]{2,1,0:T(8,128)(2,1)S(1)}, u32[]{:S(2)}, u32[]{:S(2)}) collective-permute-start(bf16[8,128,128]{2,1,0:T(8,128)(2,1)S(1)} %collective-permute-done.29.refs_12_), channel_id=1, source_target_pairs={{0,4},{4,0},{8,12},{12,8},{16,20},{20,16},{24,28},{28,24},{1,5},{5... | collective-permute-start | bytes 786440 | tf_op jit(solution)/shard_map/ppermute | solution.py:154
  159.4 7.7 %collective-permute-start.20 = (bf16[7,128,128]{2,1,0:T(8,128)(2,1)S(1)}, bf16[7,128,128]{2,1,0:T(8,128)(2,1)S(1)}, u32[]{:S(2)}, u32[]{:S(2)}) collective-permute-start(bf16[7,128,128]{2,1,0:T(8,128)(2,1)S(1)} %collective-permute-done.18.refs_13_), channel_id=1, source_target_pairs={{0,1},{1,0},{2,3},{3,2},{4,5},{5,4},{6,7},{7,6},{8,9},{9,8},{10,11... | collective-permute-start | bytes 688136 | tf_op jit(solution)/shard_map/ppermute | solution.py:157
  163.1 12.8 %collective-permute-start.31 = (bf16[8,128,128]{2,1,0:T(8,128)(2,1)S(1)}, bf16[8,128,128]{2,1,0:T(8,128)(2,1)S(1)}, u32[]{:S(2)}, u32[]{:S(2)}) collective-permute-start(bf16[8,128,128]{2,1,0:T(8,128)(2,1)S(1)} %collective-permute-done.25.refs_8_), channel_id=1, source_target_pairs={{0,1},{1,0},{2,3},{3,2},{4,5},{5,4},{6,7},{7,6},{8,9},{9,8},{10,11... | collective-permute-start | bytes 786440 | tf_op jit(solution)/shard_map/ppermute | solution.py:157
  163.2 12.7 %collective-permute-start.28 = (bf16[8,128,128]{2,1,0:T(8,128)(2,1)S(1)}, bf16[8,128,128]{2,1,0:T(8,128)(2,1)S(1)}, u32[]{:S(2)}, u32[]{:S(2)}) collective-permute-start(bf16[8,128,128]{2,1,0:T(8,128)(2,1)S(1)} %collective-permute-done.26.refs_5_), channel_id=1, source_target_pairs={{0,1},{1,0},{2,3},{3,2},{4,5},{5,4},{6,7},{7,6},{8,9},{9,8},{10,11... | collective-permute-start | bytes 786440 | tf_op jit(solution)/shard_map/ppermute | solution.py:157
  163.8 12.2 %collective-permute-start.34 = (bf16[8,128,128]{2,1,0:T(8,128)(2,1)S(1)}, bf16[8,128,128]{2,1,0:T(8,128)(2,1)S(1)}, u32[]{:S(2)}, u32[]{:S(2)}) collective-permute-start(bf16[8,128,128]{2,1,0:T(8,128)(2,1)S(1)} %collective-permute-done.29.refs_12_), channel_id=1, source_target_pairs={{0,1},{1,0},{2,3},{3,2},{4,5},{5,4},{6,7},{7,6},{8,9},{9,8},{10,11... | collective-permute-start | bytes 786440 | tf_op jit(solution)/shard_map/ppermute | solution.py:157
  165.3 10.6 %collective-permute-start.32 = (bf16[8,128,128]{2,1,0:T(8,128)(2,1)S(1)}, bf16[8,128,128]{2,1,0:T(8,128)(2,1)S(1)}, u32[]{:S(2)}, u32[]{:S(2)}) collective-permute-start(bf16[8,128,128]{2,1,0:T(8,128)(2,1)S(1)} %collective-permute-done.30.refs_9_), channel_id=1, source_target_pairs={{0,1},{1,0},{2,3},{3,2},{4,5},{5,4},{6,7},{7,6},{8,9},{9,8},{10,11... | collective-permute-start | bytes 786440 | tf_op jit(solution)/shard_map/ppermute | solution.py:157
  167.1 8.9 %collective-permute-start.35 = (bf16[8,128,128]{2,1,0:T(8,128)(2,1)S(1)}, bf16[8,128,128]{2,1,0:T(8,128)(2,1)S(1)}, u32[]{:S(2)}, u32[]{:S(2)}) collective-permute-start(bf16[8,128,128]{2,1,0:T(8,128)(2,1)S(1)} %collective-permute-done.33.refs_13_), channel_id=1, source_target_pairs={{0,1},{1,0},{2,3},{3,2},{4,5},{5,4},{6,7},{7,6},{8,9},{9,8},{10,11... | collective-permute-start | bytes 786440 | tf_op jit(solution)/shard_map/ppermute | solution.py:157
  186.0 7.7 %collective-permute-start.37 = (f32[4,128,128]{2,1,0:T(8,128)}, f32[4,128,128]{2,1,0:T(8,128)S(1)}, u32[]{:S(2)}, u32[]{:S(2)}) collective-permute-start(f32[4,128,128]{2,1,0:T(8,128)} %get-tuple-element.47), channel_id=1, source_target_pairs={{0,2},{1,3},{2,0},{3,1},{4,6},{5,7},{6,4},{7,5},{8,10},{9,11},{10,... | collective-permute-start | bytes 786440 | tf_op jit(solution)/shard_map/ppermute | solution.py:157
  186.1 13.9 %collective-permute-start.38 = (f32[4,128,128]{2,1,0:T(8,128)}, f32[4,128,128]{2,1,0:T(8,128)S(1)}, u32[]{:S(2)}, u32[]{:S(2)}) collective-permute-start(f32[4,128,128]{2,1,0:T(8,128)} %get-tuple-element.48), channel_id=1, source_target_pairs={{0,3},{1,2},{2,1},{3,0},{4,7},{5,6},{6,5},{7,4},{8,11},{9,10},{10,... | collective-permute-start | bytes 786440 | tf_op jit(solution)/shard_map/ppermute | solution.py:157
  (46 other events, 819.6 us)

commit v2 on v1

v2 whole, which is shorter than its diff:
```python
import functools

import jax
import jax.numpy as jnp
from jax import lax
from jax.experimental import pallas as pl
from jax.experimental.pallas import tpu as pltpu
from jax.sharding import PartitionSpec as P

BLOCK = 128
OPERATOR_SLOTS = 4
DENSITY_SLOTS = 7
TAIL = 16

ANY = pl.BlockSpec(memory_space=pl.ANY)
VMEM = pl.BlockSpec(memory_space=pltpu.VMEM)
SMEM = pl.BlockSpec(memory_space=pltpu.SMEM)


def estimate(flops, nbytes):
    return pl.CostEstimate(flops=flops, bytes_accessed=nbytes, transcendentals=0)


def split_kernel(place, density, hamiltonian, metric, *outs):
    spin, row = place[0], place[1]
    for v in (2, 3, 1, 0):
        other_spin = spin if v < 2 else 1 - spin
        other_row = row if v % 2 == 0 else 1 - row
        rows = pl.ds(pl.multiple_of(other_row * BLOCK, BLOCK), BLOCK)
        outs[v][0] = density[other_spin, rows, :]
        outs[v][1] = hamiltonian[other_spin, rows, :]
        outs[v][2] = metric[rows, :]


def slot_rows(slot):
    start = slot * BLOCK
    return pl.ds(start if isinstance(slot, int) else pl.multiple_of(start, BLOCK), BLOCK)


def pack_kernel(sources, col, keep, *refs):
    ins, dens_out, oper_out = refs[:sources], refs[sources], refs[sources + 1]
    per = ins[0].shape[2] // BLOCK
    here = col[0]
    lane = lax.broadcasted_iota(jnp.int32, (TAIL, BLOCK), 1)
    plans = (
        (dens_out, DENSITY_SLOTS, ((0, 0),)),
        (oper_out, 2 * OPERATOR_SLOTS, ((1, 0), (2, OPERATOR_SLOTS))),
    )
    for out, slots, mats in plans:
        out[...] = jnp.zeros_like(out)
        tail = jnp.zeros((TAIL, BLOCK), jnp.int32)
        for mat, first in mats:
            flags = [[keep[m, mat, b] for b in range(per)] for m in range(sources)]
            counts = [functools.reduce(lambda p, q: p + q, f) for f in flags]
            for m in range(sources):
                slot = jnp.int32(first)
                for n in range(sources):
                    if n != m:
                        slot += jnp.where((here ^ n) < (here ^ m), counts[n], 0)
                for b in range(per):

                    @pl.when(flags[m][b] > 0)
                    def _(slot=slot, mat=mat, m=m, b=b, out=out):
                        out[slot_rows(slot), :] = ins[m][mat, :, b * BLOCK : (b + 1) * BLOCK]

                    target = jnp.where(flags[m][b] > 0, slot, -1)
                    tail = jnp.where(lane == target, (here ^ m) * per + b, tail)
                    slot += flags[m][b]
        out[slots * BLOCK :, :] = tail.astype(jnp.float32).astype(out.dtype)


def row_of(place, key, layers):
    shift, flip, other = key
    layer = place[0] - shift
    layer = jnp.where(layer < 0, layer + layers, layer)
    side = place[1] if flip == 0 else 1 - place[1]
    half = place[2] if other == 0 else 1 - place[2]
    return (layer * 2 + side) * 2 + half


def fetch(place, keys, layers, bufs, held, sems):
    copies = [
        pltpu.make_async_copy(buf, held.at[row_of(place, key, layers)], sems.at[n])
        for n, (key, buf) in enumerate(zip(keys, bufs, strict=True))
    ]
    for copy in copies:
        copy.start()
    return copies


def tail_of(block):
    return block.astype(jnp.float32)[:1].astype(jnp.int32)


def first_kernel(keys, layers, place, own, *refs):
    count = len(keys)
    bufs, out, held, acc, tails, cols, sems = refs[:count], *refs[count:]
    nblk = held.shape[0]
    copies = fetch(place, keys, layers, bufs, held, sems)
    acc[...] = jnp.zeros_like(acc)
    tails[nblk : nblk + 1, :] = tail_of(own[2 * OPERATOR_SLOTS * BLOCK :, :])
    for copy in copies:
        copy.wait()
    for k in range(nblk):
        tails[k : k + 1, :] = tail_of(held[k, DENSITY_SLOTS * BLOCK :, :])
    pltpu.sync_copy(tails, cols)
    for u in range(2 * OPERATOR_SLOTS):
        k = cols[nblk, u]
        left = own[u * BLOCK : (u + 1) * BLOCK, :]
        base = (u // OPERATOR_SLOTS) * nblk
        for t in range(DENSITY_SLOTS):
            right = held[k, t * BLOCK : (t + 1) * BLOCK, :]
            acc[base + cols[k, t]] += jnp.dot(left, right, preferred_element_type=jnp.float32)
    out[...] = acc[...].astype(out.dtype)


def second_kernel(keys, layers, place, prods, *refs):
    count = len(keys)
    bufs, outs, (held, acc, tails, cols, sems) = refs[:count], refs[count : count + 4], refs[count + 4 :]
    nblk = held.shape[0]
    copies = fetch(place, keys, layers, bufs, held, sems)
    acc[...] = jnp.zeros_like(acc)
    for copy in copies:
        copy.wait()
    for k in range(nblk):
        tails[k : k + 1, :] = tail_of(held[k, 2 * OPERATOR_SLOTS * BLOCK :, :])
    pltpu.sync_copy(tails, cols)

    def step(k, carry):
        hp, sp = prods[k], prods[nblk + k]
        for t in range(OPERATOR_SLOTS):
            u = OPERATOR_SLOTS + t
            met = held[k, u * BLOCK : (u + 1) * BLOCK, :]
            ham = held[k, t * BLOCK : (t + 1) * BLOCK, :]
            acc[cols[k, u]] += jnp.dot(hp, met, preferred_element_type=jnp.float32)
            acc[cols[k, t]] -= jnp.dot(sp, ham, preferred_element_type=jnp.float32)
        return carry

    lax.fori_loop(0, nblk, step, 0)
    per = outs[0].shape[0]
    for v in range(4):
        for b in range(per):
            outs[v][b] = acc[place[3 + v] * per + b]


def join_kernel(place, keep, *refs):
    ins, out = refs[:4], refs[4]
    per = ins[0].shape[0]
    for v in range(4):
        spin = place[0] if v < 2 else 1 - place[0]
        row = place[1] if v % 2 == 0 else 1 - place[1]
        rows = pl.ds(pl.multiple_of(row * BLOCK, BLOCK), BLOCK)
        for b in range(per):
            value = ins[v][b]
            out[spin, rows, b * BLOCK : (b + 1) * BLOCK] = jnp.where(
                keep[row, b] > 0, value, jnp.zeros_like(value)
            )


def body(nrow, ncol, hamiltonian, metric, density, ham_keep, met_keep, dens_keep, grad_keep):
    layers, half = nrow // 2, ncol // 2
    per = ham_keep.shape[1]
    nblk = ham_keep.shape[0] * nrow
    width = per * BLOCK
    bf16, f32, i32 = jnp.bfloat16, jnp.float32, jnp.int32

    def by_row(pairs):
        return lambda a: lax.ppermute(a, "row", pairs)

    def by_mask(mask):
        return lambda a: lax.ppermute(a, "col", [(c, c ^ mask) for c in range(ncol)])

    def variant(mask):
        return (2 if mask >= half else 0) + (mask & 1)

    up = by_row([(r, (r + 2) % nrow) for r in range(nrow)])
    across = by_row([(r, r ^ 1) for r in range(nrow)])
    twin = by_mask(1)

    row, col = lax.axis_index("row").astype(i32), lax.axis_index("col").astype(i32)
    spin, part = col // half, col % 2
    z, x = row // 2, row % 2
    masks = (0, 1, half, half + 1)
    dens_rows, oper_rows = DENSITY_SLOTS * BLOCK + TAIL, 2 * OPERATOR_SLOTS * BLOCK + TAIL

    keeps = (jnp.stack([dens_keep, ham_keep, met_keep]) > 0).astype(i32)

    split = pl.pallas_call(
        split_kernel,
        out_shape=[jax.ShapeDtypeStruct((3, BLOCK, width), bf16)] * 4,
        in_specs=[SMEM, VMEM, VMEM, VMEM],
        out_specs=[VMEM] * 4,
        cost_estimate=estimate(0, 24 * BLOCK * width * 2),
        name="split",
    )(jnp.stack([spin, part]), density, hamiltonian, metric)
    got = {m: by_mask(m)(split[variant(m)]) for m in reversed(range(1, ncol))}
    got[0] = split[0]
    keep_rows = [lax.dynamic_index_in_dim(keeps, part ^ d, 1, keepdims=False) for d in (0, 1)]
    keep_got = jnp.stack(
        [keep_rows[0]] + [by_mask(m)(keep_rows[m & 1]) for m in range(1, ncol)]
    )

    dens, oper = pl.pallas_call(
        functools.partial(pack_kernel, ncol),
        out_shape=[
            jax.ShapeDtypeStruct((dens_rows, BLOCK), bf16),
            jax.ShapeDtypeStruct((oper_rows, BLOCK), bf16),
        ],
        in_specs=[SMEM, SMEM] + [VMEM] * ncol,
        out_specs=[VMEM, VMEM],
        cost_estimate=estimate(0, ncol * 3 * BLOCK * width * 2),
        name="pack",
    )(col[None], keep_got, *[got[m] for m in range(ncol)])

    dens_bufs, oper_bufs = {}, {}
    curs = [dens, oper]
    for t in range(layers):
        nexts = []
        for bufs, cur in zip((dens_bufs, oper_bufs), curs, strict=True):
            side = across(cur)
            if t < layers - 1:
                new, side = lax.optimization_barrier((up(cur), side))
                nexts.append(new)
            bufs[t, 0, 0], bufs[t, 1, 0] = cur, side
            bufs[t, 0, 1], bufs[t, 1, 1] = twin(cur), twin(side)
        curs = nexts
    keys = list(dens_bufs)

    place = jnp.stack([z, x, part] + [col ^ m for m in masks])

    prods = pl.pallas_call(
        functools.partial(first_kernel, keys, layers),
        out_shape=jax.ShapeDtypeStruct((2 * nblk, BLOCK, BLOCK), bf16),
        in_specs=[SMEM, VMEM] + [ANY] * len(keys),
        out_specs=VMEM,
        scratch_shapes=[
            pltpu.VMEM((nblk, dens_rows, BLOCK), bf16),
            pltpu.VMEM((2 * nblk, BLOCK, BLOCK), f32),
            pltpu.VMEM((nblk + 8, BLOCK), i32),
            pltpu.SMEM((nblk + 8, BLOCK), i32),
            pltpu.SemaphoreType.DMA((len(keys),)),
        ],
        cost_estimate=estimate(56 * 2 * BLOCK**3, nblk * 9 * BLOCK * BLOCK * 2),
        name="first",
    )(place, oper, *[dens_bufs[k] for k in keys])

    outs = pl.pallas_call(
        functools.partial(second_kernel, keys, layers),
        out_shape=[jax.ShapeDtypeStruct((per, BLOCK, BLOCK), f32)] * 4,
        in_specs=[SMEM, VMEM] + [ANY] * len(keys),
        out_specs=[VMEM] * 4,
        scratch_shapes=[
            pltpu.VMEM((nblk, oper_rows, BLOCK), bf16),
            pltpu.VMEM((nblk, BLOCK, BLOCK), f32),
            pltpu.VMEM((nblk, BLOCK), i32),
            pltpu.SMEM((nblk, BLOCK), i32),
            pltpu.SemaphoreType.DMA((len(keys),)),
        ],
        cost_estimate=estimate(nblk * 16 * BLOCK**3, nblk * 12 * BLOCK * BLOCK * 2),
        name="second",
    )(place, prods, *[oper_bufs[k] for k in keys])

    back = [outs[0]] + [by_mask(m)(o) for m, o in zip(masks[1:], outs[1:], strict=True)]
    return pl.pallas_call(
        join_kernel,
        out_shape=jax.ShapeDtypeStruct((2, 2 * BLOCK, width), f32),
        in_specs=[SMEM, SMEM] + [VMEM] * 4,
        out_specs=VMEM,
        cost_estimate=estimate(0, 8 * BLOCK * width * 4),
        name="join",
    )(jnp.stack([spin, part]), grad_keep, *back)


def solution(mesh):
    grid = P("row", "col")
    spins = P(None, "row", "col")
    return jax.shard_map(
        functools.partial(body, mesh.shape["row"], mesh.shape["col"]),
        mesh=mesh,
        in_specs=(spins, grid, spins, grid, grid, grid, grid),
        out_specs=spins,
        check_vma=False,
    )
```

time: 203 us -> 126 us (0.62)
  Pallas kernels: 67.6 us -> 22.2 us
  blocking collectives: 45.1 us -> 0 us
  starting transfers between devices: 25.7 us -> 37.2 us
  waiting for transfers between devices: 52.4 us -> 60.2 us
  local copies, waits for them, and re-layouts: 7.81 us -> 4.76 us
  other arithmetic: 3.72 us -> 1.24 us
    pallas_call x1, Pallas kernels: 49.5 us -> 2.48 us  [body(): pl.pallas_call(split_kernel, out_shape=[jax.ShapeDtypeStruct((3, BLOCK, w...]
    all_gather x1 -> x0, blocking collectives: 45.1 us -> none  [body(): spread = lax.all_gather(keeps, ('row', 'col'))]
    ppermute x25, starting transfers between devices: 19.2 us -> 27.6 us  [by_mask(): lax.ppermute(a, 'col', [(c, c ^ mask) for c in range(ncol)])]
    ppermute x14, waiting for transfers between devices: 24.6 us -> 32 us  [by_row(): return lambda a: lax.ppermute(a, 'row', pairs)]
    ppermute x14, starting transfers between devices: 6.54 us -> 9.57 us  [by_row(): return lambda a: lax.ppermute(a, 'row', pairs)]
    unnamed x80 -> x76, local copies, waits for them, and re-layouts: 4.64 us -> 4.07 us
  transfers between devices with their start and end apart: 39 -> 39, of which waited for: 14 -> 15; matrix products, arithmetic and copies ran while one was open for 3% -> 1% of each run, Pallas kernels for 2% -> 5%
where the time goes in v2:
time: 126 us
  waiting for transfers between devices  60.2 us (48%)
  starting transfers between devices  37.2 us (30%)
  Pallas kernels  22.2 us (18%)
  local copies, waits for them, and re-layouts  4.76 us (4%)
    ppermute x14, waiting for transfers between devices, by_row(): return lambda a: lax.ppermute(a, 'row', pairs)  32 us
    ppermute x25, waiting for transfers between devices, by_mask(): lax.ppermute(a, 'col', [(c, c ^ mask) for c in range(ncol)])  28.2 us
    ppermute x25, starting transfers between devices, by_mask(): lax.ppermute(a, 'col', [(c, c ^ mask) for c in range(ncol)])  27.6 us
    ppermute x14, starting transfers between devices, by_row(): return lambda a: lax.ppermute(a, 'row', pairs)  9.57 us
    pallas_call x1, Pallas kernels, body(): pl.pallas_call(functools.partial(second_kernel, keys, layers), out_shape=...  9.06 us
    pallas_call x1, Pallas kernels, body(): pl.pallas_call(functools.partial(first_kernel, keys, layers), out_shape=j...  5.74 us
    unnamed x76, local copies, waits for them, and re-layouts  4.07 us
    pallas_call x1, Pallas kernels, body(): pl.pallas_call(functools.partial(pack_kernel, ncol), out_shape=[jax.Shape...  2.61 us
  transfers between devices with their start and end apart: 39, of which 15 were waited for; matrix products, arithmetic and copies ran while one was open for 1% of the time, Pallas kernels for 5%

profile of v2, /device:TPU:1, one launch (start us, length us, event | category | flops | bytes accessed | tf_op | source)
XLA Modules:
  0.0 126.0 jit_solution(1183372851412187781)
XLA Ops:
  0.6 2.5 %split.1 = (bf16[3,128,512]{2,1,0:T(8,128)(2,1)}, bf16[3,128,512]{2,1,0:T(8,128)(2,1)}, bf16[3,128,512]{2,1,0:T(8,128)(2,1)}, bf16[3,128,512]{2,1,0:T(8,128)(2,1)}) custom-call(s32[2]{0:T(128)} %pad_add_fusion.1.place, bf16[2,256,512]{2,1,0:T(8,128)(2,1)} %density.1, bf16[2,256,512]{2,1,0:T(8,128)(2,1)} %hamiltonian.1, bf16[256,512]{1,0:T(8,128)(2,1)} %metric.1), custom_call_target="tpu_custom_call" | custom-call | bytes 3145728 | tf_op jit(solution)/shard_map/split/pallas_call | solution.py:188
  3.2 2.7 %collective-permute-start.4 = (bf16[3,128,512]{2,1,0:T(8,128)(2,1)}, bf16[3,128,512]{2,1,0:T(8,128)(2,1)S(1)}, u32[]{:S(2)}, u32[]{:S(2)}) collective-permute-start(bf16[3,128,512]{2,1,0:T(8,128)(2,1)} %get-tuple-element.29), channel_id=1, source_target_pairs={{0,2},{1,3},{2,0},{3,1},{4,6},{5,7},{6,4},{7,5},{8,10},{9,11},{10,... | collective-permute-start | bytes 1179656 | tf_op jit(solution)/shard_map/ppermute | solution.py:171
  6.7 1.7 %collective-permute-start.1 = (s32[3,4]{1,0:T(4,128)S(1)}, s32[3,4]{1,0:T(4,128)S(1)}, u32[]{:S(2)}, u32[]{:S(2)}) collective-permute-start(s32[3,4]{1,0:T(4,128)S(1)} %bitcast.24), channel_id=1, source_target_pairs={{0,2},{1,3},{2,0},{3,1},{4,6},{5,7},{6,4},{7,5},{8,10},{9,11},{10,... | collective-permute-start | bytes 152 | tf_op jit(solution)/shard_map/ppermute | solution.py:171
  8.7 15.2 %collective-permute-done.1 = s32[3,4]{1,0:T(4,128)S(1)} collective-permute-done((s32[3,4]{1,0:T(4,128)S(1)}, s32[3,4]{1,0:T(4,128)S(1)}, u32[]{:S(2)}, u32[]{:S(2)}) %collective-permute-start.1) | collective-permute-done | bytes 80 | tf_op jit(solution)/shard_map/ppermute | solution.py:171
  27.1 2.6 %pack.1 = (bf16[912,128]{1,0:T(8,128)(2,1)}, bf16[1040,128]{1,0:T(8,128)(2,1)}) custom-call(s32[1]{0:T(128)} %bitcast.4.col, s32[4,3,4]{2,1,0:T(4,128)} %pad_add_fusion.keep, bf16[3,128,512]{2,1,0:T(8,128)(2,1)} %get-tuple-element.27.refs_0_, bf16[3,128,512]{2,1,0:T(8,128)(2,1)} %copy-done, bf16[3,128,512]{2,1,0:T(8,128)(2,1)} %copy-done.1, ...), custom_call_target="tpu_custom_call" | custom-call | bytes 1572864 | tf_op jit(solution)/shard_map/pack/pallas_call | solution.py:203
  29.7 1.4 %collective-permute-start.7 = (bf16[912,128]{1,0:T(8,128)(2,1)}, bf16[912,128]{1,0:T(8,128)(2,1)S(1)}, u32[]{:S(2)}, u32[]{:S(2)}) collective-permute-start(bf16[912,128]{1,0:T(8,128)(2,1)} %get-tuple-element.32.refs_0_), channel_id=1, source_target_pairs={{0,4},{4,0},{8,12},{12,8},{16,20},{20,16},{24,28},{28,24},{1,5},{5... | collective-permute-start | bytes 700424 | tf_op jit(solution)/shard_map/ppermute | solution.py:168
  31.1 1.3 %collective-permute-start.6 = (bf16[912,128]{1,0:T(8,128)(2,1)}, bf16[912,128]{1,0:T(8,128)(2,1)S(1)}, u32[]{:S(2)}, u32[]{:S(2)}) collective-permute-start(bf16[912,128]{1,0:T(8,128)(2,1)} %get-tuple-element.32.refs_0_), channel_id=1, source_target_pairs={{0,8},{4,12},{8,16},{12,20},{16,24},{20,28},{24,0},{28,4},{1,9},{5... | collective-permute-start | bytes 700424 | tf_op jit(solution)/shard_map/ppermute | solution.py:168
  32.7 1.3 %collective-permute-start.21 = (bf16[1040,128]{1,0:T(8,128)(2,1)}, bf16[1040,128]{1,0:T(8,128)(2,1)S(1)}, u32[]{:S(2)}, u32[]{:S(2)}) collective-permute-start(bf16[1040,128]{1,0:T(8,128)(2,1)} %get-tuple-element.31.own.refs_0_), channel_id=1, source_target_pairs={{0,8},{4,12},{8,16},{12,20},{16,24},{20,28},{24,0},{28,4},{1,9},{5... | collective-permute-start | bytes 798728 | tf_op jit(solution)/shard_map/ppermute | solution.py:168
  34.0 2.9 %collective-permute-done.7.refs_1_ = bf16[912,128]{1,0:T(8,128)(2,1)S(1)} collective-permute-done((bf16[912,128]{1,0:T(8,128)(2,1)}, bf16[912,128]{1,0:T(8,128)(2,1)S(1)}, u32[]{:S(2)}, u32[]{:S(2)}) %collective-permute-start.7) | collective-permute-done | bytes 233504 | tf_op jit(solution)/shard_map/ppermute | solution.py:168
  36.9 3.1 %collective-permute-done.6.refs_4_ = bf16[912,128]{1,0:T(8,128)(2,1)S(1)} collective-permute-done((bf16[912,128]{1,0:T(8,128)(2,1)}, bf16[912,128]{1,0:T(8,128)(2,1)S(1)}, u32[]{:S(2)}, u32[]{:S(2)}) %collective-permute-start.6) | collective-permute-done | bytes 233504 | tf_op jit(solution)/shard_map/ppermute | solution.py:168
  40.4 2.1 %collective-permute-done.22.refs_1_ = bf16[1040,128]{1,0:T(8,128)(2,1)S(1)} collective-permute-done((bf16[1040,128]{1,0:T(8,128)(2,1)}, bf16[1040,128]{1,0:T(8,128)(2,1)S(1)}, u32[]{:S(2)}, u32[]{:S(2)}) %collective-permute-start.22) | collective-permute-done | bytes 266272 | tf_op jit(solution)/shard_map/ppermute | solution.py:168
  42.6 3.1 %collective-permute-done.21.refs_4_ = bf16[1040,128]{1,0:T(8,128)(2,1)S(1)} collective-permute-done((bf16[1040,128]{1,0:T(8,128)(2,1)}, bf16[1040,128]{1,0:T(8,128)(2,1)S(1)}, u32[]{:S(2)}, u32[]{:S(2)}) %collective-permute-start.21) | collective-permute-done | bytes 266272 | tf_op jit(solution)/shard_map/ppermute | solution.py:168
  46.1 1.7 %collective-permute-start.23 = (bf16[1040,128]{1,0:T(8,128)(2,1)}, bf16[1040,128]{1,0:T(8,128)(2,1)S(1)}, u32[]{:S(2)}, u32[]{:S(2)}) collective-permute-start(bf16[1040,128]{1,0:T(8,128)(2,1)} %get-tuple-element.31.own.refs_0_), channel_id=1, source_target_pairs={{0,1},{1,0},{2,3},{3,2},{4,5},{5,4},{6,7},{7,6},{8,9},{9,8},{10,11... | collective-permute-start | bytes 798728 | tf_op jit(solution)/shard_map/ppermute | solution.py:171
  47.8 1.3 %collective-permute-start.10 = (bf16[912,128]{1,0:T(8,128)(2,1)S(1)}, bf16[912,128]{1,0:T(8,128)(2,1)S(1)}, u32[]{:S(2)}, u32[]{:S(2)}) collective-permute-start(bf16[912,128]{1,0:T(8,128)(2,1)S(1)} %collective-permute-done.6.refs_4_), channel_id=1, source_target_pairs={{0,8},{4,12},{8,16},{12,20},{16,24},{20,28},{24,0},{28,4},{1,9},{5... | collective-permute-start | bytes 700424 | tf_op jit(solution)/shard_map/ppermute | solution.py:168
  49.4 10.0 %collective-permute-done.10.refs_8_ = bf16[912,128]{1,0:T(8,128)(2,1)S(1)} collective-permute-done((bf16[912,128]{1,0:T(8,128)(2,1)S(1)}, bf16[912,128]{1,0:T(8,128)(2,1)S(1)}, u32[]{:S(2)}, u32[]{:S(2)}) %collective-permute-start.10) | collective-permute-done | bytes 233504 | tf_op jit(solution)/shard_map/ppermute | solution.py:168
  59.4 2.4 %collective-permute-start.9 = (bf16[912,128]{1,0:T(8,128)(2,1)S(1)}, bf16[912,128]{1,0:T(8,128)(2,1)S(1)}, u32[]{:S(2)}, u32[]{:S(2)}) collective-permute-start(bf16[912,128]{1,0:T(8,128)(2,1)S(1)} %collective-permute-done.7.refs_1_), channel_id=1, source_target_pairs={{0,1},{1,0},{2,3},{3,2},{4,5},{5,4},{6,7},{7,6},{8,9},{9,8},{10,11... | collective-permute-start | bytes 700424 | tf_op jit(solution)/shard_map/ppermute | solution.py:171
  61.8 1.0 collective-permute-start.15
  64.1 5.0 %collective-permute-done.15.refs_9_ = bf16[912,128]{1,0:T(8,128)(2,1)S(1)} collective-permute-done((bf16[912,128]{1,0:T(8,128)(2,1)S(1)}, bf16[912,128]{1,0:T(8,128)(2,1)S(1)}, u32[]{:S(2)}, u32[]{:S(2)}) %collective-permute-start.15) | collective-permute-done | bytes 233504 | tf_op jit(solution)/shard_map/ppermute | solution.py:168
  69.0 1.3 %collective-permute-start.27 = (bf16[1040,128]{1,0:T(8,128)(2,1)S(1)}, bf16[1040,128]{1,0:T(8,128)(2,1)S(1)}, u32[]{:S(2)}, u32[]{:S(2)}) collective-permute-start(bf16[1040,128]{1,0:T(8,128)(2,1)S(1)} %collective-permute-done.21.refs_4_), channel_id=1, source_target_pairs={{0,1},{1,0},{2,3},{3,2},{4,5},{5,4},{6,7},{7,6},{8,9},{9,8},{10,11... | collective-permute-start | bytes 798728 | tf_op jit(solution)/shard_map/ppermute | solution.py:171
  70.3 1.3 %collective-permute-done.14.refs_12_ = bf16[912,128]{1,0:T(8,128)(2,1)S(1)} collective-permute-done((bf16[912,128]{1,0:T(8,128)(2,1)S(1)}, bf16[912,128]{1,0:T(8,128)(2,1)S(1)}, u32[]{:S(2)}, u32[]{:S(2)}) %collective-permute-start.14) | collective-permute-done | bytes 233504 | tf_op jit(solution)/shard_map/ppermute | solution.py:168
  71.7 2.6 %collective-permute-start.12 = (bf16[912,128]{1,0:T(8,128)(2,1)S(1)}, bf16[912,128]{1,0:T(8,128)(2,1)S(1)}, u32[]{:S(2)}, u32[]{:S(2)}) collective-permute-start(bf16[912,128]{1,0:T(8,128)(2,1)S(1)} %collective-permute-done.6.refs_4_), channel_id=1, source_target_pairs={{0,1},{1,0},{2,3},{3,2},{4,5},{5,4},{6,7},{7,6},{8,9},{9,8},{10,11... | collective-permute-start | bytes 700424 | tf_op jit(solution)/shard_map/ppermute | solution.py:171
  75.6 1.8 %collective-permute-done.29.refs_12_ = bf16[1040,128]{1,0:T(8,128)(2,1)S(1)} collective-permute-done((bf16[1040,128]{1,0:T(8,128)(2,1)S(1)}, bf16[1040,128]{1,0:T(8,128)(2,1)S(1)}, u32[]{:S(2)}, u32[]{:S(2)}) %collective-permute-start.29) | collective-permute-done | bytes 266272 | tf_op jit(solution)/shard_map/ppermute | solution.py:168
  78.9 2.1 %collective-permute-start.16 = (bf16[912,128]{1,0:T(8,128)(2,1)S(1)}, bf16[912,128]{1,0:T(8,128)(2,1)S(1)}, u32[]{:S(2)}, u32[]{:S(2)}) collective-permute-start(bf16[912,128]{1,0:T(8,128)(2,1)S(1)} %collective-permute-done.10.refs_8_), channel_id=1, source_target_pairs={{0,1},{1,0},{2,3},{3,2},{4,5},{5,4},{6,7},{7,6},{8,9},{9,8},{10,11... | collective-permute-start | bytes 700424 | tf_op jit(solution)/shard_map/ppermute | solution.py:171
  81.4 1.6 %collective-permute-done.18.refs_13_ = bf16[912,128]{1,0:T(8,128)(2,1)S(1)} collective-permute-done((bf16[912,128]{1,0:T(8,128)(2,1)S(1)}, bf16[912,128]{1,0:T(8,128)(2,1)S(1)}, u32[]{:S(2)}, u32[]{:S(2)}) %collective-permute-start.18) | collective-permute-done | bytes 233504 | tf_op jit(solution)/shard_map/ppermute | solution.py:168
  83.1 4.4 %collective-permute-start.20 = (bf16[912,128]{1,0:T(8,128)(2,1)S(1)}, bf16[912,128]{1,0:T(8,128)(2,1)S(1)}, u32[]{:S(2)}, u32[]{:S(2)}) collective-permute-start(bf16[912,128]{1,0:T(8,128)(2,1)S(1)} %collective-permute-done.18.refs_13_), channel_id=1, source_target_pairs={{0,1},{1,0},{2,3},{3,2},{4,5},{5,4},{6,7},{7,6},{8,9},{9,8},{10,11... | collective-permute-start | bytes 700424 | tf_op jit(solution)/shard_map/ppermute | solution.py:171
  88.8 2.4 %collective-permute-start.32 = (bf16[1040,128]{1,0:T(8,128)(2,1)S(1)}, bf16[1040,128]{1,0:T(8,128)(2,1)}, u32[]{:S(2)}, u32[]{:S(2)}) collective-permute-start(bf16[1040,128]{1,0:T(8,128)(2,1)S(1)} %collective-permute-done.30.refs_9_), channel_id=1, source_target_pairs={{0,1},{1,0},{2,3},{3,2},{4,5},{5,4},{6,7},{7,6},{8,9},{9,8},{10,11... | collective-permute-start | bytes 798728 | tf_op jit(solution)/shard_map/ppermute | solution.py:171
  92.7 5.7 %first.1.prods = bf16[32,128,128]{2,1,0:T(8,128)(2,1)} custom-call(s32[7]{0:T(128)} %stack.70.place, bf16[1040,128]{1,0:T(8,128)(2,1)} %get-tuple-element.31.own.refs_0_, bf16[912,128]{1,0:T(8,128)(2,1)} %get-tuple-element.32.refs_0_, bf16[912,128]{1,0:T(8,128)(2,1)} %copy-done.19, bf16[912,128]{1,0:T(8,128)(2,1)} %copy-done.23, ...), custom_call_target="tpu_custom_call" | custom-call | flops 234881024 | bytes 4718592 | tf_op jit(solution)/shard_map/first/pallas_call | solution.py:231
  99.5 9.1 %second.1 = (f32[4,128,128]{2,1,0:T(8,128)}, f32[4,128,128]{2,1,0:T(8,128)}, f32[4,128,128]{2,1,0:T(8,128)}, f32[4,128,128]{2,1,0:T(8,128)}) custom-call(s32[7]{0:T(128)} %stack.70.place, bf16[32,128,128]{2,1,0:T(8,128)(2,1)} %first.1.prods, bf16[1040,128]{1,0:T(8,128)(2,1)} %get-tuple-element.31.own.refs_0_, bf16[1040,128]{1,0:T(8,128)(2,1)} %copy-done.3, ...), custom_call_target="tpu_custom_call" | custom-call | flops 536870912 | bytes 6291456 | tf_op jit(solution)/shard_map/second/pallas_call | solution.py:247
  109.1 1.1 collective-permute-start.37
  110.8 6.4 %collective-permute-done.37.refs_2_ = f32[4,128,128]{2,1,0:T(8,128)S(1)} collective-permute-done((f32[4,128,128]{2,1,0:T(8,128)}, f32[4,128,128]{2,1,0:T(8,128)S(1)}, u32[]{:S(2)}, u32[]{:S(2)}) %collective-permute-start.37) | collective-permute-done | bytes 262176 | tf_op jit(solution)/shard_map/ppermute | solution.py:171
  117.2 5.8 %collective-permute-done.38.refs_3_ = f32[4,128,128]{2,1,0:T(8,128)S(1)} collective-permute-done((f32[4,128,128]{2,1,0:T(8,128)}, f32[4,128,128]{2,1,0:T(8,128)S(1)}, u32[]{:S(2)}, u32[]{:S(2)}) %collective-permute-start.38) | collective-permute-done | bytes 262176 | tf_op jit(solution)/shard_map/ppermute | solution.py:171
  123.7 2.3 %join.1 = f32[2,256,512]{2,1,0:T(8,128)} custom-call(s32[2]{0:T(128)} %pad_add_fusion.1.place, s32[2,4]{1,0:T(2,128)} %keep.1, f32[4,128,128]{2,1,0:T(8,128)} %get-tuple-element.45.refs_0_, f32[4,128,128]{2,1,0:T(8,128)} %copy-done.16, f32[4,128,128]{2,1,0:T(8,128)} %copy-done.17, f32[4,128,128]{2,1,0:T(8,128)} %copy-done.18), custom_call_target="tpu_custom_call" | custom-call | bytes 2097152 | tf_op jit(solution)/shard_map/join/pallas_call | solution.py:264
  (133 shorter events, 16.6 us)
Async XLA Ops:
  3.1 22.9 %collective-permute-start.3 = (bf16[3,128,512]{2,1,0:T(8,128)(2,1)}, bf16[3,128,512]{2,1,0:T(8,128)(2,1)S(1)}, u32[]{:S(2)}, u32[]{:S(2)}) collective-permute-start(bf16[3,128,512]{2,1,0:T(8,128)(2,1)} %get-tuple-element.28), channel_id=1, source_target_pairs={{0,1},{1,0},{2,3},{3,2},{4,5},{5,4},{6,7},{7,6},{8,9},{9,8},{10,11... | collective-permute-start | bytes 1179656 | tf_op jit(solution)/shard_map/ppermute | solution.py:171
  3.2 22.9 %collective-permute-start.4 = (bf16[3,128,512]{2,1,0:T(8,128)(2,1)}, bf16[3,128,512]{2,1,0:T(8,128)(2,1)S(1)}, u32[]{:S(2)}, u32[]{:S(2)}) collective-permute-start(bf16[3,128,512]{2,1,0:T(8,128)(2,1)} %get-tuple-element.29), channel_id=1, source_target_pairs={{0,2},{1,3},{2,0},{3,1},{4,6},{5,7},{6,4},{7,5},{8,10},{9,11},{10,... | collective-permute-start | bytes 1179656 | tf_op jit(solution)/shard_map/ppermute | solution.py:171
  5.9 20.2 %collective-permute-start.5 = (bf16[3,128,512]{2,1,0:T(8,128)(2,1)}, bf16[3,128,512]{2,1,0:T(8,128)(2,1)S(1)}, u32[]{:S(2)}, u32[]{:S(2)}) collective-permute-start(bf16[3,128,512]{2,1,0:T(8,128)(2,1)} %get-tuple-element.30), channel_id=1, source_target_pairs={{0,3},{1,2},{2,1},{3,0},{4,7},{5,6},{6,5},{7,4},{8,11},{9,10},{10,... | collective-permute-start | bytes 1179656 | tf_op jit(solution)/shard_map/ppermute | solution.py:171
  6.7 17.3 %collective-permute-start.1 = (s32[3,4]{1,0:T(4,128)S(1)}, s32[3,4]{1,0:T(4,128)S(1)}, u32[]{:S(2)}, u32[]{:S(2)}) collective-permute-start(s32[3,4]{1,0:T(4,128)S(1)} %bitcast.24), channel_id=1, source_target_pairs={{0,2},{1,3},{2,0},{3,1},{4,6},{5,7},{6,4},{7,5},{8,10},{9,11},{10,... | collective-permute-start | bytes 152 | tf_op jit(solution)/shard_map/ppermute | solution.py:171
  8.4 16.3 %collective-permute-start.2 = (s32[3,4]{1,0:T(4,128)S(1)}, s32[3,4]{1,0:T(4,128)S(1)}, u32[]{:S(2)}, u32[]{:S(2)}) collective-permute-start(s32[3,4]{1,0:T(4,128)S(1)} %bitcast.22), channel_id=1, source_target_pairs={{0,3},{1,2},{2,1},{3,0},{4,7},{5,6},{6,5},{7,4},{8,11},{9,10},{10,... | collective-permute-start | bytes 152 | tf_op jit(solution)/shard_map/ppermute | solution.py:171
  29.7 7.2 %collective-permute-start.7 = (bf16[912,128]{1,0:T(8,128)(2,1)}, bf16[912,128]{1,0:T(8,128)(2,1)S(1)}, u32[]{:S(2)}, u32[]{:S(2)}) collective-permute-start(bf16[912,128]{1,0:T(8,128)(2,1)} %get-tuple-element.32.refs_0_), channel_id=1, source_target_pairs={{0,4},{4,0},{8,12},{12,8},{16,20},{20,16},{24,28},{28,24},{1,5},{5... | collective-permute-start | bytes 700424 | tf_op jit(solution)/shard_map/ppermute | solution.py:168
  31.1 8.8 %collective-permute-start.6 = (bf16[912,128]{1,0:T(8,128)(2,1)}, bf16[912,128]{1,0:T(8,128)(2,1)S(1)}, u32[]{:S(2)}, u32[]{:S(2)}) collective-permute-start(bf16[912,128]{1,0:T(8,128)(2,1)} %get-tuple-element.32.refs_0_), channel_id=1, source_target_pairs={{0,8},{4,12},{8,16},{12,20},{16,24},{20,28},{24,0},{28,4},{1,9},{5... | collective-permute-start | bytes 700424 | tf_op jit(solution)/shard_map/ppermute | solution.py:168
  32.4 10.1 %collective-permute-start.22 = (bf16[1040,128]{1,0:T(8,128)(2,1)}, bf16[1040,128]{1,0:T(8,128)(2,1)S(1)}, u32[]{:S(2)}, u32[]{:S(2)}) collective-permute-start(bf16[1040,128]{1,0:T(8,128)(2,1)} %get-tuple-element.31.own.refs_0_), channel_id=1, source_target_pairs={{0,4},{4,0},{8,12},{12,8},{16,20},{20,16},{24,28},{28,24},{1,5},{5... | collective-permute-start | bytes 798728 | tf_op jit(solution)/shard_map/ppermute | solution.py:168
  32.7 13.0 %collective-permute-start.21 = (bf16[1040,128]{1,0:T(8,128)(2,1)}, bf16[1040,128]{1,0:T(8,128)(2,1)S(1)}, u32[]{:S(2)}, u32[]{:S(2)}) collective-permute-start(bf16[1040,128]{1,0:T(8,128)(2,1)} %get-tuple-element.31.own.refs_0_), channel_id=1, source_target_pairs={{0,8},{4,12},{8,16},{12,20},{16,24},{20,28},{24,0},{28,4},{1,9},{5... | collective-permute-start | bytes 798728 | tf_op jit(solution)/shard_map/ppermute | solution.py:168
  40.0 9.2 %collective-permute-start.11 = (bf16[912,128]{1,0:T(8,128)(2,1)S(1)}, bf16[912,128]{1,0:T(8,128)(2,1)S(1)}, u32[]{:S(2)}, u32[]{:S(2)}) collective-permute-start(bf16[912,128]{1,0:T(8,128)(2,1)S(1)} %collective-permute-done.6.refs_4_), channel_id=1, source_target_pairs={{0,4},{4,0},{8,12},{12,8},{16,20},{20,16},{24,28},{28,24},{1,5},{5... | collective-permute-start | bytes 700424 | tf_op jit(solution)/shard_map/ppermute | solution.py:168
  45.7 16.1 %collective-permute-start.26 = (bf16[1040,128]{1,0:T(8,128)(2,1)S(1)}, bf16[1040,128]{1,0:T(8,128)(2,1)S(1)}, u32[]{:S(2)}, u32[]{:S(2)}) collective-permute-start(bf16[1040,128]{1,0:T(8,128)(2,1)S(1)} %collective-permute-done.21.refs_4_), channel_id=1, source_target_pairs={{0,4},{4,0},{8,12},{12,8},{16,20},{20,16},{24,28},{28,24},{1,5},{5... | collective-permute-start | bytes 798728 | tf_op jit(solution)/shard_map/ppermute | solution.py:168
  46.1 16.6 %collective-permute-start.25 = (bf16[1040,128]{1,0:T(8,128)(2,1)S(1)}, bf16[1040,128]{1,0:T(8,128)(2,1)S(1)}, u32[]{:S(2)}, u32[]{:S(2)}) collective-permute-start(bf16[1040,128]{1,0:T(8,128)(2,1)S(1)} %collective-permute-done.21.refs_4_), channel_id=1, source_target_pairs={{0,8},{4,12},{8,16},{12,20},{16,24},{20,28},{24,0},{28,4},{1,9},{5... | collective-permute-start | bytes 798728 | tf_op jit(solution)/shard_map/ppermute | solution.py:168
  46.1 17.1 %collective-permute-start.23 = (bf16[1040,128]{1,0:T(8,128)(2,1)}, bf16[1040,128]{1,0:T(8,128)(2,1)S(1)}, u32[]{:S(2)}, u32[]{:S(2)}) collective-permute-start(bf16[1040,128]{1,0:T(8,128)(2,1)} %get-tuple-element.31.own.refs_0_), channel_id=1, source_target_pairs={{0,1},{1,0},{2,3},{3,2},{4,5},{5,4},{6,7},{7,6},{8,9},{9,8},{10,11... | collective-permute-start | bytes 798728 | tf_op jit(solution)/shard_map/ppermute | solution.py:171
  47.8 11.6 %collective-permute-start.10 = (bf16[912,128]{1,0:T(8,128)(2,1)S(1)}, bf16[912,128]{1,0:T(8,128)(2,1)S(1)}, u32[]{:S(2)}, u32[]{:S(2)}) collective-permute-start(bf16[912,128]{1,0:T(8,128)(2,1)S(1)} %collective-permute-done.6.refs_4_), channel_id=1, source_target_pairs={{0,8},{4,12},{8,16},{12,20},{16,24},{20,28},{24,0},{28,4},{1,9},{5... | collective-permute-start | bytes 700424 | tf_op jit(solution)/shard_map/ppermute | solution.py:168
  49.1 14.1 %collective-permute-start.8 = (bf16[912,128]{1,0:T(8,128)(2,1)}, bf16[912,128]{1,0:T(8,128)(2,1)S(1)}, u32[]{:S(2)}, u32[]{:S(2)}) collective-permute-start(bf16[912,128]{1,0:T(8,128)(2,1)} %get-tuple-element.32.refs_0_), channel_id=1, source_target_pairs={{0,1},{1,0},{2,3},{3,2},{4,5},{5,4},{6,7},{7,6},{8,9},{9,8},{10,11... | collective-permute-start | bytes 700424 | tf_op jit(solution)/shard_map/ppermute | solution.py:171
  61.8 7.3 %collective-permute-start.15 = (bf16[912,128]{1,0:T(8,128)(2,1)S(1)}, bf16[912,128]{1,0:T(8,128)(2,1)S(1)}, u32[]{:S(2)}, u32[]{:S(2)}) collective-permute-start(bf16[912,128]{1,0:T(8,128)(2,1)S(1)} %collective-permute-done.10.refs_8_), channel_id=1, source_target_pairs={{0,4},{4,0},{8,12},{12,8},{16,20},{20,16},{24,28},{28,24},{1,5},{5... | collective-permute-start | bytes 700424 | tf_op jit(solution)/shard_map/ppermute | solution.py:168
  62.8 12.0 %collective-permute-start.30 = (bf16[1040,128]{1,0:T(8,128)(2,1)S(1)}, bf16[1040,128]{1,0:T(8,128)(2,1)S(1)}, u32[]{:S(2)}, u32[]{:S(2)}) collective-permute-start(bf16[1040,128]{1,0:T(8,128)(2,1)S(1)} %collective-permute-done.25.refs_8_), channel_id=1, source_target_pairs={{0,4},{4,0},{8,12},{12,8},{16,20},{20,16},{24,28},{28,24},{1,5},{5... | collective-permute-start | bytes 798728 | tf_op jit(solution)/shard_map/ppermute | solution.py:168
  63.3 8.4 %collective-permute-start.14 = (bf16[912,128]{1,0:T(8,128)(2,1)S(1)}, bf16[912,128]{1,0:T(8,128)(2,1)S(1)}, u32[]{:S(2)}, u32[]{:S(2)}) collective-permute-start(bf16[912,128]{1,0:T(8,128)(2,1)S(1)} %collective-permute-done.10.refs_8_), channel_id=1, source_target_pairs={{0,8},{4,12},{8,16},{12,20},{16,24},{20,28},{24,0},{28,4},{1,9},{5... | collective-permute-start | bytes 700424 | tf_op jit(solution)/shard_map/ppermute | solution.py:168
  63.3 14.1 %collective-permute-start.29 = (bf16[1040,128]{1,0:T(8,128)(2,1)S(1)}, bf16[1040,128]{1,0:T(8,128)(2,1)S(1)}, u32[]{:S(2)}, u32[]{:S(2)}) collective-permute-start(bf16[1040,128]{1,0:T(8,128)(2,1)S(1)} %collective-permute-done.25.refs_8_), channel_id=1, source_target_pairs={{0,8},{4,12},{8,16},{12,20},{16,24},{20,28},{24,0},{28,4},{1,9},{5... | collective-permute-start | bytes 798728 | tf_op jit(solution)/shard_map/ppermute | solution.py:168
  63.4 15.5 %collective-permute-start.24 = (bf16[1040,128]{1,0:T(8,128)(2,1)S(1)}, bf16[1040,128]{1,0:T(8,128)(2,1)S(1)}, u32[]{:S(2)}, u32[]{:S(2)}) collective-permute-start(bf16[1040,128]{1,0:T(8,128)(2,1)S(1)} %collective-permute-done.22.refs_1_), channel_id=1, source_target_pairs={{0,1},{1,0},{2,3},{3,2},{4,5},{5,4},{6,7},{7,6},{8,9},{9,8},{10,11... | collective-permute-start | bytes 798728 | tf_op jit(solution)/shard_map/ppermute | solution.py:171
  69.0 11.9 %collective-permute-start.27 = (bf16[1040,128]{1,0:T(8,128)(2,1)S(1)}, bf16[1040,128]{1,0:T(8,128)(2,1)S(1)}, u32[]{:S(2)}, u32[]{:S(2)}) collective-permute-start(bf16[1040,128]{1,0:T(8,128)(2,1)S(1)} %collective-permute-done.21.refs_4_), channel_id=1, source_target_pairs={{0,1},{1,0},{2,3},{3,2},{4,5},{5,4},{6,7},{7,6},{8,9},{9,8},{10,11... | collective-permute-start | bytes 798728 | tf_op jit(solution)/shard_map/ppermute | solution.py:171
  71.7 6.7 %collective-permute-start.12 = (bf16[912,128]{1,0:T(8,128)(2,1)S(1)}, bf16[912,128]{1,0:T(8,128)(2,1)S(1)}, u32[]{:S(2)}, u32[]{:S(2)}) collective-permute-start(bf16[912,128]{1,0:T(8,128)(2,1)S(1)} %collective-permute-done.6.refs_4_), channel_id=1, source_target_pairs={{0,1},{1,0},{2,3},{3,2},{4,5},{5,4},{6,7},{7,6},{8,9},{9,8},{10,11... | collective-permute-start | bytes 700424 | tf_op jit(solution)/shard_map/ppermute | solution.py:171
  78.4 10.4 %collective-permute-start.33 = (bf16[1040,128]{1,0:T(8,128)(2,1)S(1)}, bf16[1040,128]{1,0:T(8,128)(2,1)S(1)}, u32[]{:S(2)}, u32[]{:S(2)}) collective-permute-start(bf16[1040,128]{1,0:T(8,128)(2,1)S(1)} %collective-permute-done.29.refs_12_), channel_id=1, source_target_pairs={{0,4},{4,0},{8,12},{12,8},{16,20},{20,16},{24,28},{28,24},{1,5},{5... | collective-permute-start | bytes 798728 | tf_op jit(solution)/shard_map/ppermute | solution.py:168
  78.9 8.6 %collective-permute-start.16 = (bf16[912,128]{1,0:T(8,128)(2,1)S(1)}, bf16[912,128]{1,0:T(8,128)(2,1)S(1)}, u32[]{:S(2)}, u32[]{:S(2)}) collective-permute-start(bf16[912,128]{1,0:T(8,128)(2,1)S(1)} %collective-permute-done.10.refs_8_), channel_id=1, source_target_pairs={{0,1},{1,0},{2,3},{3,2},{4,5},{5,4},{6,7},{7,6},{8,9},{9,8},{10,11... | collective-permute-start | bytes 700424 | tf_op jit(solution)/shard_map/ppermute | solution.py:171
  81.0 7.0 %collective-permute-start.19 = (bf16[912,128]{1,0:T(8,128)(2,1)S(1)}, bf16[912,128]{1,0:T(8,128)(2,1)S(1)}, u32[]{:S(2)}, u32[]{:S(2)}) collective-permute-start(bf16[912,128]{1,0:T(8,128)(2,1)S(1)} %collective-permute-done.14.refs_12_), channel_id=1, source_target_pairs={{0,1},{1,0},{2,3},{3,2},{4,5},{5,4},{6,7},{7,6},{8,9},{9,8},{10,11... | collective-permute-start | bytes 700424 | tf_op jit(solution)/shard_map/ppermute | solution.py:171
  83.1 8.1 %collective-permute-start.20 = (bf16[912,128]{1,0:T(8,128)(2,1)S(1)}, bf16[912,128]{1,0:T(8,128)(2,1)S(1)}, u32[]{:S(2)}, u32[]{:S(2)}) collective-permute-start(bf16[912,128]{1,0:T(8,128)(2,1)S(1)} %collective-permute-done.18.refs_13_), channel_id=1, source_target_pairs={{0,1},{1,0},{2,3},{3,2},{4,5},{5,4},{6,7},{7,6},{8,9},{9,8},{10,11... | collective-permute-start | bytes 700424 | tf_op jit(solution)/shard_map/ppermute | solution.py:171
  87.5 11.1 %collective-permute-start.31 = (bf16[1040,128]{1,0:T(8,128)(2,1)S(1)}, bf16[1040,128]{1,0:T(8,128)(2,1)S(1)}, u32[]{:S(2)}, u32[]{:S(2)}) collective-permute-start(bf16[1040,128]{1,0:T(8,128)(2,1)S(1)} %collective-permute-done.25.refs_8_), channel_id=1, source_target_pairs={{0,1},{1,0},{2,3},{3,2},{4,5},{5,4},{6,7},{7,6},{8,9},{9,8},{10,11... | collective-permute-start | bytes 798728 | tf_op jit(solution)/shard_map/ppermute | solution.py:171
  87.6 11.0 %collective-permute-start.28 = (bf16[1040,128]{1,0:T(8,128)(2,1)S(1)}, bf16[1040,128]{1,0:T(8,128)(2,1)S(1)}, u32[]{:S(2)}, u32[]{:S(2)}) collective-permute-start(bf16[1040,128]{1,0:T(8,128)(2,1)S(1)} %collective-permute-done.26.refs_5_), channel_id=1, source_target_pairs={{0,1},{1,0},{2,3},{3,2},{4,5},{5,4},{6,7},{7,6},{8,9},{9,8},{10,11... | collective-permute-start | bytes 798728 | tf_op jit(solution)/shard_map/ppermute | solution.py:171
  88.0 10.6 %collective-permute-start.34 = (bf16[1040,128]{1,0:T(8,128)(2,1)S(1)}, bf16[1040,128]{1,0:T(8,128)(2,1)S(1)}, u32[]{:S(2)}, u32[]{:S(2)}) collective-permute-start(bf16[1040,128]{1,0:T(8,128)(2,1)S(1)} %collective-permute-done.29.refs_12_), channel_id=1, source_target_pairs={{0,1},{1,0},{2,3},{3,2},{4,5},{5,4},{6,7},{7,6},{8,9},{9,8},{10,11... | collective-permute-start | bytes 798728 | tf_op jit(solution)/shard_map/ppermute | solution.py:171
  88.8 9.8 %collective-permute-start.32 = (bf16[1040,128]{1,0:T(8,128)(2,1)S(1)}, bf16[1040,128]{1,0:T(8,128)(2,1)}, u32[]{:S(2)}, u32[]{:S(2)}) collective-permute-start(bf16[1040,128]{1,0:T(8,128)(2,1)S(1)} %collective-permute-done.30.refs_9_), channel_id=1, source_target_pairs={{0,1},{1,0},{2,3},{3,2},{4,5},{5,4},{6,7},{7,6},{8,9},{9,8},{10,11... | collective-permute-start | bytes 798728 | tf_op jit(solution)/shard_map/ppermute | solution.py:171
  109.1 8.1 %collective-permute-start.37 = (f32[4,128,128]{2,1,0:T(8,128)}, f32[4,128,128]{2,1,0:T(8,128)S(1)}, u32[]{:S(2)}, u32[]{:S(2)}) collective-permute-start(f32[4,128,128]{2,1,0:T(8,128)} %get-tuple-element.47), channel_id=1, source_target_pairs={{0,2},{1,3},{2,0},{3,1},{4,6},{5,7},{6,4},{7,5},{8,10},{9,11},{10,... | collective-permute-start | bytes 786440 | tf_op jit(solution)/shard_map/ppermute | solution.py:171
  110.2 12.8 %collective-permute-start.38 = (f32[4,128,128]{2,1,0:T(8,128)}, f32[4,128,128]{2,1,0:T(8,128)S(1)}, u32[]{:S(2)}, u32[]{:S(2)}) collective-permute-start(f32[4,128,128]{2,1,0:T(8,128)} %get-tuple-element.48), channel_id=1, source_target_pairs={{0,3},{1,2},{2,1},{3,0},{4,7},{5,6},{6,5},{7,4},{8,11},{9,10},{10,... | collective-permute-start | bytes 786440 | tf_op jit(solution)/shard_map/ppermute | solution.py:171
  (44 other events, 687.2 us)

commit v3 on v2

v3 whole, which is shorter than its diff:
```python
import functools

import jax
import jax.numpy as jnp
from jax import lax
from jax.experimental import pallas as pl
from jax.experimental.pallas import tpu as pltpu
from jax.sharding import PartitionSpec as P

BLOCK = 128
OPERATOR_SLOTS = 4
DENSITY_SLOTS = 7
TAIL = 16

ANY = pl.BlockSpec(memory_space=pl.ANY)
VMEM = pl.BlockSpec(memory_space=pltpu.VMEM)
SMEM = pl.BlockSpec(memory_space=pltpu.SMEM)


def estimate(flops, nbytes):
    return pl.CostEstimate(flops=flops, bytes_accessed=nbytes, transcendentals=0)


def split_kernel(place, density, hamiltonian, metric, *outs):
    spin, row = place[0], place[1]
    for v in (2, 3, 1, 0):
        other_spin = spin if v < 2 else 1 - spin
        other_row = row if v % 2 == 0 else 1 - row
        rows = pl.ds(pl.multiple_of(other_row * BLOCK, BLOCK), BLOCK)
        outs[v][...] = density[other_spin, rows, :]
        outs[4 + v][...] = hamiltonian[other_spin, rows, :]
        if v < 2:
            outs[8 + v][...] = metric[rows, :]


def slot_rows(slot):
    start = slot * BLOCK
    return pl.ds(start if isinstance(slot, int) else pl.multiple_of(start, BLOCK), BLOCK)


def pack_kernel(sources, mat, slots, col, keep, *refs):
    ins, out = refs[:sources], refs[sources]
    per = ins[0].shape[1] // BLOCK
    here = col[0]
    lane = lax.broadcasted_iota(jnp.int32, (TAIL, BLOCK), 1)
    out[...] = jnp.zeros_like(out)
    tail = jnp.zeros((TAIL, BLOCK), jnp.int32)
    flags = [[keep[m, mat, b] for b in range(per)] for m in range(sources)]
    counts = [functools.reduce(lambda p, q: p + q, f) for f in flags]
    for m in range(sources):
        slot = jnp.int32(0)
        for n in range(sources):
            if n != m:
                slot += jnp.where((here ^ n) < (here ^ m), counts[n], 0)
        for b in range(per):

            @pl.when(flags[m][b] > 0)
            def _(slot=slot, m=m, b=b):
                out[slot_rows(slot), :] = ins[m][:, b * BLOCK : (b + 1) * BLOCK]

            target = jnp.where(flags[m][b] > 0, slot, -1)
            tail = jnp.where(lane == target, (here ^ m) * per + b, tail)
            slot += flags[m][b]
    out[slots * BLOCK :, :] = tail.astype(jnp.float32).astype(out.dtype)


def row_of(place, key, layers):
    shift, flip, other = key
    layer = place[0] - shift
    layer = jnp.where(layer < 0, layer + layers, layer)
    side = place[1] if flip == 0 else 1 - place[1]
    half = place[2] if other == 0 else 1 - place[2]
    return (layer * 2 + side) * 2 + half


def fetch(place, keys, layers, bufs, held, sems):
    copies = [
        pltpu.make_async_copy(buf, held.at[row_of(place, key, layers)], sems.at[n])
        for n, (key, buf) in enumerate(zip(keys, bufs, strict=True))
    ]
    for copy in copies:
        copy.start()
    return copies


def tail_of(block):
    return block.astype(jnp.float32)[:1].astype(jnp.int32)


def read_tails(slots, held, tails):
    for k in range(held.shape[0]):
        tails[k : k + 1, :] = tail_of(held[k, slots * BLOCK :, :])


def first_kernel(keys, layers, place, ham, met, *refs):
    count = len(keys)
    bufs, out, held, acc, tails, cols, sems = refs[:count], *refs[count:]
    nblk = held.shape[0]
    copies = fetch(place, keys, layers, bufs, held, sems)
    acc[...] = jnp.zeros_like(acc)
    owns = (ham, met)
    for n, own in enumerate(owns):
        tails[nblk + n : nblk + n + 1, :] = tail_of(own[OPERATOR_SLOTS * BLOCK :, :])
    for copy in copies:
        copy.wait()
    read_tails(DENSITY_SLOTS, held, tails)
    pltpu.sync_copy(tails, cols)
    for n, own in enumerate(owns):
        for u in range(OPERATOR_SLOTS):
            k = cols[nblk + n, u]
            left = own[u * BLOCK : (u + 1) * BLOCK, :]
            for t in range(DENSITY_SLOTS):
                right = held[k, t * BLOCK : (t + 1) * BLOCK, :]
                acc[n * nblk + cols[k, t]] += jnp.dot(left, right, preferred_element_type=jnp.float32)
    out[...] = acc[...].astype(out.dtype)


def second_kernel(keys, layers, which, place, prods, *refs):
    count = len(keys)
    bufs, rest = refs[:count], refs[count:]
    if which == 0:
        acc, held, tails, cols, sems = rest
        outs = ()
    else:
        before, *outs, acc, held, tails, cols, sems = rest
    nblk = held.shape[0]
    copies = fetch(place, keys, layers, bufs, held, sems)
    if which == 0:
        acc[...] = jnp.zeros_like(acc)
    else:
        acc[...] = before[...]
    for copy in copies:
        copy.wait()
    read_tails(OPERATOR_SLOTS, held, tails)
    pltpu.sync_copy(tails, cols)

    def step(k, carry):
        left = prods[which * nblk + k]
        for t in range(OPERATOR_SLOTS):
            term = jnp.dot(left, held[k, t * BLOCK : (t + 1) * BLOCK, :], preferred_element_type=jnp.float32)
            if which == 0:
                acc[cols[k, t]] += term
            else:
                acc[cols[k, t]] -= term
        return carry

    lax.fori_loop(0, nblk, step, 0, unroll=4)
    for v, out in enumerate(outs):
        for b in range(out.shape[0]):
            out[b] = acc[place[3 + v] * out.shape[0] + b]


def join_kernel(place, keep, *refs):
    ins, out = refs[:4], refs[4]
    per = ins[0].shape[0]
    for v in range(4):
        spin = place[0] if v < 2 else 1 - place[0]
        row = place[1] if v % 2 == 0 else 1 - place[1]
        rows = pl.ds(pl.multiple_of(row * BLOCK, BLOCK), BLOCK)
        for b in range(per):
            value = ins[v][b]
            out[spin, rows, b * BLOCK : (b + 1) * BLOCK] = jnp.where(
                keep[row, b] > 0, value, jnp.zeros_like(value)
            )


def body(nrow, ncol, hamiltonian, metric, density, ham_keep, met_keep, dens_keep, grad_keep):
    layers, half = nrow // 2, ncol // 2
    per = ham_keep.shape[1]
    nblk = ham_keep.shape[0] * nrow
    width = per * BLOCK
    bf16, f32, i32 = jnp.bfloat16, jnp.float32, jnp.int32

    def by_row(pairs):
        return lambda a: lax.ppermute(a, "row", pairs)

    def by_mask(mask):
        return lambda a: lax.ppermute(a, "col", [(c, c ^ mask) for c in range(ncol)])

    def variant(mask):
        return (2 if mask >= half else 0) + (mask & 1)

    up = by_row([(r, (r + 2) % nrow) for r in range(nrow)])
    across = by_row([(r, r ^ 1) for r in range(nrow)])
    twin = by_mask(1)

    row, col = lax.axis_index("row").astype(i32), lax.axis_index("col").astype(i32)
    spin, part = col // half, col % 2
    z, x = row // 2, row % 2
    masks = (0, 1, half, half + 1)

    keeps = (jnp.stack([dens_keep, ham_keep, met_keep]) > 0).astype(i32)

    piece = jax.ShapeDtypeStruct((BLOCK, width), bf16)
    split = pl.pallas_call(
        split_kernel,
        out_shape=[piece] * 10,
        in_specs=[SMEM, VMEM, VMEM, VMEM],
        out_specs=[VMEM] * 10,
        cost_estimate=estimate(0, 24 * BLOCK * width * 2),
        name="split",
    )(jnp.stack([spin, part]), density, hamiltonian, metric)
    keep_rows = [lax.dynamic_index_in_dim(keeps, part ^ d, 1, keepdims=False) for d in (0, 1)]

    def exchange(pieces):
        return [pieces[0]] + [by_mask(m)(pieces[variant(m) % len(pieces)]) for m in range(1, ncol)]

    got = [exchange(p) for p in (split[:4], split[4:8], split[8:])]
    keep_got = jnp.stack(
        [keep_rows[0]] + [by_mask(m)(keep_rows[m & 1]) for m in range(1, ncol)]
    )

    slots = (DENSITY_SLOTS, OPERATOR_SLOTS, OPERATOR_SLOTS)
    packed = [
        pl.pallas_call(
            functools.partial(pack_kernel, ncol, mat, slots[mat]),
            out_shape=jax.ShapeDtypeStruct((slots[mat] * BLOCK + TAIL, BLOCK), bf16),
            in_specs=[SMEM, SMEM] + [VMEM] * ncol,
            out_specs=VMEM,
            cost_estimate=estimate(0, ncol * BLOCK * width * 2),
            name="pack",
        )(col[None], keep_got, *got[mat])
        for mat in range(3)
    ]

    gathered = [{}, {}, {}]
    curs, sides = list(packed), [None] * 3
    for t in range(layers):
        for n in range(3):
            bufs, cur, last = gathered[n], curs[n], t == layers - 1
            moves = {"side": across(cur), "twin": twin(cur)}
            if not last:
                moves["up"] = up(cur)
            if t:
                moves["back"] = twin(sides[n])
            moves = dict(zip(moves, lax.optimization_barrier(tuple(moves.values())), strict=True))
            bufs[t, 0, 0], bufs[t, 0, 1], bufs[t, 1, 0] = cur, moves["twin"], moves["side"]
            if t:
                bufs[t - 1, 1, 1] = moves["back"]
            if last:
                bufs[t, 1, 1] = twin(moves["side"])
            else:
                curs[n] = moves["up"]
            sides[n] = moves["side"]
    keys = list(gathered[0])
    place = jnp.stack([z, x, part] + [col ^ m for m in masks])

    def held(mat, extra):
        return [
            pltpu.VMEM((nblk, slots[mat] * BLOCK + TAIL, BLOCK), bf16),
            pltpu.VMEM((nblk + extra, BLOCK), i32),
            pltpu.SMEM((nblk + extra, BLOCK), i32),
            pltpu.SemaphoreType.DMA((len(keys),)),
        ]

    scratch = held(0, 8)
    prods = pl.pallas_call(
        functools.partial(first_kernel, keys, layers),
        out_shape=jax.ShapeDtypeStruct((2 * nblk, BLOCK, BLOCK), bf16),
        in_specs=[SMEM, VMEM, VMEM] + [ANY] * len(keys),
        out_specs=VMEM,
        scratch_shapes=[scratch[0], pltpu.VMEM((2 * nblk, BLOCK, BLOCK), f32)] + scratch[1:],
        cost_estimate=estimate(56 * 2 * BLOCK**3, nblk * 9 * BLOCK * BLOCK * 2),
        name="first",
    )(place, packed[1], packed[2], *[gathered[0][k] for k in keys])

    total = jax.ShapeDtypeStruct((nblk, BLOCK, BLOCK), f32)
    cost = estimate(nblk * 8 * BLOCK**3, nblk * 6 * BLOCK * BLOCK * 2)
    half_sum = pl.pallas_call(
        functools.partial(second_kernel, keys, layers, 0),
        out_shape=total,
        in_specs=[SMEM, VMEM] + [ANY] * len(keys),
        out_specs=VMEM,
        scratch_shapes=held(2, 0),
        cost_estimate=cost,
        name="second",
    )(place, prods, *[gathered[2][k] for k in keys])
    scratch = held(1, 0)
    outs = pl.pallas_call(
        functools.partial(second_kernel, keys, layers, 1),
        out_shape=[jax.ShapeDtypeStruct((per, BLOCK, BLOCK), f32)] * 4,
        in_specs=[SMEM, VMEM] + [ANY] * len(keys) + [VMEM],
        out_specs=[VMEM] * 4,
        scratch_shapes=[pltpu.VMEM((nblk, BLOCK, BLOCK), f32)] + scratch,
        cost_estimate=cost,
        name="third",
    )(place, prods, *[gathered[1][k] for k in keys], half_sum)

    back = [outs[0]] + [by_mask(m)(o) for m, o in zip(masks[1:], outs[1:], strict=True)]
    return pl.pallas_call(
        join_kernel,
        out_shape=jax.ShapeDtypeStruct((2, 2 * BLOCK, width), f32),
        in_specs=[SMEM, SMEM] + [VMEM] * 4,
        out_specs=VMEM,
        cost_estimate=estimate(0, 8 * BLOCK * width * 4),
        name="join",
    )(jnp.stack([spin, part]), grad_keep, *back)


def solution(mesh):
    grid = P("row", "col")
    spins = P(None, "row", "col")
    return jax.shard_map(
        functools.partial(body, mesh.shape["row"], mesh.shape["col"]),
        mesh=mesh,
        in_specs=(spins, grid, spins, grid, grid, grid, grid),
        out_specs=spins,
        check_vma=False,
    )
```

time: 126 us -> 132 us (1.048)
  starting transfers between devices: 37.2 us -> 44.9 us
  waiting for transfers between devices: 60.2 us -> 52.9 us
  Pallas kernels: 22.2 us -> 28.5 us
    pallas_call x3 -> x6, Pallas kernels: 14.1 us -> 20.4 us  [the longest x1 6.29 us: body(): pl.pallas_call(functools.partial(second_kernel, keys, layers, 1), out_sha...]
    ppermute x25 -> x39, starting transfers between devices: 27.6 us -> 32.2 us  [by_mask(): lax.ppermute(a, 'col', [(c, c ^ mask) for c in range(ncol)])]
    ppermute x14 -> x21, waiting for transfers between devices: 32 us -> 28 us  [by_row(): return lambda a: lax.ppermute(a, 'row', pairs)]
    ppermute x25 -> x39, waiting for transfers between devices: 28.2 us -> 24.9 us  [by_mask(): lax.ppermute(a, 'col', [(c, c ^ mask) for c in range(ncol)])]
    ppermute x14 -> x21, starting transfers between devices: 9.57 us -> 12.7 us  [by_row(): return lambda a: lax.ppermute(a, 'row', pairs)]
    unnamed x76 -> x106, local copies, waits for them, and re-layouts: 4.07 us -> 3.46 us
  transfers between devices with their start and end apart: 39 -> 60, of which waited for: 15 -> 19; matrix products, arithmetic and copies ran while one was open for 1% -> 1% of each run, Pallas kernels for 5% -> 13%
where the time goes in v3:
time: 132 us
  waiting for transfers between devices  52.9 us (40%)
  starting transfers between devices  44.9 us (34%)
  Pallas kernels  28.5 us (22%)
  local copies, waits for them, and re-layouts  4.07 us (3%)
    ppermute x39, starting transfers between devices, by_mask(): lax.ppermute(a, 'col', [(c, c ^ mask) for c in range(ncol)])  32.2 us
    ppermute x21, waiting for transfers between devices, by_row(): return lambda a: lax.ppermute(a, 'row', pairs)  28 us
    ppermute x39, waiting for transfers between devices, by_mask(): lax.ppermute(a, 'col', [(c, c ^ mask) for c in range(ncol)])  24.9 us
    ppermute x21, starting transfers between devices, by_row(): return lambda a: lax.ppermute(a, 'row', pairs)  12.7 us
    pallas_call x1, Pallas kernels, body(): pl.pallas_call(functools.partial(second_kernel, keys, layers, 1), out_sha...  6.29 us
    pallas_call x1, Pallas kernels, body(): pl.pallas_call(functools.partial(second_kernel, keys, layers, 0), out_sha...  5.94 us
    pallas_call x1, Pallas kernels, body(): pl.pallas_call(functools.partial(first_kernel, keys, layers), out_shape=j...  5.79 us
    pallas_call x3, Pallas kernels, body(): pl.pallas_call(functools.partial(pack_kernel, ncol, mat, slots[mat]), out...  5.79 us
  transfers between devices with their start and end apart: 60, of which 19 were waited for; matrix products, arithmetic and copies ran while one was open for 1% of the time, Pallas kernels for 13%

profile of v3, /device:TPU:1, one launch (start us, length us, event | category | flops | bytes accessed | tf_op | source)
XLA Modules:
  0.0 132.1 jit_solution(2530417182497716195)
XLA Ops:
  0.6 2.4 %split.1 = (bf16[128,512]{1,0:T(8,128)(2,1)}, bf16[128,512]{1,0:T(8,128)(2,1)}, bf16[128,512]{1,0:T(8,128)(2,1)}, bf16[128,512]{1,0:T(8,128)(2,1)}, bf16[128,512...) custom-call(s32[2]{0:T(128)} %pad_add_fusion.1.place, ...), custom_call_target="tpu_custom_call" | custom-call | bytes 3145728 | tf_op jit(solution)/shard_map/split/pallas_call | solution.py:195
  3.1 2.7 %collective-permute-start.4 = (bf16[128,512]{1,0:T(8,128)(2,1)}, bf16[128,512]{1,0:T(8,128)(2,1)S(1)}, u32[]{:S(2)}, u32[]{:S(2)}) collective-permute-start(bf16[128,512]{1,0:T(8,128)(2,1)} %get-tuple-element.63), channel_id=1, source_target_pairs={{0,2},{1,3},{2,0},{3,1},{4,6},{5,7},{6,4},{7,5},{8,10},{9,11},{10,... | collective-permute-start | bytes 393224 | tf_op jit(solution)/shard_map/ppermute | solution.py:178
  6.9 1.7 %collective-permute-start.2 = (s32[3,4]{1,0:T(4,128)S(1)}, s32[3,4]{1,0:T(4,128)S(1)}, u32[]{:S(2)}, u32[]{:S(2)}) collective-permute-start(s32[3,4]{1,0:T(4,128)S(1)} %bitcast.22), channel_id=1, source_target_pairs={{0,3},{1,2},{2,1},{3,0},{4,7},{5,6},{6,5},{7,4},{8,11},{9,10},{10,... | collective-permute-start | bytes 152 | tf_op jit(solution)/shard_map/ppermute | solution.py:178
  8.7 4.0 %collective-permute-done.2 = s32[3,4]{1,0:T(4,128)S(1)} collective-permute-done((s32[3,4]{1,0:T(4,128)S(1)}, s32[3,4]{1,0:T(4,128)S(1)}, u32[]{:S(2)}, u32[]{:S(2)}) %collective-permute-start.2) | collective-permute-done | bytes 80 | tf_op jit(solution)/shard_map/ppermute | solution.py:178
  12.7 1.4 %collective-permute-start.1 = (s32[3,4]{1,0:T(4,128)S(1)}, s32[3,4]{1,0:T(4,128)S(1)}, u32[]{:S(2)}, u32[]{:S(2)}) collective-permute-start(s32[3,4]{1,0:T(4,128)S(1)} %bitcast.24), channel_id=1, source_target_pairs={{0,2},{1,3},{2,0},{3,1},{4,6},{5,7},{6,4},{7,5},{8,10},{9,11},{10,... | collective-permute-start | bytes 152 | tf_op jit(solution)/shard_map/ppermute | solution.py:178
  15.1 1.5 %collective-permute-start = (s32[3,4]{1,0:T(4,128)S(1)}, s32[3,4]{1,0:T(4,128)S(1)}, u32[]{:S(2)}, u32[]{:S(2)}) collective-permute-start(s32[3,4]{1,0:T(4,128)S(1)} %bitcast.23), channel_id=1, source_target_pairs={{0,1},{1,0},{2,3},{3,2},{4,5},{5,4},{6,7},{7,6},{8,9},{9,8},{10,11... | collective-permute-start | bytes 152 | tf_op jit(solution)/shard_map/ppermute | solution.py:178
  22.2 1.9 %pack.3.ham.refs_0_ = bf16[528,128]{1,0:T(8,128)(2,1)} custom-call(s32[1]{0:T(128)} %bitcast.4.col, s32[4,3,4]{2,1,0:T(4,128)} %pad_add_fusion.keep, bf16[128,512]{1,0:T(8,128)(2,1)} %get-tuple-element.61.refs_0_, bf16[128,512]{1,0:T(8,128)(2,1)} %copy-done.41, bf16[128,512]{1,0:T(8,128)(2,1)} %copy-done.42, bf16[128,512]{1,0:T(8,128)(2,1)} %copy-done.43), custom_call_target="tpu_custom_call" | custom-call | bytes 524288 | tf_op jit(solution)/shard_map/pack/pallas_call | solution.py:215
  25.5 5.9 %collective-permute-done.11.refs_3_ = bf16[128,512]{1,0:T(8,128)(2,1)S(1)} collective-permute-done((bf16[128,512]{1,0:T(8,128)(2,1)}, bf16[128,512]{1,0:T(8,128)(2,1)S(1)}, u32[]{:S(2)}, u32[]{:S(2)}) %collective-permute-start.11) | collective-permute-done | bytes 131104 | tf_op jit(solution)/shard_map/ppermute | solution.py:178
  32.0 2.0 %pack.5.refs_0_ = bf16[912,128]{1,0:T(8,128)(2,1)} custom-call(s32[1]{0:T(128)} %bitcast.4.col, s32[4,3,4]{2,1,0:T(4,128)} %pad_add_fusion.keep, bf16[128,512]{1,0:T(8,128)(2,1)} %get-tuple-element.67.refs_0_, bf16[128,512]{1,0:T(8,128)(2,1)} %copy-done.40, bf16[128,512]{1,0:T(8,128)(2,1)} %copy-done.47, bf16[128,512]{1,0:T(8,128)(2,1)} %copy-done.48), custom_call_target="tpu_custom_call" | custom-call | bytes 524288 | tf_op jit(solution)/shard_map/pack/pallas_call | solution.py:215
  37.1 1.3 collective-permute-start.14
  38.4 1.9 %pack.4.met.refs_0_ = bf16[528,128]{1,0:T(8,128)(2,1)} custom-call(s32[1]{0:T(128)} %bitcast.4.col, s32[4,3,4]{2,1,0:T(4,128)} %pad_add_fusion.keep, bf16[128,512]{1,0:T(8,128)(2,1)} %get-tuple-element.65.refs_0_, bf16[128,512]{1,0:T(8,128)(2,1)} %copy-done.44, bf16[128,512]{1,0:T(8,128)(2,1)} %copy-done.46, bf16[128,512]{1,0:T(8,128)(2,1)} %copy-done.45), custom_call_target="tpu_custom_call" | custom-call | bytes 524288 | tf_op jit(solution)/shard_map/pack/pallas_call | solution.py:215
  40.6 2.1 %collective-permute-done.29.refs_3_ = bf16[528,128]{1,0:T(8,128)(2,1)S(1)} collective-permute-done((bf16[528,128]{1,0:T(8,128)(2,1)S(1)}, bf16[528,128]{1,0:T(8,128)(2,1)S(1)}, u32[]{:S(2)}, u32[]{:S(2)}) %collective-permute-start.29) | collective-permute-done | bytes 135200 | tf_op jit(solution)/shard_map/ppermute | solution.py:175
  42.7 1.5 %collective-permute-start.43 = (bf16[528,128]{1,0:T(8,128)(2,1)}, bf16[528,128]{1,0:T(8,128)(2,1)}, u32[]{:S(2)}, u32[]{:S(2)}) collective-permute-start(bf16[528,128]{1,0:T(8,128)(2,1)} %pack.4.met.refs_0_), channel_id=1, source_target_pairs={{0,1},{1,0},{2,3},{3,2},{4,5},{5,4},{6,7},{7,6},{8,9},{9,8},{10,11... | collective-permute-start | bytes 405512 | tf_op jit(solution)/shard_map/ppermute | solution.py:178
  44.5 3.2 %collective-permute-done.14.refs_3_ = bf16[912,128]{1,0:T(8,128)(2,1)S(1)} collective-permute-done((bf16[912,128]{1,0:T(8,128)(2,1)}, bf16[912,128]{1,0:T(8,128)(2,1)S(1)}, u32[]{:S(2)}, u32[]{:S(2)}) %collective-permute-start.14) | collective-permute-done | bytes 233504 | tf_op jit(solution)/shard_map/ppermute | solution.py:175
  49.2 2.2 %collective-permute-done.44.refs_3_ = bf16[528,128]{1,0:T(8,128)(2,1)S(1)} collective-permute-done((bf16[528,128]{1,0:T(8,128)(2,1)}, bf16[528,128]{1,0:T(8,128)(2,1)S(1)}, u32[]{:S(2)}, u32[]{:S(2)}) %collective-permute-start.44) | collective-permute-done | bytes 135200 | tf_op jit(solution)/shard_map/ppermute | solution.py:175
  54.0 1.9 %collective-permute-start.33 = (bf16[528,128]{1,0:T(8,128)(2,1)S(1)}, bf16[528,128]{1,0:T(8,128)(2,1)}, u32[]{:S(2)}, u32[]{:S(2)}) collective-permute-start(bf16[528,128]{1,0:T(8,128)(2,1)S(1)} %collective-permute-done.27.refs_2_), channel_id=1, source_target_pairs={{0,1},{1,0},{2,3},{3,2},{4,5},{5,4},{6,7},{7,6},{8,9},{9,8},{10,11... | collective-permute-start | bytes 405512 | tf_op jit(solution)/shard_map/ppermute | solution.py:178
  56.1 2.1 %collective-permute-done.17.refs_7_ = bf16[912,128]{1,0:T(8,128)(2,1)S(1)} collective-permute-done((bf16[912,128]{1,0:T(8,128)(2,1)S(1)}, bf16[912,128]{1,0:T(8,128)(2,1)S(1)}, u32[]{:S(2)}, u32[]{:S(2)}) %collective-permute-start.17) | collective-permute-done | bytes 233504 | tf_op jit(solution)/shard_map/ppermute | solution.py:175
  58.3 1.3 collective-permute-start.46
  59.6 1.6 %collective-permute-done.32.refs_7_ = bf16[528,128]{1,0:T(8,128)(2,1)S(1)} collective-permute-done((bf16[528,128]{1,0:T(8,128)(2,1)S(1)}, bf16[528,128]{1,0:T(8,128)(2,1)S(1)}, u32[]{:S(2)}, u32[]{:S(2)}) %collective-permute-start.32) | collective-permute-done | bytes 135200 | tf_op jit(solution)/shard_map/ppermute | solution.py:175
  63.6 2.9 %collective-permute-done.47.refs_7_ = bf16[528,128]{1,0:T(8,128)(2,1)S(1)} collective-permute-done((bf16[528,128]{1,0:T(8,128)(2,1)S(1)}, bf16[528,128]{1,0:T(8,128)(2,1)S(1)}, u32[]{:S(2)}, u32[]{:S(2)}) %collective-permute-start.47) | collective-permute-done | bytes 135200 | tf_op jit(solution)/shard_map/ppermute | solution.py:175
  70.5 1.7 %collective-permute-done.21.refs_11_ = bf16[912,128]{1,0:T(8,128)(2,1)S(1)} collective-permute-done((bf16[912,128]{1,0:T(8,128)(2,1)S(1)}, bf16[912,128]{1,0:T(8,128)(2,1)S(1)}, u32[]{:S(2)}, u32[]{:S(2)}) %collective-permute-start.21) | collective-permute-done | bytes 233504 | tf_op jit(solution)/shard_map/ppermute | solution.py:175
  76.4 4.5 %collective-permute-done.51.refs_11_ = bf16[528,128]{1,0:T(8,128)(2,1)S(1)} collective-permute-done((bf16[528,128]{1,0:T(8,128)(2,1)S(1)}, bf16[528,128]{1,0:T(8,128)(2,1)S(1)}, u32[]{:S(2)}, u32[]{:S(2)}) %collective-permute-start.51) | collective-permute-done | bytes 135200 | tf_op jit(solution)/shard_map/ppermute | solution.py:175
  83.8 2.8 %collective-permute-done.36.refs_11_ = bf16[528,128]{1,0:T(8,128)(2,1)S(1)} collective-permute-done((bf16[528,128]{1,0:T(8,128)(2,1)S(1)}, bf16[528,128]{1,0:T(8,128)(2,1)S(1)}, u32[]{:S(2)}, u32[]{:S(2)}) %collective-permute-start.36) | collective-permute-done | bytes 135200 | tf_op jit(solution)/shard_map/ppermute | solution.py:175
  86.6 2.2 %collective-permute-start.26 = (bf16[912,128]{1,0:T(8,128)(2,1)S(1)}, bf16[912,128]{1,0:T(8,128)(2,1)}, u32[]{:S(2)}, u32[]{:S(2)}) collective-permute-start(bf16[912,128]{1,0:T(8,128)(2,1)S(1)} %collective-permute-done.23.refs_13_), channel_id=1, source_target_pairs={{0,1},{1,0},{2,3},{3,2},{4,5},{5,4},{6,7},{7,6},{8,9},{9,8},{10,11... | collective-permute-start | bytes 700424 | tf_op jit(solution)/shard_map/ppermute | solution.py:178
  90.9 3.2 %collective-permute-done.38.refs_13_ = bf16[528,128]{1,0:T(8,128)(2,1)} collective-permute-done((bf16[528,128]{1,0:T(8,128)(2,1)S(1)}, bf16[528,128]{1,0:T(8,128)(2,1)}, u32[]{:S(2)}, u32[]{:S(2)}) %collective-permute-start.38) | collective-permute-done | bytes 135200 | tf_op jit(solution)/shard_map/ppermute | solution.py:175
  97.0 5.8 %first.1.prods = bf16[32,128,128]{2,1,0:T(8,128)(2,1)} custom-call(s32[7]{0:T(128)} %stack.70.place, bf16[528,128]{1,0:T(8,128)(2,1)} %pack.3.ham.refs_0_, bf16[528,128]{1,0:T(8,128)(2,1)} %pack.4.met.refs_0_, bf16[912,128]{1,0:T(8,128)(2,1)} %pack.5.refs_0_, bf16[912,128]{1,0:T(8,128)(2,1)} %copy-done.5, bf16[912,128]{1,0:T(8,128)(2,1)} %copy-done.4, ...), custom_call_target="tpu_custom_call" | custom-call | flops 234881024 | bytes 4718592 | tf_op jit(solution)/shard_map/first/pallas_call | solution.py:257
  102.8 5.9 %second.1.refs_16_ = f32[16,128,128]{2,1,0:T(8,128)} custom-call(s32[7]{0:T(128)} %stack.70.place, bf16[32,128,128]{2,1,0:T(8,128)(2,1)} %first.1.prods, bf16[528,128]{1,0:T(8,128)(2,1)} %pack.4.met.refs_0_, bf16[528,128]{1,0:T(8,128)(2,1)} %collective-permute-done.43.refs_1_, bf16[528,128]{1,0:T(8,128)(2,1)} %copy-done.22, bf16[528,128]{1,0:T(8,128)(2,1)} %copy-done.23, ...), custom_call_target="tpu_custom_call" | custom-call | flops 268435456 | bytes 3145728 | tf_op jit(solution)/shard_map/second/pallas_call | solution.py:269
  108.8 6.3 %third.1 = (f32[4,128,128]{2,1,0:T(8,128)}, f32[4,128,128]{2,1,0:T(8,128)}, f32[4,128,128]{2,1,0:T(8,128)}, f32[4,128,128]{2,1,0:T(8,128)}) custom-call(s32[7]{0:T(128)} %stack.70.place, bf16[32,128,128]{2,1,0:T(8,128)(2,1)} %first.1.prods, bf16[528,128]{1,0:T(8,128)(2,1)} %pack.3.ham.refs_0_, bf16[528,128]{1,0:T(8,128)(2,1)} %copy-done.19, ...), custom_call_target="tpu_custom_call" | custom-call | flops 268435456 | bytes 3145728 | tf_op jit(solution)/shard_map/third/pallas_call | solution.py:279
  115.2 1.3 collective-permute-start.58
  117.3 5.6 %collective-permute-done.58.refs_2_ = f32[4,128,128]{2,1,0:T(8,128)S(1)} collective-permute-done((f32[4,128,128]{2,1,0:T(8,128)}, f32[4,128,128]{2,1,0:T(8,128)S(1)}, u32[]{:S(2)}, u32[]{:S(2)}) %collective-permute-start.58) | collective-permute-done | bytes 262176 | tf_op jit(solution)/shard_map/ppermute | solution.py:178
  122.9 6.2 %collective-permute-done.59.refs_3_ = f32[4,128,128]{2,1,0:T(8,128)S(1)} collective-permute-done((f32[4,128,128]{2,1,0:T(8,128)}, f32[4,128,128]{2,1,0:T(8,128)S(1)}, u32[]{:S(2)}, u32[]{:S(2)}) %collective-permute-start.59) | collective-permute-done | bytes 262176 | tf_op jit(solution)/shard_map/ppermute | solution.py:178
  129.8 2.3 %join.1 = f32[2,256,512]{2,1,0:T(8,128)} custom-call(s32[2]{0:T(128)} %pad_add_fusion.1.place, s32[2,4]{1,0:T(2,128)} %keep.1, f32[4,128,128]{2,1,0:T(8,128)} %get-tuple-element.113.refs_0_, f32[4,128,128]{2,1,0:T(8,128)} %copy-done.1, f32[4,128,128]{2,1,0:T(8,128)} %copy-done.2, f32[4,128,128]{2,1,0:T(8,128)} %copy-done.3), custom_call_target="tpu_custom_call" | custom-call | bytes 2097152 | tf_op jit(solution)/shard_map/join/pallas_call | solution.py:290
  (208 shorter events, 38.4 us)
Async XLA Ops:
  3.1 15.7 %collective-permute-start.3 = (bf16[128,512]{1,0:T(8,128)(2,1)}, bf16[128,512]{1,0:T(8,128)(2,1)S(1)}, u32[]{:S(2)}, u32[]{:S(2)}) collective-permute-start(bf16[128,512]{1,0:T(8,128)(2,1)} %get-tuple-element.62), channel_id=1, source_target_pairs={{0,1},{1,0},{2,3},{3,2},{4,5},{5,4},{6,7},{7,6},{8,9},{9,8},{10,11... | collective-permute-start | bytes 393224 | tf_op jit(solution)/shard_map/ppermute | solution.py:178
  3.1 16.2 %collective-permute-start.4 = (bf16[128,512]{1,0:T(8,128)(2,1)}, bf16[128,512]{1,0:T(8,128)(2,1)S(1)}, u32[]{:S(2)}, u32[]{:S(2)}) collective-permute-start(bf16[128,512]{1,0:T(8,128)(2,1)} %get-tuple-element.63), channel_id=1, source_target_pairs={{0,2},{1,3},{2,0},{3,1},{4,6},{5,7},{6,4},{7,5},{8,10},{9,11},{10,... | collective-permute-start | bytes 393224 | tf_op jit(solution)/shard_map/ppermute | solution.py:178
  5.8 13.8 %collective-permute-start.5 = (bf16[128,512]{1,0:T(8,128)(2,1)}, bf16[128,512]{1,0:T(8,128)(2,1)S(1)}, u32[]{:S(2)}, u32[]{:S(2)}) collective-permute-start(bf16[128,512]{1,0:T(8,128)(2,1)} %get-tuple-element.64), channel_id=1, source_target_pairs={{0,3},{1,2},{2,1},{3,0},{4,7},{5,6},{6,5},{7,4},{8,11},{9,10},{10,... | collective-permute-start | bytes 393224 | tf_op jit(solution)/shard_map/ppermute | solution.py:178
  5.9 15.0 %collective-permute-start.9 = (bf16[128,512]{1,0:T(8,128)(2,1)}, bf16[128,512]{1,0:T(8,128)(2,1)S(1)}, u32[]{:S(2)}, u32[]{:S(2)}) collective-permute-start(bf16[128,512]{1,0:T(8,128)(2,1)} %get-tuple-element.68), channel_id=1, source_target_pairs={{0,1},{1,0},{2,3},{3,2},{4,5},{5,4},{6,7},{7,6},{8,9},{9,8},{10,11... | collective-permute-start | bytes 393224 | tf_op jit(solution)/shard_map/ppermute | solution.py:178
  18.7 16.5 %collective-permute-start.6 = (bf16[128,512]{1,0:T(8,128)(2,1)}, bf16[128,512]{1,0:T(8,128)(2,1)S(1)}, u32[]{:S(2)}, u32[]{:S(2)}) collective-permute-start(bf16[128,512]{1,0:T(8,128)(2,1)} %get-tuple-element.66), channel_id=1, source_target_pairs={{0,1},{1,0},{2,3},{3,2},{4,5},{5,4},{6,7},{7,6},{8,9},{9,8},{10,11... | collective-permute-start | bytes 393224 | tf_op jit(solution)/shard_map/ppermute | solution.py:178
  19.4 16.4 %collective-permute-start.8 = (bf16[128,512]{1,0:T(8,128)(2,1)}, bf16[128,512]{1,0:T(8,128)(2,1)S(1)}, u32[]{:S(2)}, u32[]{:S(2)}) collective-permute-start(bf16[128,512]{1,0:T(8,128)(2,1)} %get-tuple-element.66), channel_id=1, source_target_pairs={{0,3},{1,2},{2,1},{3,0},{4,7},{5,6},{6,5},{7,4},{8,11},{9,10},{10,... | collective-permute-start | bytes 393224 | tf_op jit(solution)/shard_map/ppermute | solution.py:178
  19.6 15.9 %collective-permute-start.7 = (bf16[128,512]{1,0:T(8,128)(2,1)}, bf16[128,512]{1,0:T(8,128)(2,1)S(1)}, u32[]{:S(2)}, u32[]{:S(2)}) collective-permute-start(bf16[128,512]{1,0:T(8,128)(2,1)} %get-tuple-element.65.refs_0_), channel_id=1, source_target_pairs={{0,2},{1,3},{2,0},{3,1},{4,6},{5,7},{6,4},{7,5},{8,10},{9,11},{10,... | collective-permute-start | bytes 393224 | tf_op jit(solution)/shard_map/ppermute | solution.py:178
  20.8 10.5 %collective-permute-start.11 = (bf16[128,512]{1,0:T(8,128)(2,1)}, bf16[128,512]{1,0:T(8,128)(2,1)S(1)}, u32[]{:S(2)}, u32[]{:S(2)}) collective-permute-start(bf16[128,512]{1,0:T(8,128)(2,1)} %get-tuple-element.70), channel_id=1, source_target_pairs={{0,3},{1,2},{2,1},{3,0},{4,7},{5,6},{6,5},{7,4},{8,11},{9,10},{10,... | collective-permute-start | bytes 393224 | tf_op jit(solution)/shard_map/ppermute | solution.py:178
  24.2 12.9 %collective-permute-start.27 = (bf16[528,128]{1,0:T(8,128)(2,1)}, bf16[528,128]{1,0:T(8,128)(2,1)S(1)}, u32[]{:S(2)}, u32[]{:S(2)}) collective-permute-start(bf16[528,128]{1,0:T(8,128)(2,1)} %pack.3.ham.refs_0_), channel_id=1, source_target_pairs={{0,4},{4,0},{8,12},{12,8},{16,20},{20,16},{24,28},{28,24},{1,5},{5... | collective-permute-start | bytes 405512 | tf_op jit(solution)/shard_map/ppermute | solution.py:175
  34.0 10.2 %collective-permute-start.12 = (bf16[912,128]{1,0:T(8,128)(2,1)}, bf16[912,128]{1,0:T(8,128)(2,1)S(1)}, u32[]{:S(2)}, u32[]{:S(2)}) collective-permute-start(bf16[912,128]{1,0:T(8,128)(2,1)} %pack.5.refs_0_), channel_id=1, source_target_pairs={{0,4},{4,0},{8,12},{12,8},{16,20},{20,16},{24,28},{28,24},{1,5},{5... | collective-permute-start | bytes 700424 | tf_op jit(solution)/shard_map/ppermute | solution.py:175
  35.2 9.0 %collective-permute-start.13 = (bf16[912,128]{1,0:T(8,128)(2,1)}, bf16[912,128]{1,0:T(8,128)(2,1)S(1)}, u32[]{:S(2)}, u32[]{:S(2)}) collective-permute-start(bf16[912,128]{1,0:T(8,128)(2,1)} %pack.5.refs_0_), channel_id=1, source_target_pairs={{0,1},{1,0},{2,3},{3,2},{4,5},{5,4},{6,7},{7,6},{8,9},{9,8},{10,11... | collective-permute-start | bytes 700424 | tf_op jit(solution)/shard_map/ppermute | solution.py:178
  37.1 10.6 %collective-permute-start.14 = (bf16[912,128]{1,0:T(8,128)(2,1)}, bf16[912,128]{1,0:T(8,128)(2,1)S(1)}, u32[]{:S(2)}, u32[]{:S(2)}) collective-permute-start(bf16[912,128]{1,0:T(8,128)(2,1)} %pack.5.refs_0_), channel_id=1, source_target_pairs={{0,8},{4,12},{8,16},{12,20},{16,24},{20,28},{24,0},{28,4},{1,9},{5... | collective-permute-start | bytes 700424 | tf_op jit(solution)/shard_map/ppermute | solution.py:175
  40.3 7.7 %collective-permute-start.42 = (bf16[528,128]{1,0:T(8,128)(2,1)}, bf16[528,128]{1,0:T(8,128)(2,1)S(1)}, u32[]{:S(2)}, u32[]{:S(2)}) collective-permute-start(bf16[528,128]{1,0:T(8,128)(2,1)} %pack.4.met.refs_0_), channel_id=1, source_target_pairs={{0,4},{4,0},{8,12},{12,8},{16,20},{20,16},{24,28},{28,24},{1,5},{5... | collective-permute-start | bytes 405512 | tf_op jit(solution)/shard_map/ppermute | solution.py:175
  44.2 8.0 %collective-permute-start.30 = (bf16[528,128]{1,0:T(8,128)(2,1)S(1)}, bf16[528,128]{1,0:T(8,128)(2,1)S(1)}, u32[]{:S(2)}, u32[]{:S(2)}) collective-permute-start(bf16[528,128]{1,0:T(8,128)(2,1)S(1)} %collective-permute-done.29.refs_3_), channel_id=1, source_target_pairs={{0,4},{4,0},{8,12},{12,8},{16,20},{20,16},{24,28},{28,24},{1,5},{5... | collective-permute-start | bytes 405512 | tf_op jit(solution)/shard_map/ppermute | solution.py:175
  48.0 7.8 %collective-permute-start.16 = (bf16[912,128]{1,0:T(8,128)(2,1)S(1)}, bf16[912,128]{1,0:T(8,128)(2,1)S(1)}, u32[]{:S(2)}, u32[]{:S(2)}) collective-permute-start(bf16[912,128]{1,0:T(8,128)(2,1)S(1)} %collective-permute-done.14.refs_3_), channel_id=1, source_target_pairs={{0,1},{1,0},{2,3},{3,2},{4,5},{5,4},{6,7},{7,6},{8,9},{9,8},{10,11... | collective-permute-start | bytes 700424 | tf_op jit(solution)/shard_map/ppermute | solution.py:178
  49.2 9.1 %collective-permute-start.17 = (bf16[912,128]{1,0:T(8,128)(2,1)S(1)}, bf16[912,128]{1,0:T(8,128)(2,1)S(1)}, u32[]{:S(2)}, u32[]{:S(2)}) collective-permute-start(bf16[912,128]{1,0:T(8,128)(2,1)S(1)} %collective-permute-done.14.refs_3_), channel_id=1, source_target_pairs={{0,8},{4,12},{8,16},{12,20},{16,24},{20,28},{24,0},{28,4},{1,9},{5... | collective-permute-start | bytes 700424 | tf_op jit(solution)/shard_map/ppermute | solution.py:175
  51.4 8.2 %collective-permute-start.18 = (bf16[912,128]{1,0:T(8,128)(2,1)S(1)}, bf16[912,128]{1,0:T(8,128)(2,1)S(1)}, u32[]{:S(2)}, u32[]{:S(2)}) collective-permute-start(bf16[912,128]{1,0:T(8,128)(2,1)S(1)} %collective-permute-done.12.refs_2_), channel_id=1, source_target_pairs={{0,1},{1,0},{2,3},{3,2},{4,5},{5,4},{6,7},{7,6},{8,9},{9,8},{10,11... | collective-permute-start | bytes 700424 | tf_op jit(solution)/shard_map/ppermute | solution.py:178
  53.6 7.6 %collective-permute-start.32 = (bf16[528,128]{1,0:T(8,128)(2,1)S(1)}, bf16[528,128]{1,0:T(8,128)(2,1)S(1)}, u32[]{:S(2)}, u32[]{:S(2)}) collective-permute-start(bf16[528,128]{1,0:T(8,128)(2,1)S(1)} %collective-permute-done.29.refs_3_), channel_id=1, source_target_pairs={{0,8},{4,12},{8,16},{12,20},{16,24},{20,28},{24,0},{28,4},{1,9},{5... | collective-permute-start | bytes 405512 | tf_op jit(solution)/shard_map/ppermute | solution.py:175
  54.0 8.4 %collective-permute-start.33 = (bf16[528,128]{1,0:T(8,128)(2,1)S(1)}, bf16[528,128]{1,0:T(8,128)(2,1)}, u32[]{:S(2)}, u32[]{:S(2)}) collective-permute-start(bf16[528,128]{1,0:T(8,128)(2,1)S(1)} %collective-permute-done.27.refs_2_), channel_id=1, source_target_pairs={{0,1},{1,0},{2,3},{3,2},{4,5},{5,4},{6,7},{7,6},{8,9},{9,8},{10,11... | collective-permute-start | bytes 405512 | tf_op jit(solution)/shard_map/ppermute | solution.py:178
  55.8 7.7 %collective-permute-start.45 = (bf16[528,128]{1,0:T(8,128)(2,1)S(1)}, bf16[528,128]{1,0:T(8,128)(2,1)S(1)}, u32[]{:S(2)}, u32[]{:S(2)}) collective-permute-start(bf16[528,128]{1,0:T(8,128)(2,1)S(1)} %collective-permute-done.44.refs_3_), channel_id=1, source_target_pairs={{0,4},{4,0},{8,12},{12,8},{16,20},{20,16},{24,28},{28,24},{1,5},{5... | collective-permute-start | bytes 405512 | tf_op jit(solution)/shard_map/ppermute | solution.py:175
  61.2 7.4 %collective-permute-start.19 = (bf16[912,128]{1,0:T(8,128)(2,1)S(1)}, bf16[912,128]{1,0:T(8,128)(2,1)S(1)}, u32[]{:S(2)}, u32[]{:S(2)}) collective-permute-start(bf16[912,128]{1,0:T(8,128)(2,1)S(1)} %collective-permute-done.17.refs_7_), channel_id=1, source_target_pairs={{0,4},{4,0},{8,12},{12,8},{16,20},{20,16},{24,28},{28,24},{1,5},{5... | collective-permute-start | bytes 700424 | tf_op jit(solution)/shard_map/ppermute | solution.py:175
  63.6 8.6 %collective-permute-start.21 = (bf16[912,128]{1,0:T(8,128)(2,1)S(1)}, bf16[912,128]{1,0:T(8,128)(2,1)S(1)}, u32[]{:S(2)}, u32[]{:S(2)}) collective-permute-start(bf16[912,128]{1,0:T(8,128)(2,1)S(1)} %collective-permute-done.17.refs_7_), channel_id=1, source_target_pairs={{0,8},{4,12},{8,16},{12,20},{16,24},{20,28},{24,0},{28,4},{1,9},{5... | collective-permute-start | bytes 700424 | tf_op jit(solution)/shard_map/ppermute | solution.py:175
  73.5 8.5 %collective-permute-start.23 = (bf16[912,128]{1,0:T(8,128)(2,1)S(1)}, bf16[912,128]{1,0:T(8,128)(2,1)S(1)}, u32[]{:S(2)}, u32[]{:S(2)}) collective-permute-start(bf16[912,128]{1,0:T(8,128)(2,1)S(1)} %collective-permute-done.21.refs_11_), channel_id=1, source_target_pairs={{0,4},{4,0},{8,12},{12,8},{16,20},{20,16},{24,28},{28,24},{1,5},{5... | collective-permute-start | bytes 700424 | tf_op jit(solution)/shard_map/ppermute | solution.py:175
  73.8 9.4 %collective-permute-start.24 = (bf16[912,128]{1,0:T(8,128)(2,1)S(1)}, bf16[912,128]{1,0:T(8,128)(2,1)S(1)}, u32[]{:S(2)}, u32[]{:S(2)}) collective-permute-start(bf16[912,128]{1,0:T(8,128)(2,1)S(1)} %collective-permute-done.21.refs_11_), channel_id=1, source_target_pairs={{0,1},{1,0},{2,3},{3,2},{4,5},{5,4},{6,7},{7,6},{8,9},{9,8},{10,11... | collective-permute-start | bytes 700424 | tf_op jit(solution)/shard_map/ppermute | solution.py:178
  76.3 7.3 %collective-permute-start.25 = (bf16[912,128]{1,0:T(8,128)(2,1)S(1)}, bf16[912,128]{1,0:T(8,128)(2,1)S(1)}, u32[]{:S(2)}, u32[]{:S(2)}) collective-permute-start(bf16[912,128]{1,0:T(8,128)(2,1)S(1)} %collective-permute-done.19.refs_9_), channel_id=1, source_target_pairs={{0,1},{1,0},{2,3},{3,2},{4,5},{5,4},{6,7},{7,6},{8,9},{9,8},{10,11... | collective-permute-start | bytes 700424 | tf_op jit(solution)/shard_map/ppermute | solution.py:178
  80.9 7.8 %collective-permute-start.37 = (bf16[528,128]{1,0:T(8,128)(2,1)S(1)}, bf16[528,128]{1,0:T(8,128)(2,1)S(1)}, u32[]{:S(2)}, u32[]{:S(2)}) collective-permute-start(bf16[528,128]{1,0:T(8,128)(2,1)S(1)} %collective-permute-done.30.refs_5_), channel_id=1, source_target_pairs={{0,1},{1,0},{2,3},{3,2},{4,5},{5,4},{6,7},{7,6},{8,9},{9,8},{10,11... | collective-permute-start | bytes 405512 | tf_op jit(solution)/shard_map/ppermute | solution.py:178
  82.0 8.0 %collective-permute-start.53 = (bf16[528,128]{1,0:T(8,128)(2,1)S(1)}, bf16[528,128]{1,0:T(8,128)(2,1)}, u32[]{:S(2)}, u32[]{:S(2)}) collective-permute-start(bf16[528,128]{1,0:T(8,128)(2,1)S(1)} %collective-permute-done.51.refs_11_), channel_id=1, source_target_pairs={{0,4},{4,0},{8,12},{12,8},{16,20},{20,16},{24,28},{28,24},{1,5},{5... | collective-permute-start | bytes 405512 | tf_op jit(solution)/shard_map/ppermute | solution.py:175
  86.6 10.3 %collective-permute-start.26 = (bf16[912,128]{1,0:T(8,128)(2,1)S(1)}, bf16[912,128]{1,0:T(8,128)(2,1)}, u32[]{:S(2)}, u32[]{:S(2)}) collective-permute-start(bf16[912,128]{1,0:T(8,128)(2,1)S(1)} %collective-permute-done.23.refs_13_), channel_id=1, source_target_pairs={{0,1},{1,0},{2,3},{3,2},{4,5},{5,4},{6,7},{7,6},{8,9},{9,8},{10,11... | collective-permute-start | bytes 700424 | tf_op jit(solution)/shard_map/ppermute | solution.py:178
  90.6 12.2 %collective-permute-start.56 = (bf16[528,128]{1,0:T(8,128)(2,1)}, bf16[528,128]{1,0:T(8,128)(2,1)}, u32[]{:S(2)}, u32[]{:S(2)}) collective-permute-start(bf16[528,128]{1,0:T(8,128)(2,1)} %collective-permute-done.53.refs_13_), channel_id=1, source_target_pairs={{0,1},{1,0},{2,3},{3,2},{4,5},{5,4},{6,7},{7,6},{8,9},{9,8},{10,11... | collective-permute-start | bytes 405512 | tf_op jit(solution)/shard_map/ppermute | solution.py:178
  95.5 13.3 %collective-permute-start.41 = (bf16[528,128]{1,0:T(8,128)(2,1)}, bf16[528,128]{1,0:T(8,128)(2,1)}, u32[]{:S(2)}, u32[]{:S(2)}) collective-permute-start(bf16[528,128]{1,0:T(8,128)(2,1)} %collective-permute-done.38.refs_13_), channel_id=1, source_target_pairs={{0,1},{1,0},{2,3},{3,2},{4,5},{5,4},{6,7},{7,6},{8,9},{9,8},{10,11... | collective-permute-start | bytes 405512 | tf_op jit(solution)/shard_map/ppermute | solution.py:178
  115.2 7.7 %collective-permute-start.58 = (f32[4,128,128]{2,1,0:T(8,128)}, f32[4,128,128]{2,1,0:T(8,128)S(1)}, u32[]{:S(2)}, u32[]{:S(2)}) collective-permute-start(f32[4,128,128]{2,1,0:T(8,128)} %get-tuple-element.115), channel_id=1, source_target_pairs={{0,2},{1,3},{2,0},{3,1},{4,6},{5,7},{6,4},{7,5},{8,10},{9,11},{10,... | collective-permute-start | bytes 786440 | tf_op jit(solution)/shard_map/ppermute | solution.py:178
  116.5 12.6 %collective-permute-start.59 = (f32[4,128,128]{2,1,0:T(8,128)}, f32[4,128,128]{2,1,0:T(8,128)S(1)}, u32[]{:S(2)}, u32[]{:S(2)}) collective-permute-start(f32[4,128,128]{2,1,0:T(8,128)} %get-tuple-element.116), channel_id=1, source_target_pairs={{0,3},{1,2},{2,1},{3,0},{4,7},{5,6},{6,5},{7,4},{8,11},{9,10},{10,... | collective-permute-start | bytes 786440 | tf_op jit(solution)/shard_map/ppermute | solution.py:178
  (80 other events, 1013.3 us)

commit v4 on v1

v4 whole, which is shorter than its diff:
```python
import functools

import jax
import jax.numpy as jnp
from jax import lax
from jax.experimental import pallas as pl
from jax.experimental.pallas import tpu as pltpu
from jax.sharding import PartitionSpec as P

BLOCK = 128
OPERATOR_SLOTS = 4
DENSITY_SLOTS = 7
TAIL = 16

ANY = pl.BlockSpec(memory_space=pl.ANY)
VMEM = pl.BlockSpec(memory_space=pltpu.VMEM)
SMEM = pl.BlockSpec(memory_space=pltpu.SMEM)


def estimate(flops, nbytes):
    return pl.CostEstimate(flops=flops, bytes_accessed=nbytes, transcendentals=0)


def split_kernel(place, density, hamiltonian, metric, *outs):
    spin, row = place[0], place[1]
    for v in (2, 3, 1, 0):
        other_spin = spin if v < 2 else 1 - spin
        other_row = row if v % 2 == 0 else 1 - row
        rows = pl.ds(pl.multiple_of(other_row * BLOCK, BLOCK), BLOCK)
        outs[v][0] = density[other_spin, rows, :]
        outs[4 + v][0] = hamiltonian[other_spin, rows, :]
        outs[4 + v][1] = metric[rows, :]


def slot_rows(slot):
    start = slot * BLOCK
    return pl.ds(start if isinstance(slot, int) else pl.multiple_of(start, BLOCK), BLOCK)


def pack_kernel(sources, mats, slots, place, keep, *refs):
    ins, out = refs[:sources], refs[sources]
    per = ins[0].shape[2] // BLOCK
    here = place[4]
    lane = lax.broadcasted_iota(jnp.int32, (TAIL, BLOCK), 1)
    out[...] = jnp.zeros_like(out)
    tail = jnp.zeros((TAIL, BLOCK), jnp.int32)
    for i, mat in enumerate(mats):
        flags = [[keep[m, mat, b] for b in range(per)] for m in range(sources)]
        counts = [functools.reduce(lambda p, q: p + q, f) for f in flags]
        for m in range(sources):
            slot = jnp.int32(i * slots)
            for n in range(sources):
                if n != m:
                    slot += jnp.where((here ^ n) < (here ^ m), counts[n], 0)
            for b in range(per):

                @pl.when(flags[m][b] > 0)
                def _(slot=slot, m=m, b=b, i=i):
                    out[slot_rows(slot), :] = ins[m][i, :, b * BLOCK : (b + 1) * BLOCK]

                target = jnp.where(flags[m][b] > 0, slot, -1)
                tail = jnp.where(lane == target, (here ^ m) * per + b, tail)
                slot += flags[m][b]
    out[len(mats) * slots * BLOCK :, :] = tail.astype(jnp.float32).astype(out.dtype)


def row_of(place, key, layers):
    shift, flip, other = key
    layer = place[2] - shift
    layer = jnp.where(layer < 0, layer + layers, layer)
    side = place[3] if flip == 0 else 1 - place[3]
    half = place[1] if other == 0 else 1 - place[1]
    return (layer * 2 + side) * 2 + half


def tail_of(block):
    return block.astype(jnp.float32)[:1].astype(jnp.int32)


def parts_of(entries, layers, place, slots, bufs, tails):
    parts = []
    for n, (which, start, key) in enumerate(entries):
        view = bufs[which].at[start : start + slots * BLOCK + TAIL]
        tails[n : n + 1, :] = tail_of(view[slots * BLOCK :, :])
        parts.append((view, row_of(place, key, layers)))
    return parts


def first_kernel(entries, layers, count, place, own, *refs):
    bufs, out, acc, tails, cols = refs[:count], *refs[count:]
    nblk = len(entries)
    parts = parts_of(entries, layers, place, DENSITY_SLOTS, bufs, tails)
    tails[nblk : nblk + 1, :] = tail_of(own[2 * OPERATOR_SLOTS * BLOCK :, :])
    pltpu.sync_copy(tails, cols)
    acc[...] = jnp.zeros_like(acc)
    for i in range(2):
        mine = [cols[nblk, i * OPERATOR_SLOTS + u] for u in range(OPERATOR_SLOTS)]
        for n, (view, k) in enumerate(parts):
            slot = jnp.int32(-1)
            for u in reversed(range(OPERATOR_SLOTS)):
                slot = jnp.where(mine[u] == k, i * OPERATOR_SLOTS + u, slot)

            @pl.when(slot >= 0)
            def _(slot=slot, view=view, n=n, i=i):
                left = own[slot_rows(slot), :]
                for t in range(DENSITY_SLOTS):
                    right = view[t * BLOCK : (t + 1) * BLOCK, :]
                    acc[i * nblk + cols[n, t]] += jnp.dot(left, right, preferred_element_type=jnp.float32)

    out[...] = acc[...].astype(out.dtype)


def second_kernel(entries, layers, count, late, place, prods, *refs):
    bufs, rest = refs[:count], refs[count:]
    before = None
    if late:
        before, *outs, acc, tails, cols = rest
    else:
        acc, tails, cols = rest
        outs = ()
    nblk = acc.shape[0]
    parts = parts_of(entries, layers, place, 2 * OPERATOR_SLOTS, bufs, tails)
    pltpu.sync_copy(tails, cols)
    acc[...] = before[...] if late else jnp.zeros_like(acc)
    for n, (view, k) in enumerate(parts):
        hp, sp = prods[k], prods[nblk + k]
        for t in range(OPERATOR_SLOTS):
            u = OPERATOR_SLOTS + t
            ham, met = view[t * BLOCK : (t + 1) * BLOCK, :], view[u * BLOCK : (u + 1) * BLOCK, :]
            acc[cols[n, u]] += jnp.dot(hp, met, preferred_element_type=jnp.float32)
            acc[cols[n, t]] -= jnp.dot(sp, ham, preferred_element_type=jnp.float32)
    for v, out in enumerate(outs):
        for b in range(out.shape[0]):
            out[b] = acc[place[4 + v] * out.shape[0] + b].astype(out.dtype)


def join_kernel(place, keep, *refs):
    ins, out = refs[:4], refs[4]
    per = ins[0].shape[0]
    for v in range(4):
        spin = place[0] if v < 2 else 1 - place[0]
        row = place[1] if v % 2 == 0 else 1 - place[1]
        rows = pl.ds(pl.multiple_of(row * BLOCK, BLOCK), BLOCK)
        for b in range(per):
            value = ins[v][b].astype(out.dtype)
            out[spin, rows, b * BLOCK : (b + 1) * BLOCK] = jnp.where(
                keep[row, b] > 0, value, jnp.zeros_like(value)
            )


def body(nrow, ncol, hamiltonian, metric, density, ham_keep, met_keep, dens_keep, grad_keep):
    layers, half = nrow // 2, ncol // 2
    per = ham_keep.shape[1]
    nblk = ham_keep.shape[0] * nrow
    width = per * BLOCK
    bf16, f32, i32 = jnp.bfloat16, jnp.float32, jnp.int32

    def by_row(pairs):
        return lambda a: lax.ppermute(a, "row", pairs)

    def by_mask(mask):
        return lambda a: lax.ppermute(a, "col", [(c, c ^ mask) for c in range(ncol)])

    def variant(mask):
        return (2 if mask >= half else 0) + (mask & 1)

    up = by_row([(r, (r + 2) % nrow) for r in range(nrow)])
    across = by_row([(r, r ^ 1) for r in range(nrow)])
    twin = by_mask(1)

    row, col = lax.axis_index("row").astype(i32), lax.axis_index("col").astype(i32)
    spin, part = col // half, col % 2
    z, x = row // 2, row % 2
    masks = (0, 1, half, half + 1)

    keeps = (jnp.stack([dens_keep, ham_keep, met_keep]) > 0).astype(i32)
    place = jnp.stack([spin, part, z, x] + [col ^ m for m in masks])

    one, two = (jax.ShapeDtypeStruct((n, BLOCK, width), bf16) for n in (1, 2))
    split = pl.pallas_call(
        split_kernel,
        out_shape=[one] * 4 + [two] * 4,
        in_specs=[SMEM, VMEM, VMEM, VMEM],
        out_specs=[VMEM] * 8,
        cost_estimate=estimate(0, 24 * BLOCK * width * 2),
        name="split",
    )(place, density, hamiltonian, metric)
    keep_rows = [lax.dynamic_index_in_dim(keeps, part ^ d, 1, keepdims=False) for d in (0, 1)]

    def exchange(pieces):
        moved = {m: by_mask(m)(pieces[variant(m)]) for m in reversed(range(1, ncol))}
        return [pieces[0]] + [moved[m] for m in range(1, ncol)]

    got_dens = exchange(split[:4])
    keep_got = jnp.stack(exchange([keep_rows[0], keep_rows[1]] * 2))
    keep_got, *oper_pieces = lax.optimization_barrier((keep_got, *split[4:]))
    got_oper = exchange(oper_pieces)

    def pack(mats, slots, got):
        return pl.pallas_call(
            functools.partial(pack_kernel, ncol, mats, slots),
            out_shape=jax.ShapeDtypeStruct((len(mats) * slots * BLOCK + TAIL, BLOCK), bf16),
            in_specs=[SMEM, SMEM] + [VMEM] * ncol,
            out_specs=VMEM,
            cost_estimate=estimate(0, 8 * ncol * BLOCK * width * 2),
            name="pack",
        )(place, keep_got, *got)

    packed = [pack((0,), DENSITY_SLOTS, got_dens), pack((1, 2), OPERATOR_SLOTS, got_oper)]

    def twin_of(group):
        return twin(jnp.concatenate([a for a, _ in group], axis=0) if len(group) > 1 else group[0][0])

    gathered = [[], []]
    waiting = [[], []]
    curs = list(packed)
    for t in range(layers):
        for n in range(2):
            cur, last = curs[n], t == layers - 1
            size = cur.shape[0]

            def settle(arrived, group, n=n, size=size):
                for i, (_, key) in enumerate(group):
                    gathered[n].append((arrived, i * size, key[:2] + (1,)))

            gathered[n].append((cur, 0, (t, 0, 0)))
            waiting[n].append((cur, (t, 0, 0)))
            moves = [across(cur)] + ([] if last else [up(cur)])
            flush = waiting[n] if t % 2 == 1 or last else []
            if flush:
                moves.append(twin_of(flush))
            moves = list(lax.optimization_barrier(tuple(moves)))
            side = moves[0]
            gathered[n].append((side, 0, (t, 1, 0)))
            if flush:
                settle(moves[-1], flush)
                waiting[n] = []
            waiting[n].append((side, (t, 1, 0)))
            if last:
                settle(twin_of(waiting[n]), waiting[n])
            else:
                curs[n] = moves[1]

    def refs_of(entries):
        arrays = []
        for array, _, _ in entries:
            if not any(array is a for a in arrays):
                arrays.append(array)
        place_of = {id(a): i for i, a in enumerate(arrays)}
        return arrays, [(place_of[id(a)], start, key) for a, start, key in entries]

    arrays, entries = refs_of(gathered[0])
    tables = [pltpu.VMEM((nblk + 8, BLOCK), i32), pltpu.SMEM((nblk + 8, BLOCK), i32)]
    prods = pl.pallas_call(
        functools.partial(first_kernel, entries, layers, len(arrays)),
        out_shape=jax.ShapeDtypeStruct((2 * nblk, BLOCK, BLOCK), bf16),
        in_specs=[SMEM, VMEM] + [VMEM] * len(arrays),
        out_specs=VMEM,
        scratch_shapes=[pltpu.VMEM((2 * nblk, BLOCK, BLOCK), f32)] + tables,
        cost_estimate=estimate(56 * 2 * BLOCK**3, 10_000_000),
        name="first",
    )(place, packed[1], *arrays)

    final = (layers - 1, 1)
    early = [e for e in gathered[1] if e[2][:2] != final]
    late = [e for e in gathered[1] if e[2][:2] == final]
    tables = [pltpu.VMEM((nblk, BLOCK), i32), pltpu.SMEM((nblk, BLOCK), i32)]
    arrays, entries = refs_of(early)
    half_sum = pl.pallas_call(
        functools.partial(second_kernel, entries, layers, len(arrays), False),
        out_shape=jax.ShapeDtypeStruct((nblk, BLOCK, BLOCK), f32),
        in_specs=[SMEM, VMEM] + [VMEM] * len(arrays),
        out_specs=VMEM,
        scratch_shapes=tables,
        cost_estimate=estimate(nblk * 16 * BLOCK**3, 12_000_000),
        name="second",
    )(place, prods, *arrays)
    arrays, entries = refs_of(late)
    outs = pl.pallas_call(
        functools.partial(second_kernel, entries, layers, len(arrays), True),
        out_shape=[jax.ShapeDtypeStruct((per, BLOCK, BLOCK), f32 if m < half else bf16) for m in masks],
        in_specs=[SMEM, VMEM] + [VMEM] * len(arrays) + [VMEM],
        out_specs=[VMEM] * 4,
        scratch_shapes=[pltpu.VMEM((nblk, BLOCK, BLOCK), f32)] + tables,
        cost_estimate=estimate(4 * 8 * BLOCK**3, 6_000_000),
        name="third",
    )(place, prods, *arrays, half_sum)

    back = [outs[0]] + [by_mask(m)(o) for m, o in zip(masks[1:], outs[1:], strict=True)]
    return pl.pallas_call(
        join_kernel,
        out_shape=jax.ShapeDtypeStruct((2, 2 * BLOCK, width), f32),
        in_specs=[SMEM, SMEM] + [VMEM] * 4,
        out_specs=VMEM,
        cost_estimate=estimate(0, 8 * BLOCK * width * 4),
        name="join",
    )(place, grad_keep, *back)


def solution(mesh):
    grid = P("row", "col")
    spins = P(None, "row", "col")
    return jax.shard_map(
        functools.partial(body, mesh.shape["row"], mesh.shape["col"]),
        mesh=mesh,
        in_specs=(spins, grid, spins, grid, grid, grid, grid),
        out_specs=spins,
        check_vma=False,
    )
```

time: 203 us -> 115 us (0.57)
  blocking collectives: 45.1 us -> 0 us
  Pallas kernels: 67.6 us -> 23.8 us
  waiting for transfers between devices: 52.4 us -> 57.4 us
  local copies, waits for them, and re-layouts: 7.81 us -> 4.23 us
    all_gather x1 -> x0, blocking collectives: 45.1 us -> none  [body(): spread = lax.all_gather(keeps, ('row', 'col'))]
    pallas_call x4 -> x6, Pallas kernels: 65.3 us -> 21.6 us  [the longest x2 8.92 us: body(): pl.pallas_call(functools.partial(second_kernel, entries, layers, len(arra...]
    ppermute x14, waiting for transfers between devices: 24.6 us -> 40.8 us  [by_row(): return lambda a: lax.ppermute(a, 'row', pairs)]
    ppermute x25 -> x18, waiting for transfers between devices: 27.8 us -> 16.6 us  [by_mask(): lax.ppermute(a, 'col', [(c, c ^ mask) for c in range(ncol)])]
    ppermute x14, starting transfers between devices: 6.54 us -> 9.4 us  [by_row(): return lambda a: lax.ppermute(a, 'row', pairs)]
    ppermute x25 -> x18, starting transfers between devices: 19.2 us -> 16.7 us  [by_mask(): lax.ppermute(a, 'col', [(c, c ^ mask) for c in range(ncol)])]
    unnamed x80 -> x62, local copies, waits for them, and re-layouts: 4.64 us -> 3.62 us
  transfers between devices with their start and end apart: 39 -> 32, of which waited for: 14 -> 14; matrix products, arithmetic and copies ran while one was open for 3% -> 1% of each run, Pallas kernels for 2% -> 16%
where the time goes in v4:
time: 115 us
  waiting for transfers between devices  57.4 us (50%)
  starting transfers between devices  26.1 us (23%)
  Pallas kernels  23.8 us (21%)
  local copies, waits for them, and re-layouts  4.23 us (4%)
  other arithmetic  2.71 us (2%)
    ppermute x14, waiting for transfers between devices, by_row(): return lambda a: lax.ppermute(a, 'row', pairs)  40.8 us
    ppermute x18, starting transfers between devices, by_mask(): lax.ppermute(a, 'col', [(c, c ^ mask) for c in range(ncol)])  16.7 us
    ppermute x18, waiting for transfers between devices, by_mask(): lax.ppermute(a, 'col', [(c, c ^ mask) for c in range(ncol)])  16.6 us
    ppermute x14, starting transfers between devices, by_row(): return lambda a: lax.ppermute(a, 'row', pairs)  9.4 us
    pallas_call x2, Pallas kernels, body(): pl.pallas_call(functools.partial(second_kernel, entries, layers, len(arra...  8.92 us
    pallas_call x1, Pallas kernels, body(): pl.pallas_call(functools.partial(first_kernel, entries, layers, len(array...  6.01 us
    pallas_call x2, Pallas kernels, pack(): pl.pallas_call(functools.partial(pack_kernel, ncol, mats, slots), out_sha...  4.14 us
    unnamed x62, local copies, waits for them, and re-layouts  3.62 us
  transfers between devices with their start and end apart: 32, of which 14 were waited for; matrix products, arithmetic and copies ran while one was open for 1% of the time, Pallas kernels for 16%

profile of v4, /device:TPU:1, one launch (start us, length us, event | category | flops | bytes accessed | tf_op | source)
XLA Modules:
  0.0 114.5 jit_solution(12146077695451663454)
XLA Ops:
  0.7 2.7 %collective-permute-start.2 = (s32[3,4]{1,0:T(4,128)S(1)}, s32[3,4]{1,0:T(4,128)S(1)}, u32[]{:S(2)}, u32[]{:S(2)}) collective-permute-start(s32[3,4]{1,0:T(4,128)S(1)} %bitcast.22), channel_id=1, source_target_pairs={{0,3},{1,2},{2,1},{3,0},{4,7},{5,6},{6,5},{7,4},{8,11},{9,10},{10,... | collective-permute-start | bytes 152 | tf_op jit(solution)/shard_map/ppermute | solution.py:162
  4.2 2.5 %split.1 = (bf16[1,128,512]{2,1,0:T(8,128)(2,1)}, bf16[1,128,512]{2,1,0:T(8,128)(2,1)}, bf16[1,128,512]{2,1,0:T(8,128)(2,1)}, bf16[1,128,512]{2,1,0:T(8,128)(2,1...) custom-call(s32[8]{0:T(128)} %stack.62.place, ...), custom_call_target="tpu_custom_call" | custom-call | bytes 3145728 | tf_op jit(solution)/shard_map/split/pallas_call | solution.py:180
  8.1 1.3 %collective-permute-start.4 = (bf16[2,128,512]{2,1,0:T(8,128)(2,1)}, bf16[2,128,512]{2,1,0:T(8,128)(2,1)S(1)}, u32[]{:S(2)}, u32[]{:S(2)}) collective-permute-start(bf16[2,128,512]{2,1,0:T(8,128)(2,1)} %get-tuple-element.47), channel_id=1, source_target_pairs={{0,2},{1,3},{2,0},{3,1},{4,6},{5,7},{6,4},{7,5},{8,10},{9,11},{10,... | collective-permute-start | bytes 786440 | tf_op jit(solution)/shard_map/ppermute | solution.py:162
  10.0 1.3 %collective-permute-start.7 = (bf16[1,128,512]{2,1,0:T(8,128)(2,1)}, bf16[1,128,512]{2,1,0:T(8,128)(2,1)S(1)}, u32[]{:S(2)}, u32[]{:S(2)}) collective-permute-start(bf16[1,128,512]{2,1,0:T(8,128)(2,1)} %get-tuple-element.51), channel_id=1, source_target_pairs={{0,2},{1,3},{2,0},{3,1},{4,6},{5,7},{6,4},{7,5},{8,10},{9,11},{10,... | collective-permute-start | bytes 393224 | tf_op jit(solution)/shard_map/ppermute | solution.py:162
  11.9 4.4 %collective-permute-done.4.refs_2_ = bf16[2,128,512]{2,1,0:T(8,128)(2,1)S(1)} collective-permute-done((bf16[2,128,512]{2,1,0:T(8,128)(2,1)}, bf16[2,128,512]{2,1,0:T(8,128)(2,1)S(1)}, u32[]{:S(2)}, u32[]{:S(2)}) %collective-permute-start.4) | collective-permute-done | bytes 262176 | tf_op jit(solution)/shard_map/ppermute | solution.py:162
  16.3 6.1 %collective-permute-done.5.refs_3_ = bf16[2,128,512]{2,1,0:T(8,128)(2,1)S(1)} collective-permute-done((bf16[2,128,512]{2,1,0:T(8,128)(2,1)}, bf16[2,128,512]{2,1,0:T(8,128)(2,1)S(1)}, u32[]{:S(2)}, u32[]{:S(2)}) %collective-permute-start.5) | collective-permute-done | bytes 262176 | tf_op jit(solution)/shard_map/ppermute | solution.py:162
  23.1 2.2 %pack.2.own.refs_0_ = bf16[1040,128]{1,0:T(8,128)(2,1)} custom-call(s32[8]{0:T(128)} %stack.62.place, s32[4,3,4]{2,1,0:T(4,128)} %pad_add_fusion.keep, bf16[2,128,512]{2,1,0:T(8,128)(2,1)} %get-tuple-element.45.refs_0_, bf16[2,128,512]{2,1,0:T(8,128)(2,1)} %copy-done.19, bf16[2,128,512]{2,1,0:T(8,128)(2,1)} %copy-done.20, bf16[2,128,512]{2,1,0:T(8,128)(2,1)} %copy-done.21), custom_call_target="tpu_custom_call" | custom-call | bytes 4194304 | tf_op jit(solution)/shard_map/pack/pallas_call | solution.py:200
  25.3 1.3 %collective-permute-start.19 = (bf16[1040,128]{1,0:T(8,128)(2,1)}, bf16[1040,128]{1,0:T(8,128)(2,1)S(1)}, u32[]{:S(2)}, u32[]{:S(2)}) collective-permute-start(bf16[1040,128]{1,0:T(8,128)(2,1)} %pack.2.own.refs_0_), channel_id=1, source_target_pairs={{0,4},{4,0},{8,12},{12,8},{16,20},{20,16},{24,28},{28,24},{1,5},{5... | collective-permute-start | bytes 798728 | tf_op jit(solution)/shard_map/ppermute | solution.py:159
  26.5 1.3 %collective-permute-start.20 = (bf16[1040,128]{1,0:T(8,128)(2,1)}, bf16[1040,128]{1,0:T(8,128)(2,1)S(1)}, u32[]{:S(2)}, u32[]{:S(2)}) collective-permute-start(bf16[1040,128]{1,0:T(8,128)(2,1)} %pack.2.own.refs_0_), channel_id=1, source_target_pairs={{0,8},{4,12},{8,16},{12,20},{16,24},{20,28},{24,0},{28,4},{1,9},{5... | collective-permute-start | bytes 798728 | tf_op jit(solution)/shard_map/ppermute | solution.py:159
  28.6 1.9 %pack.3.refs_0_ = bf16[912,128]{1,0:T(8,128)(2,1)} custom-call(s32[8]{0:T(128)} %stack.62.place, s32[4,3,4]{2,1,0:T(4,128)} %pad_add_fusion.keep, bf16[1,128,512]{2,1,0:T(8,128)(2,1)} %get-tuple-element.49.refs_0_, bf16[1,128,512]{2,1,0:T(8,128)(2,1)} %copy-done.25, bf16[1,128,512]{2,1,0:T(8,128)(2,1)} %copy-done.26, bf16[1,128,512]{2,1,0:T(8,128)(2,1)} %copy-done.27), custom_call_target="tpu_custom_call" | custom-call | bytes 4194304 | tf_op jit(solution)/shard_map/pack/pallas_call | solution.py:200
  31.5 1.3 %collective-permute-start.10 = (bf16[912,128]{1,0:T(8,128)(2,1)}, bf16[912,128]{1,0:T(8,128)(2,1)S(1)}, u32[]{:S(2)}, u32[]{:S(2)}) collective-permute-start(bf16[912,128]{1,0:T(8,128)(2,1)} %pack.3.refs_0_), channel_id=1, source_target_pairs={{0,8},{4,12},{8,16},{12,20},{16,24},{20,28},{24,0},{28,4},{1,9},{5... | collective-permute-start | bytes 700424 | tf_op jit(solution)/shard_map/ppermute | solution.py:159
  32.8 5.6 %collective-permute-done.9.refs_1_ = bf16[912,128]{1,0:T(8,128)(2,1)S(1)} collective-permute-done((bf16[912,128]{1,0:T(8,128)(2,1)}, bf16[912,128]{1,0:T(8,128)(2,1)S(1)}, u32[]{:S(2)}, u32[]{:S(2)}) %collective-permute-start.9) | collective-permute-done | bytes 233504 | tf_op jit(solution)/shard_map/ppermute | solution.py:159
  38.4 3.2 %collective-permute-done.10.refs_2_ = bf16[912,128]{1,0:T(8,128)(2,1)S(1)} collective-permute-done((bf16[912,128]{1,0:T(8,128)(2,1)}, bf16[912,128]{1,0:T(8,128)(2,1)S(1)}, u32[]{:S(2)}, u32[]{:S(2)}) %collective-permute-start.10) | collective-permute-done | bytes 233504 | tf_op jit(solution)/shard_map/ppermute | solution.py:159
  41.6 1.2 %pad_maximum_fusion.2 = bf16[3120,128]{1,0:T(8,128)(2,1)S(1)} fusion(bf16[1040,128]{1,0:T(8,128)(2,1)S(1)} %collective-permute-done.20.refs_2_, bf16[1040,128]{1,0:T(8,128)(2,1)S(1)} %collective-permute-done.19.refs_1_, bf16[1040,128]{1,0:T(8,128)(2,1)} %pack.2.own.refs_0_), kind=kLoop, calls=%fused_computation.2 | loop fusion | flops 2396160 | bytes 1597440 | tf_op jit(solution)/shard_map/concatenate | solution.py:212
  45.4 6.1 %collective-permute-done.21.refs_3_ = bf16[1040,128]{1,0:T(8,128)(2,1)S(1)} collective-permute-done((bf16[1040,128]{1,0:T(8,128)(2,1)S(1)}, bf16[1040,128]{1,0:T(8,128)(2,1)S(1)}, u32[]{:S(2)}, u32[]{:S(2)}) %collective-permute-start.21) | collective-permute-done | bytes 266272 | tf_op jit(solution)/shard_map/ppermute | solution.py:159
  51.5 1.7 %collective-permute-done.22.refs_5_ = bf16[1040,128]{1,0:T(8,128)(2,1)S(1)} collective-permute-done((bf16[1040,128]{1,0:T(8,128)(2,1)S(1)}, bf16[1040,128]{1,0:T(8,128)(2,1)S(1)}, u32[]{:S(2)}, u32[]{:S(2)}) %collective-permute-start.22) | collective-permute-done | bytes 266272 | tf_op jit(solution)/shard_map/ppermute | solution.py:159
  53.3 1.3 %collective-permute-start.24 = (bf16[1040,128]{1,0:T(8,128)(2,1)S(1)}, bf16[1040,128]{1,0:T(8,128)(2,1)S(1)}, u32[]{:S(2)}, u32[]{:S(2)}) collective-permute-start(bf16[1040,128]{1,0:T(8,128)(2,1)S(1)} %collective-permute-done.22.refs_5_), channel_id=1, source_target_pairs={{0,4},{4,0},{8,12},{12,8},{16,20},{20,16},{24,28},{28,24},{1,5},{5... | collective-permute-start | bytes 798728 | tf_op jit(solution)/shard_map/ppermute | solution.py:159
  54.5 2.0 %collective-permute-done.11.refs_3_ = bf16[912,128]{1,0:T(8,128)(2,1)S(1)} collective-permute-done((bf16[912,128]{1,0:T(8,128)(2,1)S(1)}, bf16[912,128]{1,0:T(8,128)(2,1)S(1)}, u32[]{:S(2)}, u32[]{:S(2)}) %collective-permute-start.11) | collective-permute-done | bytes 233504 | tf_op jit(solution)/shard_map/ppermute | solution.py:159
  56.5 1.7 %collective-permute-done.12.refs_5_ = bf16[912,128]{1,0:T(8,128)(2,1)S(1)} collective-permute-done((bf16[912,128]{1,0:T(8,128)(2,1)S(1)}, bf16[912,128]{1,0:T(8,128)(2,1)S(1)}, u32[]{:S(2)}, u32[]{:S(2)}) %collective-permute-start.12) | collective-permute-done | bytes 233504 | tf_op jit(solution)/shard_map/ppermute | solution.py:159
  58.6 7.0 %collective-permute-done.14.refs_6_ = bf16[912,128]{1,0:T(8,128)(2,1)S(1)} collective-permute-done((bf16[912,128]{1,0:T(8,128)(2,1)S(1)}, bf16[912,128]{1,0:T(8,128)(2,1)S(1)}, u32[]{:S(2)}, u32[]{:S(2)}) %collective-permute-start.14) | collective-permute-done | bytes 233504 | tf_op jit(solution)/shard_map/ppermute | solution.py:159
  65.6 3.4 %collective-permute-done.15.refs_7_ = bf16[912,128]{1,0:T(8,128)(2,1)S(1)} collective-permute-done((bf16[912,128]{1,0:T(8,128)(2,1)S(1)}, bf16[912,128]{1,0:T(8,128)(2,1)S(1)}, u32[]{:S(2)}, u32[]{:S(2)}) %collective-permute-start.15) | collective-permute-done | bytes 233504 | tf_op jit(solution)/shard_map/ppermute | solution.py:159
  69.2 3.3 %collective-permute-start.27 = (bf16[4160,128]{1,0:T(8,128)(2,1)S(1)}, bf16[4160,128]{1,0:T(8,128)(2,1)S(1)}, u32[]{:S(2)}, u32[]{:S(2)}) collective-permute-start(bf16[4160,128]{1,0:T(8,128)(2,1)S(1)} %pad_maximum_fusion), channel_id=1, source_target_pairs={{0,1},{1,0},{2,3},{3,2},{4,5},{5,4},{6,7},{7,6},{8,9},{9,8},{10,11... | collective-permute-start | bytes 3194888 | tf_op jit(solution)/shard_map/ppermute | solution.py:162
  74.5 5.8 %collective-permute-done.16.refs_8_ = bf16[912,128]{1,0:T(8,128)(2,1)S(1)} collective-permute-done((bf16[912,128]{1,0:T(8,128)(2,1)S(1)}, bf16[912,128]{1,0:T(8,128)(2,1)S(1)}, u32[]{:S(2)}, u32[]{:S(2)}) %collective-permute-start.16) | collective-permute-done | bytes 233504 | tf_op jit(solution)/shard_map/ppermute | solution.py:159
  80.3 1.4 %collective-permute-start.18 = (bf16[912,128]{1,0:T(8,128)(2,1)S(1)}, bf16[912,128]{1,0:T(8,128)(2,1)S(1)}, u32[]{:S(2)}, u32[]{:S(2)}) collective-permute-start(bf16[912,128]{1,0:T(8,128)(2,1)S(1)} %collective-permute-done.16.refs_8_), channel_id=1, source_target_pairs={{0,1},{1,0},{2,3},{3,2},{4,5},{5,4},{6,7},{7,6},{8,9},{9,8},{10,11... | collective-permute-start | bytes 700424 | tf_op jit(solution)/shard_map/ppermute | solution.py:162
  81.7 4.3 %collective-permute-done.26.refs_0_ = bf16[1040,128]{1,0:T(8,128)(2,1)S(1)} collective-permute-done((bf16[1040,128]{1,0:T(8,128)(2,1)S(1)}, bf16[1040,128]{1,0:T(8,128)(2,1)S(1)}, u32[]{:S(2)}, u32[]{:S(2)}) %collective-permute-start.26) | collective-permute-done | bytes 266272 | tf_op jit(solution)/shard_map/ppermute | solution.py:159
  87.6 6.0 %first.1.prods = bf16[32,128,128]{2,1,0:T(8,128)(2,1)} custom-call(s32[8]{0:T(128)} %stack.62.place, bf16[1040,128]{1,0:T(8,128)(2,1)} %pack.2.own.refs_0_, bf16[912,128]{1,0:T(8,128)(2,1)} %pack.3.refs_0_, bf16[912,128]{1,0:T(8,128)(2,1)} %copy-done.13, bf16[912,128]{1,0:T(8,128)(2,1)} %copy-done.14, bf16[912,128]{1,0:T(8,128)(2,1)} %copy-done.8, ...), custom_call_target="tpu_custom_call" | custom-call | flops 234881024 | bytes 10000000 | tf_op jit(solution)/shard_map/first/pallas_call | solution.py:254
  93.7 5.3 %second.1.refs_2_ = f32[16,128,128]{2,1,0:T(8,128)} custom-call(s32[8]{0:T(128)} %stack.62.place, bf16[32,128,128]{2,1,0:T(8,128)(2,1)} %first.1.prods, bf16[1040,128]{1,0:T(8,128)(2,1)} %pack.2.own.refs_0_, bf16[1040,128]{1,0:T(8,128)(2,1)} %copy-done.1, bf16[1040,128]{1,0:T(8,128)(2,1)} %copy-done.2, bf16[1040,128]{1,0:T(8,128)(2,1)} %copy-done.4, ...), custom_call_target="tpu_custom_call" | custom-call | flops 536870912 | bytes 12000000 | tf_op jit(solution)/shard_map/second/pallas_call | solution.py:269
  99.7 3.6 %third.1 = (f32[4,128,128]{2,1,0:T(8,128)}, f32[4,128,128]{2,1,0:T(8,128)}, bf16[4,128,128]{2,1,0:T(8,128)(2,1)}, bf16[4,128,128]{2,1,0:T(8,128)(2,1)}) custom-call(s32[8]{0:T(128)} %stack.62.place, bf16[32,128,128]{2,1,0:T(8,128)(2,1)} %first.1.prods, bf16[1040,128]{1,0:T(8,128)(2,1)} %copy-done.17, bf16[1040,128]{1,0:T(8,128)(2,1)} %copy-done.18, ...), custom_call_target="tpu_custom_call" | custom-call | flops 67108864 | bytes 6000000 | tf_op jit(solution)/shard_map/third/pallas_call | solution.py:279
  103.3 1.3 %collective-permute-start.30 = (bf16[4,128,128]{2,1,0:T(8,128)(2,1)}, bf16[4,128,128]{2,1,0:T(8,128)(2,1)S(1)}, u32[]{:S(2)}, u32[]{:S(2)}) collective-permute-start(bf16[4,128,128]{2,1,0:T(8,128)(2,1)} %get-tuple-element.73), channel_id=1, source_target_pairs={{0,2},{1,3},{2,0},{3,1},{4,6},{5,7},{6,4},{7,5},{8,10},{9,11},{10,... | collective-permute-start | bytes 393224 | tf_op jit(solution)/shard_map/ppermute | solution.py:162
  105.4 2.7 %collective-permute-done.30.refs_2_ = bf16[4,128,128]{2,1,0:T(8,128)(2,1)S(1)} collective-permute-done((bf16[4,128,128]{2,1,0:T(8,128)(2,1)}, bf16[4,128,128]{2,1,0:T(8,128)(2,1)S(1)}, u32[]{:S(2)}, u32[]{:S(2)}) %collective-permute-start.30) | collective-permute-done | bytes 131104 | tf_op jit(solution)/shard_map/ppermute | solution.py:162
  108.1 3.5 %collective-permute-done.31.refs_3_ = bf16[4,128,128]{2,1,0:T(8,128)(2,1)S(1)} collective-permute-done((bf16[4,128,128]{2,1,0:T(8,128)(2,1)}, bf16[4,128,128]{2,1,0:T(8,128)(2,1)S(1)}, u32[]{:S(2)}, u32[]{:S(2)}) %collective-permute-start.31) | collective-permute-done | bytes 131104 | tf_op jit(solution)/shard_map/ppermute | solution.py:162
  112.3 2.2 %join.1 = f32[2,256,512]{2,1,0:T(8,128)} custom-call(s32[8]{0:T(128)} %stack.62.place, s32[2,4]{1,0:T(2,128)} %keep.1, f32[4,128,128]{2,1,0:T(8,128)} %get-tuple-element.71.refs_0_, f32[4,128,128]{2,1,0:T(8,128)} %copy-done.22, bf16[4,128,128]{2,1,0:T(8,128)(2,1)} %copy-done.28, bf16[4,128,128]{2,1,0:T(8,128)(2,1)} %copy-done.29), custom_call_target="tpu_custom_call" | custom-call | bytes 2097152 | tf_op jit(solution)/shard_map/join/pallas_call | solution.py:290
  (110 shorter events, 15.6 us)
Async XLA Ops:
  0.7 6.0 %collective-permute-start.2 = (s32[3,4]{1,0:T(4,128)S(1)}, s32[3,4]{1,0:T(4,128)S(1)}, u32[]{:S(2)}, u32[]{:S(2)}) collective-permute-start(s32[3,4]{1,0:T(4,128)S(1)} %bitcast.22), channel_id=1, source_target_pairs={{0,3},{1,2},{2,1},{3,0},{4,7},{5,6},{6,5},{7,4},{8,11},{9,10},{10,... | collective-permute-start | bytes 152 | tf_op jit(solution)/shard_map/ppermute | solution.py:162
  3.4 3.3 %collective-permute-start = (s32[3,4]{1,0:T(4,128)S(1)}, s32[3,4]{1,0:T(4,128)S(1)}, u32[]{:S(2)}, u32[]{:S(2)}) collective-permute-start(s32[3,4]{1,0:T(4,128)S(1)} %bitcast.23), channel_id=1, source_target_pairs={{0,1},{1,0},{2,3},{3,2},{4,5},{5,4},{6,7},{7,6},{8,9},{9,8},{10,11... | collective-permute-start | bytes 152 | tf_op jit(solution)/shard_map/ppermute | solution.py:162
  3.4 3.3 %collective-permute-start.1 = (s32[3,4]{1,0:T(4,128)S(1)}, s32[3,4]{1,0:T(4,128)S(1)}, u32[]{:S(2)}, u32[]{:S(2)}) collective-permute-start(s32[3,4]{1,0:T(4,128)S(1)} %bitcast.24), channel_id=1, source_target_pairs={{0,2},{1,3},{2,0},{3,1},{4,6},{5,7},{6,4},{7,5},{8,10},{9,11},{10,... | collective-permute-start | bytes 152 | tf_op jit(solution)/shard_map/ppermute | solution.py:162
  7.4 3.9 %collective-permute-start.3 = (bf16[2,128,512]{2,1,0:T(8,128)(2,1)}, bf16[2,128,512]{2,1,0:T(8,128)(2,1)S(1)}, u32[]{:S(2)}, u32[]{:S(2)}) collective-permute-start(bf16[2,128,512]{2,1,0:T(8,128)(2,1)} %get-tuple-element.46), channel_id=1, source_target_pairs={{0,1},{1,0},{2,3},{3,2},{4,5},{5,4},{6,7},{7,6},{8,9},{9,8},{10,11... | collective-permute-start | bytes 786440 | tf_op jit(solution)/shard_map/ppermute | solution.py:162
  8.1 8.1 %collective-permute-start.4 = (bf16[2,128,512]{2,1,0:T(8,128)(2,1)}, bf16[2,128,512]{2,1,0:T(8,128)(2,1)S(1)}, u32[]{:S(2)}, u32[]{:S(2)}) collective-permute-start(bf16[2,128,512]{2,1,0:T(8,128)(2,1)} %get-tuple-element.47), channel_id=1, source_target_pairs={{0,2},{1,3},{2,0},{3,1},{4,6},{5,7},{6,4},{7,5},{8,10},{9,11},{10,... | collective-permute-start | bytes 786440 | tf_op jit(solution)/shard_map/ppermute | solution.py:162
  9.4 13.0 %collective-permute-start.5 = (bf16[2,128,512]{2,1,0:T(8,128)(2,1)}, bf16[2,128,512]{2,1,0:T(8,128)(2,1)S(1)}, u32[]{:S(2)}, u32[]{:S(2)}) collective-permute-start(bf16[2,128,512]{2,1,0:T(8,128)(2,1)} %get-tuple-element.48), channel_id=1, source_target_pairs={{0,3},{1,2},{2,1},{3,0},{4,7},{5,6},{6,5},{7,4},{8,11},{9,10},{10,... | collective-permute-start | bytes 786440 | tf_op jit(solution)/shard_map/ppermute | solution.py:162
  9.8 18.1 %collective-permute-start.6 = (bf16[1,128,512]{2,1,0:T(8,128)(2,1)}, bf16[1,128,512]{2,1,0:T(8,128)(2,1)S(1)}, u32[]{:S(2)}, u32[]{:S(2)}) collective-permute-start(bf16[1,128,512]{2,1,0:T(8,128)(2,1)} %get-tuple-element.50), channel_id=1, source_target_pairs={{0,1},{1,0},{2,3},{3,2},{4,5},{5,4},{6,7},{7,6},{8,9},{9,8},{10,11... | collective-permute-start | bytes 393224 | tf_op jit(solution)/shard_map/ppermute | solution.py:162
  10.0 17.8 %collective-permute-start.7 = (bf16[1,128,512]{2,1,0:T(8,128)(2,1)}, bf16[1,128,512]{2,1,0:T(8,128)(2,1)S(1)}, u32[]{:S(2)}, u32[]{:S(2)}) collective-permute-start(bf16[1,128,512]{2,1,0:T(8,128)(2,1)} %get-tuple-element.51), channel_id=1, source_target_pairs={{0,2},{1,3},{2,0},{3,1},{4,6},{5,7},{6,4},{7,5},{8,10},{9,11},{10,... | collective-permute-start | bytes 393224 | tf_op jit(solution)/shard_map/ppermute | solution.py:162
  11.3 16.6 %collective-permute-start.8 = (bf16[1,128,512]{2,1,0:T(8,128)(2,1)}, bf16[1,128,512]{2,1,0:T(8,128)(2,1)S(1)}, u32[]{:S(2)}, u32[]{:S(2)}) collective-permute-start(bf16[1,128,512]{2,1,0:T(8,128)(2,1)} %get-tuple-element.52), channel_id=1, source_target_pairs={{0,3},{1,2},{2,1},{3,0},{4,7},{5,6},{6,5},{7,4},{8,11},{9,10},{10,... | collective-permute-start | bytes 393224 | tf_op jit(solution)/shard_map/ppermute | solution.py:162
  25.3 16.3 %collective-permute-start.19 = (bf16[1040,128]{1,0:T(8,128)(2,1)}, bf16[1040,128]{1,0:T(8,128)(2,1)S(1)}, u32[]{:S(2)}, u32[]{:S(2)}) collective-permute-start(bf16[1040,128]{1,0:T(8,128)(2,1)} %pack.2.own.refs_0_), channel_id=1, source_target_pairs={{0,4},{4,0},{8,12},{12,8},{16,20},{20,16},{24,28},{28,24},{1,5},{5... | collective-permute-start | bytes 798728 | tf_op jit(solution)/shard_map/ppermute | solution.py:159
  26.5 15.0 %collective-permute-start.20 = (bf16[1040,128]{1,0:T(8,128)(2,1)}, bf16[1040,128]{1,0:T(8,128)(2,1)S(1)}, u32[]{:S(2)}, u32[]{:S(2)}) collective-permute-start(bf16[1040,128]{1,0:T(8,128)(2,1)} %pack.2.own.refs_0_), channel_id=1, source_target_pairs={{0,8},{4,12},{8,16},{12,20},{16,24},{20,28},{24,0},{28,4},{1,9},{5... | collective-permute-start | bytes 798728 | tf_op jit(solution)/shard_map/ppermute | solution.py:159
  30.5 7.9 %collective-permute-start.9 = (bf16[912,128]{1,0:T(8,128)(2,1)}, bf16[912,128]{1,0:T(8,128)(2,1)S(1)}, u32[]{:S(2)}, u32[]{:S(2)}) collective-permute-start(bf16[912,128]{1,0:T(8,128)(2,1)} %pack.3.refs_0_), channel_id=1, source_target_pairs={{0,4},{4,0},{8,12},{12,8},{16,20},{20,16},{24,28},{28,24},{1,5},{5... | collective-permute-start | bytes 700424 | tf_op jit(solution)/shard_map/ppermute | solution.py:159
  31.5 10.1 %collective-permute-start.10 = (bf16[912,128]{1,0:T(8,128)(2,1)}, bf16[912,128]{1,0:T(8,128)(2,1)S(1)}, u32[]{:S(2)}, u32[]{:S(2)}) collective-permute-start(bf16[912,128]{1,0:T(8,128)(2,1)} %pack.3.refs_0_), channel_id=1, source_target_pairs={{0,8},{4,12},{8,16},{12,20},{16,24},{20,28},{24,0},{28,4},{1,9},{5... | collective-permute-start | bytes 700424 | tf_op jit(solution)/shard_map/ppermute | solution.py:159
  42.8 10.5 %collective-permute-start.23 = (bf16[3120,128]{1,0:T(8,128)(2,1)S(1)}, bf16[3120,128]{1,0:T(8,128)(2,1)S(1)}, u32[]{:S(2)}, u32[]{:S(2)}) collective-permute-start(bf16[3120,128]{1,0:T(8,128)(2,1)S(1)} %pad_maximum_fusion.2), channel_id=1, source_target_pairs={{0,1},{1,0},{2,3},{3,2},{4,5},{5,4},{6,7},{7,6},{8,9},{9,8},{10,11... | collective-permute-start | bytes 2396168 | tf_op jit(solution)/shard_map/ppermute | solution.py:162
  43.8 14.4 %collective-permute-start.13 = (bf16[2736,128]{1,0:T(8,128)(2,1)S(1)}, bf16[2736,128]{1,0:T(8,128)(2,1)S(1)}, u32[]{:S(2)}, u32[]{:S(2)}) collective-permute-start(bf16[2736,128]{1,0:T(8,128)(2,1)S(1)} %pad_maximum_fusion.3), channel_id=1, source_target_pairs={{0,1},{1,0},{2,3},{3,2},{4,5},{5,4},{6,7},{7,6},{8,9},{9,8},{10,11... | collective-permute-start | bytes 2101256 | tf_op jit(solution)/shard_map/ppermute | solution.py:162
  43.9 7.6 %collective-permute-start.21 = (bf16[1040,128]{1,0:T(8,128)(2,1)S(1)}, bf16[1040,128]{1,0:T(8,128)(2,1)S(1)}, u32[]{:S(2)}, u32[]{:S(2)}) collective-permute-start(bf16[1040,128]{1,0:T(8,128)(2,1)S(1)} %collective-permute-done.20.refs_2_), channel_id=1, source_target_pairs={{0,4},{4,0},{8,12},{12,8},{16,20},{20,16},{24,28},{28,24},{1,5},{5... | collective-permute-start | bytes 798728 | tf_op jit(solution)/shard_map/ppermute | solution.py:159
  44.2 9.0 %collective-permute-start.22 = (bf16[1040,128]{1,0:T(8,128)(2,1)S(1)}, bf16[1040,128]{1,0:T(8,128)(2,1)S(1)}, u32[]{:S(2)}, u32[]{:S(2)}) collective-permute-start(bf16[1040,128]{1,0:T(8,128)(2,1)S(1)} %collective-permute-done.20.refs_2_), channel_id=1, source_target_pairs={{0,8},{4,12},{8,16},{12,20},{16,24},{20,28},{24,0},{28,4},{1,9},{5... | collective-permute-start | bytes 798728 | tf_op jit(solution)/shard_map/ppermute | solution.py:159
  44.2 12.3 %collective-permute-start.11 = (bf16[912,128]{1,0:T(8,128)(2,1)S(1)}, bf16[912,128]{1,0:T(8,128)(2,1)S(1)}, u32[]{:S(2)}, u32[]{:S(2)}) collective-permute-start(bf16[912,128]{1,0:T(8,128)(2,1)S(1)} %collective-permute-done.10.refs_2_), channel_id=1, source_target_pairs={{0,4},{4,0},{8,12},{12,8},{16,20},{20,16},{24,28},{28,24},{1,5},{5... | collective-permute-start | bytes 700424 | tf_op jit(solution)/shard_map/ppermute | solution.py:159
  51.5 6.7 %collective-permute-start.12 = (bf16[912,128]{1,0:T(8,128)(2,1)S(1)}, bf16[912,128]{1,0:T(8,128)(2,1)S(1)}, u32[]{:S(2)}, u32[]{:S(2)}) collective-permute-start(bf16[912,128]{1,0:T(8,128)(2,1)S(1)} %collective-permute-done.10.refs_2_), channel_id=1, source_target_pairs={{0,8},{4,12},{8,16},{12,20},{16,24},{20,28},{24,0},{28,4},{1,9},{5... | collective-permute-start | bytes 700424 | tf_op jit(solution)/shard_map/ppermute | solution.py:159
  53.3 15.8 %collective-permute-start.24 = (bf16[1040,128]{1,0:T(8,128)(2,1)S(1)}, bf16[1040,128]{1,0:T(8,128)(2,1)S(1)}, u32[]{:S(2)}, u32[]{:S(2)}) collective-permute-start(bf16[1040,128]{1,0:T(8,128)(2,1)S(1)} %collective-permute-done.22.refs_5_), channel_id=1, source_target_pairs={{0,4},{4,0},{8,12},{12,8},{16,20},{20,16},{24,28},{28,24},{1,5},{5... | collective-permute-start | bytes 798728 | tf_op jit(solution)/shard_map/ppermute | solution.py:159
  54.5 14.5 %collective-permute-start.25 = (bf16[1040,128]{1,0:T(8,128)(2,1)S(1)}, bf16[1040,128]{1,0:T(8,128)(2,1)S(1)}, u32[]{:S(2)}, u32[]{:S(2)}) collective-permute-start(bf16[1040,128]{1,0:T(8,128)(2,1)S(1)} %collective-permute-done.22.refs_5_), channel_id=1, source_target_pairs={{0,8},{4,12},{8,16},{12,20},{16,24},{20,28},{24,0},{28,4},{1,9},{5... | collective-permute-start | bytes 798728 | tf_op jit(solution)/shard_map/ppermute | solution.py:159
  58.2 7.4 %collective-permute-start.14 = (bf16[912,128]{1,0:T(8,128)(2,1)S(1)}, bf16[912,128]{1,0:T(8,128)(2,1)S(1)}, u32[]{:S(2)}, u32[]{:S(2)}) collective-permute-start(bf16[912,128]{1,0:T(8,128)(2,1)S(1)} %collective-permute-done.12.refs_5_), channel_id=1, source_target_pairs={{0,4},{4,0},{8,12},{12,8},{16,20},{20,16},{24,28},{28,24},{1,5},{5... | collective-permute-start | bytes 700424 | tf_op jit(solution)/shard_map/ppermute | solution.py:159
  58.5 10.5 %collective-permute-start.15 = (bf16[912,128]{1,0:T(8,128)(2,1)S(1)}, bf16[912,128]{1,0:T(8,128)(2,1)S(1)}, u32[]{:S(2)}, u32[]{:S(2)}) collective-permute-start(bf16[912,128]{1,0:T(8,128)(2,1)S(1)} %collective-permute-done.12.refs_5_), channel_id=1, source_target_pairs={{0,8},{4,12},{8,16},{12,20},{16,24},{20,28},{24,0},{28,4},{1,9},{5... | collective-permute-start | bytes 700424 | tf_op jit(solution)/shard_map/ppermute | solution.py:159
  69.2 16.8 %collective-permute-start.27 = (bf16[4160,128]{1,0:T(8,128)(2,1)S(1)}, bf16[4160,128]{1,0:T(8,128)(2,1)S(1)}, u32[]{:S(2)}, u32[]{:S(2)}) collective-permute-start(bf16[4160,128]{1,0:T(8,128)(2,1)S(1)} %pad_maximum_fusion), channel_id=1, source_target_pairs={{0,1},{1,0},{2,3},{3,2},{4,5},{5,4},{6,7},{7,6},{8,9},{9,8},{10,11... | collective-permute-start | bytes 3194888 | tf_op jit(solution)/shard_map/ppermute | solution.py:162
  72.5 7.7 %collective-permute-start.17 = (bf16[3648,128]{1,0:T(8,128)(2,1)S(1)}, bf16[3648,128]{1,0:T(8,128)(2,1)S(1)}, u32[]{:S(2)}, u32[]{:S(2)}) collective-permute-start(bf16[3648,128]{1,0:T(8,128)(2,1)S(1)} %pad_maximum_fusion.1), channel_id=1, source_target_pairs={{0,1},{1,0},{2,3},{3,2},{4,5},{5,4},{6,7},{7,6},{8,9},{9,8},{10,11... | collective-permute-start | bytes 2801672 | tf_op jit(solution)/shard_map/ppermute | solution.py:162
  73.0 7.3 %collective-permute-start.16 = (bf16[912,128]{1,0:T(8,128)(2,1)S(1)}, bf16[912,128]{1,0:T(8,128)(2,1)S(1)}, u32[]{:S(2)}, u32[]{:S(2)}) collective-permute-start(bf16[912,128]{1,0:T(8,128)(2,1)S(1)} %collective-permute-done.15.refs_7_), channel_id=1, source_target_pairs={{0,4},{4,0},{8,12},{12,8},{16,20},{20,16},{24,28},{28,24},{1,5},{5... | collective-permute-start | bytes 700424 | tf_op jit(solution)/shard_map/ppermute | solution.py:159
  74.2 11.8 %collective-permute-start.26 = (bf16[1040,128]{1,0:T(8,128)(2,1)S(1)}, bf16[1040,128]{1,0:T(8,128)(2,1)S(1)}, u32[]{:S(2)}, u32[]{:S(2)}) collective-permute-start(bf16[1040,128]{1,0:T(8,128)(2,1)S(1)} %collective-permute-done.25.refs_7_), channel_id=1, source_target_pairs={{0,4},{4,0},{8,12},{12,8},{16,20},{20,16},{24,28},{28,24},{1,5},{5... | collective-permute-start | bytes 798728 | tf_op jit(solution)/shard_map/ppermute | solution.py:159
  80.3 6.7 %collective-permute-start.18 = (bf16[912,128]{1,0:T(8,128)(2,1)S(1)}, bf16[912,128]{1,0:T(8,128)(2,1)S(1)}, u32[]{:S(2)}, u32[]{:S(2)}) collective-permute-start(bf16[912,128]{1,0:T(8,128)(2,1)S(1)} %collective-permute-done.16.refs_8_), channel_id=1, source_target_pairs={{0,1},{1,0},{2,3},{3,2},{4,5},{5,4},{6,7},{7,6},{8,9},{9,8},{10,11... | collective-permute-start | bytes 700424 | tf_op jit(solution)/shard_map/ppermute | solution.py:162
  86.0 13.0 %collective-permute-start.28 = (bf16[1040,128]{1,0:T(8,128)(2,1)S(1)}, bf16[1040,128]{1,0:T(8,128)(2,1)S(1)}, u32[]{:S(2)}, u32[]{:S(2)}) collective-permute-start(bf16[1040,128]{1,0:T(8,128)(2,1)S(1)} %collective-permute-done.26.refs_0_), channel_id=1, source_target_pairs={{0,1},{1,0},{2,3},{3,2},{4,5},{5,4},{6,7},{7,6},{8,9},{9,8},{10,11... | collective-permute-start | bytes 798728 | tf_op jit(solution)/shard_map/ppermute | solution.py:162
  103.3 8.3 %collective-permute-start.29 = (f32[4,128,128]{2,1,0:T(8,128)}, f32[4,128,128]{2,1,0:T(8,128)S(1)}, u32[]{:S(2)}, u32[]{:S(2)}) collective-permute-start(f32[4,128,128]{2,1,0:T(8,128)} %get-tuple-element.72), channel_id=1, source_target_pairs={{0,1},{1,0},{2,3},{3,2},{4,5},{5,4},{6,7},{7,6},{8,9},{9,8},{10,11... | collective-permute-start | bytes 786440 | tf_op jit(solution)/shard_map/ppermute | solution.py:162
  103.3 4.8 %collective-permute-start.30 = (bf16[4,128,128]{2,1,0:T(8,128)(2,1)}, bf16[4,128,128]{2,1,0:T(8,128)(2,1)S(1)}, u32[]{:S(2)}, u32[]{:S(2)}) collective-permute-start(bf16[4,128,128]{2,1,0:T(8,128)(2,1)} %get-tuple-element.73), channel_id=1, source_target_pairs={{0,2},{1,3},{2,0},{3,1},{4,6},{5,7},{6,4},{7,5},{8,10},{9,11},{10,... | collective-permute-start | bytes 393224 | tf_op jit(solution)/shard_map/ppermute | solution.py:162
  104.5 7.0 %collective-permute-start.31 = (bf16[4,128,128]{2,1,0:T(8,128)(2,1)}, bf16[4,128,128]{2,1,0:T(8,128)(2,1)S(1)}, u32[]{:S(2)}, u32[]{:S(2)}) collective-permute-start(bf16[4,128,128]{2,1,0:T(8,128)(2,1)} %get-tuple-element.74), channel_id=1, source_target_pairs={{0,3},{1,2},{2,1},{3,0},{4,7},{5,6},{6,5},{7,4},{8,11},{9,10},{10,... | collective-permute-start | bytes 393224 | tf_op jit(solution)/shard_map/ppermute | solution.py:162
  (30 other events, 204.2 us)

commit v5 on v4

--- a/solution.py
+++ b/solution.py
@@ -21,15 +21,15 @@
     return pl.CostEstimate(flops=flops, bytes_accessed=nbytes, transcendentals=0)
 
 
-def split_kernel(place, density, hamiltonian, metric, *outs):
+def split_kernel(place, *refs):
+    arrays, outs = refs[: len(refs) - 4], refs[len(refs) - 4 :]
     spin, row = place[0], place[1]
     for v in (2, 3, 1, 0):
         other_spin = spin if v < 2 else 1 - spin
         other_row = row if v % 2 == 0 else 1 - row
         rows = pl.ds(pl.multiple_of(other_row * BLOCK, BLOCK), BLOCK)
-        outs[v][0] = density[other_spin, rows, :]
-        outs[4 + v][0] = hamiltonian[other_spin, rows, :]
-        outs[4 + v][1] = metric[rows, :]
+        for i, array in enumerate(arrays):
+            outs[v][i] = array[rows, :] if array.ndim == 2 else array[other_spin, rows, :]
 
 
 def slot_rows(slot):
@@ -86,15 +86,19 @@
     return parts
 
 
-def first_kernel(entries, layers, count, place, own, *refs):
-    bufs, out, acc, tails, cols = refs[:count], *refs[count:]
-    nblk = len(entries)
+def first_kernel(entries, layers, count, late, place, own, *refs):
+    bufs, rest = refs[:count], refs[count:]
+    if late:
+        before, out, acc, tails, cols = rest
+    else:
+        acc, tails, cols = rest
+    nblk, last = acc.shape[0] // 2, len(entries)
     parts = parts_of(entries, layers, place, DENSITY_SLOTS, bufs, tails)
-    tails[nblk : nblk + 1, :] = tail_of(own[2 * OPERATOR_SLOTS * BLOCK :, :])
+    tails[last : last + 1, :] = tail_of(own[2 * OPERATOR_SLOTS * BLOCK :, :])
     pltpu.sync_copy(tails, cols)
-    acc[...] = jnp.zeros_like(acc)
+    acc[...] = before[...] if late else jnp.zeros_like(acc)
     for i in range(2):
-        mine = [cols[nblk, i * OPERATOR_SLOTS + u] for u in range(OPERATOR_SLOTS)]
+        mine = [cols[last, i * OPERATOR_SLOTS + u] for u in range(OPERATOR_SLOTS)]
         for n, (view, k) in enumerate(parts):
             slot = jnp.int32(-1)
             for u in reversed(range(OPERATOR_SLOTS)):
@@ -107,12 +111,12 @@
                     right = view[t * BLOCK : (t + 1) * BLOCK, :]
                     acc[i * nblk + cols[n, t]] += jnp.dot(left, right, preferred_element_type=jnp.float32)
 
-    out[...] = acc[...].astype(out.dtype)
+    if late:
+        out[...] = acc[...].astype(out.dtype)
 
 
 def second_kernel(entries, layers, count, late, place, prods, *refs):
     bufs, rest = refs[:count], refs[count:]
-    before = None
     if late:
         before, *outs, acc, tails, cols = rest
     else:
@@ -176,25 +180,28 @@
     keeps = (jnp.stack([dens_keep, ham_keep, met_keep]) > 0).astype(i32)
     place = jnp.stack([spin, part, z, x] + [col ^ m for m in masks])
 
-    one, two = (jax.ShapeDtypeStruct((n, BLOCK, width), bf16) for n in (1, 2))
-    split = pl.pallas_call(
-        split_kernel,
-        out_shape=[one] * 4 + [two] * 4,
-        in_specs=[SMEM, VMEM, VMEM, VMEM],
-        out_specs=[VMEM] * 8,
-        cost_estimate=estimate(0, 24 * BLOCK * width * 2),
-        name="split",
-    )(place, density, hamiltonian, metric)
-    keep_rows = [lax.dynamic_index_in_dim(keeps, part ^ d, 1, keepdims=False) for d in (0, 1)]
+    def cut(name, *arrays):
+        piece = jax.ShapeDtypeStruct((len(arrays), BLOCK, width), bf16)
+        return pl.pallas_call(
+            split_kernel,
+            out_shape=[piece] * 4,
+            in_specs=[SMEM] + [VMEM] * len(arrays),
+            out_specs=[VMEM] * 4,
+            cost_estimate=estimate(0, 12 * len(arrays) * BLOCK * width * 2),
+            name=name,
+        )(place, *arrays)
 
     def exchange(pieces):
         moved = {m: by_mask(m)(pieces[variant(m)]) for m in reversed(range(1, ncol))}
         return [pieces[0]] + [moved[m] for m in range(1, ncol)]
 
-    got_dens = exchange(split[:4])
+    pieces = cut("cutp", density)
+    keeps, *pieces = lax.optimization_barrier((keeps, *pieces))
+    got_dens = exchange(pieces)
+    keep_rows = [lax.dynamic_index_in_dim(keeps, part ^ d, 1, keepdims=False) for d in (0, 1)]
     keep_got = jnp.stack(exchange([keep_rows[0], keep_rows[1]] * 2))
-    keep_got, *oper_pieces = lax.optimization_barrier((keep_got, *split[4:]))
-    got_oper = exchange(oper_pieces)
+    keep_got, hamiltonian, metric = lax.optimization_barrier((keep_got, hamiltonian, metric))
+    oper_pieces = cut("cuth", hamiltonian, metric)
 
     def pack(mats, slots, got):
         return pl.pallas_call(
@@ -206,40 +213,11 @@
             name="pack",
         )(place, keep_got, *got)
 
-    packed = [pack((0,), DENSITY_SLOTS, got_dens), pack((1, 2), OPERATOR_SLOTS, got_oper)]
+    dens, *oper_pieces = lax.optimization_barrier((pack((0,), DENSITY_SLOTS, got_dens), *oper_pieces))
+    got_oper = exchange(oper_pieces)
 
     def twin_of(group):
         return twin(jnp.concatenate([a for a, _ in group], axis=0) if len(group) > 1 else group[0][0])
-
-    gathered = [[], []]
-    waiting = [[], []]
-    curs = list(packed)
-    for t in range(layers):
-        for n in range(2):
-            cur, last = curs[n], t == layers - 1
-            size = cur.shape[0]
-
-            def settle(arrived, group, n=n, size=size):
-                for i, (_, key) in enumerate(group):
-                    gathered[n].append((arrived, i * size, key[:2] + (1,)))
-
-            gathered[n].append((cur, 0, (t, 0, 0)))
-            waiting[n].append((cur, (t, 0, 0)))
-            moves = [across(cur)] + ([] if last else [up(cur)])
-            flush = waiting[n] if t % 2 == 1 or last else []
-            if flush:
-                moves.append(twin_of(flush))
-            moves = list(lax.optimization_barrier(tuple(moves)))
-            side = moves[0]
-            gathered[n].append((side, 0, (t, 1, 0)))
-            if flush:
-                settle(moves[-1], flush)
-                waiting[n] = []
-            waiting[n].append((side, (t, 1, 0)))
-            if last:
-                settle(twin_of(waiting[n]), waiting[n])
-            else:
-                curs[n] = moves[1]
 
     def refs_of(entries):
         arrays = []
@@ -249,42 +227,89 @@
         place_of = {id(a): i for i, a in enumerate(arrays)}
         return arrays, [(place_of[id(a)], start, key) for a, start, key in entries]
 
-    arrays, entries = refs_of(gathered[0])
-    tables = [pltpu.VMEM((nblk + 8, BLOCK), i32), pltpu.SMEM((nblk + 8, BLOCK), i32)]
-    prods = pl.pallas_call(
-        functools.partial(first_kernel, entries, layers, len(arrays)),
-        out_shape=jax.ShapeDtypeStruct((2 * nblk, BLOCK, BLOCK), bf16),
-        in_specs=[SMEM, VMEM] + [VMEM] * len(arrays),
-        out_specs=VMEM,
-        scratch_shapes=[pltpu.VMEM((2 * nblk, BLOCK, BLOCK), f32)] + tables,
-        cost_estimate=estimate(56 * 2 * BLOCK**3, 10_000_000),
-        name="first",
-    )(place, packed[1], *arrays)
-
     final = (layers - 1, 1)
-    early = [e for e in gathered[1] if e[2][:2] != final]
-    late = [e for e in gathered[1] if e[2][:2] == final]
-    tables = [pltpu.VMEM((nblk, BLOCK), i32), pltpu.SMEM((nblk, BLOCK), i32)]
-    arrays, entries = refs_of(early)
-    half_sum = pl.pallas_call(
-        functools.partial(second_kernel, entries, layers, len(arrays), False),
-        out_shape=jax.ShapeDtypeStruct((nblk, BLOCK, BLOCK), f32),
-        in_specs=[SMEM, VMEM] + [VMEM] * len(arrays),
-        out_specs=VMEM,
-        scratch_shapes=tables,
-        cost_estimate=estimate(nblk * 16 * BLOCK**3, 12_000_000),
-        name="second",
-    )(place, prods, *arrays)
-    arrays, entries = refs_of(late)
-    outs = pl.pallas_call(
-        functools.partial(second_kernel, entries, layers, len(arrays), True),
-        out_shape=[jax.ShapeDtypeStruct((per, BLOCK, BLOCK), f32 if m < half else bf16) for m in masks],
-        in_specs=[SMEM, VMEM] + [VMEM] * len(arrays) + [VMEM],
-        out_specs=[VMEM] * 4,
-        scratch_shapes=[pltpu.VMEM((nblk, BLOCK, BLOCK), f32)] + tables,
-        cost_estimate=estimate(4 * 8 * BLOCK**3, 6_000_000),
-        name="third",
-    )(place, prods, *arrays, half_sum)
+    tables = [pltpu.VMEM((2 * nblk, BLOCK), i32), pltpu.SMEM((2 * nblk, BLOCK), i32)]
+
+    def total(n):
+        return jax.ShapeDtypeStruct(((2 - n) * nblk, BLOCK, BLOCK), f32)
+
+    def start_sum(kernel, n, given, cost, name):
+        arrays, entries = refs_of([e for e in gathered[n] if e[2][:2] != final])
+        return pl.pallas_call(
+            functools.partial(kernel, entries, layers, len(arrays), False),
+            out_shape=total(n),
+            in_specs=[SMEM] + [VMEM] * (1 + len(arrays)),
+            out_specs=VMEM,
+            scratch_shapes=tables,
+            cost_estimate=cost,
+            name=name,
+        )(place, given, *arrays)
+
+    def end_sum(kernel, n, given, acc, shapes, name):
+        arrays, entries = refs_of([e for e in gathered[n] if e[2][:2] == final])
+        return pl.pallas_call(
+            functools.partial(kernel, entries, layers, len(arrays), True),
+            out_shape=shapes,
+            in_specs=[SMEM] + [VMEM] * (2 + len(arrays)),
+            out_specs=[VMEM] * len(shapes),
+            scratch_shapes=[pltpu.VMEM(total(n).shape, f32)] + tables,
+            cost_estimate=estimate(0, 6_000_000),
+            name=name,
+        )(place, given, *arrays, acc)
+
+    gathered = [[], []]
+    waiting = [[], []]
+    curs = [dens, None]
+
+    def settle(n, arrived, group):
+        for i, (a, key) in enumerate(group):
+            gathered[n].append((arrived, i * a.shape[0], key[:2] + (1,)))
+
+    for slot in range(layers + 2):
+        moves, names = [], []
+        for n in range(2):
+            t = slot - n
+            if not 0 <= t <= layers:
+                continue
+            if t < layers:
+                gathered[n].append((curs[n], 0, (t, 0, 0)))
+                waiting[n].append((curs[n], (t, 0, 0)))
+                moves.append(across(curs[n]))
+                names.append((n, "side"))
+            if t < layers - 1:
+                moves.append(up(curs[n]))
+                names.append((n, "up"))
+            if t % 2 == 1 or t == layers:
+                moves.append(twin_of(waiting[n]))
+                settle(n, moves[-1], waiting[n])
+                waiting[n] = []
+                names.append((n, "twin"))
+        extra = got_oper[1:] if slot == 0 else []
+        if slot == layers:
+            extra = [start_sum(first_kernel, 0, oper, estimate(56 * 2 * BLOCK**3, 12_000_000), "first")]
+        tied = moves
+        if len(moves) > 1:
+            tied = lax.optimization_barrier((*moves, *extra))
+            extra = tied[len(moves) :]
+            tied = tied[: len(moves)]
+        if slot == 0:
+            oper = pack((1, 2), OPERATOR_SLOTS, [got_oper[0], *extra])
+            curs[1] = oper
+        if slot == layers:
+            dens_sum = extra[0]
+        for raw, value, (n, name) in zip(moves, tied, names, strict=True):
+            if name == "up":
+                curs[n] = value
+            if name == "side":
+                gathered[n].append((raw, 0, (slot - n, 1, 0)))
+                waiting[n].append((value, (slot - n, 1, 0)))
+
+    prods = end_sum(
+        first_kernel, 0, oper, dens_sum, [jax.ShapeDtypeStruct((2 * nblk, BLOCK, BLOCK), bf16)], "firstb"
+    )[0]
+    oper_sum = start_sum(second_kernel, 1, prods, estimate(nblk * 16 * BLOCK**3, 12_000_000), "second")
+    parts = [jax.ShapeDtypeStruct((per, BLOCK, BLOCK), f32 if m < half else bf16) for m in masks]
+    outs = end_sum(second_kernel, 1, prods, oper_sum, parts, "secondb")
 
     back = [outs[0]] + [by_mask(m)(o) for m, o in zip(masks[1:], outs[1:], strict=True)]
     return pl.pallas_call(

time: 115 us -> 121 us (1.052)
  Pallas kernels: 23.8 us -> 29.8 us
    pallas_call x4 -> x6, Pallas kernels: 17.4 us -> 23.4 us  [the longest x2 11.7 us: start_sum(): pl.pallas_call(functools.partial(kernel, entries, layers, len(arrays), Fa...]
    ppermute x18, waiting for transfers between devices: 16.6 us -> 13.1 us  [by_mask(): lax.ppermute(a, 'col', [(c, c ^ mask) for c in range(ncol)])]
    ppermute x14, starting transfers between devices: 9.4 us -> 11.8 us  [by_row(): return lambda a: lax.ppermute(a, 'row', pairs)]
    ppermute x14, waiting for transfers between devices: 40.8 us -> 43.1 us  [by_row(): return lambda a: lax.ppermute(a, 'row', pairs)]
    ppermute x18, starting transfers between devices: 16.7 us -> 15.3 us  [by_mask(): lax.ppermute(a, 'col', [(c, c ^ mask) for c in range(ncol)])]
    unnamed x62 -> x54, local copies, waits for them, and re-layouts: 3.62 us -> 2.87 us
  transfers between devices with their start and end apart: 32 -> 32, of which waited for: 14 -> 12; matrix products, arithmetic and copies ran while one was open for 1% -> 1% of each run, Pallas kernels for 16% -> 17%
where the time goes in v5:
time: 121 us
  waiting for transfers between devices  56.2 us (46%)
  Pallas kernels  29.8 us (25%)
  starting transfers between devices  27.1 us (22%)
  other arithmetic  3.74 us (3%)
  local copies, waits for them, and re-layouts  3.56 us (3%)
    ppermute x14, waiting for transfers between devices, by_row(): return lambda a: lax.ppermute(a, 'row', pairs)  43.1 us
    ppermute x18, starting transfers between devices, by_mask(): lax.ppermute(a, 'col', [(c, c ^ mask) for c in range(ncol)])  15.3 us
    ppermute x18, waiting for transfers between devices, by_mask(): lax.ppermute(a, 'col', [(c, c ^ mask) for c in range(ncol)])  13.1 us
    ppermute x14, starting transfers between devices, by_row(): return lambda a: lax.ppermute(a, 'row', pairs)  11.8 us
    pallas_call x2, Pallas kernels, start_sum(): pl.pallas_call(functools.partial(kernel, entries, layers, len(arrays), Fa...  11.7 us
    pallas_call x2, Pallas kernels, end_sum(): pl.pallas_call(functools.partial(kernel, entries, layers, len(arrays), Tr...  7.74 us
    pallas_call x2, Pallas kernels, pack(): pl.pallas_call(functools.partial(pack_kernel, ncol, mats, slots), out_sha...  4.13 us
    pallas_call x2, Pallas kernels, cut(): pl.pallas_call(split_kernel, out_shape=[piece] * 4, in_specs=[SMEM] + [VM...  4.01 us
  transfers between devices with their start and end apart: 32, of which 12 were waited for; matrix products, arithmetic and copies ran while one was open for 1% of the time, Pallas kernels for 17%

profile of v5, /device:TPU:1, one launch (start us, length us, event | category | flops | bytes accessed | tf_op | source)
XLA Modules:
  0.0 120.6 jit_solution(3050040499947083103)
XLA Ops:
  0.7 1.9 %cutp.1 = (bf16[1,128,512]{2,1,0:T(8,128)(2,1)}, bf16[1,128,512]{2,1,0:T(8,128)(2,1)}, bf16[1,128,512]{2,1,0:T(8,128)(2,1)}, bf16[1,128,512]{2,1,0:T(8,128)(2,1)}) custom-call(s32[8]{0:T(128)} %stack.62.place, bf16[2,256,512]{2,1,0:T(8,128)(2,1)} %refs_0_.1), custom_call_target="tpu_custom_call" | custom-call | bytes 1572864 | tf_op jit(solution)/shard_map/cutp/pallas_call | solution.py:185
  3.3 2.7 %collective-permute-start.4 = (bf16[1,128,512]{2,1,0:T(8,128)(2,1)}, bf16[1,128,512]{2,1,0:T(8,128)(2,1)S(1)}, u32[]{:S(2)}, u32[]{:S(2)}) collective-permute-start(bf16[1,128,512]{2,1,0:T(8,128)(2,1)} %get-tuple-element.56), channel_id=1, source_target_pairs={{0,2},{1,3},{2,0},{3,1},{4,6},{5,7},{6,4},{7,5},{8,10},{9,11},{10,... | collective-permute-start | bytes 393224 | tf_op jit(solution)/shard_map/ppermute | solution.py:166
  6.5 1.7 %collective-permute-start.2 = (s32[3,4]{1,0:T(4,128)S(1)}, s32[3,4]{1,0:T(4,128)S(1)}, u32[]{:S(2)}, u32[]{:S(2)}) collective-permute-start(s32[3,4]{1,0:T(4,128)S(1)} %bitcast.23), channel_id=1, source_target_pairs={{0,3},{1,2},{2,1},{3,0},{4,7},{5,6},{6,5},{7,4},{8,11},{9,10},{10,... | collective-permute-start | bytes 152 | tf_op jit(solution)/shard_map/ppermute | solution.py:166
  8.9 3.9 %collective-permute-done.1 = s32[3,4]{1,0:T(4,128)S(1)} collective-permute-done((s32[3,4]{1,0:T(4,128)S(1)}, s32[3,4]{1,0:T(4,128)S(1)}, u32[]{:S(2)}, u32[]{:S(2)}) %collective-permute-start.1) | collective-permute-done | bytes 80 | tf_op jit(solution)/shard_map/ppermute | solution.py:166
  13.5 2.1 %cuth.1 = (bf16[2,128,512]{2,1,0:T(8,128)(2,1)}, bf16[2,128,512]{2,1,0:T(8,128)(2,1)}, bf16[2,128,512]{2,1,0:T(8,128)(2,1)}, bf16[2,128,512]{2,1,0:T(8,128)(2,1)}) custom-call(s32[8]{0:T(128)} %stack.62.place, bf16[2,256,512]{2,1,0:T(8,128)(2,1)} %refs_0_.2, bf16[256,512]{1,0:T(8,128)(2,1)} %refs_1_), custom_call_target="tpu_custom_call" | custom-call | bytes 3145728 | tf_op jit(solution)/shard_map/cuth/pallas_call | solution.py:185
  17.0 1.9 %pack.2.refs_0_ = bf16[912,128]{1,0:T(8,128)(2,1)} custom-call(s32[8]{0:T(128)} %stack.62.place, s32[4,3,4]{2,1,0:T(4,128)} %pad_add_fusion.keep, bf16[1,128,512]{2,1,0:T(8,128)(2,1)} %get-tuple-element.54.refs_0_, bf16[1,128,512]{2,1,0:T(8,128)(2,1)} %copy-done.21, bf16[1,128,512]{2,1,0:T(8,128)(2,1)} %copy-done.22, bf16[1,128,512]{2,1,0:T(8,128)(2,1)} %copy-done.23), custom_call_target="tpu_custom_call" | custom-call | bytes 4194304 | tf_op jit(solution)/shard_map/pack/pallas_call | solution.py:207
  18.9 2.0 %collective-permute-start.10 = (bf16[2,128,512]{2,1,0:T(8,128)(2,1)}, bf16[2,128,512]{2,1,0:T(8,128)(2,1)S(1)}, u32[]{:S(2)}, u32[]{:S(2)}) collective-permute-start(bf16[2,128,512]{2,1,0:T(8,128)(2,1)} %get-tuple-element.68), channel_id=1, source_target_pairs={{0,3},{1,2},{2,1},{3,0},{4,7},{5,6},{6,5},{7,4},{8,11},{9,10},{10,... | collective-permute-start | bytes 786440 | tf_op jit(solution)/shard_map/ppermute | solution.py:166
  21.1 1.3 %collective-permute-start.6 = (bf16[912,128]{1,0:T(8,128)(2,1)}, bf16[912,128]{1,0:T(8,128)(2,1)S(1)}, u32[]{:S(2)}, u32[]{:S(2)}) collective-permute-start(bf16[912,128]{1,0:T(8,128)(2,1)} %pack.2.refs_0_), channel_id=1, source_target_pairs={{0,4},{4,0},{8,12},{12,8},{16,20},{20,16},{24,28},{28,24},{1,5},{5... | collective-permute-start | bytes 700424 | tf_op jit(solution)/shard_map/ppermute | solution.py:163
  22.4 1.3 %collective-permute-start.7 = (bf16[912,128]{1,0:T(8,128)(2,1)}, bf16[912,128]{1,0:T(8,128)(2,1)S(1)}, u32[]{:S(2)}, u32[]{:S(2)}) collective-permute-start(bf16[912,128]{1,0:T(8,128)(2,1)} %pack.2.refs_0_), channel_id=1, source_target_pairs={{0,8},{4,12},{8,16},{12,20},{16,24},{20,28},{24,0},{28,4},{1,9},{5... | collective-permute-start | bytes 700424 | tf_op jit(solution)/shard_map/ppermute | solution.py:163
  23.7 4.1 %collective-permute-done.6.refs_1_ = bf16[912,128]{1,0:T(8,128)(2,1)S(1)} collective-permute-done((bf16[912,128]{1,0:T(8,128)(2,1)}, bf16[912,128]{1,0:T(8,128)(2,1)S(1)}, u32[]{:S(2)}, u32[]{:S(2)}) %collective-permute-start.6) | collective-permute-done | bytes 233504 | tf_op jit(solution)/shard_map/ppermute | solution.py:163
  27.9 2.9 %collective-permute-done.7.refs_2_ = bf16[912,128]{1,0:T(8,128)(2,1)S(1)} collective-permute-done((bf16[912,128]{1,0:T(8,128)(2,1)}, bf16[912,128]{1,0:T(8,128)(2,1)S(1)}, u32[]{:S(2)}, u32[]{:S(2)}) %collective-permute-start.7) | collective-permute-done | bytes 233504 | tf_op jit(solution)/shard_map/ppermute | solution.py:163
  30.7 2.6 %collective-permute-done.9.refs_2_ = bf16[2,128,512]{2,1,0:T(8,128)(2,1)S(1)} collective-permute-done((bf16[2,128,512]{2,1,0:T(8,128)(2,1)}, bf16[2,128,512]{2,1,0:T(8,128)(2,1)S(1)}, u32[]{:S(2)}, u32[]{:S(2)}) %collective-permute-start.9) | collective-permute-done | bytes 262176 | tf_op jit(solution)/shard_map/ppermute | solution.py:166
  35.2 2.2 %pack.3.own.refs_0_ = bf16[1040,128]{1,0:T(8,128)(2,1)} custom-call(s32[8]{0:T(128)} %stack.62.place, s32[4,3,4]{2,1,0:T(4,128)} %pad_add_fusion.keep, bf16[2,128,512]{2,1,0:T(8,128)(2,1)} %get-tuple-element.64.refs_0_, bf16[2,128,512]{2,1,0:T(8,128)(2,1)} %copy-done.16, bf16[2,128,512]{2,1,0:T(8,128)(2,1)} %copy-done.17, bf16[2,128,512]{2,1,0:T(8,128)(2,1)} %copy-done.15), custom_call_target="tpu_custom_call" | custom-call | bytes 4194304 | tf_op jit(solution)/shard_map/pack/pallas_call | solution.py:207
  37.4 1.4 %collective-permute-start.14 = (bf16[1040,128]{1,0:T(8,128)(2,1)}, bf16[1040,128]{1,0:T(8,128)(2,1)S(1)}, u32[]{:S(2)}, u32[]{:S(2)}) collective-permute-start(bf16[1040,128]{1,0:T(8,128)(2,1)} %pack.3.own.refs_0_), channel_id=1, source_target_pairs={{0,4},{4,0},{8,12},{12,8},{16,20},{20,16},{24,28},{28,24},{1,5},{5... | collective-permute-start | bytes 798728 | tf_op jit(solution)/shard_map/ppermute | solution.py:163
  38.9 1.3 %collective-permute-start.15 = (bf16[1040,128]{1,0:T(8,128)(2,1)}, bf16[1040,128]{1,0:T(8,128)(2,1)S(1)}, u32[]{:S(2)}, u32[]{:S(2)}) collective-permute-start(bf16[1040,128]{1,0:T(8,128)(2,1)} %pack.3.own.refs_0_), channel_id=1, source_target_pairs={{0,8},{4,12},{8,16},{12,20},{16,24},{20,28},{24,0},{28,4},{1,9},{5... | collective-permute-start | bytes 798728 | tf_op jit(solution)/shard_map/ppermute | solution.py:163
  40.4 1.3 %collective-permute-start.12 = (bf16[912,128]{1,0:T(8,128)(2,1)S(1)}, bf16[912,128]{1,0:T(8,128)(2,1)S(1)}, u32[]{:S(2)}, u32[]{:S(2)}) collective-permute-start(bf16[912,128]{1,0:T(8,128)(2,1)S(1)} %collective-permute-done.7.refs_2_), channel_id=1, source_target_pairs={{0,8},{4,12},{8,16},{12,20},{16,24},{20,28},{24,0},{28,4},{1,9},{5... | collective-permute-start | bytes 700424 | tf_op jit(solution)/shard_map/ppermute | solution.py:163
  41.7 8.9 %collective-permute-done.11.refs_4_ = bf16[912,128]{1,0:T(8,128)(2,1)S(1)} collective-permute-done((bf16[912,128]{1,0:T(8,128)(2,1)S(1)}, bf16[912,128]{1,0:T(8,128)(2,1)S(1)}, u32[]{:S(2)}, u32[]{:S(2)}) %collective-permute-start.11) | collective-permute-done | bytes 233504 | tf_op jit(solution)/shard_map/ppermute | solution.py:163
  50.6 3.1 %collective-permute-done.12.refs_5_ = bf16[912,128]{1,0:T(8,128)(2,1)S(1)} collective-permute-done((bf16[912,128]{1,0:T(8,128)(2,1)S(1)}, bf16[912,128]{1,0:T(8,128)(2,1)S(1)}, u32[]{:S(2)}, u32[]{:S(2)}) %collective-permute-start.12) | collective-permute-done | bytes 233504 | tf_op jit(solution)/shard_map/ppermute | solution.py:163
  58.3 10.8 %collective-permute-done.16.refs_6_ = bf16[912,128]{1,0:T(8,128)(2,1)S(1)} collective-permute-done((bf16[912,128]{1,0:T(8,128)(2,1)S(1)}, bf16[912,128]{1,0:T(8,128)(2,1)S(1)}, u32[]{:S(2)}, u32[]{:S(2)}) %collective-permute-start.16) | collective-permute-done | bytes 233504 | tf_op jit(solution)/shard_map/ppermute | solution.py:163
  69.0 1.7 %collective-permute-done.17.refs_7_ = bf16[912,128]{1,0:T(8,128)(2,1)S(1)} collective-permute-done((bf16[912,128]{1,0:T(8,128)(2,1)S(1)}, bf16[912,128]{1,0:T(8,128)(2,1)S(1)}, u32[]{:S(2)}, u32[]{:S(2)}) %collective-permute-start.17) | collective-permute-done | bytes 233504 | tf_op jit(solution)/shard_map/ppermute | solution.py:163
  70.9 1.2 %collective-permute-start.22 = (bf16[3648,128]{1,0:T(8,128)(2,1)S(1)}, bf16[3648,128]{1,0:T(8,128)(2,1)}, u32[]{:S(2)}, u32[]{:S(2)}) collective-permute-start(bf16[3648,128]{1,0:T(8,128)(2,1)S(1)} %pad_maximum_fusion.1), channel_id=1, source_target_pairs={{0,1},{1,0},{2,3},{3,2},{4,5},{5,4},{6,7},{7,6},{8,9},{9,8},{10,11... | collective-permute-start | bytes 2801672 | tf_op jit(solution)/shard_map/ppermute | solution.py:166
  72.2 1.2 %collective-permute-start.23 = (bf16[1040,128]{1,0:T(8,128)(2,1)S(1)}, bf16[1040,128]{1,0:T(8,128)(2,1)S(1)}, u32[]{:S(2)}, u32[]{:S(2)}) collective-permute-start(bf16[1040,128]{1,0:T(8,128)(2,1)S(1)} %collective-permute-done.19.refs_5_), channel_id=1, source_target_pairs={{0,4},{4,0},{8,12},{12,8},{16,20},{20,16},{24,28},{28,24},{1,5},{5... | collective-permute-start | bytes 798728 | tf_op jit(solution)/shard_map/ppermute | solution.py:163
  73.7 11.5 %collective-permute-done.21.refs_0_ = bf16[912,128]{1,0:T(8,128)(2,1)S(1)} collective-permute-done((bf16[912,128]{1,0:T(8,128)(2,1)S(1)}, bf16[912,128]{1,0:T(8,128)(2,1)S(1)}, u32[]{:S(2)}, u32[]{:S(2)}) %collective-permute-start.21) | collective-permute-done | bytes 233504 | tf_op jit(solution)/shard_map/ppermute | solution.py:163
  86.2 1.2 %collective-permute-start.26 = (bf16[1040,128]{1,0:T(8,128)(2,1)S(1)}, bf16[1040,128]{1,0:T(8,128)(2,1)S(1)}, u32[]{:S(2)}, u32[]{:S(2)}) collective-permute-start(bf16[1040,128]{1,0:T(8,128)(2,1)S(1)} %collective-permute-done.24.refs_7_), channel_id=1, source_target_pairs={{0,4},{4,0},{8,12},{12,8},{16,20},{20,16},{24,28},{28,24},{1,5},{5... | collective-permute-start | bytes 798728 | tf_op jit(solution)/shard_map/ppermute | solution.py:163
  87.8 6.3 %first.1.refs_2_ = f32[32,128,128]{2,1,0:T(8,128)} custom-call(s32[8]{0:T(128)} %stack.62.place, bf16[1040,128]{1,0:T(8,128)(2,1)} %pack.3.own.refs_0_, bf16[912,128]{1,0:T(8,128)(2,1)} %pack.2.refs_0_, bf16[912,128]{1,0:T(8,128)(2,1)} %copy-done.11, bf16[912,128]{1,0:T(8,128)(2,1)} %copy-done.12, bf16[2736,128]{1,0:T(8,128)(2,1)} %collective-permute-done.13.refs_3_, ...), custom_call_target="tpu_custom_call" | custom-call | flops 234881024 | bytes 12000000 | tf_op jit(solution)/shard_map/first/pallas_call | solution.py:238
  95.1 4.0 %firstb.1.prods = bf16[32,128,128]{2,1,0:T(8,128)(2,1)} custom-call(s32[8]{0:T(128)} %stack.62.place, bf16[1040,128]{1,0:T(8,128)(2,1)} %pack.3.own.refs_0_, bf16[912,128]{1,0:T(8,128)(2,1)} %copy-done.19, bf16[912,128]{1,0:T(8,128)(2,1)} %copy-done.20, f32[32,128,128]{2,1,0:T(8,128)} %first.1.refs_2_), custom_call_target="tpu_custom_call" | custom-call | bytes 6000000 | tf_op jit(solution)/shard_map/firstb/pallas_call | solution.py:250
  99.1 5.4 %second.1.refs_2_ = f32[16,128,128]{2,1,0:T(8,128)} custom-call(s32[8]{0:T(128)} %stack.62.place, bf16[32,128,128]{2,1,0:T(8,128)(2,1)} %firstb.1.prods, bf16[1040,128]{1,0:T(8,128)(2,1)} %pack.3.own.refs_0_, bf16[1040,128]{1,0:T(8,128)(2,1)} %copy-done, bf16[1040,128]{1,0:T(8,128)(2,1)} %copy-done.1, bf16[3120,128]{1,0:T(8,128)(2,1)} %collective-permute-done.20.refs_3_, ...), custom_call_target="tpu_custom_call" | custom-call | flops 536870912 | bytes 12000000 | tf_op jit(solution)/shard_map/second/pallas_call | solution.py:238
  105.2 3.8 %secondb.1 = (f32[4,128,128]{2,1,0:T(8,128)}, f32[4,128,128]{2,1,0:T(8,128)}, bf16[4,128,128]{2,1,0:T(8,128)(2,1)}, bf16[4,128,128]{2,1,0:T(8,128)(2,1)}) custom-call(s32[8]{0:T(128)} %stack.62.place, bf16[32,128,128]{2,1,0:T(8,128)(2,1)} %firstb.1.prods, bf16[1040,128]{1,0:T(8,128)(2,1)} %copy-done.13, bf16[1040,128]{1,0:T(8,128)(2,1)} %copy-done.14, ...), custom_call_target="tpu_custom_call" | custom-call | bytes 6000000 | tf_op jit(solution)/shard_map/secondb/pallas_call | solution.py:250
  109.4 1.2 %collective-permute-start.30 = (bf16[4,128,128]{2,1,0:T(8,128)(2,1)}, bf16[4,128,128]{2,1,0:T(8,128)(2,1)S(1)}, u32[]{:S(2)}, u32[]{:S(2)}) collective-permute-start(bf16[4,128,128]{2,1,0:T(8,128)(2,1)} %get-tuple-element.89), channel_id=1, source_target_pairs={{0,2},{1,3},{2,0},{3,1},{4,6},{5,7},{6,4},{7,5},{8,10},{9,11},{10,... | collective-permute-start | bytes 393224 | tf_op jit(solution)/shard_map/ppermute | solution.py:166
  111.2 3.4 %collective-permute-done.30.refs_2_ = bf16[4,128,128]{2,1,0:T(8,128)(2,1)S(1)} collective-permute-done((bf16[4,128,128]{2,1,0:T(8,128)(2,1)}, bf16[4,128,128]{2,1,0:T(8,128)(2,1)S(1)}, u32[]{:S(2)}, u32[]{:S(2)}) %collective-permute-start.30) | collective-permute-done | bytes 131104 | tf_op jit(solution)/shard_map/ppermute | solution.py:166
  114.6 3.1 %collective-permute-done.31.refs_3_ = bf16[4,128,128]{2,1,0:T(8,128)(2,1)S(1)} collective-permute-done((bf16[4,128,128]{2,1,0:T(8,128)(2,1)}, bf16[4,128,128]{2,1,0:T(8,128)(2,1)S(1)}, u32[]{:S(2)}, u32[]{:S(2)}) %collective-permute-start.31) | collective-permute-done | bytes 131104 | tf_op jit(solution)/shard_map/ppermute | solution.py:166
  118.4 2.2 %join.1 = f32[2,256,512]{2,1,0:T(8,128)} custom-call(s32[8]{0:T(128)} %stack.62.place, s32[2,4]{1,0:T(2,128)} %keep.1, f32[4,128,128]{2,1,0:T(8,128)} %get-tuple-element.87.refs_0_, f32[4,128,128]{2,1,0:T(8,128)} %copy-done.18, bf16[4,128,128]{2,1,0:T(8,128)(2,1)} %copy-done.24, bf16[4,128,128]{2,1,0:T(8,128)(2,1)} %copy-done.25), custom_call_target="tpu_custom_call" | custom-call | bytes 2097152 | tf_op jit(solution)/shard_map/join/pallas_call | solution.py:315
  (104 shorter events, 16.6 us)
Async XLA Ops:
  3.3 12.4 %collective-permute-start.3 = (bf16[1,128,512]{2,1,0:T(8,128)(2,1)}, bf16[1,128,512]{2,1,0:T(8,128)(2,1)S(1)}, u32[]{:S(2)}, u32[]{:S(2)}) collective-permute-start(bf16[1,128,512]{2,1,0:T(8,128)(2,1)} %get-tuple-element.55), channel_id=1, source_target_pairs={{0,1},{1,0},{2,3},{3,2},{4,5},{5,4},{6,7},{7,6},{8,9},{9,8},{10,11... | collective-permute-start | bytes 393224 | tf_op jit(solution)/shard_map/ppermute | solution.py:166
  3.3 12.3 %collective-permute-start.4 = (bf16[1,128,512]{2,1,0:T(8,128)(2,1)}, bf16[1,128,512]{2,1,0:T(8,128)(2,1)S(1)}, u32[]{:S(2)}, u32[]{:S(2)}) collective-permute-start(bf16[1,128,512]{2,1,0:T(8,128)(2,1)} %get-tuple-element.56), channel_id=1, source_target_pairs={{0,2},{1,3},{2,0},{3,1},{4,6},{5,7},{6,4},{7,5},{8,10},{9,11},{10,... | collective-permute-start | bytes 393224 | tf_op jit(solution)/shard_map/ppermute | solution.py:166
  6.0 9.6 %collective-permute-start.5 = (bf16[1,128,512]{2,1,0:T(8,128)(2,1)}, bf16[1,128,512]{2,1,0:T(8,128)(2,1)S(1)}, u32[]{:S(2)}, u32[]{:S(2)}) collective-permute-start(bf16[1,128,512]{2,1,0:T(8,128)(2,1)} %get-tuple-element.57), channel_id=1, source_target_pairs={{0,3},{1,2},{2,1},{3,0},{4,7},{5,6},{6,5},{7,4},{8,11},{9,10},{10,... | collective-permute-start | bytes 393224 | tf_op jit(solution)/shard_map/ppermute | solution.py:166
  6.1 2.1 %collective-permute-start = (s32[3,4]{1,0:T(4,128)S(1)}, s32[3,4]{1,0:T(4,128)S(1)}, u32[]{:S(2)}, u32[]{:S(2)}) collective-permute-start(s32[3,4]{1,0:T(4,128)S(1)} %bitcast.22), channel_id=1, source_target_pairs={{0,1},{1,0},{2,3},{3,2},{4,5},{5,4},{6,7},{7,6},{8,9},{9,8},{10,11... | collective-permute-start | bytes 152 | tf_op jit(solution)/shard_map/ppermute | solution.py:166
  6.5 6.4 %collective-permute-start.2 = (s32[3,4]{1,0:T(4,128)S(1)}, s32[3,4]{1,0:T(4,128)S(1)}, u32[]{:S(2)}, u32[]{:S(2)}) collective-permute-start(s32[3,4]{1,0:T(4,128)S(1)} %bitcast.23), channel_id=1, source_target_pairs={{0,3},{1,2},{2,1},{3,0},{4,7},{5,6},{6,5},{7,4},{8,11},{9,10},{10,... | collective-permute-start | bytes 152 | tf_op jit(solution)/shard_map/ppermute | solution.py:166
  8.2 4.7 %collective-permute-start.1 = (s32[3,4]{1,0:T(4,128)S(1)}, s32[3,4]{1,0:T(4,128)S(1)}, u32[]{:S(2)}, u32[]{:S(2)}) collective-permute-start(s32[3,4]{1,0:T(4,128)S(1)} %bitcast.24), channel_id=1, source_target_pairs={{0,2},{1,3},{2,0},{3,1},{4,6},{5,7},{6,4},{7,5},{8,10},{9,11},{10,... | collective-permute-start | bytes 152 | tf_op jit(solution)/shard_map/ppermute | solution.py:166
  18.9 11.8 %collective-permute-start.10 = (bf16[2,128,512]{2,1,0:T(8,128)(2,1)}, bf16[2,128,512]{2,1,0:T(8,128)(2,1)S(1)}, u32[]{:S(2)}, u32[]{:S(2)}) collective-permute-start(bf16[2,128,512]{2,1,0:T(8,128)(2,1)} %get-tuple-element.68), channel_id=1, source_target_pairs={{0,3},{1,2},{2,1},{3,0},{4,7},{5,6},{6,5},{7,4},{8,11},{9,10},{10,... | collective-permute-start | bytes 786440 | tf_op jit(solution)/shard_map/ppermute | solution.py:166
  21.0 9.8 %collective-permute-start.8 = (bf16[2,128,512]{2,1,0:T(8,128)(2,1)}, bf16[2,128,512]{2,1,0:T(8,128)(2,1)S(1)}, u32[]{:S(2)}, u32[]{:S(2)}) collective-permute-start(bf16[2,128,512]{2,1,0:T(8,128)(2,1)} %get-tuple-element.66), channel_id=1, source_target_pairs={{0,1},{1,0},{2,3},{3,2},{4,5},{5,4},{6,7},{7,6},{8,9},{9,8},{10,11... | collective-permute-start | bytes 786440 | tf_op jit(solution)/shard_map/ppermute | solution.py:166
  21.0 12.4 %collective-permute-start.9 = (bf16[2,128,512]{2,1,0:T(8,128)(2,1)}, bf16[2,128,512]{2,1,0:T(8,128)(2,1)S(1)}, u32[]{:S(2)}, u32[]{:S(2)}) collective-permute-start(bf16[2,128,512]{2,1,0:T(8,128)(2,1)} %get-tuple-element.67), channel_id=1, source_target_pairs={{0,2},{1,3},{2,0},{3,1},{4,6},{5,7},{6,4},{7,5},{8,10},{9,11},{10,... | collective-permute-start | bytes 786440 | tf_op jit(solution)/shard_map/ppermute | solution.py:166
  21.1 6.8 %collective-permute-start.6 = (bf16[912,128]{1,0:T(8,128)(2,1)}, bf16[912,128]{1,0:T(8,128)(2,1)S(1)}, u32[]{:S(2)}, u32[]{:S(2)}) collective-permute-start(bf16[912,128]{1,0:T(8,128)(2,1)} %pack.2.refs_0_), channel_id=1, source_target_pairs={{0,4},{4,0},{8,12},{12,8},{16,20},{20,16},{24,28},{28,24},{1,5},{5... | collective-permute-start | bytes 700424 | tf_op jit(solution)/shard_map/ppermute | solution.py:163
  22.4 8.3 %collective-permute-start.7 = (bf16[912,128]{1,0:T(8,128)(2,1)}, bf16[912,128]{1,0:T(8,128)(2,1)S(1)}, u32[]{:S(2)}, u32[]{:S(2)}) collective-permute-start(bf16[912,128]{1,0:T(8,128)(2,1)} %pack.2.refs_0_), channel_id=1, source_target_pairs={{0,8},{4,12},{8,16},{12,20},{16,24},{20,28},{24,0},{28,4},{1,9},{5... | collective-permute-start | bytes 700424 | tf_op jit(solution)/shard_map/ppermute | solution.py:163
  34.4 19.3 %collective-permute-start.13 = (bf16[2736,128]{1,0:T(8,128)(2,1)S(1)}, bf16[2736,128]{1,0:T(8,128)(2,1)}, u32[]{:S(2)}, u32[]{:S(2)}) collective-permute-start(bf16[2736,128]{1,0:T(8,128)(2,1)S(1)} %pad_maximum_fusion.3), channel_id=1, source_target_pairs={{0,1},{1,0},{2,3},{3,2},{4,5},{5,4},{6,7},{7,6},{8,9},{9,8},{10,11... | collective-permute-start | bytes 2101256 | tf_op jit(solution)/shard_map/ppermute | solution.py:166
  37.4 16.3 %collective-permute-start.14 = (bf16[1040,128]{1,0:T(8,128)(2,1)}, bf16[1040,128]{1,0:T(8,128)(2,1)S(1)}, u32[]{:S(2)}, u32[]{:S(2)}) collective-permute-start(bf16[1040,128]{1,0:T(8,128)(2,1)} %pack.3.own.refs_0_), channel_id=1, source_target_pairs={{0,4},{4,0},{8,12},{12,8},{16,20},{20,16},{24,28},{28,24},{1,5},{5... | collective-permute-start | bytes 798728 | tf_op jit(solution)/shard_map/ppermute | solution.py:163
  38.9 14.9 %collective-permute-start.15 = (bf16[1040,128]{1,0:T(8,128)(2,1)}, bf16[1040,128]{1,0:T(8,128)(2,1)S(1)}, u32[]{:S(2)}, u32[]{:S(2)}) collective-permute-start(bf16[1040,128]{1,0:T(8,128)(2,1)} %pack.3.own.refs_0_), channel_id=1, source_target_pairs={{0,8},{4,12},{8,16},{12,20},{16,24},{20,28},{24,0},{28,4},{1,9},{5... | collective-permute-start | bytes 798728 | tf_op jit(solution)/shard_map/ppermute | solution.py:163
  40.1 10.5 %collective-permute-start.11 = (bf16[912,128]{1,0:T(8,128)(2,1)S(1)}, bf16[912,128]{1,0:T(8,128)(2,1)S(1)}, u32[]{:S(2)}, u32[]{:S(2)}) collective-permute-start(bf16[912,128]{1,0:T(8,128)(2,1)S(1)} %collective-permute-done.7.refs_2_), channel_id=1, source_target_pairs={{0,4},{4,0},{8,12},{12,8},{16,20},{20,16},{24,28},{28,24},{1,5},{5... | collective-permute-start | bytes 700424 | tf_op jit(solution)/shard_map/ppermute | solution.py:163
  40.4 13.3 %collective-permute-start.12 = (bf16[912,128]{1,0:T(8,128)(2,1)S(1)}, bf16[912,128]{1,0:T(8,128)(2,1)S(1)}, u32[]{:S(2)}, u32[]{:S(2)}) collective-permute-start(bf16[912,128]{1,0:T(8,128)(2,1)S(1)} %collective-permute-done.7.refs_2_), channel_id=1, source_target_pairs={{0,8},{4,12},{8,16},{12,20},{16,24},{20,28},{24,0},{28,4},{1,9},{5... | collective-permute-start | bytes 700424 | tf_op jit(solution)/shard_map/ppermute | solution.py:163
  55.0 15.9 %collective-permute-start.20 = (bf16[3120,128]{1,0:T(8,128)(2,1)S(1)}, bf16[3120,128]{1,0:T(8,128)(2,1)}, u32[]{:S(2)}, u32[]{:S(2)}) collective-permute-start(bf16[3120,128]{1,0:T(8,128)(2,1)S(1)} %pad_maximum_fusion.2), channel_id=1, source_target_pairs={{0,1},{1,0},{2,3},{3,2},{4,5},{5,4},{6,7},{7,6},{8,9},{9,8},{10,11... | collective-permute-start | bytes 2396168 | tf_op jit(solution)/shard_map/ppermute | solution.py:166
  56.1 14.7 %collective-permute-start.18 = (bf16[1040,128]{1,0:T(8,128)(2,1)S(1)}, bf16[1040,128]{1,0:T(8,128)(2,1)S(1)}, u32[]{:S(2)}, u32[]{:S(2)}) collective-permute-start(bf16[1040,128]{1,0:T(8,128)(2,1)S(1)} %collective-permute-done.15.refs_2_), channel_id=1, source_target_pairs={{0,4},{4,0},{8,12},{12,8},{16,20},{20,16},{24,28},{28,24},{1,5},{5... | collective-permute-start | bytes 798728 | tf_op jit(solution)/shard_map/ppermute | solution.py:163
  56.3 14.4 %collective-permute-start.19 = (bf16[1040,128]{1,0:T(8,128)(2,1)S(1)}, bf16[1040,128]{1,0:T(8,128)(2,1)S(1)}, u32[]{:S(2)}, u32[]{:S(2)}) collective-permute-start(bf16[1040,128]{1,0:T(8,128)(2,1)S(1)} %collective-permute-done.15.refs_2_), channel_id=1, source_target_pairs={{0,8},{4,12},{8,16},{12,20},{16,24},{20,28},{24,0},{28,4},{1,9},{5... | collective-permute-start | bytes 798728 | tf_op jit(solution)/shard_map/ppermute | solution.py:163
  56.4 12.7 %collective-permute-start.16 = (bf16[912,128]{1,0:T(8,128)(2,1)S(1)}, bf16[912,128]{1,0:T(8,128)(2,1)S(1)}, u32[]{:S(2)}, u32[]{:S(2)}) collective-permute-start(bf16[912,128]{1,0:T(8,128)(2,1)S(1)} %collective-permute-done.12.refs_5_), channel_id=1, source_target_pairs={{0,4},{4,0},{8,12},{12,8},{16,20},{20,16},{24,28},{28,24},{1,5},{5... | collective-permute-start | bytes 700424 | tf_op jit(solution)/shard_map/ppermute | solution.py:163
  57.6 13.2 %collective-permute-start.17 = (bf16[912,128]{1,0:T(8,128)(2,1)S(1)}, bf16[912,128]{1,0:T(8,128)(2,1)S(1)}, u32[]{:S(2)}, u32[]{:S(2)}) collective-permute-start(bf16[912,128]{1,0:T(8,128)(2,1)S(1)} %collective-permute-done.12.refs_5_), channel_id=1, source_target_pairs={{0,8},{4,12},{8,16},{12,20},{16,24},{20,28},{24,0},{28,4},{1,9},{5... | collective-permute-start | bytes 700424 | tf_op jit(solution)/shard_map/ppermute | solution.py:163
  70.9 14.3 %collective-permute-start.22 = (bf16[3648,128]{1,0:T(8,128)(2,1)S(1)}, bf16[3648,128]{1,0:T(8,128)(2,1)}, u32[]{:S(2)}, u32[]{:S(2)}) collective-permute-start(bf16[3648,128]{1,0:T(8,128)(2,1)S(1)} %pad_maximum_fusion.1), channel_id=1, source_target_pairs={{0,1},{1,0},{2,3},{3,2},{4,5},{5,4},{6,7},{7,6},{8,9},{9,8},{10,11... | collective-permute-start | bytes 2801672 | tf_op jit(solution)/shard_map/ppermute | solution.py:166
  72.2 13.0 %collective-permute-start.23 = (bf16[1040,128]{1,0:T(8,128)(2,1)S(1)}, bf16[1040,128]{1,0:T(8,128)(2,1)S(1)}, u32[]{:S(2)}, u32[]{:S(2)}) collective-permute-start(bf16[1040,128]{1,0:T(8,128)(2,1)S(1)} %collective-permute-done.19.refs_5_), channel_id=1, source_target_pairs={{0,4},{4,0},{8,12},{12,8},{16,20},{20,16},{24,28},{28,24},{1,5},{5... | collective-permute-start | bytes 798728 | tf_op jit(solution)/shard_map/ppermute | solution.py:163
  73.4 11.8 %collective-permute-start.24 = (bf16[1040,128]{1,0:T(8,128)(2,1)S(1)}, bf16[1040,128]{1,0:T(8,128)(2,1)S(1)}, u32[]{:S(2)}, u32[]{:S(2)}) collective-permute-start(bf16[1040,128]{1,0:T(8,128)(2,1)S(1)} %collective-permute-done.19.refs_5_), channel_id=1, source_target_pairs={{0,8},{4,12},{8,16},{12,20},{16,24},{20,28},{24,0},{28,4},{1,9},{5... | collective-permute-start | bytes 798728 | tf_op jit(solution)/shard_map/ppermute | solution.py:163
  73.4 11.8 %collective-permute-start.21 = (bf16[912,128]{1,0:T(8,128)(2,1)S(1)}, bf16[912,128]{1,0:T(8,128)(2,1)S(1)}, u32[]{:S(2)}, u32[]{:S(2)}) collective-permute-start(bf16[912,128]{1,0:T(8,128)(2,1)S(1)} %collective-permute-done.17.refs_7_), channel_id=1, source_target_pairs={{0,4},{4,0},{8,12},{12,8},{16,20},{20,16},{24,28},{28,24},{1,5},{5... | collective-permute-start | bytes 700424 | tf_op jit(solution)/shard_map/ppermute | solution.py:163
  85.3 8.9 %collective-permute-start.27 = (bf16[4160,128]{1,0:T(8,128)(2,1)S(1)}, bf16[4160,128]{1,0:T(8,128)(2,1)S(1)}, u32[]{:S(2)}, u32[]{:S(2)}) collective-permute-start(bf16[4160,128]{1,0:T(8,128)(2,1)S(1)} %pad_maximum_fusion), channel_id=1, source_target_pairs={{0,1},{1,0},{2,3},{3,2},{4,5},{5,4},{6,7},{7,6},{8,9},{9,8},{10,11... | collective-permute-start | bytes 3194888 | tf_op jit(solution)/shard_map/ppermute | solution.py:166
  86.2 8.0 %collective-permute-start.26 = (bf16[1040,128]{1,0:T(8,128)(2,1)S(1)}, bf16[1040,128]{1,0:T(8,128)(2,1)S(1)}, u32[]{:S(2)}, u32[]{:S(2)}) collective-permute-start(bf16[1040,128]{1,0:T(8,128)(2,1)S(1)} %collective-permute-done.24.refs_7_), channel_id=1, source_target_pairs={{0,4},{4,0},{8,12},{12,8},{16,20},{20,16},{24,28},{28,24},{1,5},{5... | collective-permute-start | bytes 798728 | tf_op jit(solution)/shard_map/ppermute | solution.py:163
  87.4 6.6 %collective-permute-start.25 = (bf16[912,128]{1,0:T(8,128)(2,1)S(1)}, bf16[912,128]{1,0:T(8,128)(2,1)S(1)}, u32[]{:S(2)}, u32[]{:S(2)}) collective-permute-start(bf16[912,128]{1,0:T(8,128)(2,1)S(1)} %collective-permute-done.21.refs_0_), channel_id=1, source_target_pairs={{0,1},{1,0},{2,3},{3,2},{4,5},{5,4},{6,7},{7,6},{8,9},{9,8},{10,11... | collective-permute-start | bytes 700424 | tf_op jit(solution)/shard_map/ppermute | solution.py:166
  94.2 10.3 %collective-permute-start.28 = (bf16[1040,128]{1,0:T(8,128)(2,1)S(1)}, bf16[1040,128]{1,0:T(8,128)(2,1)S(1)}, u32[]{:S(2)}, u32[]{:S(2)}) collective-permute-start(bf16[1040,128]{1,0:T(8,128)(2,1)S(1)} %collective-permute-done.26.refs_0_), channel_id=1, source_target_pairs={{0,1},{1,0},{2,3},{3,2},{4,5},{5,4},{6,7},{7,6},{8,9},{9,8},{10,11... | collective-permute-start | bytes 798728 | tf_op jit(solution)/shard_map/ppermute | solution.py:166
  109.0 8.6 %collective-permute-start.29 = (f32[4,128,128]{2,1,0:T(8,128)}, f32[4,128,128]{2,1,0:T(8,128)S(1)}, u32[]{:S(2)}, u32[]{:S(2)}) collective-permute-start(f32[4,128,128]{2,1,0:T(8,128)} %get-tuple-element.88), channel_id=1, source_target_pairs={{0,1},{1,0},{2,3},{3,2},{4,5},{5,4},{6,7},{7,6},{8,9},{9,8},{10,11... | collective-permute-start | bytes 786440 | tf_op jit(solution)/shard_map/ppermute | solution.py:166
  109.4 5.2 %collective-permute-start.30 = (bf16[4,128,128]{2,1,0:T(8,128)(2,1)}, bf16[4,128,128]{2,1,0:T(8,128)(2,1)S(1)}, u32[]{:S(2)}, u32[]{:S(2)}) collective-permute-start(bf16[4,128,128]{2,1,0:T(8,128)(2,1)} %get-tuple-element.89), channel_id=1, source_target_pairs={{0,2},{1,3},{2,0},{3,1},{4,6},{5,7},{6,4},{7,5},{8,10},{9,11},{10,... | collective-permute-start | bytes 393224 | tf_op jit(solution)/shard_map/ppermute | solution.py:166
  110.6 7.0 %collective-permute-start.31 = (bf16[4,128,128]{2,1,0:T(8,128)(2,1)}, bf16[4,128,128]{2,1,0:T(8,128)(2,1)S(1)}, u32[]{:S(2)}, u32[]{:S(2)}) collective-permute-start(bf16[4,128,128]{2,1,0:T(8,128)(2,1)} %get-tuple-element.90), channel_id=1, source_target_pairs={{0,3},{1,2},{2,1},{3,0},{4,7},{5,6},{6,5},{7,4},{8,11},{9,10},{10,... | collective-permute-start | bytes 393224 | tf_op jit(solution)/shard_map/ppermute | solution.py:166
  (26 other events, 202.4 us)

commit v6 on v4

--- a/solution.py
+++ b/solution.py
@@ -21,15 +21,24 @@
     return pl.CostEstimate(flops=flops, bytes_accessed=nbytes, transcendentals=0)
 
 
-def split_kernel(place, density, hamiltonian, metric, *outs):
+def split_kernel(place, dens_keep, ham_keep, met_keep, density, hamiltonian, metric, *outs):
     spin, row = place[0], place[1]
+    per = dens_keep.shape[1]
+    lane = lax.broadcasted_iota(jnp.int32, (TAIL, BLOCK), 1)
     for v in (2, 3, 1, 0):
         other_spin = spin if v < 2 else 1 - spin
         other_row = row if v % 2 == 0 else 1 - row
         rows = pl.ds(pl.multiple_of(other_row * BLOCK, BLOCK), BLOCK)
-        outs[v][0] = density[other_spin, rows, :]
-        outs[4 + v][0] = hamiltonian[other_spin, rows, :]
-        outs[4 + v][1] = metric[rows, :]
+        outs[v][:BLOCK] = density[other_spin, rows, :]
+        outs[v][BLOCK : 2 * BLOCK] = hamiltonian[other_spin, rows, :]
+        outs[v][2 * BLOCK : 3 * BLOCK] = metric[rows, :]
+        tail = jnp.zeros((TAIL, BLOCK), jnp.int32)
+        for mat, keep in enumerate((dens_keep, ham_keep, met_keep)):
+            for b in range(per):
+                kept = jnp.where(keep[other_row, b] > 0, 1, 0)
+                tail = jnp.where(lane == mat * per + b, kept, tail)
+        outs[v][3 * BLOCK :, :BLOCK] = tail.astype(jnp.float32).astype(outs[v].dtype)
+        outs[v][3 * BLOCK :, BLOCK:] = jnp.zeros((TAIL, outs[v].shape[1] - BLOCK), outs[v].dtype)
 
 
 def slot_rows(slot):
@@ -37,31 +46,41 @@
     return pl.ds(start if isinstance(slot, int) else pl.multiple_of(start, BLOCK), BLOCK)
 
 
-def pack_kernel(sources, mats, slots, place, keep, *refs):
-    ins, out = refs[:sources], refs[sources]
-    per = ins[0].shape[2] // BLOCK
+def tail_of(block):
+    return block.astype(jnp.float32)[:1].astype(jnp.int32)
+
+
+def pack_kernel(sources, place, *refs):
+    ins, outs, (tails, keep) = refs[:sources], refs[sources : sources + 2], refs[sources + 2 :]
+    per = ins[0].shape[1] // BLOCK
     here = place[4]
+    for m in range(sources):
+        tails[m : m + 1, :] = tail_of(ins[m][3 * BLOCK :, :BLOCK])
+    pltpu.sync_copy(tails, keep)
     lane = lax.broadcasted_iota(jnp.int32, (TAIL, BLOCK), 1)
-    out[...] = jnp.zeros_like(out)
-    tail = jnp.zeros((TAIL, BLOCK), jnp.int32)
-    for i, mat in enumerate(mats):
-        flags = [[keep[m, mat, b] for b in range(per)] for m in range(sources)]
-        counts = [functools.reduce(lambda p, q: p + q, f) for f in flags]
-        for m in range(sources):
-            slot = jnp.int32(i * slots)
-            for n in range(sources):
-                if n != m:
-                    slot += jnp.where((here ^ n) < (here ^ m), counts[n], 0)
-            for b in range(per):
-
-                @pl.when(flags[m][b] > 0)
-                def _(slot=slot, m=m, b=b, i=i):
-                    out[slot_rows(slot), :] = ins[m][i, :, b * BLOCK : (b + 1) * BLOCK]
-
-                target = jnp.where(flags[m][b] > 0, slot, -1)
-                tail = jnp.where(lane == target, (here ^ m) * per + b, tail)
-                slot += flags[m][b]
-    out[len(mats) * slots * BLOCK :, :] = tail.astype(jnp.float32).astype(out.dtype)
+    for out, mats, slots in ((outs[0], (0,), DENSITY_SLOTS), (outs[1], (1, 2), OPERATOR_SLOTS)):
+        out[...] = jnp.zeros_like(out)
+        tail = jnp.zeros((TAIL, BLOCK), jnp.int32)
+        for i, mat in enumerate(mats):
+            flags = [[keep[m, mat * per + b] for b in range(per)] for m in range(sources)]
+            counts = [functools.reduce(lambda p, q: p + q, f) for f in flags]
+            for m in range(sources):
+                slot = jnp.int32(i * slots)
+                for n in range(sources):
+                    if n != m:
+                        slot += jnp.where((here ^ n) < (here ^ m), counts[n], 0)
+                for b in range(per):
+
+                    @pl.when(flags[m][b] > 0)
+                    def _(slot=slot, m=m, b=b, mat=mat, out=out):
+                        out[slot_rows(slot), :] = ins[m][
+                            mat * BLOCK : (mat + 1) * BLOCK, b * BLOCK : (b + 1) * BLOCK
+                        ]
+
+                    target = jnp.where(flags[m][b] > 0, slot, -1)
+                    tail = jnp.where(lane == target, (here ^ m) * per + b, tail)
+                    slot += flags[m][b]
+        out[len(mats) * slots * BLOCK :, :] = tail.astype(jnp.float32).astype(out.dtype)
 
 
 def row_of(place, key, layers):
@@ -71,10 +90,6 @@
     side = place[3] if flip == 0 else 1 - place[3]
     half = place[1] if other == 0 else 1 - place[1]
     return (layer * 2 + side) * 2 + half
-
-
-def tail_of(block):
-    return block.astype(jnp.float32)[:1].astype(jnp.int32)
 
 
 def parts_of(entries, layers, place, slots, bufs, tails):
@@ -110,18 +125,12 @@
     out[...] = acc[...].astype(out.dtype)
 
 
-def second_kernel(entries, layers, count, late, place, prods, *refs):
-    bufs, rest = refs[:count], refs[count:]
-    before = None
-    if late:
-        before, *outs, acc, tails, cols = rest
-    else:
-        acc, tails, cols = rest
-        outs = ()
+def second_kernel(entries, layers, count, place, prods, *refs):
+    bufs, outs, (acc, tails, cols) = refs[:count], refs[count : count + 4], refs[count + 4 :]
     nblk = acc.shape[0]
     parts = parts_of(entries, layers, place, 2 * OPERATOR_SLOTS, bufs, tails)
     pltpu.sync_copy(tails, cols)
-    acc[...] = before[...] if late else jnp.zeros_like(acc)
+    acc[...] = jnp.zeros_like(acc)
     for n, (view, k) in enumerate(parts):
         hp, sp = prods[k], prods[nblk + k]
         for t in range(OPERATOR_SLOTS):
@@ -173,40 +182,34 @@
     z, x = row // 2, row % 2
     masks = (0, 1, half, half + 1)
 
-    keeps = (jnp.stack([dens_keep, ham_keep, met_keep]) > 0).astype(i32)
     place = jnp.stack([spin, part, z, x] + [col ^ m for m in masks])
 
-    one, two = (jax.ShapeDtypeStruct((n, BLOCK, width), bf16) for n in (1, 2))
     split = pl.pallas_call(
         split_kernel,
-        out_shape=[one] * 4 + [two] * 4,
-        in_specs=[SMEM, VMEM, VMEM, VMEM],
-        out_specs=[VMEM] * 8,
+        out_shape=[jax.ShapeDtypeStruct((3 * BLOCK + TAIL, width), bf16)] * 4,
+        in_specs=[SMEM] * 4 + [VMEM] * 3,
+        out_specs=[VMEM] * 4,
         cost_estimate=estimate(0, 24 * BLOCK * width * 2),
         name="split",
-    )(place, density, hamiltonian, metric)
-    keep_rows = [lax.dynamic_index_in_dim(keeps, part ^ d, 1, keepdims=False) for d in (0, 1)]
+    )(place, dens_keep, ham_keep, met_keep, density, hamiltonian, metric)
 
     def exchange(pieces):
         moved = {m: by_mask(m)(pieces[variant(m)]) for m in reversed(range(1, ncol))}
         return [pieces[0]] + [moved[m] for m in range(1, ncol)]
 
-    got_dens = exchange(split[:4])
-    keep_got = jnp.stack(exchange([keep_rows[0], keep_rows[1]] * 2))
-    keep_got, *oper_pieces = lax.optimization_barrier((keep_got, *split[4:]))
-    got_oper = exchange(oper_pieces)
-
-    def pack(mats, slots, got):
-        return pl.pallas_call(
-            functools.partial(pack_kernel, ncol, mats, slots),
-            out_shape=jax.ShapeDtypeStruct((len(mats) * slots * BLOCK + TAIL, BLOCK), bf16),
-            in_specs=[SMEM, SMEM] + [VMEM] * ncol,
-            out_specs=VMEM,
-            cost_estimate=estimate(0, 8 * ncol * BLOCK * width * 2),
-            name="pack",
-        )(place, keep_got, *got)
-
-    packed = [pack((0,), DENSITY_SLOTS, got_dens), pack((1, 2), OPERATOR_SLOTS, got_oper)]
+    got = exchange(split)
+
+    packed = pl.pallas_call(
+        functools.partial(pack_kernel, ncol),
+        out_shape=[
+            jax.ShapeDtypeStruct((n * BLOCK + TAIL, BLOCK), bf16) for n in (DENSITY_SLOTS, 2 * OPERATOR_SLOTS)
+        ],
+        in_specs=[SMEM] + [VMEM] * ncol,
+        out_specs=[VMEM] * 2,
+        scratch_shapes=[pltpu.VMEM((ncol, BLOCK), i32), pltpu.SMEM((ncol, BLOCK), i32)],
+        cost_estimate=estimate(0, 3 * ncol * BLOCK * width * 2),
+        name="pack",
+    )(place, *got)
 
     def twin_of(group):
         return twin(jnp.concatenate([a for a, _ in group], axis=0) if len(group) > 1 else group[0][0])
@@ -214,6 +217,8 @@
     gathered = [[], []]
     waiting = [[], []]
     curs = list(packed)
+    flushes = ((-1,), (-1,))
+    pending = [[], []]
     for t in range(layers):
         for n in range(2):
             cur, last = curs[n], t == layers - 1
@@ -225,16 +230,16 @@
 
             gathered[n].append((cur, 0, (t, 0, 0)))
             waiting[n].append((cur, (t, 0, 0)))
-            moves = [across(cur)] + ([] if last else [up(cur)])
-            flush = waiting[n] if t % 2 == 1 or last else []
-            if flush:
-                moves.append(twin_of(flush))
-            moves = list(lax.optimization_barrier(tuple(moves)))
+            moves = [across(cur)] + ([] if last else [up(cur)]) + pending[n]
+            pending[n] = []
+            if t - layers in flushes[n]:
+                arrived = twin_of(waiting[n])
+                settle(arrived, waiting[n])
+                waiting[n] = []
+                moves.append(arrived)
+            moves = lax.optimization_barrier(tuple(moves))
             side = moves[0]
             gathered[n].append((side, 0, (t, 1, 0)))
-            if flush:
-                settle(moves[-1], flush)
-                waiting[n] = []
             waiting[n].append((side, (t, 1, 0)))
             if last:
                 settle(twin_of(waiting[n]), waiting[n])
@@ -261,30 +266,17 @@
         name="first",
     )(place, packed[1], *arrays)
 
-    final = (layers - 1, 1)
-    early = [e for e in gathered[1] if e[2][:2] != final]
-    late = [e for e in gathered[1] if e[2][:2] == final]
+    arrays, entries = refs_of(gathered[1])
     tables = [pltpu.VMEM((nblk, BLOCK), i32), pltpu.SMEM((nblk, BLOCK), i32)]
-    arrays, entries = refs_of(early)
-    half_sum = pl.pallas_call(
-        functools.partial(second_kernel, entries, layers, len(arrays), False),
-        out_shape=jax.ShapeDtypeStruct((nblk, BLOCK, BLOCK), f32),
+    outs = pl.pallas_call(
+        functools.partial(second_kernel, entries, layers, len(arrays)),
+        out_shape=[jax.ShapeDtypeStruct((per, BLOCK, BLOCK), f32 if m < half else bf16) for m in masks],
         in_specs=[SMEM, VMEM] + [VMEM] * len(arrays),
-        out_specs=VMEM,
-        scratch_shapes=tables,
+        out_specs=[VMEM] * 4,
+        scratch_shapes=[pltpu.VMEM((nblk, BLOCK, BLOCK), f32)] + tables,
         cost_estimate=estimate(nblk * 16 * BLOCK**3, 12_000_000),
         name="second",
     )(place, prods, *arrays)
-    arrays, entries = refs_of(late)
-    outs = pl.pallas_call(
-        functools.partial(second_kernel, entries, layers, len(arrays), True),
-        out_shape=[jax.ShapeDtypeStruct((per, BLOCK, BLOCK), f32 if m < half else bf16) for m in masks],
-        in_specs=[SMEM, VMEM] + [VMEM] * len(arrays) + [VMEM],
-        out_specs=[VMEM] * 4,
-        scratch_shapes=[pltpu.VMEM((nblk, BLOCK, BLOCK), f32)] + tables,
-        cost_estimate=estimate(4 * 8 * BLOCK**3, 6_000_000),
-        name="third",
-    )(place, prods, *arrays, half_sum)
 
     back = [outs[0]] + [by_mask(m)(o) for m, o in zip(masks[1:], outs[1:], strict=True)]
     return pl.pallas_call(

time: 115 us -> 106 us (0.922)
  starting transfers between devices: 26.1 us -> 18.2 us
  waiting for transfers between devices: 57.4 us -> 63.3 us
  Pallas kernels: 23.8 us -> 19.5 us
  other arithmetic: 2.71 us -> 0 us
    ppermute x18 -> x10, waiting for transfers between devices: 16.6 us -> 26.1 us  [by_mask(): lax.ppermute(a, 'col', [(c, c ^ mask) for c in range(ncol)])]
    ppermute x18 -> x10, starting transfers between devices: 16.7 us -> 11.2 us  [by_mask(): lax.ppermute(a, 'col', [(c, c ^ mask) for c in range(ncol)])]
    ppermute x14, waiting for transfers between devices: 40.8 us -> 37.2 us  [by_row(): return lambda a: lax.ppermute(a, 'row', pairs)]
    pallas_call x2 -> x1, Pallas kernels: 8.92 us -> 5.5 us  [body(): pl.pallas_call(functools.partial(second_kernel, entries, layers, len(arra...]
    ppermute x14, starting transfers between devices: 9.4 us -> 7.04 us  [by_row(): return lambda a: lax.ppermute(a, 'row', pairs)]
    concatenate x4 -> x0, other arithmetic: 1.39 us -> none  [twin_of(): jnp.concatenate([a for a, _ in group], axis=0)]
    pallas_call x3 -> x2, Pallas kernels: 6.63 us -> 5.73 us  [the longest x1 3.19 us: body(): pl.pallas_call(functools.partial(pack_kernel, ncol), out_shape=[jax.Shape...]
    unnamed x62 -> x54, local copies, waits for them, and re-layouts: 3.62 us -> 3.88 us
  transfers between devices with their start and end apart: 32 -> 24, of which waited for: 14 -> 17; matrix products, arithmetic and copies ran while one was open for 1% -> 2% of each run, Pallas kernels for 16% -> 6%
where the time goes in v6:
time: 106 us
  waiting for transfers between devices  63.3 us (60%)
  Pallas kernels  19.5 us (18%)
  starting transfers between devices  18.2 us (17%)
  local copies, waits for them, and re-layouts  4.55 us (4%)
    ppermute x14, waiting for transfers between devices, by_row(): return lambda a: lax.ppermute(a, 'row', pairs)  37.2 us
    ppermute x10, waiting for transfers between devices, by_mask(): lax.ppermute(a, 'col', [(c, c ^ mask) for c in range(ncol)])  26.1 us
    ppermute x10, starting transfers between devices, by_mask(): lax.ppermute(a, 'col', [(c, c ^ mask) for c in range(ncol)])  11.2 us
    ppermute x14, starting transfers between devices, by_row(): return lambda a: lax.ppermute(a, 'row', pairs)  7.04 us
    pallas_call x1, Pallas kernels, body(): pl.pallas_call(functools.partial(first_kernel, entries, layers, len(array...  6.06 us
    pallas_call x1, Pallas kernels, body(): pl.pallas_call(functools.partial(second_kernel, entries, layers, len(arra...  5.5 us
    unnamed x54, local copies, waits for them, and re-layouts  3.88 us
    pallas_call x1, Pallas kernels, body(): pl.pallas_call(functools.partial(pack_kernel, ncol), out_shape=[jax.Shape...  3.19 us
  transfers between devices with their start and end apart: 24, of which 17 were waited for; matrix products, arithmetic and copies ran while one was open for 2% of the time, Pallas kernels for 6%

profile of v6, /device:TPU:1, one launch (start us, length us, event | category | flops | bytes accessed | tf_op | source)
XLA Modules:
  0.0 105.8 jit_solution(5162923699026313529)
XLA Ops:
  0.6 2.5 %split.1 = (bf16[400,512]{1,0:T(8,128)(2,1)}, bf16[400,512]{1,0:T(8,128)(2,1)}, bf16[400,512]{1,0:T(8,128)(2,1)}, bf16[400,512]{1,0:T(8,128)(2,1)}) custom-call(s32[8]{0:T(128)} %stack.35.place, s32[2,4]{1,0:T(2,128)} %dens_keep.1, s32[2,4]{1,0:T(2,128)} %ham_keep.1, s32[2,4]{1,0:T(2,128)} %met_keep.1, bf16[2,256,512]{2,1,0:T(8,128)(2,1)} %density.1, ...), custom_call_target="tpu_custom_call" | custom-call | bytes 3145728 | tf_op jit(solution)/shard_map/split/pallas_call | solution.py:187
  3.2 2.7 %collective-permute-start.1 = (bf16[400,512]{1,0:T(8,128)(2,1)}, bf16[400,512]{1,0:T(8,128)(2,1)S(1)}, u32[]{:S(2)}, u32[]{:S(2)}) collective-permute-start(bf16[400,512]{1,0:T(8,128)(2,1)} %get-tuple-element.31), channel_id=1, source_target_pairs={{0,2},{1,3},{2,0},{3,1},{4,6},{5,7},{6,4},{7,5},{8,10},{9,11},{10,... | collective-permute-start | bytes 1228808 | tf_op jit(solution)/shard_map/ppermute | solution.py:171
  5.9 9.9 %collective-permute-done.1.refs_2_ = bf16[400,512]{1,0:T(8,128)(2,1)S(1)} collective-permute-done((bf16[400,512]{1,0:T(8,128)(2,1)}, bf16[400,512]{1,0:T(8,128)(2,1)S(1)}, u32[]{:S(2)}, u32[]{:S(2)}) %collective-permute-start.1) | collective-permute-done | bytes 409632 | tf_op jit(solution)/shard_map/ppermute | solution.py:171
  15.9 8.8 %collective-permute-done.2.refs_3_ = bf16[400,512]{1,0:T(8,128)(2,1)S(1)} collective-permute-done((bf16[400,512]{1,0:T(8,128)(2,1)}, bf16[400,512]{1,0:T(8,128)(2,1)S(1)}, u32[]{:S(2)}, u32[]{:S(2)}) %collective-permute-start.2) | collective-permute-done | bytes 409632 | tf_op jit(solution)/shard_map/ppermute | solution.py:171
  25.4 3.2 %pack.1 = (bf16[912,128]{1,0:T(8,128)(2,1)}, bf16[1040,128]{1,0:T(8,128)(2,1)}) custom-call(s32[8]{0:T(128)} %stack.35.place, bf16[400,512]{1,0:T(8,128)(2,1)} %get-tuple-element.29.refs_0_, bf16[400,512]{1,0:T(8,128)(2,1)} %copy-done.14, bf16[400,512]{1,0:T(8,128)(2,1)} %copy-done.15, bf16[400,512]{1,0:T(8,128)(2,1)} %copy-done.16), custom_call_target="tpu_custom_call" | custom-call | bytes 1572864 | tf_op jit(solution)/shard_map/pack/pallas_call | solution.py:202
  28.6 1.4 %collective-permute-start.3 = (bf16[912,128]{1,0:T(8,128)(2,1)}, bf16[912,128]{1,0:T(8,128)(2,1)S(1)}, u32[]{:S(2)}, u32[]{:S(2)}) collective-permute-start(bf16[912,128]{1,0:T(8,128)(2,1)} %get-tuple-element.34.refs_0_), channel_id=1, source_target_pairs={{0,4},{4,0},{8,12},{12,8},{16,20},{20,16},{24,28},{28,24},{1,5},{5... | collective-permute-start | bytes 700424 | tf_op jit(solution)/shard_map/ppermute | solution.py:168
  30.0 1.3 %collective-permute-start.4 = (bf16[912,128]{1,0:T(8,128)(2,1)}, bf16[912,128]{1,0:T(8,128)(2,1)S(1)}, u32[]{:S(2)}, u32[]{:S(2)}) collective-permute-start(bf16[912,128]{1,0:T(8,128)(2,1)} %get-tuple-element.34.refs_0_), channel_id=1, source_target_pairs={{0,8},{4,12},{8,16},{12,20},{16,24},{20,28},{24,0},{28,4},{1,9},{5... | collective-permute-start | bytes 700424 | tf_op jit(solution)/shard_map/ppermute | solution.py:168
  31.6 1.3 %collective-permute-start.13 = (bf16[1040,128]{1,0:T(8,128)(2,1)}, bf16[1040,128]{1,0:T(8,128)(2,1)S(1)}, u32[]{:S(2)}, u32[]{:S(2)}) collective-permute-start(bf16[1040,128]{1,0:T(8,128)(2,1)} %get-tuple-element.33.own.refs_0_), channel_id=1, source_target_pairs={{0,8},{4,12},{8,16},{12,20},{16,24},{20,28},{24,0},{28,4},{1,9},{5... | collective-permute-start | bytes 798728 | tf_op jit(solution)/shard_map/ppermute | solution.py:168
  32.8 1.0 constant_dynamic-update-slice_fusion.13
  33.9 1.0 constant_dynamic-update-slice_fusion.6
  34.8 0.9 collective-permute-done.3.refs_1_
  35.7 3.2 %collective-permute-done.4.refs_2_ = bf16[912,128]{1,0:T(8,128)(2,1)S(1)} collective-permute-done((bf16[912,128]{1,0:T(8,128)(2,1)}, bf16[912,128]{1,0:T(8,128)(2,1)S(1)}, u32[]{:S(2)}, u32[]{:S(2)}) %collective-permute-start.4) | collective-permute-done | bytes 233504 | tf_op jit(solution)/shard_map/ppermute | solution.py:168
  39.3 2.1 %collective-permute-done.12.refs_1_ = bf16[1040,128]{1,0:T(8,128)(2,1)S(1)} collective-permute-done((bf16[1040,128]{1,0:T(8,128)(2,1)}, bf16[1040,128]{1,0:T(8,128)(2,1)S(1)}, u32[]{:S(2)}, u32[]{:S(2)}) %collective-permute-start.12) | collective-permute-done | bytes 266272 | tf_op jit(solution)/shard_map/ppermute | solution.py:168
  41.4 3.2 %collective-permute-done.13.refs_2_ = bf16[1040,128]{1,0:T(8,128)(2,1)S(1)} collective-permute-done((bf16[1040,128]{1,0:T(8,128)(2,1)}, bf16[1040,128]{1,0:T(8,128)(2,1)S(1)}, u32[]{:S(2)}, u32[]{:S(2)}) %collective-permute-start.13) | collective-permute-done | bytes 266272 | tf_op jit(solution)/shard_map/ppermute | solution.py:168
  45.5 3.9 %collective-permute-done.6.refs_4_ = bf16[912,128]{1,0:T(8,128)(2,1)S(1)} collective-permute-done((bf16[912,128]{1,0:T(8,128)(2,1)S(1)}, bf16[912,128]{1,0:T(8,128)(2,1)S(1)}, u32[]{:S(2)}, u32[]{:S(2)}) %collective-permute-start.6) | collective-permute-done | bytes 233504 | tf_op jit(solution)/shard_map/ppermute | solution.py:168
  49.5 1.1 %collective-permute-done.14.refs_3_ = bf16[1040,128]{1,0:T(8,128)(2,1)S(1)} collective-permute-done((bf16[1040,128]{1,0:T(8,128)(2,1)S(1)}, bf16[1040,128]{1,0:T(8,128)(2,1)S(1)}, u32[]{:S(2)}, u32[]{:S(2)}) %collective-permute-start.14) | collective-permute-done | bytes 266272 | tf_op jit(solution)/shard_map/ppermute | solution.py:168
  50.5 3.9 %collective-permute-done.15.refs_4_ = bf16[1040,128]{1,0:T(8,128)(2,1)S(1)} collective-permute-done((bf16[1040,128]{1,0:T(8,128)(2,1)S(1)}, bf16[1040,128]{1,0:T(8,128)(2,1)S(1)}, u32[]{:S(2)}, u32[]{:S(2)}) %collective-permute-start.15) | collective-permute-done | bytes 266272 | tf_op jit(solution)/shard_map/ppermute | solution.py:168
  55.2 5.7 %collective-permute-done.16.refs_5_ = bf16[1040,128]{1,0:T(8,128)(2,1)S(1)} collective-permute-done((bf16[1040,128]{1,0:T(8,128)(2,1)S(1)}, bf16[1040,128]{1,0:T(8,128)(2,1)S(1)}, u32[]{:S(2)}, u32[]{:S(2)}) %collective-permute-start.16) | collective-permute-done | bytes 266272 | tf_op jit(solution)/shard_map/ppermute | solution.py:168
  60.9 3.8 %collective-permute-done.17.refs_6_ = bf16[1040,128]{1,0:T(8,128)(2,1)S(1)} collective-permute-done((bf16[1040,128]{1,0:T(8,128)(2,1)S(1)}, bf16[1040,128]{1,0:T(8,128)(2,1)S(1)}, u32[]{:S(2)}, u32[]{:S(2)}) %collective-permute-start.17) | collective-permute-done | bytes 266272 | tf_op jit(solution)/shard_map/ppermute | solution.py:168
  64.8 2.7 %collective-permute-start.18 = (bf16[7280,128]{1,0:T(8,128)(2,1)S(1)}, bf16[7280,128]{1,0:T(8,128)(2,1)S(1)}, u32[]{:S(2)}, u32[]{:S(2)}) collective-permute-start(bf16[7280,128]{1,0:T(8,128)(2,1)S(1)} %constant_dynamic-update-slice_fusion.7), channel_id=1, source_target_pairs={{0,1},{1,0},{2,3},{3,2},{4,5},{5,4},{6,7},{7,6},{8,9},{9,8},{10,11... | collective-permute-start | bytes 5591048 | tf_op jit(solution)/shard_map/ppermute | solution.py:171
  67.7 1.1 %collective-permute-start.19 = (bf16[1040,128]{1,0:T(8,128)(2,1)S(1)}, bf16[1040,128]{1,0:T(8,128)(2,1)}, u32[]{:S(2)}, u32[]{:S(2)}) collective-permute-start(bf16[1040,128]{1,0:T(8,128)(2,1)S(1)} %collective-permute-done.17.refs_6_), channel_id=1, source_target_pairs={{0,4},{4,0},{8,12},{12,8},{16,20},{20,16},{24,28},{28,24},{1,5},{5... | collective-permute-start | bytes 798728 | tf_op jit(solution)/shard_map/ppermute | solution.py:168
  69.3 6.2 %collective-permute-done.19.refs_8_ = bf16[1040,128]{1,0:T(8,128)(2,1)} collective-permute-done((bf16[1040,128]{1,0:T(8,128)(2,1)S(1)}, bf16[1040,128]{1,0:T(8,128)(2,1)}, u32[]{:S(2)}, u32[]{:S(2)}) %collective-permute-start.19) | collective-permute-done | bytes 266272 | tf_op jit(solution)/shard_map/ppermute | solution.py:168
  75.4 2.1 %collective-permute-start.20 = (bf16[1040,128]{1,0:T(8,128)(2,1)}, bf16[1040,128]{1,0:T(8,128)(2,1)}, u32[]{:S(2)}, u32[]{:S(2)}) collective-permute-start(bf16[1040,128]{1,0:T(8,128)(2,1)} %collective-permute-done.19.refs_8_), channel_id=1, source_target_pairs={{0,1},{1,0},{2,3},{3,2},{4,5},{5,4},{6,7},{7,6},{8,9},{9,8},{10,11... | collective-permute-start | bytes 798728 | tf_op jit(solution)/shard_map/ppermute | solution.py:171
  77.6 2.7 %collective-permute-done.10.refs_8_ = bf16[912,128]{1,0:T(8,128)(2,1)S(1)} collective-permute-done((bf16[912,128]{1,0:T(8,128)(2,1)S(1)}, bf16[912,128]{1,0:T(8,128)(2,1)S(1)}, u32[]{:S(2)}, u32[]{:S(2)}) %collective-permute-start.10) | collective-permute-done | bytes 233504 | tf_op jit(solution)/shard_map/ppermute | solution.py:168
  80.4 1.3 %collective-permute-start.11 = (bf16[912,128]{1,0:T(8,128)(2,1)S(1)}, bf16[912,128]{1,0:T(8,128)(2,1)}, u32[]{:S(2)}, u32[]{:S(2)}) collective-permute-start(bf16[912,128]{1,0:T(8,128)(2,1)S(1)} %collective-permute-done.10.refs_8_), channel_id=1, source_target_pairs={{0,1},{1,0},{2,3},{3,2},{4,5},{5,4},{6,7},{7,6},{8,9},{9,8},{10,11... | collective-permute-start | bytes 700424 | tf_op jit(solution)/shard_map/ppermute | solution.py:171
  81.7 1.2 %collective-permute-done.11.refs_9_ = bf16[912,128]{1,0:T(8,128)(2,1)} collective-permute-done((bf16[912,128]{1,0:T(8,128)(2,1)S(1)}, bf16[912,128]{1,0:T(8,128)(2,1)}, u32[]{:S(2)}, u32[]{:S(2)}) %collective-permute-start.11) | collective-permute-done | bytes 233504 | tf_op jit(solution)/shard_map/ppermute | solution.py:171
  83.0 6.1 %first.1.prods = bf16[32,128,128]{2,1,0:T(8,128)(2,1)} custom-call(s32[8]{0:T(128)} %stack.35.place, bf16[1040,128]{1,0:T(8,128)(2,1)} %get-tuple-element.33.own.refs_0_, bf16[912,128]{1,0:T(8,128)(2,1)} %get-tuple-element.34.refs_0_, bf16[912,128]{1,0:T(8,128)(2,1)} %copy-done.8, bf16[912,128]{1,0:T(8,128)(2,1)} %copy-done.9, bf16[912,128]{1,0:T(8,128)(2,1)} %copy-done.10, ...), custom_call_target="tpu_custom_call" | custom-call | flops 234881024 | bytes 10000000 | tf_op jit(solution)/shard_map/first/pallas_call | solution.py:259
  89.0 5.5 %second.1 = (f32[4,128,128]{2,1,0:T(8,128)}, f32[4,128,128]{2,1,0:T(8,128)}, bf16[4,128,128]{2,1,0:T(8,128)(2,1)}, bf16[4,128,128]{2,1,0:T(8,128)(2,1)}) custom-call(s32[8]{0:T(128)} %stack.35.place, bf16[32,128,128]{2,1,0:T(8,128)(2,1)} %first.1.prods, bf16[1040,128]{1,0:T(8,128)(2,1)} %get-tuple-element.33.own.refs_0_, bf16[1040,128]{1,0:T(8,128)(2,1)} %copy-done.2, ...), custom_call_target="tpu_custom_call" | custom-call | flops 536870912 | bytes 12000000 | tf_op jit(solution)/shard_map/second/pallas_call | solution.py:271
  94.5 1.3 %collective-permute-start.22 = (bf16[4,128,128]{2,1,0:T(8,128)(2,1)}, bf16[4,128,128]{2,1,0:T(8,128)(2,1)S(1)}, u32[]{:S(2)}, u32[]{:S(2)}) collective-permute-start(bf16[4,128,128]{2,1,0:T(8,128)(2,1)} %get-tuple-element.51), channel_id=1, source_target_pairs={{0,2},{1,3},{2,0},{3,1},{4,6},{5,7},{6,4},{7,5},{8,10},{9,11},{10,... | collective-permute-start | bytes 393224 | tf_op jit(solution)/shard_map/ppermute | solution.py:171
  96.7 2.8 %collective-permute-done.22.refs_2_ = bf16[4,128,128]{2,1,0:T(8,128)(2,1)S(1)} collective-permute-done((bf16[4,128,128]{2,1,0:T(8,128)(2,1)}, bf16[4,128,128]{2,1,0:T(8,128)(2,1)S(1)}, u32[]{:S(2)}, u32[]{:S(2)}) %collective-permute-start.22) | collective-permute-done | bytes 131104 | tf_op jit(solution)/shard_map/ppermute | solution.py:171
  99.4 3.4 %collective-permute-done.23.refs_3_ = bf16[4,128,128]{2,1,0:T(8,128)(2,1)S(1)} collective-permute-done((bf16[4,128,128]{2,1,0:T(8,128)(2,1)}, bf16[4,128,128]{2,1,0:T(8,128)(2,1)S(1)}, u32[]{:S(2)}, u32[]{:S(2)}) %collective-permute-start.23) | collective-permute-done | bytes 131104 | tf_op jit(solution)/shard_map/ppermute | solution.py:171
  103.6 2.2 %join.1 = f32[2,256,512]{2,1,0:T(8,128)} custom-call(s32[8]{0:T(128)} %stack.35.place, s32[2,4]{1,0:T(2,128)} %keep.1, f32[4,128,128]{2,1,0:T(8,128)} %get-tuple-element.49.refs_0_, f32[4,128,128]{2,1,0:T(8,128)} %copy-done.17, bf16[4,128,128]{2,1,0:T(8,128)(2,1)} %copy-done.19, bf16[4,128,128]{2,1,0:T(8,128)(2,1)} %copy-done.20), custom_call_target="tpu_custom_call" | custom-call | bytes 2097152 | tf_op jit(solution)/shard_map/join/pallas_call | solution.py:282
  (78 shorter events, 6.1 us)
Async XLA Ops:
  3.1 2.8 %collective-permute-start = (bf16[400,512]{1,0:T(8,128)(2,1)}, bf16[400,512]{1,0:T(8,128)(2,1)S(1)}, u32[]{:S(2)}, u32[]{:S(2)}) collective-permute-start(bf16[400,512]{1,0:T(8,128)(2,1)} %get-tuple-element.30), channel_id=1, source_target_pairs={{0,1},{1,0},{2,3},{3,2},{4,5},{5,4},{6,7},{7,6},{8,9},{9,8},{10,11... | collective-permute-start | bytes 1228808 | tf_op jit(solution)/shard_map/ppermute | solution.py:171
  3.2 12.7 %collective-permute-start.1 = (bf16[400,512]{1,0:T(8,128)(2,1)}, bf16[400,512]{1,0:T(8,128)(2,1)S(1)}, u32[]{:S(2)}, u32[]{:S(2)}) collective-permute-start(bf16[400,512]{1,0:T(8,128)(2,1)} %get-tuple-element.31), channel_id=1, source_target_pairs={{0,2},{1,3},{2,0},{3,1},{4,6},{5,7},{6,4},{7,5},{8,10},{9,11},{10,... | collective-permute-start | bytes 1228808 | tf_op jit(solution)/shard_map/ppermute | solution.py:171
  5.9 18.8 %collective-permute-start.2 = (bf16[400,512]{1,0:T(8,128)(2,1)}, bf16[400,512]{1,0:T(8,128)(2,1)S(1)}, u32[]{:S(2)}, u32[]{:S(2)}) collective-permute-start(bf16[400,512]{1,0:T(8,128)(2,1)} %get-tuple-element.32), channel_id=1, source_target_pairs={{0,3},{1,2},{2,1},{3,0},{4,7},{5,6},{6,5},{7,4},{8,11},{9,10},{10,... | collective-permute-start | bytes 1228808 | tf_op jit(solution)/shard_map/ppermute | solution.py:171
  5.9 18.7 %copy-start.14 = (bf16[400,512]{1,0:T(8,128)(2,1)}, bf16[400,512]{1,0:T(8,128)(2,1)S(1)}, u32[]{:S(2)}) copy-start(bf16[400,512]{1,0:T(8,128)(2,1)S(1)} %collective-permute-done.refs_1_) | copy-start | bytes 1228804
  28.6 7.1 %collective-permute-start.3 = (bf16[912,128]{1,0:T(8,128)(2,1)}, bf16[912,128]{1,0:T(8,128)(2,1)S(1)}, u32[]{:S(2)}, u32[]{:S(2)}) collective-permute-start(bf16[912,128]{1,0:T(8,128)(2,1)} %get-tuple-element.34.refs_0_), channel_id=1, source_target_pairs={{0,4},{4,0},{8,12},{12,8},{16,20},{20,16},{24,28},{28,24},{1,5},{5... | collective-permute-start | bytes 700424 | tf_op jit(solution)/shard_map/ppermute | solution.py:168
  30.0 8.9 %collective-permute-start.4 = (bf16[912,128]{1,0:T(8,128)(2,1)}, bf16[912,128]{1,0:T(8,128)(2,1)S(1)}, u32[]{:S(2)}, u32[]{:S(2)}) collective-permute-start(bf16[912,128]{1,0:T(8,128)(2,1)} %get-tuple-element.34.refs_0_), channel_id=1, source_target_pairs={{0,8},{4,12},{8,16},{12,20},{16,24},{20,28},{24,0},{28,4},{1,9},{5... | collective-permute-start | bytes 700424 | tf_op jit(solution)/shard_map/ppermute | solution.py:168
  31.3 10.1 %collective-permute-start.12 = (bf16[1040,128]{1,0:T(8,128)(2,1)}, bf16[1040,128]{1,0:T(8,128)(2,1)S(1)}, u32[]{:S(2)}, u32[]{:S(2)}) collective-permute-start(bf16[1040,128]{1,0:T(8,128)(2,1)} %get-tuple-element.33.own.refs_0_), channel_id=1, source_target_pairs={{0,4},{4,0},{8,12},{12,8},{16,20},{20,16},{24,28},{28,24},{1,5},{5... | collective-permute-start | bytes 798728 | tf_op jit(solution)/shard_map/ppermute | solution.py:168
  31.6 13.1 %collective-permute-start.13 = (bf16[1040,128]{1,0:T(8,128)(2,1)}, bf16[1040,128]{1,0:T(8,128)(2,1)S(1)}, u32[]{:S(2)}, u32[]{:S(2)}) collective-permute-start(bf16[1040,128]{1,0:T(8,128)(2,1)} %get-tuple-element.33.own.refs_0_), channel_id=1, source_target_pairs={{0,8},{4,12},{8,16},{12,20},{16,24},{20,28},{24,0},{28,4},{1,9},{5... | collective-permute-start | bytes 798728 | tf_op jit(solution)/shard_map/ppermute | solution.py:168
  38.9 6.6 %collective-permute-start.5 = (bf16[912,128]{1,0:T(8,128)(2,1)S(1)}, bf16[912,128]{1,0:T(8,128)(2,1)S(1)}, u32[]{:S(2)}, u32[]{:S(2)}) collective-permute-start(bf16[912,128]{1,0:T(8,128)(2,1)S(1)} %collective-permute-done.4.refs_2_), channel_id=1, source_target_pairs={{0,4},{4,0},{8,12},{12,8},{16,20},{20,16},{24,28},{28,24},{1,5},{5... | collective-permute-start | bytes 700424 | tf_op jit(solution)/shard_map/ppermute | solution.py:168
  39.2 10.2 %collective-permute-start.6 = (bf16[912,128]{1,0:T(8,128)(2,1)S(1)}, bf16[912,128]{1,0:T(8,128)(2,1)S(1)}, u32[]{:S(2)}, u32[]{:S(2)}) collective-permute-start(bf16[912,128]{1,0:T(8,128)(2,1)S(1)} %collective-permute-done.4.refs_2_), channel_id=1, source_target_pairs={{0,8},{4,12},{8,16},{12,20},{16,24},{20,28},{24,0},{28,4},{1,9},{5... | collective-permute-start | bytes 700424 | tf_op jit(solution)/shard_map/ppermute | solution.py:168
  41.4 26.1 %copy-start.2 = (bf16[1040,128]{1,0:T(8,128)(2,1)}, bf16[1040,128]{1,0:T(8,128)(2,1)S(1)}, u32[]{:S(2)}) copy-start(bf16[1040,128]{1,0:T(8,128)(2,1)S(1)} %collective-permute-done.12.refs_1_) | copy-start | bytes 798724
  44.6 22.9 %copy-start.3 = (bf16[1040,128]{1,0:T(8,128)(2,1)}, bf16[1040,128]{1,0:T(8,128)(2,1)S(1)}, u32[]{:S(2)}) copy-start(bf16[1040,128]{1,0:T(8,128)(2,1)S(1)} %collective-permute-done.13.refs_2_) | copy-start | bytes 798724
  44.6 5.9 %collective-permute-start.14 = (bf16[1040,128]{1,0:T(8,128)(2,1)S(1)}, bf16[1040,128]{1,0:T(8,128)(2,1)S(1)}, u32[]{:S(2)}, u32[]{:S(2)}) collective-permute-start(bf16[1040,128]{1,0:T(8,128)(2,1)S(1)} %collective-permute-done.13.refs_2_), channel_id=1, source_target_pairs={{0,4},{4,0},{8,12},{12,8},{16,20},{20,16},{24,28},{28,24},{1,5},{5... | collective-permute-start | bytes 798728 | tf_op jit(solution)/shard_map/ppermute | solution.py:168
  44.9 9.5 %collective-permute-start.15 = (bf16[1040,128]{1,0:T(8,128)(2,1)S(1)}, bf16[1040,128]{1,0:T(8,128)(2,1)S(1)}, u32[]{:S(2)}, u32[]{:S(2)}) collective-permute-start(bf16[1040,128]{1,0:T(8,128)(2,1)S(1)} %collective-permute-done.13.refs_2_), channel_id=1, source_target_pairs={{0,8},{4,12},{8,16},{12,20},{16,24},{20,28},{24,0},{28,4},{1,9},{5... | collective-permute-start | bytes 798728 | tf_op jit(solution)/shard_map/ppermute | solution.py:168
  49.4 18.2 %copy-start.11 = (bf16[912,128]{1,0:T(8,128)(2,1)}, bf16[912,128]{1,0:T(8,128)(2,1)S(1)}, u32[]{:S(2)}) copy-start(bf16[912,128]{1,0:T(8,128)(2,1)S(1)} %collective-permute-done.6.refs_4_) | copy-start | bytes 700420
  49.4 18.1 %collective-permute-start.7 = (bf16[912,128]{1,0:T(8,128)(2,1)S(1)}, bf16[912,128]{1,0:T(8,128)(2,1)S(1)}, u32[]{:S(2)}, u32[]{:S(2)}) collective-permute-start(bf16[912,128]{1,0:T(8,128)(2,1)S(1)} %collective-permute-done.6.refs_4_), channel_id=1, source_target_pairs={{0,4},{4,0},{8,12},{12,8},{16,20},{20,16},{24,28},{28,24},{1,5},{5... | collective-permute-start | bytes 700424 | tf_op jit(solution)/shard_map/ppermute | solution.py:168
  49.4 18.1 %collective-permute-start.8 = (bf16[912,128]{1,0:T(8,128)(2,1)S(1)}, bf16[912,128]{1,0:T(8,128)(2,1)S(1)}, u32[]{:S(2)}, u32[]{:S(2)}) collective-permute-start(bf16[912,128]{1,0:T(8,128)(2,1)S(1)} %collective-permute-done.6.refs_4_), channel_id=1, source_target_pairs={{0,8},{4,12},{8,16},{12,20},{16,24},{20,28},{24,0},{28,4},{1,9},{5... | collective-permute-start | bytes 700424 | tf_op jit(solution)/shard_map/ppermute | solution.py:168
  50.5 29.8 %copy-start.4 = (bf16[1040,128]{1,0:T(8,128)(2,1)}, bf16[1040,128]{1,0:T(8,128)(2,1)S(1)}, u32[]{:S(2)}) copy-start(bf16[1040,128]{1,0:T(8,128)(2,1)S(1)} %collective-permute-done.14.refs_3_) | copy-start | bytes 798724
  54.4 27.3 %copy-start.5 = (bf16[1040,128]{1,0:T(8,128)(2,1)}, bf16[1040,128]{1,0:T(8,128)(2,1)S(1)}, u32[]{:S(2)}) copy-start(bf16[1040,128]{1,0:T(8,128)(2,1)S(1)} %collective-permute-done.15.refs_4_) | copy-start | bytes 798724
  54.4 6.5 %collective-permute-start.16 = (bf16[1040,128]{1,0:T(8,128)(2,1)S(1)}, bf16[1040,128]{1,0:T(8,128)(2,1)S(1)}, u32[]{:S(2)}, u32[]{:S(2)}) collective-permute-start(bf16[1040,128]{1,0:T(8,128)(2,1)S(1)} %collective-permute-done.15.refs_4_), channel_id=1, source_target_pairs={{0,4},{4,0},{8,12},{12,8},{16,20},{20,16},{24,28},{28,24},{1,5},{5... | collective-permute-start | bytes 798728 | tf_op jit(solution)/shard_map/ppermute | solution.py:168
  54.4 10.3 %collective-permute-start.17 = (bf16[1040,128]{1,0:T(8,128)(2,1)S(1)}, bf16[1040,128]{1,0:T(8,128)(2,1)S(1)}, u32[]{:S(2)}, u32[]{:S(2)}) collective-permute-start(bf16[1040,128]{1,0:T(8,128)(2,1)S(1)} %collective-permute-done.15.refs_4_), channel_id=1, source_target_pairs={{0,8},{4,12},{8,16},{12,20},{16,24},{20,28},{24,0},{28,4},{1,9},{5... | collective-permute-start | bytes 798728 | tf_op jit(solution)/shard_map/ppermute | solution.py:168
  60.9 20.8 %copy-start.6 = (bf16[1040,128]{1,0:T(8,128)(2,1)}, bf16[1040,128]{1,0:T(8,128)(2,1)S(1)}, u32[]{:S(2)}) copy-start(bf16[1040,128]{1,0:T(8,128)(2,1)S(1)} %collective-permute-done.16.refs_5_) | copy-start | bytes 798724
  64.7 17.0 %copy-start.7 = (bf16[1040,128]{1,0:T(8,128)(2,1)}, bf16[1040,128]{1,0:T(8,128)(2,1)S(1)}, u32[]{:S(2)}) copy-start(bf16[1040,128]{1,0:T(8,128)(2,1)S(1)} %collective-permute-done.17.refs_6_) | copy-start | bytes 798724
  64.8 10.7 %collective-permute-start.18 = (bf16[7280,128]{1,0:T(8,128)(2,1)S(1)}, bf16[7280,128]{1,0:T(8,128)(2,1)S(1)}, u32[]{:S(2)}, u32[]{:S(2)}) collective-permute-start(bf16[7280,128]{1,0:T(8,128)(2,1)S(1)} %constant_dynamic-update-slice_fusion.7), channel_id=1, source_target_pairs={{0,1},{1,0},{2,3},{3,2},{4,5},{5,4},{6,7},{7,6},{8,9},{9,8},{10,11... | collective-permute-start | bytes 5591048 | tf_op jit(solution)/shard_map/ppermute | solution.py:171
  67.7 12.7 %collective-permute-start.9 = (bf16[6384,128]{1,0:T(8,128)(2,1)S(1)}, bf16[6384,128]{1,0:T(8,128)(2,1)S(1)}, u32[]{:S(2)}, u32[]{:S(2)}) collective-permute-start(bf16[6384,128]{1,0:T(8,128)(2,1)S(1)} %constant_dynamic-update-slice_fusion), channel_id=1, source_target_pairs={{0,1},{1,0},{2,3},{3,2},{4,5},{5,4},{6,7},{7,6},{8,9},{9,8},{10,11... | collective-permute-start | bytes 4902920 | tf_op jit(solution)/shard_map/ppermute | solution.py:171
  67.7 7.7 %collective-permute-start.19 = (bf16[1040,128]{1,0:T(8,128)(2,1)S(1)}, bf16[1040,128]{1,0:T(8,128)(2,1)}, u32[]{:S(2)}, u32[]{:S(2)}) collective-permute-start(bf16[1040,128]{1,0:T(8,128)(2,1)S(1)} %collective-permute-done.17.refs_6_), channel_id=1, source_target_pairs={{0,4},{4,0},{8,12},{12,8},{16,20},{20,16},{24,28},{28,24},{1,5},{5... | collective-permute-start | bytes 798728 | tf_op jit(solution)/shard_map/ppermute | solution.py:168
  68.8 11.5 %collective-permute-start.10 = (bf16[912,128]{1,0:T(8,128)(2,1)S(1)}, bf16[912,128]{1,0:T(8,128)(2,1)S(1)}, u32[]{:S(2)}, u32[]{:S(2)}) collective-permute-start(bf16[912,128]{1,0:T(8,128)(2,1)S(1)} %collective-permute-done.8.refs_6_), channel_id=1, source_target_pairs={{0,4},{4,0},{8,12},{12,8},{16,20},{20,16},{24,28},{28,24},{1,5},{5... | collective-permute-start | bytes 700424 | tf_op jit(solution)/shard_map/ppermute | solution.py:168
  75.4 13.6 %collective-permute-start.20 = (bf16[1040,128]{1,0:T(8,128)(2,1)}, bf16[1040,128]{1,0:T(8,128)(2,1)}, u32[]{:S(2)}, u32[]{:S(2)}) collective-permute-start(bf16[1040,128]{1,0:T(8,128)(2,1)} %collective-permute-done.19.refs_8_), channel_id=1, source_target_pairs={{0,1},{1,0},{2,3},{3,2},{4,5},{5,4},{6,7},{7,6},{8,9},{9,8},{10,11... | collective-permute-start | bytes 798728 | tf_op jit(solution)/shard_map/ppermute | solution.py:171
  80.4 2.6 %collective-permute-start.11 = (bf16[912,128]{1,0:T(8,128)(2,1)S(1)}, bf16[912,128]{1,0:T(8,128)(2,1)}, u32[]{:S(2)}, u32[]{:S(2)}) collective-permute-start(bf16[912,128]{1,0:T(8,128)(2,1)S(1)} %collective-permute-done.10.refs_8_), channel_id=1, source_target_pairs={{0,1},{1,0},{2,3},{3,2},{4,5},{5,4},{6,7},{7,6},{8,9},{9,8},{10,11... | collective-permute-start | bytes 700424 | tf_op jit(solution)/shard_map/ppermute | solution.py:171
  94.5 8.3 %collective-permute-start.21 = (f32[4,128,128]{2,1,0:T(8,128)}, f32[4,128,128]{2,1,0:T(8,128)S(1)}, u32[]{:S(2)}, u32[]{:S(2)}) collective-permute-start(f32[4,128,128]{2,1,0:T(8,128)} %get-tuple-element.50), channel_id=1, source_target_pairs={{0,1},{1,0},{2,3},{3,2},{4,5},{5,4},{6,7},{7,6},{8,9},{9,8},{10,11... | collective-permute-start | bytes 786440 | tf_op jit(solution)/shard_map/ppermute | solution.py:171
  94.5 4.9 %collective-permute-start.22 = (bf16[4,128,128]{2,1,0:T(8,128)(2,1)}, bf16[4,128,128]{2,1,0:T(8,128)(2,1)S(1)}, u32[]{:S(2)}, u32[]{:S(2)}) collective-permute-start(bf16[4,128,128]{2,1,0:T(8,128)(2,1)} %get-tuple-element.51), channel_id=1, source_target_pairs={{0,2},{1,3},{2,0},{3,1},{4,6},{5,7},{6,4},{7,5},{8,10},{9,11},{10,... | collective-permute-start | bytes 393224 | tf_op jit(solution)/shard_map/ppermute | solution.py:171
  95.8 7.0 %collective-permute-start.23 = (bf16[4,128,128]{2,1,0:T(8,128)(2,1)}, bf16[4,128,128]{2,1,0:T(8,128)(2,1)S(1)}, u32[]{:S(2)}, u32[]{:S(2)}) collective-permute-start(bf16[4,128,128]{2,1,0:T(8,128)(2,1)} %get-tuple-element.52), channel_id=1, source_target_pairs={{0,3},{1,2},{2,1},{3,0},{4,7},{5,6},{6,5},{7,4},{8,11},{9,10},{10,... | collective-permute-start | bytes 393224 | tf_op jit(solution)/shard_map/ppermute | solution.py:171
  (13 other events, 82.6 us)

commit v7 on v6

--- a/solution.py
+++ b/solution.py
@@ -25,20 +25,25 @@
     spin, row = place[0], place[1]
     per = dens_keep.shape[1]
     lane = lax.broadcasted_iota(jnp.int32, (TAIL, BLOCK), 1)
-    for v in (2, 3, 1, 0):
-        other_spin = spin if v < 2 else 1 - spin
-        other_row = row if v % 2 == 0 else 1 - row
-        rows = pl.ds(pl.multiple_of(other_row * BLOCK, BLOCK), BLOCK)
-        outs[v][:BLOCK] = density[other_spin, rows, :]
-        outs[v][BLOCK : 2 * BLOCK] = hamiltonian[other_spin, rows, :]
-        outs[v][2 * BLOCK : 3 * BLOCK] = metric[rows, :]
-        tail = jnp.zeros((TAIL, BLOCK), jnp.int32)
-        for mat, keep in enumerate((dens_keep, ham_keep, met_keep)):
-            for b in range(per):
-                kept = jnp.where(keep[other_row, b] > 0, 1, 0)
-                tail = jnp.where(lane == mat * per + b, kept, tail)
-        outs[v][3 * BLOCK :, :BLOCK] = tail.astype(jnp.float32).astype(outs[v].dtype)
-        outs[v][3 * BLOCK :, BLOCK:] = jnp.zeros((TAIL, outs[v].shape[1] - BLOCK), outs[v].dtype)
+    for first, keeps in ((0, (dens_keep,)), (4, (ham_keep, met_keep))):
+        for v in (2, 3, 1, 0):
+            out = outs[first + v]
+            other_spin = spin if v < 2 else 1 - spin
+            other_row = row if v % 2 == 0 else 1 - row
+            rows = pl.ds(pl.multiple_of(other_row * BLOCK, BLOCK), BLOCK)
+            if first == 0:
+                out[:BLOCK] = density[other_spin, rows, :]
+            else:
+                out[:BLOCK] = hamiltonian[other_spin, rows, :]
+                out[BLOCK : 2 * BLOCK] = metric[rows, :]
+            tail = jnp.zeros((TAIL, BLOCK), jnp.int32)
+            for i, keep in enumerate(keeps):
+                for b in range(per):
+                    kept = jnp.where(keep[other_row, b] > 0, 1, 0)
+                    tail = jnp.where(lane == i * per + b, kept, tail)
+            end = len(keeps) * BLOCK
+            out[end:, :BLOCK] = tail.astype(jnp.float32).astype(out.dtype)
+            out[end:, BLOCK:] = jnp.zeros((TAIL, out.shape[1] - BLOCK), out.dtype)
 
 
 def slot_rows(slot):
@@ -50,37 +55,34 @@
     return block.astype(jnp.float32)[:1].astype(jnp.int32)
 
 
-def pack_kernel(sources, place, *refs):
-    ins, outs, (tails, keep) = refs[:sources], refs[sources : sources + 2], refs[sources + 2 :]
+def pack_kernel(sources, mats, slots, place, *refs):
+    ins, out, (tails, keep) = refs[:sources], refs[sources], refs[sources + 1 :]
     per = ins[0].shape[1] // BLOCK
     here = place[4]
     for m in range(sources):
-        tails[m : m + 1, :] = tail_of(ins[m][3 * BLOCK :, :BLOCK])
+        tails[m : m + 1, :] = tail_of(ins[m][mats * BLOCK :, :BLOCK])
     pltpu.sync_copy(tails, keep)
     lane = lax.broadcasted_iota(jnp.int32, (TAIL, BLOCK), 1)
-    for out, mats, slots in ((outs[0], (0,), DENSITY_SLOTS), (outs[1], (1, 2), OPERATOR_SLOTS)):
-        out[...] = jnp.zeros_like(out)
-        tail = jnp.zeros((TAIL, BLOCK), jnp.int32)
-        for i, mat in enumerate(mats):
-            flags = [[keep[m, mat * per + b] for b in range(per)] for m in range(sources)]
-            counts = [functools.reduce(lambda p, q: p + q, f) for f in flags]
-            for m in range(sources):
-                slot = jnp.int32(i * slots)
-                for n in range(sources):
-                    if n != m:
-                        slot += jnp.where((here ^ n) < (here ^ m), counts[n], 0)
-                for b in range(per):
-
-                    @pl.when(flags[m][b] > 0)
-                    def _(slot=slot, m=m, b=b, mat=mat, out=out):
-                        out[slot_rows(slot), :] = ins[m][
-                            mat * BLOCK : (mat + 1) * BLOCK, b * BLOCK : (b + 1) * BLOCK
-                        ]
-
-                    target = jnp.where(flags[m][b] > 0, slot, -1)
-                    tail = jnp.where(lane == target, (here ^ m) * per + b, tail)
-                    slot += flags[m][b]
-        out[len(mats) * slots * BLOCK :, :] = tail.astype(jnp.float32).astype(out.dtype)
+    out[...] = jnp.zeros_like(out)
+    tail = jnp.zeros((TAIL, BLOCK), jnp.int32)
+    for i in range(mats):
+        flags = [[keep[m, i * per + b] for b in range(per)] for m in range(sources)]
+        counts = [functools.reduce(lambda p, q: p + q, f) for f in flags]
+        for m in range(sources):
+            slot = jnp.int32(i * slots)
+            for n in range(sources):
+                if n != m:
+                    slot += jnp.where((here ^ n) < (here ^ m), counts[n], 0)
+            for b in range(per):
+
+                @pl.when(flags[m][b] > 0)
+                def _(slot=slot, m=m, b=b, i=i):
+                    out[slot_rows(slot), :] = ins[m][i * BLOCK : (i + 1) * BLOCK, b * BLOCK : (b + 1) * BLOCK]
+
+                target = jnp.where(flags[m][b] > 0, slot, -1)
+                tail = jnp.where(lane == target, (here ^ m) * per + b, tail)
+                slot += flags[m][b]
+    out[mats * slots * BLOCK :, :] = tail.astype(jnp.float32).astype(out.dtype)
 
 
 def row_of(place, key, layers):
@@ -186,9 +188,9 @@
 
     split = pl.pallas_call(
         split_kernel,
-        out_shape=[jax.ShapeDtypeStruct((3 * BLOCK + TAIL, width), bf16)] * 4,
+        out_shape=[jax.ShapeDtypeStruct((n * BLOCK + TAIL, width), bf16) for n in (1, 1, 1, 1, 2, 2, 2, 2)],
         in_specs=[SMEM] * 4 + [VMEM] * 3,
-        out_specs=[VMEM] * 4,
+        out_specs=[VMEM] * 8,
         cost_estimate=estimate(0, 24 * BLOCK * width * 2),
         name="split",
     )(place, dens_keep, ham_keep, met_keep, density, hamiltonian, metric)
@@ -197,54 +199,25 @@
         moved = {m: by_mask(m)(pieces[variant(m)]) for m in reversed(range(1, ncol))}
         return [pieces[0]] + [moved[m] for m in range(1, ncol)]
 
-    got = exchange(split)
-
-    packed = pl.pallas_call(
-        functools.partial(pack_kernel, ncol),
-        out_shape=[
-            jax.ShapeDtypeStruct((n * BLOCK + TAIL, BLOCK), bf16) for n in (DENSITY_SLOTS, 2 * OPERATOR_SLOTS)
-        ],
-        in_specs=[SMEM] + [VMEM] * ncol,
-        out_specs=[VMEM] * 2,
-        scratch_shapes=[pltpu.VMEM((ncol, BLOCK), i32), pltpu.SMEM((ncol, BLOCK), i32)],
-        cost_estimate=estimate(0, 3 * ncol * BLOCK * width * 2),
-        name="pack",
-    )(place, *got)
+    got_dens = exchange(split[:4])
+    got_dens[1], *oper_pieces = lax.optimization_barrier((got_dens[1], *split[4:]))
+    got_oper = exchange(oper_pieces)
+
+    def pack(mats, slots, got):
+        return pl.pallas_call(
+            functools.partial(pack_kernel, ncol, mats, slots),
+            out_shape=jax.ShapeDtypeStruct((mats * slots * BLOCK + TAIL, BLOCK), bf16),
+            in_specs=[SMEM] + [VMEM] * ncol,
+            out_specs=VMEM,
+            scratch_shapes=[pltpu.VMEM((ncol, BLOCK), i32), pltpu.SMEM((ncol, BLOCK), i32)],
+            cost_estimate=estimate(0, 3 * ncol * BLOCK * width * 2),
+            name="pack",
+        )(place, *got)
+
+    packed = [pack(1, DENSITY_SLOTS, got_dens), pack(2, OPERATOR_SLOTS, got_oper)]
 
     def twin_of(group):
         return twin(jnp.concatenate([a for a, _ in group], axis=0) if len(group) > 1 else group[0][0])
-
-    gathered = [[], []]
-    waiting = [[], []]
-    curs = list(packed)
-    flushes = ((-1,), (-1,))
-    pending = [[], []]
-    for t in range(layers):
-        for n in range(2):
-            cur, last = curs[n], t == layers - 1
-            size = cur.shape[0]
-
-            def settle(arrived, group, n=n, size=size):
-                for i, (_, key) in enumerate(group):
-                    gathered[n].append((arrived, i * size, key[:2] + (1,)))
-
-            gathered[n].append((cur, 0, (t, 0, 0)))
-            waiting[n].append((cur, (t, 0, 0)))
-            moves = [across(cur)] + ([] if last else [up(cur)]) + pending[n]
-            pending[n] = []
-            if t - layers in flushes[n]:
-                arrived = twin_of(waiting[n])
-                settle(arrived, waiting[n])
-                waiting[n] = []
-                moves.append(arrived)
-            moves = lax.optimization_barrier(tuple(moves))
-            side = moves[0]
-            gathered[n].append((side, 0, (t, 1, 0)))
-            waiting[n].append((side, (t, 1, 0)))
-            if last:
-                settle(twin_of(waiting[n]), waiting[n])
-            else:
-                curs[n] = moves[1]
 
     def refs_of(entries):
         arrays = []
@@ -254,17 +227,62 @@
         place_of = {id(a): i for i, a in enumerate(arrays)}
         return arrays, [(place_of[id(a)], start, key) for a, start, key in entries]
 
-    arrays, entries = refs_of(gathered[0])
-    tables = [pltpu.VMEM((nblk + 8, BLOCK), i32), pltpu.SMEM((nblk + 8, BLOCK), i32)]
-    prods = pl.pallas_call(
-        functools.partial(first_kernel, entries, layers, len(arrays)),
-        out_shape=jax.ShapeDtypeStruct((2 * nblk, BLOCK, BLOCK), bf16),
-        in_specs=[SMEM, VMEM] + [VMEM] * len(arrays),
-        out_specs=VMEM,
-        scratch_shapes=[pltpu.VMEM((2 * nblk, BLOCK, BLOCK), f32)] + tables,
-        cost_estimate=estimate(56 * 2 * BLOCK**3, 10_000_000),
-        name="first",
-    )(place, packed[1], *arrays)
+    gathered = [[], []]
+    waiting = [[], []]
+    curs = list(packed)
+    def first_product():
+        arrays, entries = refs_of(gathered[0])
+        tables = [pltpu.VMEM((nblk + 8, BLOCK), i32), pltpu.SMEM((nblk + 8, BLOCK), i32)]
+        return pl.pallas_call(
+            functools.partial(first_kernel, entries, layers, len(arrays)),
+            out_shape=jax.ShapeDtypeStruct((2 * nblk, BLOCK, BLOCK), bf16),
+            in_specs=[SMEM, VMEM] + [VMEM] * len(arrays),
+            out_specs=VMEM,
+            scratch_shapes=[pltpu.VMEM((2 * nblk, BLOCK, BLOCK), f32)] + tables,
+            cost_estimate=estimate(56 * 2 * BLOCK**3, 10_000_000),
+            name="first",
+        )(place, packed[1], *arrays)
+
+    def settle(n, group, joined=None):
+        arrived = twin_of(group) if joined is None else twin(joined)
+        for i, (a, key) in enumerate(group):
+            gathered[n].append((arrived, i * a.shape[0], key[:2] + (1,)))
+        return arrived
+
+    joined = [None, None]
+
+    def advance(n, t, extra=()):
+        cur, last = curs[n], t == layers - 1
+        gathered[n].append((cur, 0, (t, 0, 0)))
+        waiting[n].append((cur, (t, 0, 0)))
+        moves = [across(cur)]
+        if last:
+            early, pair = waiting[n][:-2], waiting[n][-2:]
+            moves.append(settle(n, early, joined[n]))
+            moves += ([settle(n, pair)] if n == 0 else [settle(n, [one]) for one in pair])
+        else:
+            moves.append(up(cur))
+            if t == layers - 2:
+                moves.append(jnp.concatenate([a for a, _ in waiting[n]], axis=0))
+        tied = lax.optimization_barrier((*moves, *extra))
+        side = tied[0]
+        gathered[n].append((side, 0, (t, 1, 0)))
+        if last:
+            settle(n, [(side, (t, 1, 0))])
+        else:
+            waiting[n].append((side, (t, 1, 0)))
+            curs[n] = tied[1]
+            if t == layers - 2:
+                joined[n] = tied[2]
+        return list(tied[: len(moves)]), list(tied[len(moves) :])
+
+    ahead, _ = advance(0, 0)
+    for t in range(layers):
+        if t < layers - 1:
+            ahead, _ = advance(0, t + 1)
+            advance(1, t, ahead)
+        else:
+            prods = advance(1, t, [first_product()])[1][0]
 
     arrays, entries = refs_of(gathered[1])
     tables = [pltpu.VMEM((nblk, BLOCK), i32), pltpu.SMEM((nblk, BLOCK), i32)]

time: 106 us -> 101 us (0.953)
  waiting for transfers between devices: 63.3 us -> 45.5 us
  local copies, waits for them, and re-layouts: 4.55 us -> 9.91 us
  starting transfers between devices: 18.2 us -> 22.9 us
  Pallas kernels: 19.5 us -> 21.7 us
    ppermute x14, waiting for transfers between devices: 37.2 us -> 21.3 us  [by_row(): return lambda a: lax.ppermute(a, 'row', pairs)]
    ppermute x14, starting transfers between devices: 7.04 us -> 12.4 us  [by_row(): return lambda a: lax.ppermute(a, 'row', pairs)]
    unnamed x54 -> x62, local copies, waits for them, and re-layouts: 3.88 us -> 8.53 us
    pallas_call x3 -> x4, Pallas kernels: 11.8 us -> 14 us  [the longest x1 6.07 us: first_product(): pl.pallas_call(functools.partial(first_kernel, entries, layers, len(array...]
    ppermute x10 -> x16, waiting for transfers between devices: 26.1 us -> 24.3 us  [by_mask(): lax.ppermute(a, 'col', [(c, c ^ mask) for c in range(ncol)])]
    ppermute x10 -> x16, starting transfers between devices: 11.2 us -> 10.5 us  [by_mask(): lax.ppermute(a, 'col', [(c, c ^ mask) for c in range(ncol)])]
  transfers between devices with their start and end apart: 24 -> 30, of which waited for: 17 -> 16; matrix products, arithmetic and copies ran while one was open for 2% -> 6% of each run, Pallas kernels for 6% -> 9%
where the time goes in v7:
time: 101 us; the launch traced here: 100 us
  waiting for transfers between devices  45.5 us (45%)
  starting transfers between devices  22.9 us (23%)
  Pallas kernels  21.7 us (21%)
  local copies, waits for them, and re-layouts  9.91 us (10%)
    ppermute x16, waiting for transfers between devices, by_mask(): lax.ppermute(a, 'col', [(c, c ^ mask) for c in range(ncol)])  24.3 us
    ppermute x14, waiting for transfers between devices, by_row(): return lambda a: lax.ppermute(a, 'row', pairs)  21.3 us
    ppermute x14, starting transfers between devices, by_row(): return lambda a: lax.ppermute(a, 'row', pairs)  12.4 us
    ppermute x16, starting transfers between devices, by_mask(): lax.ppermute(a, 'col', [(c, c ^ mask) for c in range(ncol)])  10.5 us
    unnamed x62, local copies, waits for them, and re-layouts  8.53 us
    pallas_call x1, Pallas kernels, first_product(): pl.pallas_call(functools.partial(first_kernel, entries, layers, len(array...  6.07 us
    pallas_call x1, Pallas kernels, body(): pl.pallas_call(functools.partial(second_kernel, entries, layers, len(arra...  5.49 us
    pallas_call x2, Pallas kernels, pack(): pl.pallas_call(functools.partial(pack_kernel, ncol, mats, slots), out_sha...  5.34 us
  transfers between devices with their start and end apart: 30, of which 16 were waited for; matrix products, arithmetic and copies ran while one was open for 6% of the time, Pallas kernels for 9%

profile of v7, /device:TPU:1, one launch (start us, length us, event | category | flops | bytes accessed | tf_op | source)
XLA Modules:
  0.0 100.3 jit_solution(10741591308900240985)
XLA Ops:
  0.6 2.6 %split.1 = (bf16[144,512]{1,0:T(8,128)(2,1)}, bf16[144,512]{1,0:T(8,128)(2,1)}, bf16[144,512]{1,0:T(8,128)(2,1)}, bf16[144,512]{1,0:T(8,128)(2,1)}, bf16[272,512...) custom-call(s32[8]{0:T(128)} %stack.35.place, ...), custom_call_target="tpu_custom_call" | custom-call | bytes 3145728 | tf_op jit(solution)/shard_map/split/pallas_call | solution.py:189
  3.2 2.7 %collective-permute-start.6 = (bf16[144,512]{1,0:T(8,128)(2,1)}, bf16[144,512]{1,0:T(8,128)(2,1)S(1)}, u32[]{:S(2)}, u32[]{:S(2)}) collective-permute-start(bf16[144,512]{1,0:T(8,128)(2,1)} %get-tuple-element.50), channel_id=1, source_target_pairs={{0,2},{1,3},{2,0},{3,1},{4,6},{5,7},{6,4},{7,5},{8,10},{9,11},{10,... | collective-permute-start | bytes 442376 | tf_op jit(solution)/shard_map/ppermute | solution.py:173
  6.0 4.3 %collective-permute-done.6.refs_2_ = bf16[144,512]{1,0:T(8,128)(2,1)S(1)} collective-permute-done((bf16[144,512]{1,0:T(8,128)(2,1)}, bf16[144,512]{1,0:T(8,128)(2,1)S(1)}, u32[]{:S(2)}, u32[]{:S(2)}) %collective-permute-start.6) | collective-permute-done | bytes 147488 | tf_op jit(solution)/shard_map/ppermute | solution.py:173
  10.3 3.2 %collective-permute-done.7.refs_3_ = bf16[144,512]{1,0:T(8,128)(2,1)S(1)} collective-permute-done((bf16[144,512]{1,0:T(8,128)(2,1)}, bf16[144,512]{1,0:T(8,128)(2,1)S(1)}, u32[]{:S(2)}, u32[]{:S(2)}) %collective-permute-start.7) | collective-permute-done | bytes 147488 | tf_op jit(solution)/shard_map/ppermute | solution.py:173
  14.1 2.5 %pack.3.refs_0_ = bf16[912,128]{1,0:T(8,128)(2,1)} custom-call(s32[8]{0:T(128)} %stack.35.place, bf16[144,512]{1,0:T(8,128)(2,1)} %get-tuple-element.48.refs_0_, bf16[144,512]{1,0:T(8,128)(2,1)} %copy-done.22, bf16[144,512]{1,0:T(8,128)(2,1)} %copy-done.23, bf16[144,512]{1,0:T(8,128)(2,1)} %copy-done.24), custom_call_target="tpu_custom_call" | custom-call | bytes 1572864 | tf_op jit(solution)/shard_map/pack/pallas_call | solution.py:207
  16.7 1.4 %collective-permute-start.8 = (bf16[912,128]{1,0:T(8,128)(2,1)}, bf16[912,128]{1,0:T(8,128)(2,1)S(1)}, u32[]{:S(2)}, u32[]{:S(2)}) collective-permute-start(bf16[912,128]{1,0:T(8,128)(2,1)} %pack.3.refs_0_), channel_id=1, source_target_pairs={{0,4},{4,0},{8,12},{12,8},{16,20},{20,16},{24,28},{28,24},{1,5},{5... | collective-permute-start | bytes 700424 | tf_op jit(solution)/shard_map/ppermute | solution.py:170
  18.1 1.3 %collective-permute-start.9 = (bf16[912,128]{1,0:T(8,128)(2,1)}, bf16[912,128]{1,0:T(8,128)(2,1)S(1)}, u32[]{:S(2)}, u32[]{:S(2)}) collective-permute-start(bf16[912,128]{1,0:T(8,128)(2,1)} %pack.3.refs_0_), channel_id=1, source_target_pairs={{0,8},{4,12},{8,16},{12,20},{16,24},{20,28},{24,0},{28,4},{1,9},{5... | collective-permute-start | bytes 700424 | tf_op jit(solution)/shard_map/ppermute | solution.py:170
  20.1 1.2 %collective-permute-start.2 = (bf16[272,512]{1,0:T(8,128)(2,1)}, bf16[272,512]{1,0:T(8,128)(2,1)S(1)}, u32[]{:S(2)}, u32[]{:S(2)}) collective-permute-start(bf16[272,512]{1,0:T(8,128)(2,1)} %get-tuple-element.46), channel_id=1, source_target_pairs={{0,2},{1,3},{2,0},{3,1},{4,6},{5,7},{6,4},{7,5},{8,10},{9,11},{10,... | collective-permute-start | bytes 835592 | tf_op jit(solution)/shard_map/ppermute | solution.py:173
  23.7 3.3 %collective-permute-done.9.refs_2_ = bf16[912,128]{1,0:T(8,128)(2,1)S(1)} collective-permute-done((bf16[912,128]{1,0:T(8,128)(2,1)}, bf16[912,128]{1,0:T(8,128)(2,1)S(1)}, u32[]{:S(2)}, u32[]{:S(2)}) %collective-permute-start.9) | collective-permute-done | bytes 233504 | tf_op jit(solution)/shard_map/ppermute | solution.py:170
  27.4 1.2 %collective-permute-done.2.refs_2_ = bf16[272,512]{1,0:T(8,128)(2,1)S(1)} collective-permute-done((bf16[272,512]{1,0:T(8,128)(2,1)}, bf16[272,512]{1,0:T(8,128)(2,1)S(1)}, u32[]{:S(2)}, u32[]{:S(2)}) %collective-permute-start.2) | collective-permute-done | bytes 278560 | tf_op jit(solution)/shard_map/ppermute | solution.py:173
  28.6 6.4 %collective-permute-done.3.refs_3_ = bf16[272,512]{1,0:T(8,128)(2,1)S(1)} collective-permute-done((bf16[272,512]{1,0:T(8,128)(2,1)}, bf16[272,512]{1,0:T(8,128)(2,1)S(1)}, u32[]{:S(2)}, u32[]{:S(2)}) %collective-permute-start.3) | collective-permute-done | bytes 278560 | tf_op jit(solution)/shard_map/ppermute | solution.py:173
  35.7 2.8 %pack.2.own.refs_0_ = bf16[1040,128]{1,0:T(8,128)(2,1)} custom-call(s32[8]{0:T(128)} %stack.35.place, bf16[272,512]{1,0:T(8,128)(2,1)} %get-tuple-element.44.refs_0_, bf16[272,512]{1,0:T(8,128)(2,1)} %copy-done.13, bf16[272,512]{1,0:T(8,128)(2,1)} %copy-done.14, bf16[272,512]{1,0:T(8,128)(2,1)} %copy-done.15), custom_call_target="tpu_custom_call" | custom-call | bytes 1572864 | tf_op jit(solution)/shard_map/pack/pallas_call | solution.py:207
  39.8 1.7 %constant_dynamic-update-slice_fusion.9 = bf16[5200,128]{1,0:T(8,128)(2,1)} fusion(bf16[1040,128]{1,0:T(8,128)(2,1)} %pack.2.own.refs_0_), kind=kLoop, calls=%fused_computation.10 | loop fusion | bytes 532480
  41.5 1.3 %collective-permute-start.14 = (bf16[912,128]{1,0:T(8,128)(2,1)S(1)}, bf16[912,128]{1,0:T(8,128)(2,1)S(1)}, u32[]{:S(2)}, u32[]{:S(2)}) collective-permute-start(bf16[912,128]{1,0:T(8,128)(2,1)S(1)} %collective-permute-done.11.refs_4_), channel_id=1, source_target_pairs={{0,4},{4,0},{8,12},{12,8},{16,20},{20,16},{24,28},{28,24},{1,5},{5... | collective-permute-start | bytes 700424 | tf_op jit(solution)/shard_map/ppermute | solution.py:170
  42.8 1.3 %collective-permute-start.15 = (bf16[912,128]{1,0:T(8,128)(2,1)S(1)}, bf16[912,128]{1,0:T(8,128)(2,1)S(1)}, u32[]{:S(2)}, u32[]{:S(2)}) collective-permute-start(bf16[912,128]{1,0:T(8,128)(2,1)S(1)} %collective-permute-done.11.refs_4_), channel_id=1, source_target_pairs={{0,8},{4,12},{8,16},{12,20},{16,24},{20,28},{24,0},{28,4},{1,9},{5... | collective-permute-start | bytes 700424 | tf_op jit(solution)/shard_map/ppermute | solution.py:170
  44.1 2.6 %collective-permute-done.4.refs_1_ = bf16[1040,128]{1,0:T(8,128)(2,1)S(1)} collective-permute-done((bf16[1040,128]{1,0:T(8,128)(2,1)}, bf16[1040,128]{1,0:T(8,128)(2,1)S(1)}, u32[]{:S(2)}, u32[]{:S(2)}) %collective-permute-start.4) | collective-permute-done | bytes 266272 | tf_op jit(solution)/shard_map/ppermute | solution.py:170
  46.7 1.7 %collective-permute-done.5.refs_2_ = bf16[1040,128]{1,0:T(8,128)(2,1)S(1)} collective-permute-done((bf16[1040,128]{1,0:T(8,128)(2,1)}, bf16[1040,128]{1,0:T(8,128)(2,1)S(1)}, u32[]{:S(2)}, u32[]{:S(2)}) %collective-permute-start.5) | collective-permute-done | bytes 266272 | tf_op jit(solution)/shard_map/ppermute | solution.py:170
  48.5 1.2 %collective-permute-start.12 = (bf16[1040,128]{1,0:T(8,128)(2,1)S(1)}, bf16[1040,128]{1,0:T(8,128)(2,1)S(1)}, u32[]{:S(2)}, u32[]{:S(2)}) collective-permute-start(bf16[1040,128]{1,0:T(8,128)(2,1)S(1)} %collective-permute-done.5.refs_2_), channel_id=1, source_target_pairs={{0,4},{4,0},{8,12},{12,8},{16,20},{20,16},{24,28},{28,24},{1,5},{5... | collective-permute-start | bytes 798728 | tf_op jit(solution)/shard_map/ppermute | solution.py:170
  49.7 2.1 %collective-permute-done.14.refs_5_ = bf16[912,128]{1,0:T(8,128)(2,1)S(1)} collective-permute-done((bf16[912,128]{1,0:T(8,128)(2,1)S(1)}, bf16[912,128]{1,0:T(8,128)(2,1)S(1)}, u32[]{:S(2)}, u32[]{:S(2)}) %collective-permute-start.14) | collective-permute-done | bytes 233504 | tf_op jit(solution)/shard_map/ppermute | solution.py:170
  51.7 1.7 %collective-permute-done.15.refs_6_ = bf16[912,128]{1,0:T(8,128)(2,1)S(1)} collective-permute-done((bf16[912,128]{1,0:T(8,128)(2,1)S(1)}, bf16[912,128]{1,0:T(8,128)(2,1)S(1)}, u32[]{:S(2)}, u32[]{:S(2)}) %collective-permute-start.15) | collective-permute-done | bytes 233504 | tf_op jit(solution)/shard_map/ppermute | solution.py:170
  56.0 1.9 %collective-permute-start.18 = (bf16[912,128]{1,0:T(8,128)(2,1)S(1)}, bf16[912,128]{1,0:T(8,128)(2,1)S(1)}, u32[]{:S(2)}, u32[]{:S(2)}) collective-permute-start(bf16[912,128]{1,0:T(8,128)(2,1)S(1)} %collective-permute-done.15.refs_6_), channel_id=1, source_target_pairs={{0,4},{4,0},{8,12},{12,8},{16,20},{20,16},{24,28},{28,24},{1,5},{5... | collective-permute-start | bytes 700424 | tf_op jit(solution)/shard_map/ppermute | solution.py:170
  60.9 3.0 %collective-permute-done.18.refs_9_ = bf16[912,128]{1,0:T(8,128)(2,1)S(1)} collective-permute-done((bf16[912,128]{1,0:T(8,128)(2,1)S(1)}, bf16[912,128]{1,0:T(8,128)(2,1)S(1)}, u32[]{:S(2)}, u32[]{:S(2)}) %collective-permute-start.18) | collective-permute-done | bytes 233504 | tf_op jit(solution)/shard_map/ppermute | solution.py:170
  64.0 5.8 %collective-permute-done.16.refs_5_ = bf16[1040,128]{1,0:T(8,128)(2,1)} collective-permute-done((bf16[1040,128]{1,0:T(8,128)(2,1)S(1)}, bf16[1040,128]{1,0:T(8,128)(2,1)}, u32[]{:S(2)}, u32[]{:S(2)}) %collective-permute-start.16) | collective-permute-done | bytes 266272 | tf_op jit(solution)/shard_map/ppermute | solution.py:170
  70.5 1.5 %collective-permute-start.21 = (bf16[1040,128]{1,0:T(8,128)(2,1)}, bf16[1040,128]{1,0:T(8,128)(2,1)S(1)}, u32[]{:S(2)}, u32[]{:S(2)}) collective-permute-start(bf16[1040,128]{1,0:T(8,128)(2,1)} %collective-permute-done.17.refs_6_), channel_id=1, source_target_pairs={{0,4},{4,0},{8,12},{12,8},{16,20},{20,16},{24,28},{28,24},{1,5},{5... | collective-permute-start | bytes 798728 | tf_op jit(solution)/shard_map/ppermute | solution.py:170
  72.8 1.5 %collective-permute-done.25.refs_10_ = bf16[912,128]{1,0:T(8,128)(2,1)S(1)} collective-permute-done((bf16[912,128]{1,0:T(8,128)(2,1)S(1)}, bf16[912,128]{1,0:T(8,128)(2,1)S(1)}, u32[]{:S(2)}, u32[]{:S(2)}) %collective-permute-start.25) | collective-permute-done | bytes 233504 | tf_op jit(solution)/shard_map/ppermute | solution.py:173
  75.0 6.1 %first.1.prods = bf16[32,128,128]{2,1,0:T(8,128)(2,1)} custom-call(s32[8]{0:T(128)} %stack.35.place, bf16[1040,128]{1,0:T(8,128)(2,1)} %pack.2.own.refs_0_, bf16[912,128]{1,0:T(8,128)(2,1)} %pack.3.refs_0_, bf16[912,128]{1,0:T(8,128)(2,1)} %copy-done.8, bf16[912,128]{1,0:T(8,128)(2,1)} %copy-done.9, bf16[912,128]{1,0:T(8,128)(2,1)} %copy-done.10, ...), custom_call_target="tpu_custom_call" | custom-call | flops 234881024 | bytes 10000000 | tf_op jit(solution)/shard_map/first/pallas_call | solution.py:236
  81.2 1.5 %collective-permute-done.26.refs_11_ = bf16[1040,128]{1,0:T(8,128)(2,1)S(1)} collective-permute-done((bf16[1040,128]{1,0:T(8,128)(2,1)S(1)}, bf16[1040,128]{1,0:T(8,128)(2,1)S(1)}, u32[]{:S(2)}, u32[]{:S(2)}) %collective-permute-start.26) | collective-permute-done | bytes 266272 | tf_op jit(solution)/shard_map/ppermute | solution.py:173
  83.4 5.5 %second.1 = (f32[4,128,128]{2,1,0:T(8,128)}, f32[4,128,128]{2,1,0:T(8,128)}, bf16[4,128,128]{2,1,0:T(8,128)(2,1)}, bf16[4,128,128]{2,1,0:T(8,128)(2,1)}) custom-call(s32[8]{0:T(128)} %stack.35.place, bf16[32,128,128]{2,1,0:T(8,128)(2,1)} %first.1.prods, bf16[1040,128]{1,0:T(8,128)(2,1)} %pack.2.own.refs_0_, bf16[1040,128]{1,0:T(8,128)(2,1)} %copy-done.2, ...), custom_call_target="tpu_custom_call" | custom-call | flops 536870912 | bytes 12000000 | tf_op jit(solution)/shard_map/second/pallas_call | solution.py:289
  89.1 1.2 %collective-permute-start.28 = (bf16[4,128,128]{2,1,0:T(8,128)(2,1)}, bf16[4,128,128]{2,1,0:T(8,128)(2,1)S(1)}, u32[]{:S(2)}, u32[]{:S(2)}) collective-permute-start(bf16[4,128,128]{2,1,0:T(8,128)(2,1)} %get-tuple-element.71), channel_id=1, source_target_pairs={{0,2},{1,3},{2,0},{3,1},{4,6},{5,7},{6,4},{7,5},{8,10},{9,11},{10,... | collective-permute-start | bytes 393224 | tf_op jit(solution)/shard_map/ppermute | solution.py:173
  91.1 2.9 %collective-permute-done.28.refs_2_ = bf16[4,128,128]{2,1,0:T(8,128)(2,1)S(1)} collective-permute-done((bf16[4,128,128]{2,1,0:T(8,128)(2,1)}, bf16[4,128,128]{2,1,0:T(8,128)(2,1)S(1)}, u32[]{:S(2)}, u32[]{:S(2)}) %collective-permute-start.28) | collective-permute-done | bytes 131104 | tf_op jit(solution)/shard_map/ppermute | solution.py:173
  94.0 3.3 %collective-permute-done.29.refs_3_ = bf16[4,128,128]{2,1,0:T(8,128)(2,1)S(1)} collective-permute-done((bf16[4,128,128]{2,1,0:T(8,128)(2,1)}, bf16[4,128,128]{2,1,0:T(8,128)(2,1)S(1)}, u32[]{:S(2)}, u32[]{:S(2)}) %collective-permute-start.29) | collective-permute-done | bytes 131104 | tf_op jit(solution)/shard_map/ppermute | solution.py:173
  98.1 2.2 %join.1 = f32[2,256,512]{2,1,0:T(8,128)} custom-call(s32[8]{0:T(128)} %stack.35.place, s32[2,4]{1,0:T(2,128)} %keep.1, f32[4,128,128]{2,1,0:T(8,128)} %get-tuple-element.69.refs_0_, f32[4,128,128]{2,1,0:T(8,128)} %copy-done.19, bf16[4,128,128]{2,1,0:T(8,128)(2,1)} %copy-done.25, bf16[4,128,128]{2,1,0:T(8,128)(2,1)} %copy-done.26), custom_call_target="tpu_custom_call" | custom-call | bytes 2097152 | tf_op jit(solution)/shard_map/join/pallas_call | solution.py:300
  (100 shorter events, 17.2 us)
Async XLA Ops:
  3.2 2.8 %collective-permute-start = (bf16[144,512]{1,0:T(8,128)(2,1)}, bf16[144,512]{1,0:T(8,128)(2,1)S(1)}, u32[]{:S(2)}, u32[]{:S(2)}) collective-permute-start(bf16[144,512]{1,0:T(8,128)(2,1)} %get-tuple-element.39), channel_id=1, source_target_pairs={{0,1},{1,0},{2,3},{3,2},{4,5},{5,4},{6,7},{7,6},{8,9},{9,8},{10,11... | collective-permute-start | bytes 442376 | tf_op jit(solution)/shard_map/ppermute | solution.py:173
  3.2 7.0 %collective-permute-start.6 = (bf16[144,512]{1,0:T(8,128)(2,1)}, bf16[144,512]{1,0:T(8,128)(2,1)S(1)}, u32[]{:S(2)}, u32[]{:S(2)}) collective-permute-start(bf16[144,512]{1,0:T(8,128)(2,1)} %get-tuple-element.50), channel_id=1, source_target_pairs={{0,2},{1,3},{2,0},{3,1},{4,6},{5,7},{6,4},{7,5},{8,10},{9,11},{10,... | collective-permute-start | bytes 442376 | tf_op jit(solution)/shard_map/ppermute | solution.py:173
  5.9 7.5 %collective-permute-start.7 = (bf16[144,512]{1,0:T(8,128)(2,1)}, bf16[144,512]{1,0:T(8,128)(2,1)S(1)}, u32[]{:S(2)}, u32[]{:S(2)}) collective-permute-start(bf16[144,512]{1,0:T(8,128)(2,1)} %get-tuple-element.51), channel_id=1, source_target_pairs={{0,3},{1,2},{2,1},{3,0},{4,7},{5,6},{6,5},{7,4},{8,11},{9,10},{10,... | collective-permute-start | bytes 442376 | tf_op jit(solution)/shard_map/ppermute | solution.py:173
  16.7 7.1 %collective-permute-start.8 = (bf16[912,128]{1,0:T(8,128)(2,1)}, bf16[912,128]{1,0:T(8,128)(2,1)S(1)}, u32[]{:S(2)}, u32[]{:S(2)}) collective-permute-start(bf16[912,128]{1,0:T(8,128)(2,1)} %pack.3.refs_0_), channel_id=1, source_target_pairs={{0,4},{4,0},{8,12},{12,8},{16,20},{20,16},{24,28},{28,24},{1,5},{5... | collective-permute-start | bytes 700424 | tf_op jit(solution)/shard_map/ppermute | solution.py:170
  18.1 9.0 %collective-permute-start.9 = (bf16[912,128]{1,0:T(8,128)(2,1)}, bf16[912,128]{1,0:T(8,128)(2,1)S(1)}, u32[]{:S(2)}, u32[]{:S(2)}) collective-permute-start(bf16[912,128]{1,0:T(8,128)(2,1)} %pack.3.refs_0_), channel_id=1, source_target_pairs={{0,8},{4,12},{8,16},{12,20},{16,24},{20,28},{24,0},{28,4},{1,9},{5... | collective-permute-start | bytes 700424 | tf_op jit(solution)/shard_map/ppermute | solution.py:170
  19.4 8.0 %collective-permute-start.1 = (bf16[272,512]{1,0:T(8,128)(2,1)}, bf16[272,512]{1,0:T(8,128)(2,1)S(1)}, u32[]{:S(2)}, u32[]{:S(2)}) collective-permute-start(bf16[272,512]{1,0:T(8,128)(2,1)} %get-tuple-element.45), channel_id=1, source_target_pairs={{0,1},{1,0},{2,3},{3,2},{4,5},{5,4},{6,7},{7,6},{8,9},{9,8},{10,11... | collective-permute-start | bytes 835592 | tf_op jit(solution)/shard_map/ppermute | solution.py:173
  20.1 8.5 %collective-permute-start.2 = (bf16[272,512]{1,0:T(8,128)(2,1)}, bf16[272,512]{1,0:T(8,128)(2,1)S(1)}, u32[]{:S(2)}, u32[]{:S(2)}) collective-permute-start(bf16[272,512]{1,0:T(8,128)(2,1)} %get-tuple-element.46), channel_id=1, source_target_pairs={{0,2},{1,3},{2,0},{3,1},{4,6},{5,7},{6,4},{7,5},{8,10},{9,11},{10,... | collective-permute-start | bytes 835592 | tf_op jit(solution)/shard_map/ppermute | solution.py:173
  21.4 13.6 %collective-permute-start.3 = (bf16[272,512]{1,0:T(8,128)(2,1)}, bf16[272,512]{1,0:T(8,128)(2,1)S(1)}, u32[]{:S(2)}, u32[]{:S(2)}) collective-permute-start(bf16[272,512]{1,0:T(8,128)(2,1)} %get-tuple-element.47), channel_id=1, source_target_pairs={{0,3},{1,2},{2,1},{3,0},{4,7},{5,6},{6,5},{7,4},{8,11},{9,10},{10,... | collective-permute-start | bytes 835592 | tf_op jit(solution)/shard_map/ppermute | solution.py:173
  27.0 14.4 %collective-permute-start.10 = (bf16[912,128]{1,0:T(8,128)(2,1)S(1)}, bf16[912,128]{1,0:T(8,128)(2,1)S(1)}, u32[]{:S(2)}, u32[]{:S(2)}) collective-permute-start(bf16[912,128]{1,0:T(8,128)(2,1)S(1)} %collective-permute-done.9.refs_2_), channel_id=1, source_target_pairs={{0,4},{4,0},{8,12},{12,8},{16,20},{20,16},{24,28},{28,24},{1,5},{5... | collective-permute-start | bytes 700424 | tf_op jit(solution)/shard_map/ppermute | solution.py:170
  27.3 14.2 %collective-permute-start.11 = (bf16[912,128]{1,0:T(8,128)(2,1)S(1)}, bf16[912,128]{1,0:T(8,128)(2,1)S(1)}, u32[]{:S(2)}, u32[]{:S(2)}) collective-permute-start(bf16[912,128]{1,0:T(8,128)(2,1)S(1)} %collective-permute-done.9.refs_2_), channel_id=1, source_target_pairs={{0,8},{4,12},{8,16},{12,20},{16,24},{20,28},{24,0},{28,4},{1,9},{5... | collective-permute-start | bytes 700424 | tf_op jit(solution)/shard_map/ppermute | solution.py:170
  38.5 8.2 %collective-permute-start.4 = (bf16[1040,128]{1,0:T(8,128)(2,1)}, bf16[1040,128]{1,0:T(8,128)(2,1)S(1)}, u32[]{:S(2)}, u32[]{:S(2)}) collective-permute-start(bf16[1040,128]{1,0:T(8,128)(2,1)} %pack.2.own.refs_0_), channel_id=1, source_target_pairs={{0,4},{4,0},{8,12},{12,8},{16,20},{20,16},{24,28},{28,24},{1,5},{5... | collective-permute-start | bytes 798728 | tf_op jit(solution)/shard_map/ppermute | solution.py:170
  38.8 9.7 %collective-permute-start.5 = (bf16[1040,128]{1,0:T(8,128)(2,1)}, bf16[1040,128]{1,0:T(8,128)(2,1)S(1)}, u32[]{:S(2)}, u32[]{:S(2)}) collective-permute-start(bf16[1040,128]{1,0:T(8,128)(2,1)} %pack.2.own.refs_0_), channel_id=1, source_target_pairs={{0,8},{4,12},{8,16},{12,20},{16,24},{20,28},{24,0},{28,4},{1,9},{5... | collective-permute-start | bytes 798728 | tf_op jit(solution)/shard_map/ppermute | solution.py:170
  41.5 16.5 %copy-start.11 = (bf16[912,128]{1,0:T(8,128)(2,1)}, bf16[912,128]{1,0:T(8,128)(2,1)S(1)}, u32[]{:S(2)}) copy-start(bf16[912,128]{1,0:T(8,128)(2,1)S(1)} %collective-permute-done.11.refs_4_) | copy-start | bytes 700420
  41.5 10.2 %collective-permute-start.14 = (bf16[912,128]{1,0:T(8,128)(2,1)S(1)}, bf16[912,128]{1,0:T(8,128)(2,1)S(1)}, u32[]{:S(2)}, u32[]{:S(2)}) collective-permute-start(bf16[912,128]{1,0:T(8,128)(2,1)S(1)} %collective-permute-done.11.refs_4_), channel_id=1, source_target_pairs={{0,4},{4,0},{8,12},{12,8},{16,20},{20,16},{24,28},{28,24},{1,5},{5... | collective-permute-start | bytes 700424 | tf_op jit(solution)/shard_map/ppermute | solution.py:170
  42.8 10.7 %collective-permute-start.15 = (bf16[912,128]{1,0:T(8,128)(2,1)S(1)}, bf16[912,128]{1,0:T(8,128)(2,1)S(1)}, u32[]{:S(2)}, u32[]{:S(2)}) collective-permute-start(bf16[912,128]{1,0:T(8,128)(2,1)S(1)} %collective-permute-done.11.refs_4_), channel_id=1, source_target_pairs={{0,8},{4,12},{8,16},{12,20},{16,24},{20,28},{24,0},{28,4},{1,9},{5... | collective-permute-start | bytes 700424 | tf_op jit(solution)/shard_map/ppermute | solution.py:170
  48.5 9.9 %collective-permute-start.12 = (bf16[1040,128]{1,0:T(8,128)(2,1)S(1)}, bf16[1040,128]{1,0:T(8,128)(2,1)S(1)}, u32[]{:S(2)}, u32[]{:S(2)}) collective-permute-start(bf16[1040,128]{1,0:T(8,128)(2,1)S(1)} %collective-permute-done.5.refs_2_), channel_id=1, source_target_pairs={{0,4},{4,0},{8,12},{12,8},{16,20},{20,16},{24,28},{28,24},{1,5},{5... | collective-permute-start | bytes 798728 | tf_op jit(solution)/shard_map/ppermute | solution.py:170
  49.7 8.7 %collective-permute-start.13 = (bf16[1040,128]{1,0:T(8,128)(2,1)S(1)}, bf16[1040,128]{1,0:T(8,128)(2,1)S(1)}, u32[]{:S(2)}, u32[]{:S(2)}) collective-permute-start(bf16[1040,128]{1,0:T(8,128)(2,1)S(1)} %collective-permute-done.5.refs_2_), channel_id=1, source_target_pairs={{0,8},{4,12},{8,16},{12,20},{16,24},{20,28},{24,0},{28,4},{1,9},{5... | collective-permute-start | bytes 798728 | tf_op jit(solution)/shard_map/ppermute | solution.py:170
  53.5 10.5 %collective-permute-start.19 = (bf16[4560,128]{1,0:T(8,128)(2,1)S(1)}, bf16[4560,128]{1,0:T(8,128)(2,1)S(1)}, u32[]{:S(2)}, u32[]{:S(2)}) collective-permute-start(bf16[4560,128]{1,0:T(8,128)(2,1)S(1)} %constant_dynamic-update-slice_fusion), channel_id=1, source_target_pairs={{0,1},{1,0},{2,3},{3,2},{4,5},{5,4},{6,7},{7,6},{8,9},{9,8},{10,11... | collective-permute-start | bytes 3502088 | tf_op jit(solution)/shard_map/ppermute | solution.py:173
  56.0 7.9 %collective-permute-start.18 = (bf16[912,128]{1,0:T(8,128)(2,1)S(1)}, bf16[912,128]{1,0:T(8,128)(2,1)S(1)}, u32[]{:S(2)}, u32[]{:S(2)}) collective-permute-start(bf16[912,128]{1,0:T(8,128)(2,1)S(1)} %collective-permute-done.15.refs_6_), channel_id=1, source_target_pairs={{0,4},{4,0},{8,12},{12,8},{16,20},{20,16},{24,28},{28,24},{1,5},{5... | collective-permute-start | bytes 700424 | tf_op jit(solution)/shard_map/ppermute | solution.py:170
  58.0 6.0 %collective-permute-start.20 = (bf16[1824,128]{1,0:T(8,128)(2,1)S(1)}, bf16[1824,128]{1,0:T(8,128)(2,1)S(1)}, u32[]{:S(2)}, u32[]{:S(2)}) collective-permute-start(bf16[1824,128]{1,0:T(8,128)(2,1)S(1)} %pad_maximum_fusion), channel_id=1, source_target_pairs={{0,1},{1,0},{2,3},{3,2},{4,5},{5,4},{6,7},{7,6},{8,9},{9,8},{10,11... | collective-permute-start | bytes 1400840 | tf_op jit(solution)/shard_map/ppermute | solution.py:173
  58.4 22.6 %copy-start.4 = (bf16[1040,128]{1,0:T(8,128)(2,1)}, bf16[1040,128]{1,0:T(8,128)(2,1)S(1)}, u32[]{:S(2)}) copy-start(bf16[1040,128]{1,0:T(8,128)(2,1)S(1)} %collective-permute-done.12.refs_3_) | copy-start | bytes 798724
  58.4 11.3 %collective-permute-start.16 = (bf16[1040,128]{1,0:T(8,128)(2,1)S(1)}, bf16[1040,128]{1,0:T(8,128)(2,1)}, u32[]{:S(2)}, u32[]{:S(2)}) collective-permute-start(bf16[1040,128]{1,0:T(8,128)(2,1)S(1)} %collective-permute-done.13.refs_4_), channel_id=1, source_target_pairs={{0,4},{4,0},{8,12},{12,8},{16,20},{20,16},{24,28},{28,24},{1,5},{5... | collective-permute-start | bytes 798728 | tf_op jit(solution)/shard_map/ppermute | solution.py:170
  59.4 10.3 %collective-permute-start.17 = (bf16[1040,128]{1,0:T(8,128)(2,1)S(1)}, bf16[1040,128]{1,0:T(8,128)(2,1)}, u32[]{:S(2)}, u32[]{:S(2)}) collective-permute-start(bf16[1040,128]{1,0:T(8,128)(2,1)S(1)} %collective-permute-done.13.refs_4_), channel_id=1, source_target_pairs={{0,8},{4,12},{8,16},{12,20},{16,24},{20,28},{24,0},{28,4},{1,9},{5... | collective-permute-start | bytes 798728 | tf_op jit(solution)/shard_map/ppermute | solution.py:170
  69.8 11.3 %collective-permute-start.22 = (bf16[5200,128]{1,0:T(8,128)(2,1)}, bf16[5200,128]{1,0:T(8,128)(2,1)S(1)}, u32[]{:S(2)}, u32[]{:S(2)}) collective-permute-start(bf16[5200,128]{1,0:T(8,128)(2,1)} %constant_dynamic-update-slice_fusion.5), channel_id=1, source_target_pairs={{0,1},{1,0},{2,3},{3,2},{4,5},{5,4},{6,7},{7,6},{8,9},{9,8},{10,11... | collective-permute-start | bytes 3993608 | tf_op jit(solution)/shard_map/ppermute | solution.py:173
  70.5 10.6 %collective-permute-start.21 = (bf16[1040,128]{1,0:T(8,128)(2,1)}, bf16[1040,128]{1,0:T(8,128)(2,1)S(1)}, u32[]{:S(2)}, u32[]{:S(2)}) collective-permute-start(bf16[1040,128]{1,0:T(8,128)(2,1)} %collective-permute-done.17.refs_6_), channel_id=1, source_target_pairs={{0,4},{4,0},{8,12},{12,8},{16,20},{20,16},{24,28},{28,24},{1,5},{5... | collective-permute-start | bytes 798728 | tf_op jit(solution)/shard_map/ppermute | solution.py:170
  72.0 9.1 %collective-permute-start.23 = (bf16[1040,128]{1,0:T(8,128)(2,1)}, bf16[1040,128]{1,0:T(8,128)(2,1)S(1)}, u32[]{:S(2)}, u32[]{:S(2)}) collective-permute-start(bf16[1040,128]{1,0:T(8,128)(2,1)} %collective-permute-done.16.refs_5_), channel_id=1, source_target_pairs={{0,1},{1,0},{2,3},{3,2},{4,5},{5,4},{6,7},{7,6},{8,9},{9,8},{10,11... | collective-permute-start | bytes 798728 | tf_op jit(solution)/shard_map/ppermute | solution.py:173
  72.3 8.8 %collective-permute-start.24 = (bf16[1040,128]{1,0:T(8,128)(2,1)}, bf16[1040,128]{1,0:T(8,128)(2,1)}, u32[]{:S(2)}, u32[]{:S(2)}) collective-permute-start(bf16[1040,128]{1,0:T(8,128)(2,1)} %collective-permute-done.17.refs_6_), channel_id=1, source_target_pairs={{0,1},{1,0},{2,3},{3,2},{4,5},{5,4},{6,7},{7,6},{8,9},{9,8},{10,11... | collective-permute-start | bytes 798728 | tf_op jit(solution)/shard_map/ppermute | solution.py:173
  72.5 1.8 %collective-permute-start.25 = (bf16[912,128]{1,0:T(8,128)(2,1)S(1)}, bf16[912,128]{1,0:T(8,128)(2,1)S(1)}, u32[]{:S(2)}, u32[]{:S(2)}) collective-permute-start(bf16[912,128]{1,0:T(8,128)(2,1)S(1)} %collective-permute-done.18.refs_9_), channel_id=1, source_target_pairs={{0,1},{1,0},{2,3},{3,2},{4,5},{5,4},{6,7},{7,6},{8,9},{9,8},{10,11... | collective-permute-start | bytes 700424 | tf_op jit(solution)/shard_map/ppermute | solution.py:173
  81.1 1.6 %collective-permute-start.26 = (bf16[1040,128]{1,0:T(8,128)(2,1)S(1)}, bf16[1040,128]{1,0:T(8,128)(2,1)S(1)}, u32[]{:S(2)}, u32[]{:S(2)}) collective-permute-start(bf16[1040,128]{1,0:T(8,128)(2,1)S(1)} %collective-permute-done.21.refs_10_), channel_id=1, source_target_pairs={{0,1},{1,0},{2,3},{3,2},{4,5},{5,4},{6,7},{7,6},{8,9},{9,8},{10,11... | collective-permute-start | bytes 798728 | tf_op jit(solution)/shard_map/ppermute | solution.py:173
  88.9 8.4 %collective-permute-start.27 = (f32[4,128,128]{2,1,0:T(8,128)}, f32[4,128,128]{2,1,0:T(8,128)S(1)}, u32[]{:S(2)}, u32[]{:S(2)}) collective-permute-start(f32[4,128,128]{2,1,0:T(8,128)} %get-tuple-element.70), channel_id=1, source_target_pairs={{0,1},{1,0},{2,3},{3,2},{4,5},{5,4},{6,7},{7,6},{8,9},{9,8},{10,11... | collective-permute-start | bytes 786440 | tf_op jit(solution)/shard_map/ppermute | solution.py:173
  89.1 4.9 %collective-permute-start.28 = (bf16[4,128,128]{2,1,0:T(8,128)(2,1)}, bf16[4,128,128]{2,1,0:T(8,128)(2,1)S(1)}, u32[]{:S(2)}, u32[]{:S(2)}) collective-permute-start(bf16[4,128,128]{2,1,0:T(8,128)(2,1)} %get-tuple-element.71), channel_id=1, source_target_pairs={{0,2},{1,3},{2,0},{3,1},{4,6},{5,7},{6,4},{7,5},{8,10},{9,11},{10,... | collective-permute-start | bytes 393224 | tf_op jit(solution)/shard_map/ppermute | solution.py:173
  90.3 7.0 %collective-permute-start.29 = (bf16[4,128,128]{2,1,0:T(8,128)(2,1)}, bf16[4,128,128]{2,1,0:T(8,128)(2,1)S(1)}, u32[]{:S(2)}, u32[]{:S(2)}) collective-permute-start(bf16[4,128,128]{2,1,0:T(8,128)(2,1)} %get-tuple-element.72), channel_id=1, source_target_pairs={{0,3},{1,2},{2,1},{3,0},{4,7},{5,6},{6,5},{7,4},{8,11},{9,10},{10,... | collective-permute-start | bytes 393224 | tf_op jit(solution)/shard_map/ppermute | solution.py:173
  (25 other events, 139.5 us)

commit v8 on v7

--- a/solution.py
+++ b/solution.py
@@ -200,7 +200,7 @@
         return [pieces[0]] + [moved[m] for m in range(1, ncol)]
 
     got_dens = exchange(split[:4])
-    got_dens[1], *oper_pieces = lax.optimization_barrier((got_dens[1], *split[4:]))
+    got_dens[half], *oper_pieces = lax.optimization_barrier((got_dens[half], *split[4:]))
     got_oper = exchange(oper_pieces)
 
     def pack(mats, slots, got):
@@ -280,7 +280,7 @@
     for t in range(layers):
         if t < layers - 1:
             ahead, _ = advance(0, t + 1)
-            advance(1, t, ahead)
+            advance(1, t, ahead[:1])
         else:
             prods = advance(1, t, [first_product()])[1][0]
 

time: 101 us -> 99.4 us (0.984)
  waiting for transfers between devices: 45.5 us -> 44.2 us
    ppermute x16, waiting for transfers between devices: 24.3 us -> 22.7 us  [by_mask(): lax.ppermute(a, 'col', [(c, c ^ mask) for c in range(ncol)])]
where the time goes in v8:
time: 99.4 us; the launch traced here: 99.1 us
  waiting for transfers between devices  44.2 us (44%)
  starting transfers between devices  23.1 us (23%)
  Pallas kernels  21.6 us (22%)
  local copies, waits for them, and re-layouts  9.91 us (10%)
    ppermute x16, waiting for transfers between devices, by_mask(): lax.ppermute(a, 'col', [(c, c ^ mask) for c in range(ncol)])  22.7 us
    ppermute x14, waiting for transfers between devices, by_row(): return lambda a: lax.ppermute(a, 'row', pairs)  21.6 us
    ppermute x14, starting transfers between devices, by_row(): return lambda a: lax.ppermute(a, 'row', pairs)  12.6 us
    ppermute x16, starting transfers between devices, by_mask(): lax.ppermute(a, 'col', [(c, c ^ mask) for c in range(ncol)])  10.4 us
    unnamed x62, local copies, waits for them, and re-layouts  8.53 us
    pallas_call x1, Pallas kernels, first_product(): pl.pallas_call(functools.partial(first_kernel, entries, layers, len(array...  6.04 us
    pallas_call x1, Pallas kernels, body(): pl.pallas_call(functools.partial(second_kernel, entries, layers, len(arra...  5.5 us
    pallas_call x2, Pallas kernels, pack(): pl.pallas_call(functools.partial(pack_kernel, ncol, mats, slots), out_sha...  5.35 us
  transfers between devices with their start and end apart: 30, of which 16 were waited for; matrix products, arithmetic and copies ran while one was open for 6% of the time, Pallas kernels for 9%

profile of v8, /device:TPU:1, one launch (start us, length us, event | category | flops | bytes accessed | tf_op | source)
XLA Modules:
  0.0 99.1 jit_solution(6910576904025402669)
XLA Ops:
  0.6 2.6 %split.1 = (bf16[144,512]{1,0:T(8,128)(2,1)}, bf16[144,512]{1,0:T(8,128)(2,1)}, bf16[144,512]{1,0:T(8,128)(2,1)}, bf16[144,512]{1,0:T(8,128)(2,1)}, bf16[272,512...) custom-call(s32[8]{0:T(128)} %stack.35.place, ...), custom_call_target="tpu_custom_call" | custom-call | bytes 3145728 | tf_op jit(solution)/shard_map/split/pallas_call | solution.py:189
  3.2 2.1 %collective-permute-start = (bf16[144,512]{1,0:T(8,128)(2,1)}, bf16[144,512]{1,0:T(8,128)(2,1)S(1)}, u32[]{:S(2)}, u32[]{:S(2)}) collective-permute-start(bf16[144,512]{1,0:T(8,128)(2,1)} %get-tuple-element.39), channel_id=1, source_target_pairs={{0,2},{1,3},{2,0},{3,1},{4,6},{5,7},{6,4},{7,5},{8,10},{9,11},{10,... | collective-permute-start | bytes 442376 | tf_op jit(solution)/shard_map/ppermute | solution.py:173
  6.2 2.8 %collective-permute-done.refs_2_ = bf16[144,512]{1,0:T(8,128)(2,1)S(1)} collective-permute-done((bf16[144,512]{1,0:T(8,128)(2,1)}, bf16[144,512]{1,0:T(8,128)(2,1)S(1)}, u32[]{:S(2)}, u32[]{:S(2)}) %collective-permute-start) | collective-permute-done | bytes 147488 | tf_op jit(solution)/shard_map/ppermute | solution.py:173
  9.0 3.7 %collective-permute-done.7.refs_3_ = bf16[144,512]{1,0:T(8,128)(2,1)S(1)} collective-permute-done((bf16[144,512]{1,0:T(8,128)(2,1)}, bf16[144,512]{1,0:T(8,128)(2,1)S(1)}, u32[]{:S(2)}, u32[]{:S(2)}) %collective-permute-start.7) | collective-permute-done | bytes 147488 | tf_op jit(solution)/shard_map/ppermute | solution.py:173
  13.4 2.5 %pack.3.refs_0_ = bf16[912,128]{1,0:T(8,128)(2,1)} custom-call(s32[8]{0:T(128)} %stack.35.place, bf16[144,512]{1,0:T(8,128)(2,1)} %get-tuple-element.48.refs_0_, bf16[144,512]{1,0:T(8,128)(2,1)} %copy-done.23, bf16[144,512]{1,0:T(8,128)(2,1)} %copy-done.22, bf16[144,512]{1,0:T(8,128)(2,1)} %copy-done.24), custom_call_target="tpu_custom_call" | custom-call | bytes 1572864 | tf_op jit(solution)/shard_map/pack/pallas_call | solution.py:207
  15.9 1.4 %collective-permute-start.8 = (bf16[912,128]{1,0:T(8,128)(2,1)}, bf16[912,128]{1,0:T(8,128)(2,1)S(1)}, u32[]{:S(2)}, u32[]{:S(2)}) collective-permute-start(bf16[912,128]{1,0:T(8,128)(2,1)} %pack.3.refs_0_), channel_id=1, source_target_pairs={{0,4},{4,0},{8,12},{12,8},{16,20},{20,16},{24,28},{28,24},{1,5},{5... | collective-permute-start | bytes 700424 | tf_op jit(solution)/shard_map/ppermute | solution.py:170
  17.4 1.3 %collective-permute-start.9 = (bf16[912,128]{1,0:T(8,128)(2,1)}, bf16[912,128]{1,0:T(8,128)(2,1)S(1)}, u32[]{:S(2)}, u32[]{:S(2)}) collective-permute-start(bf16[912,128]{1,0:T(8,128)(2,1)} %pack.3.refs_0_), channel_id=1, source_target_pairs={{0,8},{4,12},{8,16},{12,20},{16,24},{20,28},{24,0},{28,4},{1,9},{5... | collective-permute-start | bytes 700424 | tf_op jit(solution)/shard_map/ppermute | solution.py:170
  21.8 1.6 %collective-permute-done.8.refs_1_ = bf16[912,128]{1,0:T(8,128)(2,1)S(1)} collective-permute-done((bf16[912,128]{1,0:T(8,128)(2,1)}, bf16[912,128]{1,0:T(8,128)(2,1)S(1)}, u32[]{:S(2)}, u32[]{:S(2)}) %collective-permute-start.8) | collective-permute-done | bytes 233504 | tf_op jit(solution)/shard_map/ppermute | solution.py:170
  23.4 3.4 %collective-permute-done.9.refs_2_ = bf16[912,128]{1,0:T(8,128)(2,1)S(1)} collective-permute-done((bf16[912,128]{1,0:T(8,128)(2,1)}, bf16[912,128]{1,0:T(8,128)(2,1)S(1)}, u32[]{:S(2)}, u32[]{:S(2)}) %collective-permute-start.9) | collective-permute-done | bytes 233504 | tf_op jit(solution)/shard_map/ppermute | solution.py:170
  27.4 6.5 %collective-permute-done.3.refs_3_ = bf16[272,512]{1,0:T(8,128)(2,1)S(1)} collective-permute-done((bf16[272,512]{1,0:T(8,128)(2,1)}, bf16[272,512]{1,0:T(8,128)(2,1)S(1)}, u32[]{:S(2)}, u32[]{:S(2)}) %collective-permute-start.3) | collective-permute-done | bytes 278560 | tf_op jit(solution)/shard_map/ppermute | solution.py:173
  34.6 2.8 %pack.2.own.refs_0_ = bf16[1040,128]{1,0:T(8,128)(2,1)} custom-call(s32[8]{0:T(128)} %stack.35.place, bf16[272,512]{1,0:T(8,128)(2,1)} %get-tuple-element.44.refs_0_, bf16[272,512]{1,0:T(8,128)(2,1)} %copy-done.13, bf16[272,512]{1,0:T(8,128)(2,1)} %copy-done.14, bf16[272,512]{1,0:T(8,128)(2,1)} %copy-done.15), custom_call_target="tpu_custom_call" | custom-call | bytes 1572864 | tf_op jit(solution)/shard_map/pack/pallas_call | solution.py:207
  37.7 1.3 %collective-permute-start.5 = (bf16[1040,128]{1,0:T(8,128)(2,1)}, bf16[1040,128]{1,0:T(8,128)(2,1)S(1)}, u32[]{:S(2)}, u32[]{:S(2)}) collective-permute-start(bf16[1040,128]{1,0:T(8,128)(2,1)} %pack.2.own.refs_0_), channel_id=1, source_target_pairs={{0,8},{4,12},{8,16},{12,20},{16,24},{20,28},{24,0},{28,4},{1,9},{5... | collective-permute-start | bytes 798728 | tf_op jit(solution)/shard_map/ppermute | solution.py:170
  39.0 1.7 %constant_dynamic-update-slice_fusion.9 = bf16[5200,128]{1,0:T(8,128)(2,1)} fusion(bf16[1040,128]{1,0:T(8,128)(2,1)} %pack.2.own.refs_0_), kind=kLoop, calls=%fused_computation.10 | loop fusion | bytes 532480
  41.7 1.3 %collective-permute-start.15 = (bf16[912,128]{1,0:T(8,128)(2,1)S(1)}, bf16[912,128]{1,0:T(8,128)(2,1)S(1)}, u32[]{:S(2)}, u32[]{:S(2)}) collective-permute-start(bf16[912,128]{1,0:T(8,128)(2,1)S(1)} %collective-permute-done.11.refs_4_), channel_id=1, source_target_pairs={{0,8},{4,12},{8,16},{12,20},{16,24},{20,28},{24,0},{28,4},{1,9},{5... | collective-permute-start | bytes 700424 | tf_op jit(solution)/shard_map/ppermute | solution.py:170
  43.1 2.7 %collective-permute-done.4.refs_1_ = bf16[1040,128]{1,0:T(8,128)(2,1)S(1)} collective-permute-done((bf16[1040,128]{1,0:T(8,128)(2,1)}, bf16[1040,128]{1,0:T(8,128)(2,1)S(1)}, u32[]{:S(2)}, u32[]{:S(2)}) %collective-permute-start.4) | collective-permute-done | bytes 266272 | tf_op jit(solution)/shard_map/ppermute | solution.py:170
  45.8 1.9 %collective-permute-done.5.refs_2_ = bf16[1040,128]{1,0:T(8,128)(2,1)S(1)} collective-permute-done((bf16[1040,128]{1,0:T(8,128)(2,1)}, bf16[1040,128]{1,0:T(8,128)(2,1)S(1)}, u32[]{:S(2)}, u32[]{:S(2)}) %collective-permute-start.5) | collective-permute-done | bytes 266272 | tf_op jit(solution)/shard_map/ppermute | solution.py:170
  47.7 1.2 %collective-permute-start.12 = (bf16[1040,128]{1,0:T(8,128)(2,1)S(1)}, bf16[1040,128]{1,0:T(8,128)(2,1)S(1)}, u32[]{:S(2)}, u32[]{:S(2)}) collective-permute-start(bf16[1040,128]{1,0:T(8,128)(2,1)S(1)} %collective-permute-done.5.refs_2_), channel_id=1, source_target_pairs={{0,4},{4,0},{8,12},{12,8},{16,20},{20,16},{24,28},{28,24},{1,5},{5... | collective-permute-start | bytes 798728 | tf_op jit(solution)/shard_map/ppermute | solution.py:170
  48.9 1.9 %collective-permute-done.14.refs_5_ = bf16[912,128]{1,0:T(8,128)(2,1)S(1)} collective-permute-done((bf16[912,128]{1,0:T(8,128)(2,1)S(1)}, bf16[912,128]{1,0:T(8,128)(2,1)S(1)}, u32[]{:S(2)}, u32[]{:S(2)}) %collective-permute-start.14) | collective-permute-done | bytes 233504 | tf_op jit(solution)/shard_map/ppermute | solution.py:170
  50.8 1.9 %collective-permute-done.15.refs_6_ = bf16[912,128]{1,0:T(8,128)(2,1)S(1)} collective-permute-done((bf16[912,128]{1,0:T(8,128)(2,1)S(1)}, bf16[912,128]{1,0:T(8,128)(2,1)S(1)}, u32[]{:S(2)}, u32[]{:S(2)}) %collective-permute-start.15) | collective-permute-done | bytes 233504 | tf_op jit(solution)/shard_map/ppermute | solution.py:170
  55.0 1.7 %collective-permute-start.18 = (bf16[912,128]{1,0:T(8,128)(2,1)S(1)}, bf16[912,128]{1,0:T(8,128)(2,1)S(1)}, u32[]{:S(2)}, u32[]{:S(2)}) collective-permute-start(bf16[912,128]{1,0:T(8,128)(2,1)S(1)} %collective-permute-done.15.refs_6_), channel_id=1, source_target_pairs={{0,4},{4,0},{8,12},{12,8},{16,20},{20,16},{24,28},{28,24},{1,5},{5... | collective-permute-start | bytes 700424 | tf_op jit(solution)/shard_map/ppermute | solution.py:170
  57.2 1.5 %collective-permute-start.16 = (bf16[1040,128]{1,0:T(8,128)(2,1)S(1)}, bf16[1040,128]{1,0:T(8,128)(2,1)}, u32[]{:S(2)}, u32[]{:S(2)}) collective-permute-start(bf16[1040,128]{1,0:T(8,128)(2,1)S(1)} %collective-permute-done.13.refs_4_), channel_id=1, source_target_pairs={{0,4},{4,0},{8,12},{12,8},{16,20},{20,16},{24,28},{28,24},{1,5},{5... | collective-permute-start | bytes 798728 | tf_op jit(solution)/shard_map/ppermute | solution.py:170
  60.1 2.5 %collective-permute-done.18.refs_9_ = bf16[912,128]{1,0:T(8,128)(2,1)S(1)} collective-permute-done((bf16[912,128]{1,0:T(8,128)(2,1)S(1)}, bf16[912,128]{1,0:T(8,128)(2,1)S(1)}, u32[]{:S(2)}, u32[]{:S(2)}) %collective-permute-start.18) | collective-permute-done | bytes 233504 | tf_op jit(solution)/shard_map/ppermute | solution.py:170
  62.6 5.8 %collective-permute-done.16.refs_5_ = bf16[1040,128]{1,0:T(8,128)(2,1)} collective-permute-done((bf16[1040,128]{1,0:T(8,128)(2,1)S(1)}, bf16[1040,128]{1,0:T(8,128)(2,1)}, u32[]{:S(2)}, u32[]{:S(2)}) %collective-permute-start.16) | collective-permute-done | bytes 266272 | tf_op jit(solution)/shard_map/ppermute | solution.py:170
  69.3 1.3 %collective-permute-start.21 = (bf16[1040,128]{1,0:T(8,128)(2,1)}, bf16[1040,128]{1,0:T(8,128)(2,1)S(1)}, u32[]{:S(2)}, u32[]{:S(2)}) collective-permute-start(bf16[1040,128]{1,0:T(8,128)(2,1)} %collective-permute-done.17.refs_6_), channel_id=1, source_target_pairs={{0,4},{4,0},{8,12},{12,8},{16,20},{20,16},{24,28},{28,24},{1,5},{5... | collective-permute-start | bytes 798728 | tf_op jit(solution)/shard_map/ppermute | solution.py:170
  71.5 1.6 %collective-permute-done.25.refs_10_ = bf16[912,128]{1,0:T(8,128)(2,1)S(1)} collective-permute-done((bf16[912,128]{1,0:T(8,128)(2,1)S(1)}, bf16[912,128]{1,0:T(8,128)(2,1)S(1)}, u32[]{:S(2)}, u32[]{:S(2)}) %collective-permute-start.25) | collective-permute-done | bytes 233504 | tf_op jit(solution)/shard_map/ppermute | solution.py:173
  73.8 6.0 %first.1.prods = bf16[32,128,128]{2,1,0:T(8,128)(2,1)} custom-call(s32[8]{0:T(128)} %stack.35.place, bf16[1040,128]{1,0:T(8,128)(2,1)} %pack.2.own.refs_0_, bf16[912,128]{1,0:T(8,128)(2,1)} %pack.3.refs_0_, bf16[912,128]{1,0:T(8,128)(2,1)} %copy-done.8, bf16[912,128]{1,0:T(8,128)(2,1)} %copy-done.9, bf16[912,128]{1,0:T(8,128)(2,1)} %copy-done.10, ...), custom_call_target="tpu_custom_call" | custom-call | flops 234881024 | bytes 10000000 | tf_op jit(solution)/shard_map/first/pallas_call | solution.py:236
  80.0 1.5 %collective-permute-done.26.refs_11_ = bf16[1040,128]{1,0:T(8,128)(2,1)S(1)} collective-permute-done((bf16[1040,128]{1,0:T(8,128)(2,1)S(1)}, bf16[1040,128]{1,0:T(8,128)(2,1)S(1)}, u32[]{:S(2)}, u32[]{:S(2)}) %collective-permute-start.26) | collective-permute-done | bytes 266272 | tf_op jit(solution)/shard_map/ppermute | solution.py:173
  82.3 5.5 %second.1 = (f32[4,128,128]{2,1,0:T(8,128)}, f32[4,128,128]{2,1,0:T(8,128)}, bf16[4,128,128]{2,1,0:T(8,128)(2,1)}, bf16[4,128,128]{2,1,0:T(8,128)(2,1)}) custom-call(s32[8]{0:T(128)} %stack.35.place, bf16[32,128,128]{2,1,0:T(8,128)(2,1)} %first.1.prods, bf16[1040,128]{1,0:T(8,128)(2,1)} %pack.2.own.refs_0_, bf16[1040,128]{1,0:T(8,128)(2,1)} %copy-done.2, ...), custom_call_target="tpu_custom_call" | custom-call | flops 536870912 | bytes 12000000 | tf_op jit(solution)/shard_map/second/pallas_call | solution.py:289
  87.9 1.0 %collective-permute-start.28 = (bf16[4,128,128]{2,1,0:T(8,128)(2,1)}, bf16[4,128,128]{2,1,0:T(8,128)(2,1)S(1)}, u32[]{:S(2)}, u32[]{:S(2)}) collective-permute-start(bf16[4,128,128]{2,1,0:T(8,128)(2,1)} %get-tuple-element.71), channel_id=1, source_target_pairs={{0,2},{1,3},{2,0},{3,1},{4,6},{5,7},{6,4},{7,5},{8,10},{9,11},{10,... | collective-permute-start | bytes 393224 | tf_op jit(solution)/shard_map/ppermute | solution.py:173
  89.9 2.9 %collective-permute-done.28.refs_2_ = bf16[4,128,128]{2,1,0:T(8,128)(2,1)S(1)} collective-permute-done((bf16[4,128,128]{2,1,0:T(8,128)(2,1)}, bf16[4,128,128]{2,1,0:T(8,128)(2,1)S(1)}, u32[]{:S(2)}, u32[]{:S(2)}) %collective-permute-start.28) | collective-permute-done | bytes 131104 | tf_op jit(solution)/shard_map/ppermute | solution.py:173
  92.8 3.3 %collective-permute-done.29.refs_3_ = bf16[4,128,128]{2,1,0:T(8,128)(2,1)S(1)} collective-permute-done((bf16[4,128,128]{2,1,0:T(8,128)(2,1)}, bf16[4,128,128]{2,1,0:T(8,128)(2,1)S(1)}, u32[]{:S(2)}, u32[]{:S(2)}) %collective-permute-start.29) | collective-permute-done | bytes 131104 | tf_op jit(solution)/shard_map/ppermute | solution.py:173
  96.9 2.2 %join.1 = f32[2,256,512]{2,1,0:T(8,128)} custom-call(s32[8]{0:T(128)} %stack.35.place, s32[2,4]{1,0:T(2,128)} %keep.1, f32[4,128,128]{2,1,0:T(8,128)} %get-tuple-element.69.refs_0_, f32[4,128,128]{2,1,0:T(8,128)} %copy-done.19, bf16[4,128,128]{2,1,0:T(8,128)(2,1)} %copy-done.25, bf16[4,128,128]{2,1,0:T(8,128)(2,1)} %copy-done.26), custom_call_target="tpu_custom_call" | custom-call | bytes 2097152 | tf_op jit(solution)/shard_map/join/pallas_call | solution.py:300
  (100 shorter events, 17.4 us)
Async XLA Ops:
  3.2 5.9 %collective-permute-start = (bf16[144,512]{1,0:T(8,128)(2,1)}, bf16[144,512]{1,0:T(8,128)(2,1)S(1)}, u32[]{:S(2)}, u32[]{:S(2)}) collective-permute-start(bf16[144,512]{1,0:T(8,128)(2,1)} %get-tuple-element.39), channel_id=1, source_target_pairs={{0,2},{1,3},{2,0},{3,1},{4,6},{5,7},{6,4},{7,5},{8,10},{9,11},{10,... | collective-permute-start | bytes 442376 | tf_op jit(solution)/shard_map/ppermute | solution.py:173
  5.2 3.8 %collective-permute-start.6 = (bf16[144,512]{1,0:T(8,128)(2,1)}, bf16[144,512]{1,0:T(8,128)(2,1)S(1)}, u32[]{:S(2)}, u32[]{:S(2)}) collective-permute-start(bf16[144,512]{1,0:T(8,128)(2,1)} %get-tuple-element.49), channel_id=1, source_target_pairs={{0,1},{1,0},{2,3},{3,2},{4,5},{5,4},{6,7},{7,6},{8,9},{9,8},{10,11... | collective-permute-start | bytes 442376 | tf_op jit(solution)/shard_map/ppermute | solution.py:173
  6.2 6.5 %collective-permute-start.7 = (bf16[144,512]{1,0:T(8,128)(2,1)}, bf16[144,512]{1,0:T(8,128)(2,1)S(1)}, u32[]{:S(2)}, u32[]{:S(2)}) collective-permute-start(bf16[144,512]{1,0:T(8,128)(2,1)} %get-tuple-element.51), channel_id=1, source_target_pairs={{0,3},{1,2},{2,1},{3,0},{4,7},{5,6},{6,5},{7,4},{8,11},{9,10},{10,... | collective-permute-start | bytes 442376 | tf_op jit(solution)/shard_map/ppermute | solution.py:173
  15.9 7.5 %collective-permute-start.8 = (bf16[912,128]{1,0:T(8,128)(2,1)}, bf16[912,128]{1,0:T(8,128)(2,1)S(1)}, u32[]{:S(2)}, u32[]{:S(2)}) collective-permute-start(bf16[912,128]{1,0:T(8,128)(2,1)} %pack.3.refs_0_), channel_id=1, source_target_pairs={{0,4},{4,0},{8,12},{12,8},{16,20},{20,16},{24,28},{28,24},{1,5},{5... | collective-permute-start | bytes 700424 | tf_op jit(solution)/shard_map/ppermute | solution.py:170
  17.4 9.4 %collective-permute-start.9 = (bf16[912,128]{1,0:T(8,128)(2,1)}, bf16[912,128]{1,0:T(8,128)(2,1)S(1)}, u32[]{:S(2)}, u32[]{:S(2)}) collective-permute-start(bf16[912,128]{1,0:T(8,128)(2,1)} %pack.3.refs_0_), channel_id=1, source_target_pairs={{0,8},{4,12},{8,16},{12,20},{16,24},{20,28},{24,0},{28,4},{1,9},{5... | collective-permute-start | bytes 700424 | tf_op jit(solution)/shard_map/ppermute | solution.py:170
  18.7 8.4 %collective-permute-start.1 = (bf16[272,512]{1,0:T(8,128)(2,1)}, bf16[272,512]{1,0:T(8,128)(2,1)S(1)}, u32[]{:S(2)}, u32[]{:S(2)}) collective-permute-start(bf16[272,512]{1,0:T(8,128)(2,1)} %get-tuple-element.45), channel_id=1, source_target_pairs={{0,1},{1,0},{2,3},{3,2},{4,5},{5,4},{6,7},{7,6},{8,9},{9,8},{10,11... | collective-permute-start | bytes 835592 | tf_op jit(solution)/shard_map/ppermute | solution.py:173
  19.1 8.3 %collective-permute-start.2 = (bf16[272,512]{1,0:T(8,128)(2,1)}, bf16[272,512]{1,0:T(8,128)(2,1)S(1)}, u32[]{:S(2)}, u32[]{:S(2)}) collective-permute-start(bf16[272,512]{1,0:T(8,128)(2,1)} %get-tuple-element.46), channel_id=1, source_target_pairs={{0,2},{1,3},{2,0},{3,1},{4,6},{5,7},{6,4},{7,5},{8,10},{9,11},{10,... | collective-permute-start | bytes 835592 | tf_op jit(solution)/shard_map/ppermute | solution.py:173
  20.0 13.9 %collective-permute-start.3 = (bf16[272,512]{1,0:T(8,128)(2,1)}, bf16[272,512]{1,0:T(8,128)(2,1)S(1)}, u32[]{:S(2)}, u32[]{:S(2)}) collective-permute-start(bf16[272,512]{1,0:T(8,128)(2,1)} %get-tuple-element.47), channel_id=1, source_target_pairs={{0,3},{1,2},{2,1},{3,0},{4,7},{5,6},{6,5},{7,4},{8,11},{9,10},{10,... | collective-permute-start | bytes 835592 | tf_op jit(solution)/shard_map/ppermute | solution.py:173
  26.8 13.9 %collective-permute-start.10 = (bf16[912,128]{1,0:T(8,128)(2,1)S(1)}, bf16[912,128]{1,0:T(8,128)(2,1)S(1)}, u32[]{:S(2)}, u32[]{:S(2)}) collective-permute-start(bf16[912,128]{1,0:T(8,128)(2,1)S(1)} %collective-permute-done.9.refs_2_), channel_id=1, source_target_pairs={{0,4},{4,0},{8,12},{12,8},{16,20},{20,16},{24,28},{28,24},{1,5},{5... | collective-permute-start | bytes 700424 | tf_op jit(solution)/shard_map/ppermute | solution.py:170
  27.1 13.7 %collective-permute-start.11 = (bf16[912,128]{1,0:T(8,128)(2,1)S(1)}, bf16[912,128]{1,0:T(8,128)(2,1)S(1)}, u32[]{:S(2)}, u32[]{:S(2)}) collective-permute-start(bf16[912,128]{1,0:T(8,128)(2,1)S(1)} %collective-permute-done.9.refs_2_), channel_id=1, source_target_pairs={{0,8},{4,12},{8,16},{12,20},{16,24},{20,28},{24,0},{28,4},{1,9},{5... | collective-permute-start | bytes 700424 | tf_op jit(solution)/shard_map/ppermute | solution.py:170
  37.4 8.3 %collective-permute-start.4 = (bf16[1040,128]{1,0:T(8,128)(2,1)}, bf16[1040,128]{1,0:T(8,128)(2,1)S(1)}, u32[]{:S(2)}, u32[]{:S(2)}) collective-permute-start(bf16[1040,128]{1,0:T(8,128)(2,1)} %pack.2.own.refs_0_), channel_id=1, source_target_pairs={{0,4},{4,0},{8,12},{12,8},{16,20},{20,16},{24,28},{28,24},{1,5},{5... | collective-permute-start | bytes 798728 | tf_op jit(solution)/shard_map/ppermute | solution.py:170
  37.7 10.0 %collective-permute-start.5 = (bf16[1040,128]{1,0:T(8,128)(2,1)}, bf16[1040,128]{1,0:T(8,128)(2,1)S(1)}, u32[]{:S(2)}, u32[]{:S(2)}) collective-permute-start(bf16[1040,128]{1,0:T(8,128)(2,1)} %pack.2.own.refs_0_), channel_id=1, source_target_pairs={{0,8},{4,12},{8,16},{12,20},{16,24},{20,28},{24,0},{28,4},{1,9},{5... | collective-permute-start | bytes 798728 | tf_op jit(solution)/shard_map/ppermute | solution.py:170
  40.7 16.0 %copy-start.11 = (bf16[912,128]{1,0:T(8,128)(2,1)}, bf16[912,128]{1,0:T(8,128)(2,1)S(1)}, u32[]{:S(2)}) copy-start(bf16[912,128]{1,0:T(8,128)(2,1)S(1)} %collective-permute-done.11.refs_4_) | copy-start | bytes 700420
  40.7 10.0 %collective-permute-start.14 = (bf16[912,128]{1,0:T(8,128)(2,1)S(1)}, bf16[912,128]{1,0:T(8,128)(2,1)S(1)}, u32[]{:S(2)}, u32[]{:S(2)}) collective-permute-start(bf16[912,128]{1,0:T(8,128)(2,1)S(1)} %collective-permute-done.11.refs_4_), channel_id=1, source_target_pairs={{0,4},{4,0},{8,12},{12,8},{16,20},{20,16},{24,28},{28,24},{1,5},{5... | collective-permute-start | bytes 700424 | tf_op jit(solution)/shard_map/ppermute | solution.py:170
  41.7 10.9 %collective-permute-start.15 = (bf16[912,128]{1,0:T(8,128)(2,1)S(1)}, bf16[912,128]{1,0:T(8,128)(2,1)S(1)}, u32[]{:S(2)}, u32[]{:S(2)}) collective-permute-start(bf16[912,128]{1,0:T(8,128)(2,1)S(1)} %collective-permute-done.11.refs_4_), channel_id=1, source_target_pairs={{0,8},{4,12},{8,16},{12,20},{16,24},{20,28},{24,0},{28,4},{1,9},{5... | collective-permute-start | bytes 700424 | tf_op jit(solution)/shard_map/ppermute | solution.py:170
  47.7 9.5 %collective-permute-start.12 = (bf16[1040,128]{1,0:T(8,128)(2,1)S(1)}, bf16[1040,128]{1,0:T(8,128)(2,1)S(1)}, u32[]{:S(2)}, u32[]{:S(2)}) collective-permute-start(bf16[1040,128]{1,0:T(8,128)(2,1)S(1)} %collective-permute-done.5.refs_2_), channel_id=1, source_target_pairs={{0,4},{4,0},{8,12},{12,8},{16,20},{20,16},{24,28},{28,24},{1,5},{5... | collective-permute-start | bytes 798728 | tf_op jit(solution)/shard_map/ppermute | solution.py:170
  48.9 8.3 %collective-permute-start.13 = (bf16[1040,128]{1,0:T(8,128)(2,1)S(1)}, bf16[1040,128]{1,0:T(8,128)(2,1)S(1)}, u32[]{:S(2)}, u32[]{:S(2)}) collective-permute-start(bf16[1040,128]{1,0:T(8,128)(2,1)S(1)} %collective-permute-done.5.refs_2_), channel_id=1, source_target_pairs={{0,8},{4,12},{8,16},{12,20},{16,24},{20,28},{24,0},{28,4},{1,9},{5... | collective-permute-start | bytes 798728 | tf_op jit(solution)/shard_map/ppermute | solution.py:170
  52.7 9.9 %collective-permute-start.19 = (bf16[4560,128]{1,0:T(8,128)(2,1)S(1)}, bf16[4560,128]{1,0:T(8,128)(2,1)S(1)}, u32[]{:S(2)}, u32[]{:S(2)}) collective-permute-start(bf16[4560,128]{1,0:T(8,128)(2,1)S(1)} %constant_dynamic-update-slice_fusion), channel_id=1, source_target_pairs={{0,1},{1,0},{2,3},{3,2},{4,5},{5,4},{6,7},{7,6},{8,9},{9,8},{10,11... | collective-permute-start | bytes 3502088 | tf_op jit(solution)/shard_map/ppermute | solution.py:173
  55.0 7.6 %collective-permute-start.18 = (bf16[912,128]{1,0:T(8,128)(2,1)S(1)}, bf16[912,128]{1,0:T(8,128)(2,1)S(1)}, u32[]{:S(2)}, u32[]{:S(2)}) collective-permute-start(bf16[912,128]{1,0:T(8,128)(2,1)S(1)} %collective-permute-done.15.refs_6_), channel_id=1, source_target_pairs={{0,4},{4,0},{8,12},{12,8},{16,20},{20,16},{24,28},{28,24},{1,5},{5... | collective-permute-start | bytes 700424 | tf_op jit(solution)/shard_map/ppermute | solution.py:170
  56.7 5.9 %collective-permute-start.20 = (bf16[1824,128]{1,0:T(8,128)(2,1)S(1)}, bf16[1824,128]{1,0:T(8,128)(2,1)S(1)}, u32[]{:S(2)}, u32[]{:S(2)}) collective-permute-start(bf16[1824,128]{1,0:T(8,128)(2,1)S(1)} %pad_maximum_fusion), channel_id=1, source_target_pairs={{0,1},{1,0},{2,3},{3,2},{4,5},{5,4},{6,7},{7,6},{8,9},{9,8},{10,11... | collective-permute-start | bytes 1400840 | tf_op jit(solution)/shard_map/ppermute | solution.py:173
  57.1 22.7 %copy-start.4 = (bf16[1040,128]{1,0:T(8,128)(2,1)}, bf16[1040,128]{1,0:T(8,128)(2,1)S(1)}, u32[]{:S(2)}) copy-start(bf16[1040,128]{1,0:T(8,128)(2,1)S(1)} %collective-permute-done.12.refs_3_) | copy-start | bytes 798724
  57.2 11.3 %collective-permute-start.16 = (bf16[1040,128]{1,0:T(8,128)(2,1)S(1)}, bf16[1040,128]{1,0:T(8,128)(2,1)}, u32[]{:S(2)}, u32[]{:S(2)}) collective-permute-start(bf16[1040,128]{1,0:T(8,128)(2,1)S(1)} %collective-permute-done.13.refs_4_), channel_id=1, source_target_pairs={{0,4},{4,0},{8,12},{12,8},{16,20},{20,16},{24,28},{28,24},{1,5},{5... | collective-permute-start | bytes 798728 | tf_op jit(solution)/shard_map/ppermute | solution.py:170
  58.6 9.8 %collective-permute-start.17 = (bf16[1040,128]{1,0:T(8,128)(2,1)S(1)}, bf16[1040,128]{1,0:T(8,128)(2,1)}, u32[]{:S(2)}, u32[]{:S(2)}) collective-permute-start(bf16[1040,128]{1,0:T(8,128)(2,1)S(1)} %collective-permute-done.13.refs_4_), channel_id=1, source_target_pairs={{0,8},{4,12},{8,16},{12,20},{16,24},{20,28},{24,0},{28,4},{1,9},{5... | collective-permute-start | bytes 798728 | tf_op jit(solution)/shard_map/ppermute | solution.py:170
  68.4 11.5 %collective-permute-start.22 = (bf16[5200,128]{1,0:T(8,128)(2,1)}, bf16[5200,128]{1,0:T(8,128)(2,1)S(1)}, u32[]{:S(2)}, u32[]{:S(2)}) collective-permute-start(bf16[5200,128]{1,0:T(8,128)(2,1)} %constant_dynamic-update-slice_fusion.5), channel_id=1, source_target_pairs={{0,1},{1,0},{2,3},{3,2},{4,5},{5,4},{6,7},{7,6},{8,9},{9,8},{10,11... | collective-permute-start | bytes 3993608 | tf_op jit(solution)/shard_map/ppermute | solution.py:173
  69.3 10.5 %collective-permute-start.21 = (bf16[1040,128]{1,0:T(8,128)(2,1)}, bf16[1040,128]{1,0:T(8,128)(2,1)S(1)}, u32[]{:S(2)}, u32[]{:S(2)}) collective-permute-start(bf16[1040,128]{1,0:T(8,128)(2,1)} %collective-permute-done.17.refs_6_), channel_id=1, source_target_pairs={{0,4},{4,0},{8,12},{12,8},{16,20},{20,16},{24,28},{28,24},{1,5},{5... | collective-permute-start | bytes 798728 | tf_op jit(solution)/shard_map/ppermute | solution.py:170
  70.7 9.2 %collective-permute-start.23 = (bf16[1040,128]{1,0:T(8,128)(2,1)}, bf16[1040,128]{1,0:T(8,128)(2,1)S(1)}, u32[]{:S(2)}, u32[]{:S(2)}) collective-permute-start(bf16[1040,128]{1,0:T(8,128)(2,1)} %collective-permute-done.16.refs_5_), channel_id=1, source_target_pairs={{0,1},{1,0},{2,3},{3,2},{4,5},{5,4},{6,7},{7,6},{8,9},{9,8},{10,11... | collective-permute-start | bytes 798728 | tf_op jit(solution)/shard_map/ppermute | solution.py:173
  71.0 8.9 %collective-permute-start.24 = (bf16[1040,128]{1,0:T(8,128)(2,1)}, bf16[1040,128]{1,0:T(8,128)(2,1)}, u32[]{:S(2)}, u32[]{:S(2)}) collective-permute-start(bf16[1040,128]{1,0:T(8,128)(2,1)} %collective-permute-done.17.refs_6_), channel_id=1, source_target_pairs={{0,1},{1,0},{2,3},{3,2},{4,5},{5,4},{6,7},{7,6},{8,9},{9,8},{10,11... | collective-permute-start | bytes 798728 | tf_op jit(solution)/shard_map/ppermute | solution.py:173
  71.2 1.9 %collective-permute-start.25 = (bf16[912,128]{1,0:T(8,128)(2,1)S(1)}, bf16[912,128]{1,0:T(8,128)(2,1)S(1)}, u32[]{:S(2)}, u32[]{:S(2)}) collective-permute-start(bf16[912,128]{1,0:T(8,128)(2,1)S(1)} %collective-permute-done.18.refs_9_), channel_id=1, source_target_pairs={{0,1},{1,0},{2,3},{3,2},{4,5},{5,4},{6,7},{7,6},{8,9},{9,8},{10,11... | collective-permute-start | bytes 700424 | tf_op jit(solution)/shard_map/ppermute | solution.py:173
  79.9 1.6 %collective-permute-start.26 = (bf16[1040,128]{1,0:T(8,128)(2,1)S(1)}, bf16[1040,128]{1,0:T(8,128)(2,1)S(1)}, u32[]{:S(2)}, u32[]{:S(2)}) collective-permute-start(bf16[1040,128]{1,0:T(8,128)(2,1)S(1)} %collective-permute-done.21.refs_10_), channel_id=1, source_target_pairs={{0,1},{1,0},{2,3},{3,2},{4,5},{5,4},{6,7},{7,6},{8,9},{9,8},{10,11... | collective-permute-start | bytes 798728 | tf_op jit(solution)/shard_map/ppermute | solution.py:173
  87.8 8.4 %collective-permute-start.27 = (f32[4,128,128]{2,1,0:T(8,128)}, f32[4,128,128]{2,1,0:T(8,128)S(1)}, u32[]{:S(2)}, u32[]{:S(2)}) collective-permute-start(f32[4,128,128]{2,1,0:T(8,128)} %get-tuple-element.70), channel_id=1, source_target_pairs={{0,1},{1,0},{2,3},{3,2},{4,5},{5,4},{6,7},{7,6},{8,9},{9,8},{10,11... | collective-permute-start | bytes 786440 | tf_op jit(solution)/shard_map/ppermute | solution.py:173
  87.9 4.9 %collective-permute-start.28 = (bf16[4,128,128]{2,1,0:T(8,128)(2,1)}, bf16[4,128,128]{2,1,0:T(8,128)(2,1)S(1)}, u32[]{:S(2)}, u32[]{:S(2)}) collective-permute-start(bf16[4,128,128]{2,1,0:T(8,128)(2,1)} %get-tuple-element.71), channel_id=1, source_target_pairs={{0,2},{1,3},{2,0},{3,1},{4,6},{5,7},{6,4},{7,5},{8,10},{9,11},{10,... | collective-permute-start | bytes 393224 | tf_op jit(solution)/shard_map/ppermute | solution.py:173
  88.9 7.2 %collective-permute-start.29 = (bf16[4,128,128]{2,1,0:T(8,128)(2,1)}, bf16[4,128,128]{2,1,0:T(8,128)(2,1)S(1)}, u32[]{:S(2)}, u32[]{:S(2)}) collective-permute-start(bf16[4,128,128]{2,1,0:T(8,128)(2,1)} %get-tuple-element.72), channel_id=1, source_target_pairs={{0,3},{1,2},{2,1},{3,0},{4,7},{5,6},{6,5},{7,4},{8,11},{9,10},{10,... | collective-permute-start | bytes 393224 | tf_op jit(solution)/shard_map/ppermute | solution.py:173
  (25 other events, 135.5 us)

commit v9 on v8

--- a/solution.py
+++ b/solution.py
@@ -21,8 +21,9 @@
     return pl.CostEstimate(flops=flops, bytes_accessed=nbytes, transcendentals=0)
 
 
-def split_kernel(place, dens_keep, ham_keep, met_keep, density, hamiltonian, metric, *outs):
-    spin, row = place[0], place[1]
+def split_kernel(half, dens_keep, ham_keep, met_keep, density, hamiltonian, metric, *outs):
+    col = lax.axis_index("col")
+    spin, row = jnp.where(col >= half, 1, 0), lax.rem(col, 2)
     per = dens_keep.shape[1]
     lane = lax.broadcasted_iota(jnp.int32, (TAIL, BLOCK), 1)
     for first, keeps in ((0, (dens_keep,)), (4, (ham_keep, met_keep))):
@@ -187,13 +188,13 @@
     place = jnp.stack([spin, part, z, x] + [col ^ m for m in masks])
 
     split = pl.pallas_call(
-        split_kernel,
+        functools.partial(split_kernel, half),
         out_shape=[jax.ShapeDtypeStruct((n * BLOCK + TAIL, width), bf16) for n in (1, 1, 1, 1, 2, 2, 2, 2)],
-        in_specs=[SMEM] * 4 + [VMEM] * 3,
+        in_specs=[SMEM] * 3 + [VMEM] * 3,
         out_specs=[VMEM] * 8,
         cost_estimate=estimate(0, 24 * BLOCK * width * 2),
         name="split",
-    )(place, dens_keep, ham_keep, met_keep, density, hamiltonian, metric)
+    )(dens_keep, ham_keep, met_keep, density, hamiltonian, metric)
 
     def exchange(pieces):
         moved = {m: by_mask(m)(pieces[variant(m)]) for m in reversed(range(1, ncol))}

time: 99.4 us -> 98.8 us (level)
  no operation moved by 1% of the time
where the time goes in v9:
time: 98.8 us; the launch traced here: 98.5 us
  waiting for transfers between devices  43.7 us (44%)
  starting transfers between devices  23 us (23%)
  Pallas kernels  21.6 us (22%)
  local copies, waits for them, and re-layouts  9.91 us (10%)
    ppermute x16, waiting for transfers between devices, by_mask(): lax.ppermute(a, 'col', [(c, c ^ mask) for c in range(ncol)])  22 us
    ppermute x14, waiting for transfers between devices, by_row(): return lambda a: lax.ppermute(a, 'row', pairs)  21.6 us
    ppermute x14, starting transfers between devices, by_row(): return lambda a: lax.ppermute(a, 'row', pairs)  12.6 us
    ppermute x16, starting transfers between devices, by_mask(): lax.ppermute(a, 'col', [(c, c ^ mask) for c in range(ncol)])  10.4 us
    unnamed x62, local copies, waits for them, and re-layouts  8.53 us
    pallas_call x1, Pallas kernels, first_product(): pl.pallas_call(functools.partial(first_kernel, entries, layers, len(array...  6.05 us
    pallas_call x1, Pallas kernels, body(): pl.pallas_call(functools.partial(second_kernel, entries, layers, len(arra...  5.49 us
    pallas_call x2, Pallas kernels, pack(): pl.pallas_call(functools.partial(pack_kernel, ncol, mats, slots), out_sha...  5.34 us
  transfers between devices with their start and end apart: 30, of which 16 were waited for; matrix products, arithmetic and copies ran while one was open for 6% of the time, Pallas kernels for 9%

profile of v9, /device:TPU:1, one launch (start us, length us, event | category | flops | bytes accessed | tf_op | source)
XLA Modules:
  0.0 98.5 jit_solution(3087474259874599226)
XLA Ops:
  0.0 2.6 %split.1 = (bf16[144,512]{1,0:T(8,128)(2,1)}, bf16[144,512]{1,0:T(8,128)(2,1)}, bf16[144,512]{1,0:T(8,128)(2,1)}, bf16[144,512]{1,0:T(8,128)(2,1)}, bf16[272,512...) custom-call(s32[2,4]{1,0:T(2,128)} %dens_keep.1, ...), custom_call_target="tpu_custom_call" | custom-call | bytes 3145728 | tf_op jit(solution)/shard_map/split/pallas_call | solution.py:190
  2.6 2.1 %collective-permute-start = (bf16[144,512]{1,0:T(8,128)(2,1)}, bf16[144,512]{1,0:T(8,128)(2,1)S(1)}, u32[]{:S(2)}, u32[]{:S(2)}) collective-permute-start(bf16[144,512]{1,0:T(8,128)(2,1)} %get-tuple-element.39), channel_id=1, source_target_pairs={{0,2},{1,3},{2,0},{3,1},{4,6},{5,7},{6,4},{7,5},{8,10},{9,11},{10,... | collective-permute-start | bytes 442376 | tf_op jit(solution)/shard_map/ppermute | solution.py:174
  6.2 2.2 %collective-permute-done.refs_2_ = bf16[144,512]{1,0:T(8,128)(2,1)S(1)} collective-permute-done((bf16[144,512]{1,0:T(8,128)(2,1)}, bf16[144,512]{1,0:T(8,128)(2,1)S(1)}, u32[]{:S(2)}, u32[]{:S(2)}) %collective-permute-start) | collective-permute-done | bytes 147488 | tf_op jit(solution)/shard_map/ppermute | solution.py:174
  8.4 3.7 %collective-permute-done.7.refs_3_ = bf16[144,512]{1,0:T(8,128)(2,1)S(1)} collective-permute-done((bf16[144,512]{1,0:T(8,128)(2,1)}, bf16[144,512]{1,0:T(8,128)(2,1)S(1)}, u32[]{:S(2)}, u32[]{:S(2)}) %collective-permute-start.7) | collective-permute-done | bytes 147488 | tf_op jit(solution)/shard_map/ppermute | solution.py:174
  12.8 2.5 %pack.3.refs_0_ = bf16[912,128]{1,0:T(8,128)(2,1)} custom-call(s32[8]{0:T(128)} %stack.35.place, bf16[144,512]{1,0:T(8,128)(2,1)} %get-tuple-element.48.refs_0_, bf16[144,512]{1,0:T(8,128)(2,1)} %copy-done.23, bf16[144,512]{1,0:T(8,128)(2,1)} %copy-done.22, bf16[144,512]{1,0:T(8,128)(2,1)} %copy-done.24), custom_call_target="tpu_custom_call" | custom-call | bytes 1572864 | tf_op jit(solution)/shard_map/pack/pallas_call | solution.py:208
  15.3 1.4 %collective-permute-start.8 = (bf16[912,128]{1,0:T(8,128)(2,1)}, bf16[912,128]{1,0:T(8,128)(2,1)S(1)}, u32[]{:S(2)}, u32[]{:S(2)}) collective-permute-start(bf16[912,128]{1,0:T(8,128)(2,1)} %pack.3.refs_0_), channel_id=1, source_target_pairs={{0,4},{4,0},{8,12},{12,8},{16,20},{20,16},{24,28},{28,24},{1,5},{5... | collective-permute-start | bytes 700424 | tf_op jit(solution)/shard_map/ppermute | solution.py:171
  16.8 1.3 %collective-permute-start.9 = (bf16[912,128]{1,0:T(8,128)(2,1)}, bf16[912,128]{1,0:T(8,128)(2,1)S(1)}, u32[]{:S(2)}, u32[]{:S(2)}) collective-permute-start(bf16[912,128]{1,0:T(8,128)(2,1)} %pack.3.refs_0_), channel_id=1, source_target_pairs={{0,8},{4,12},{8,16},{12,20},{16,24},{20,28},{24,0},{28,4},{1,9},{5... | collective-permute-start | bytes 700424 | tf_op jit(solution)/shard_map/ppermute | solution.py:171
  21.2 1.6 %collective-permute-done.8.refs_1_ = bf16[912,128]{1,0:T(8,128)(2,1)S(1)} collective-permute-done((bf16[912,128]{1,0:T(8,128)(2,1)}, bf16[912,128]{1,0:T(8,128)(2,1)S(1)}, u32[]{:S(2)}, u32[]{:S(2)}) %collective-permute-start.8) | collective-permute-done | bytes 233504 | tf_op jit(solution)/shard_map/ppermute | solution.py:171
  22.8 3.4 %collective-permute-done.9.refs_2_ = bf16[912,128]{1,0:T(8,128)(2,1)S(1)} collective-permute-done((bf16[912,128]{1,0:T(8,128)(2,1)}, bf16[912,128]{1,0:T(8,128)(2,1)S(1)}, u32[]{:S(2)}, u32[]{:S(2)}) %collective-permute-start.9) | collective-permute-done | bytes 233504 | tf_op jit(solution)/shard_map/ppermute | solution.py:171
  26.8 6.5 %collective-permute-done.3.refs_3_ = bf16[272,512]{1,0:T(8,128)(2,1)S(1)} collective-permute-done((bf16[272,512]{1,0:T(8,128)(2,1)}, bf16[272,512]{1,0:T(8,128)(2,1)S(1)}, u32[]{:S(2)}, u32[]{:S(2)}) %collective-permute-start.3) | collective-permute-done | bytes 278560 | tf_op jit(solution)/shard_map/ppermute | solution.py:174
  34.0 2.8 %pack.2.own.refs_0_ = bf16[1040,128]{1,0:T(8,128)(2,1)} custom-call(s32[8]{0:T(128)} %stack.35.place, bf16[272,512]{1,0:T(8,128)(2,1)} %get-tuple-element.44.refs_0_, bf16[272,512]{1,0:T(8,128)(2,1)} %copy-done.13, bf16[272,512]{1,0:T(8,128)(2,1)} %copy-done.14, bf16[272,512]{1,0:T(8,128)(2,1)} %copy-done.15), custom_call_target="tpu_custom_call" | custom-call | bytes 1572864 | tf_op jit(solution)/shard_map/pack/pallas_call | solution.py:208
  37.1 1.3 %collective-permute-start.5 = (bf16[1040,128]{1,0:T(8,128)(2,1)}, bf16[1040,128]{1,0:T(8,128)(2,1)S(1)}, u32[]{:S(2)}, u32[]{:S(2)}) collective-permute-start(bf16[1040,128]{1,0:T(8,128)(2,1)} %pack.2.own.refs_0_), channel_id=1, source_target_pairs={{0,8},{4,12},{8,16},{12,20},{16,24},{20,28},{24,0},{28,4},{1,9},{5... | collective-permute-start | bytes 798728 | tf_op jit(solution)/shard_map/ppermute | solution.py:171
  38.4 1.7 %constant_dynamic-update-slice_fusion.9 = bf16[5200,128]{1,0:T(8,128)(2,1)} fusion(bf16[1040,128]{1,0:T(8,128)(2,1)} %pack.2.own.refs_0_), kind=kLoop, calls=%fused_computation.10 | loop fusion | bytes 532480
  41.1 1.3 %collective-permute-start.15 = (bf16[912,128]{1,0:T(8,128)(2,1)S(1)}, bf16[912,128]{1,0:T(8,128)(2,1)S(1)}, u32[]{:S(2)}, u32[]{:S(2)}) collective-permute-start(bf16[912,128]{1,0:T(8,128)(2,1)S(1)} %collective-permute-done.11.refs_4_), channel_id=1, source_target_pairs={{0,8},{4,12},{8,16},{12,20},{16,24},{20,28},{24,0},{28,4},{1,9},{5... | collective-permute-start | bytes 700424 | tf_op jit(solution)/shard_map/ppermute | solution.py:171
  42.5 2.7 %collective-permute-done.4.refs_1_ = bf16[1040,128]{1,0:T(8,128)(2,1)S(1)} collective-permute-done((bf16[1040,128]{1,0:T(8,128)(2,1)}, bf16[1040,128]{1,0:T(8,128)(2,1)S(1)}, u32[]{:S(2)}, u32[]{:S(2)}) %collective-permute-start.4) | collective-permute-done | bytes 266272 | tf_op jit(solution)/shard_map/ppermute | solution.py:171
  45.2 1.9 %collective-permute-done.5.refs_2_ = bf16[1040,128]{1,0:T(8,128)(2,1)S(1)} collective-permute-done((bf16[1040,128]{1,0:T(8,128)(2,1)}, bf16[1040,128]{1,0:T(8,128)(2,1)S(1)}, u32[]{:S(2)}, u32[]{:S(2)}) %collective-permute-start.5) | collective-permute-done | bytes 266272 | tf_op jit(solution)/shard_map/ppermute | solution.py:171
  47.1 1.2 %collective-permute-start.12 = (bf16[1040,128]{1,0:T(8,128)(2,1)S(1)}, bf16[1040,128]{1,0:T(8,128)(2,1)S(1)}, u32[]{:S(2)}, u32[]{:S(2)}) collective-permute-start(bf16[1040,128]{1,0:T(8,128)(2,1)S(1)} %collective-permute-done.5.refs_2_), channel_id=1, source_target_pairs={{0,4},{4,0},{8,12},{12,8},{16,20},{20,16},{24,28},{28,24},{1,5},{5... | collective-permute-start | bytes 798728 | tf_op jit(solution)/shard_map/ppermute | solution.py:171
  48.3 1.9 %collective-permute-done.14.refs_5_ = bf16[912,128]{1,0:T(8,128)(2,1)S(1)} collective-permute-done((bf16[912,128]{1,0:T(8,128)(2,1)S(1)}, bf16[912,128]{1,0:T(8,128)(2,1)S(1)}, u32[]{:S(2)}, u32[]{:S(2)}) %collective-permute-start.14) | collective-permute-done | bytes 233504 | tf_op jit(solution)/shard_map/ppermute | solution.py:171
  50.2 1.9 %collective-permute-done.15.refs_6_ = bf16[912,128]{1,0:T(8,128)(2,1)S(1)} collective-permute-done((bf16[912,128]{1,0:T(8,128)(2,1)S(1)}, bf16[912,128]{1,0:T(8,128)(2,1)S(1)}, u32[]{:S(2)}, u32[]{:S(2)}) %collective-permute-start.15) | collective-permute-done | bytes 233504 | tf_op jit(solution)/shard_map/ppermute | solution.py:171
  54.4 1.7 %collective-permute-start.18 = (bf16[912,128]{1,0:T(8,128)(2,1)S(1)}, bf16[912,128]{1,0:T(8,128)(2,1)S(1)}, u32[]{:S(2)}, u32[]{:S(2)}) collective-permute-start(bf16[912,128]{1,0:T(8,128)(2,1)S(1)} %collective-permute-done.15.refs_6_), channel_id=1, source_target_pairs={{0,4},{4,0},{8,12},{12,8},{16,20},{20,16},{24,28},{28,24},{1,5},{5... | collective-permute-start | bytes 700424 | tf_op jit(solution)/shard_map/ppermute | solution.py:171
  56.5 1.5 %collective-permute-start.16 = (bf16[1040,128]{1,0:T(8,128)(2,1)S(1)}, bf16[1040,128]{1,0:T(8,128)(2,1)}, u32[]{:S(2)}, u32[]{:S(2)}) collective-permute-start(bf16[1040,128]{1,0:T(8,128)(2,1)S(1)} %collective-permute-done.13.refs_4_), channel_id=1, source_target_pairs={{0,4},{4,0},{8,12},{12,8},{16,20},{20,16},{24,28},{28,24},{1,5},{5... | collective-permute-start | bytes 798728 | tf_op jit(solution)/shard_map/ppermute | solution.py:171
  59.5 2.5 %collective-permute-done.18.refs_9_ = bf16[912,128]{1,0:T(8,128)(2,1)S(1)} collective-permute-done((bf16[912,128]{1,0:T(8,128)(2,1)S(1)}, bf16[912,128]{1,0:T(8,128)(2,1)S(1)}, u32[]{:S(2)}, u32[]{:S(2)}) %collective-permute-start.18) | collective-permute-done | bytes 233504 | tf_op jit(solution)/shard_map/ppermute | solution.py:171
  62.0 5.8 %collective-permute-done.16.refs_5_ = bf16[1040,128]{1,0:T(8,128)(2,1)} collective-permute-done((bf16[1040,128]{1,0:T(8,128)(2,1)S(1)}, bf16[1040,128]{1,0:T(8,128)(2,1)}, u32[]{:S(2)}, u32[]{:S(2)}) %collective-permute-start.16) | collective-permute-done | bytes 266272 | tf_op jit(solution)/shard_map/ppermute | solution.py:171
  68.7 1.3 %collective-permute-start.21 = (bf16[1040,128]{1,0:T(8,128)(2,1)}, bf16[1040,128]{1,0:T(8,128)(2,1)S(1)}, u32[]{:S(2)}, u32[]{:S(2)}) collective-permute-start(bf16[1040,128]{1,0:T(8,128)(2,1)} %collective-permute-done.17.refs_6_), channel_id=1, source_target_pairs={{0,4},{4,0},{8,12},{12,8},{16,20},{20,16},{24,28},{28,24},{1,5},{5... | collective-permute-start | bytes 798728 | tf_op jit(solution)/shard_map/ppermute | solution.py:171
  70.9 1.6 %collective-permute-done.25.refs_10_ = bf16[912,128]{1,0:T(8,128)(2,1)S(1)} collective-permute-done((bf16[912,128]{1,0:T(8,128)(2,1)S(1)}, bf16[912,128]{1,0:T(8,128)(2,1)S(1)}, u32[]{:S(2)}, u32[]{:S(2)}) %collective-permute-start.25) | collective-permute-done | bytes 233504 | tf_op jit(solution)/shard_map/ppermute | solution.py:174
  73.2 6.0 %first.1.prods = bf16[32,128,128]{2,1,0:T(8,128)(2,1)} custom-call(s32[8]{0:T(128)} %stack.35.place, bf16[1040,128]{1,0:T(8,128)(2,1)} %pack.2.own.refs_0_, bf16[912,128]{1,0:T(8,128)(2,1)} %pack.3.refs_0_, bf16[912,128]{1,0:T(8,128)(2,1)} %copy-done.8, bf16[912,128]{1,0:T(8,128)(2,1)} %copy-done.9, bf16[912,128]{1,0:T(8,128)(2,1)} %copy-done.10, ...), custom_call_target="tpu_custom_call" | custom-call | flops 234881024 | bytes 10000000 | tf_op jit(solution)/shard_map/first/pallas_call | solution.py:237
  79.4 1.5 %collective-permute-done.26.refs_11_ = bf16[1040,128]{1,0:T(8,128)(2,1)S(1)} collective-permute-done((bf16[1040,128]{1,0:T(8,128)(2,1)S(1)}, bf16[1040,128]{1,0:T(8,128)(2,1)S(1)}, u32[]{:S(2)}, u32[]{:S(2)}) %collective-permute-start.26) | collective-permute-done | bytes 266272 | tf_op jit(solution)/shard_map/ppermute | solution.py:174
  81.7 5.5 %second.1 = (f32[4,128,128]{2,1,0:T(8,128)}, f32[4,128,128]{2,1,0:T(8,128)}, bf16[4,128,128]{2,1,0:T(8,128)(2,1)}, bf16[4,128,128]{2,1,0:T(8,128)(2,1)}) custom-call(s32[8]{0:T(128)} %stack.35.place, bf16[32,128,128]{2,1,0:T(8,128)(2,1)} %first.1.prods, bf16[1040,128]{1,0:T(8,128)(2,1)} %pack.2.own.refs_0_, bf16[1040,128]{1,0:T(8,128)(2,1)} %copy-done.2, ...), custom_call_target="tpu_custom_call" | custom-call | flops 536870912 | bytes 12000000 | tf_op jit(solution)/shard_map/second/pallas_call | solution.py:290
  87.3 1.0 %collective-permute-start.28 = (bf16[4,128,128]{2,1,0:T(8,128)(2,1)}, bf16[4,128,128]{2,1,0:T(8,128)(2,1)S(1)}, u32[]{:S(2)}, u32[]{:S(2)}) collective-permute-start(bf16[4,128,128]{2,1,0:T(8,128)(2,1)} %get-tuple-element.71), channel_id=1, source_target_pairs={{0,2},{1,3},{2,0},{3,1},{4,6},{5,7},{6,4},{7,5},{8,10},{9,11},{10,... | collective-permute-start | bytes 393224 | tf_op jit(solution)/shard_map/ppermute | solution.py:174
  89.3 2.9 %collective-permute-done.28.refs_2_ = bf16[4,128,128]{2,1,0:T(8,128)(2,1)S(1)} collective-permute-done((bf16[4,128,128]{2,1,0:T(8,128)(2,1)}, bf16[4,128,128]{2,1,0:T(8,128)(2,1)S(1)}, u32[]{:S(2)}, u32[]{:S(2)}) %collective-permute-start.28) | collective-permute-done | bytes 131104 | tf_op jit(solution)/shard_map/ppermute | solution.py:174
  92.2 3.3 %collective-permute-done.29.refs_3_ = bf16[4,128,128]{2,1,0:T(8,128)(2,1)S(1)} collective-permute-done((bf16[4,128,128]{2,1,0:T(8,128)(2,1)}, bf16[4,128,128]{2,1,0:T(8,128)(2,1)S(1)}, u32[]{:S(2)}, u32[]{:S(2)}) %collective-permute-start.29) | collective-permute-done | bytes 131104 | tf_op jit(solution)/shard_map/ppermute | solution.py:174
  96.3 2.2 %join.1 = f32[2,256,512]{2,1,0:T(8,128)} custom-call(s32[8]{0:T(128)} %stack.35.place, s32[2,4]{1,0:T(2,128)} %keep.1, f32[4,128,128]{2,1,0:T(8,128)} %get-tuple-element.69.refs_0_, f32[4,128,128]{2,1,0:T(8,128)} %copy-done.19, bf16[4,128,128]{2,1,0:T(8,128)(2,1)} %copy-done.25, bf16[4,128,128]{2,1,0:T(8,128)(2,1)} %copy-done.26), custom_call_target="tpu_custom_call" | custom-call | bytes 2097152 | tf_op jit(solution)/shard_map/join/pallas_call | solution.py:301
  (100 shorter events, 17.4 us)
Async XLA Ops:
  2.6 5.9 %collective-permute-start = (bf16[144,512]{1,0:T(8,128)(2,1)}, bf16[144,512]{1,0:T(8,128)(2,1)S(1)}, u32[]{:S(2)}, u32[]{:S(2)}) collective-permute-start(bf16[144,512]{1,0:T(8,128)(2,1)} %get-tuple-element.39), channel_id=1, source_target_pairs={{0,2},{1,3},{2,0},{3,1},{4,6},{5,7},{6,4},{7,5},{8,10},{9,11},{10,... | collective-permute-start | bytes 442376 | tf_op jit(solution)/shard_map/ppermute | solution.py:174
  4.6 3.8 %collective-permute-start.6 = (bf16[144,512]{1,0:T(8,128)(2,1)}, bf16[144,512]{1,0:T(8,128)(2,1)S(1)}, u32[]{:S(2)}, u32[]{:S(2)}) collective-permute-start(bf16[144,512]{1,0:T(8,128)(2,1)} %get-tuple-element.49), channel_id=1, source_target_pairs={{0,1},{1,0},{2,3},{3,2},{4,5},{5,4},{6,7},{7,6},{8,9},{9,8},{10,11... | collective-permute-start | bytes 442376 | tf_op jit(solution)/shard_map/ppermute | solution.py:174
  5.6 6.5 %collective-permute-start.7 = (bf16[144,512]{1,0:T(8,128)(2,1)}, bf16[144,512]{1,0:T(8,128)(2,1)S(1)}, u32[]{:S(2)}, u32[]{:S(2)}) collective-permute-start(bf16[144,512]{1,0:T(8,128)(2,1)} %get-tuple-element.51), channel_id=1, source_target_pairs={{0,3},{1,2},{2,1},{3,0},{4,7},{5,6},{6,5},{7,4},{8,11},{9,10},{10,... | collective-permute-start | bytes 442376 | tf_op jit(solution)/shard_map/ppermute | solution.py:174
  15.3 7.5 %collective-permute-start.8 = (bf16[912,128]{1,0:T(8,128)(2,1)}, bf16[912,128]{1,0:T(8,128)(2,1)S(1)}, u32[]{:S(2)}, u32[]{:S(2)}) collective-permute-start(bf16[912,128]{1,0:T(8,128)(2,1)} %pack.3.refs_0_), channel_id=1, source_target_pairs={{0,4},{4,0},{8,12},{12,8},{16,20},{20,16},{24,28},{28,24},{1,5},{5... | collective-permute-start | bytes 700424 | tf_op jit(solution)/shard_map/ppermute | solution.py:171
  16.8 9.4 %collective-permute-start.9 = (bf16[912,128]{1,0:T(8,128)(2,1)}, bf16[912,128]{1,0:T(8,128)(2,1)S(1)}, u32[]{:S(2)}, u32[]{:S(2)}) collective-permute-start(bf16[912,128]{1,0:T(8,128)(2,1)} %pack.3.refs_0_), channel_id=1, source_target_pairs={{0,8},{4,12},{8,16},{12,20},{16,24},{20,28},{24,0},{28,4},{1,9},{5... | collective-permute-start | bytes 700424 | tf_op jit(solution)/shard_map/ppermute | solution.py:171
  18.1 8.4 %collective-permute-start.1 = (bf16[272,512]{1,0:T(8,128)(2,1)}, bf16[272,512]{1,0:T(8,128)(2,1)S(1)}, u32[]{:S(2)}, u32[]{:S(2)}) collective-permute-start(bf16[272,512]{1,0:T(8,128)(2,1)} %get-tuple-element.45), channel_id=1, source_target_pairs={{0,1},{1,0},{2,3},{3,2},{4,5},{5,4},{6,7},{7,6},{8,9},{9,8},{10,11... | collective-permute-start | bytes 835592 | tf_op jit(solution)/shard_map/ppermute | solution.py:174
  18.5 8.3 %collective-permute-start.2 = (bf16[272,512]{1,0:T(8,128)(2,1)}, bf16[272,512]{1,0:T(8,128)(2,1)S(1)}, u32[]{:S(2)}, u32[]{:S(2)}) collective-permute-start(bf16[272,512]{1,0:T(8,128)(2,1)} %get-tuple-element.46), channel_id=1, source_target_pairs={{0,2},{1,3},{2,0},{3,1},{4,6},{5,7},{6,4},{7,5},{8,10},{9,11},{10,... | collective-permute-start | bytes 835592 | tf_op jit(solution)/shard_map/ppermute | solution.py:174
  19.4 13.9 %collective-permute-start.3 = (bf16[272,512]{1,0:T(8,128)(2,1)}, bf16[272,512]{1,0:T(8,128)(2,1)S(1)}, u32[]{:S(2)}, u32[]{:S(2)}) collective-permute-start(bf16[272,512]{1,0:T(8,128)(2,1)} %get-tuple-element.47), channel_id=1, source_target_pairs={{0,3},{1,2},{2,1},{3,0},{4,7},{5,6},{6,5},{7,4},{8,11},{9,10},{10,... | collective-permute-start | bytes 835592 | tf_op jit(solution)/shard_map/ppermute | solution.py:174
  26.2 13.9 %collective-permute-start.10 = (bf16[912,128]{1,0:T(8,128)(2,1)S(1)}, bf16[912,128]{1,0:T(8,128)(2,1)S(1)}, u32[]{:S(2)}, u32[]{:S(2)}) collective-permute-start(bf16[912,128]{1,0:T(8,128)(2,1)S(1)} %collective-permute-done.9.refs_2_), channel_id=1, source_target_pairs={{0,4},{4,0},{8,12},{12,8},{16,20},{20,16},{24,28},{28,24},{1,5},{5... | collective-permute-start | bytes 700424 | tf_op jit(solution)/shard_map/ppermute | solution.py:171
  26.4 13.7 %collective-permute-start.11 = (bf16[912,128]{1,0:T(8,128)(2,1)S(1)}, bf16[912,128]{1,0:T(8,128)(2,1)S(1)}, u32[]{:S(2)}, u32[]{:S(2)}) collective-permute-start(bf16[912,128]{1,0:T(8,128)(2,1)S(1)} %collective-permute-done.9.refs_2_), channel_id=1, source_target_pairs={{0,8},{4,12},{8,16},{12,20},{16,24},{20,28},{24,0},{28,4},{1,9},{5... | collective-permute-start | bytes 700424 | tf_op jit(solution)/shard_map/ppermute | solution.py:171
  36.8 8.3 %collective-permute-start.4 = (bf16[1040,128]{1,0:T(8,128)(2,1)}, bf16[1040,128]{1,0:T(8,128)(2,1)S(1)}, u32[]{:S(2)}, u32[]{:S(2)}) collective-permute-start(bf16[1040,128]{1,0:T(8,128)(2,1)} %pack.2.own.refs_0_), channel_id=1, source_target_pairs={{0,4},{4,0},{8,12},{12,8},{16,20},{20,16},{24,28},{28,24},{1,5},{5... | collective-permute-start | bytes 798728 | tf_op jit(solution)/shard_map/ppermute | solution.py:171
  37.1 10.0 %collective-permute-start.5 = (bf16[1040,128]{1,0:T(8,128)(2,1)}, bf16[1040,128]{1,0:T(8,128)(2,1)S(1)}, u32[]{:S(2)}, u32[]{:S(2)}) collective-permute-start(bf16[1040,128]{1,0:T(8,128)(2,1)} %pack.2.own.refs_0_), channel_id=1, source_target_pairs={{0,8},{4,12},{8,16},{12,20},{16,24},{20,28},{24,0},{28,4},{1,9},{5... | collective-permute-start | bytes 798728 | tf_op jit(solution)/shard_map/ppermute | solution.py:171
  40.1 16.0 %copy-start.11 = (bf16[912,128]{1,0:T(8,128)(2,1)}, bf16[912,128]{1,0:T(8,128)(2,1)S(1)}, u32[]{:S(2)}) copy-start(bf16[912,128]{1,0:T(8,128)(2,1)S(1)} %collective-permute-done.11.refs_4_) | copy-start | bytes 700420
  40.1 10.0 %collective-permute-start.14 = (bf16[912,128]{1,0:T(8,128)(2,1)S(1)}, bf16[912,128]{1,0:T(8,128)(2,1)S(1)}, u32[]{:S(2)}, u32[]{:S(2)}) collective-permute-start(bf16[912,128]{1,0:T(8,128)(2,1)S(1)} %collective-permute-done.11.refs_4_), channel_id=1, source_target_pairs={{0,4},{4,0},{8,12},{12,8},{16,20},{20,16},{24,28},{28,24},{1,5},{5... | collective-permute-start | bytes 700424 | tf_op jit(solution)/shard_map/ppermute | solution.py:171
  41.1 10.9 %collective-permute-start.15 = (bf16[912,128]{1,0:T(8,128)(2,1)S(1)}, bf16[912,128]{1,0:T(8,128)(2,1)S(1)}, u32[]{:S(2)}, u32[]{:S(2)}) collective-permute-start(bf16[912,128]{1,0:T(8,128)(2,1)S(1)} %collective-permute-done.11.refs_4_), channel_id=1, source_target_pairs={{0,8},{4,12},{8,16},{12,20},{16,24},{20,28},{24,0},{28,4},{1,9},{5... | collective-permute-start | bytes 700424 | tf_op jit(solution)/shard_map/ppermute | solution.py:171
  47.1 9.5 %collective-permute-start.12 = (bf16[1040,128]{1,0:T(8,128)(2,1)S(1)}, bf16[1040,128]{1,0:T(8,128)(2,1)S(1)}, u32[]{:S(2)}, u32[]{:S(2)}) collective-permute-start(bf16[1040,128]{1,0:T(8,128)(2,1)S(1)} %collective-permute-done.5.refs_2_), channel_id=1, source_target_pairs={{0,4},{4,0},{8,12},{12,8},{16,20},{20,16},{24,28},{28,24},{1,5},{5... | collective-permute-start | bytes 798728 | tf_op jit(solution)/shard_map/ppermute | solution.py:171
  48.3 8.3 %collective-permute-start.13 = (bf16[1040,128]{1,0:T(8,128)(2,1)S(1)}, bf16[1040,128]{1,0:T(8,128)(2,1)S(1)}, u32[]{:S(2)}, u32[]{:S(2)}) collective-permute-start(bf16[1040,128]{1,0:T(8,128)(2,1)S(1)} %collective-permute-done.5.refs_2_), channel_id=1, source_target_pairs={{0,8},{4,12},{8,16},{12,20},{16,24},{20,28},{24,0},{28,4},{1,9},{5... | collective-permute-start | bytes 798728 | tf_op jit(solution)/shard_map/ppermute | solution.py:171
  52.1 9.9 %collective-permute-start.19 = (bf16[4560,128]{1,0:T(8,128)(2,1)S(1)}, bf16[4560,128]{1,0:T(8,128)(2,1)S(1)}, u32[]{:S(2)}, u32[]{:S(2)}) collective-permute-start(bf16[4560,128]{1,0:T(8,128)(2,1)S(1)} %constant_dynamic-update-slice_fusion), channel_id=1, source_target_pairs={{0,1},{1,0},{2,3},{3,2},{4,5},{5,4},{6,7},{7,6},{8,9},{9,8},{10,11... | collective-permute-start | bytes 3502088 | tf_op jit(solution)/shard_map/ppermute | solution.py:174
  54.4 7.6 %collective-permute-start.18 = (bf16[912,128]{1,0:T(8,128)(2,1)S(1)}, bf16[912,128]{1,0:T(8,128)(2,1)S(1)}, u32[]{:S(2)}, u32[]{:S(2)}) collective-permute-start(bf16[912,128]{1,0:T(8,128)(2,1)S(1)} %collective-permute-done.15.refs_6_), channel_id=1, source_target_pairs={{0,4},{4,0},{8,12},{12,8},{16,20},{20,16},{24,28},{28,24},{1,5},{5... | collective-permute-start | bytes 700424 | tf_op jit(solution)/shard_map/ppermute | solution.py:171
  56.1 5.9 %collective-permute-start.20 = (bf16[1824,128]{1,0:T(8,128)(2,1)S(1)}, bf16[1824,128]{1,0:T(8,128)(2,1)S(1)}, u32[]{:S(2)}, u32[]{:S(2)}) collective-permute-start(bf16[1824,128]{1,0:T(8,128)(2,1)S(1)} %pad_maximum_fusion), channel_id=1, source_target_pairs={{0,1},{1,0},{2,3},{3,2},{4,5},{5,4},{6,7},{7,6},{8,9},{9,8},{10,11... | collective-permute-start | bytes 1400840 | tf_op jit(solution)/shard_map/ppermute | solution.py:174
  56.5 22.7 %copy-start.4 = (bf16[1040,128]{1,0:T(8,128)(2,1)}, bf16[1040,128]{1,0:T(8,128)(2,1)S(1)}, u32[]{:S(2)}) copy-start(bf16[1040,128]{1,0:T(8,128)(2,1)S(1)} %collective-permute-done.12.refs_3_) | copy-start | bytes 798724
  56.5 11.3 %collective-permute-start.16 = (bf16[1040,128]{1,0:T(8,128)(2,1)S(1)}, bf16[1040,128]{1,0:T(8,128)(2,1)}, u32[]{:S(2)}, u32[]{:S(2)}) collective-permute-start(bf16[1040,128]{1,0:T(8,128)(2,1)S(1)} %collective-permute-done.13.refs_4_), channel_id=1, source_target_pairs={{0,4},{4,0},{8,12},{12,8},{16,20},{20,16},{24,28},{28,24},{1,5},{5... | collective-permute-start | bytes 798728 | tf_op jit(solution)/shard_map/ppermute | solution.py:171
  58.0 9.8 %collective-permute-start.17 = (bf16[1040,128]{1,0:T(8,128)(2,1)S(1)}, bf16[1040,128]{1,0:T(8,128)(2,1)}, u32[]{:S(2)}, u32[]{:S(2)}) collective-permute-start(bf16[1040,128]{1,0:T(8,128)(2,1)S(1)} %collective-permute-done.13.refs_4_), channel_id=1, source_target_pairs={{0,8},{4,12},{8,16},{12,20},{16,24},{20,28},{24,0},{28,4},{1,9},{5... | collective-permute-start | bytes 798728 | tf_op jit(solution)/shard_map/ppermute | solution.py:171
  67.8 11.5 %collective-permute-start.22 = (bf16[5200,128]{1,0:T(8,128)(2,1)}, bf16[5200,128]{1,0:T(8,128)(2,1)S(1)}, u32[]{:S(2)}, u32[]{:S(2)}) collective-permute-start(bf16[5200,128]{1,0:T(8,128)(2,1)} %constant_dynamic-update-slice_fusion.5), channel_id=1, source_target_pairs={{0,1},{1,0},{2,3},{3,2},{4,5},{5,4},{6,7},{7,6},{8,9},{9,8},{10,11... | collective-permute-start | bytes 3993608 | tf_op jit(solution)/shard_map/ppermute | solution.py:174
  68.7 10.5 %collective-permute-start.21 = (bf16[1040,128]{1,0:T(8,128)(2,1)}, bf16[1040,128]{1,0:T(8,128)(2,1)S(1)}, u32[]{:S(2)}, u32[]{:S(2)}) collective-permute-start(bf16[1040,128]{1,0:T(8,128)(2,1)} %collective-permute-done.17.refs_6_), channel_id=1, source_target_pairs={{0,4},{4,0},{8,12},{12,8},{16,20},{20,16},{24,28},{28,24},{1,5},{5... | collective-permute-start | bytes 798728 | tf_op jit(solution)/shard_map/ppermute | solution.py:171
  70.1 9.2 %collective-permute-start.23 = (bf16[1040,128]{1,0:T(8,128)(2,1)}, bf16[1040,128]{1,0:T(8,128)(2,1)S(1)}, u32[]{:S(2)}, u32[]{:S(2)}) collective-permute-start(bf16[1040,128]{1,0:T(8,128)(2,1)} %collective-permute-done.16.refs_5_), channel_id=1, source_target_pairs={{0,1},{1,0},{2,3},{3,2},{4,5},{5,4},{6,7},{7,6},{8,9},{9,8},{10,11... | collective-permute-start | bytes 798728 | tf_op jit(solution)/shard_map/ppermute | solution.py:174
  70.4 8.9 %collective-permute-start.24 = (bf16[1040,128]{1,0:T(8,128)(2,1)}, bf16[1040,128]{1,0:T(8,128)(2,1)}, u32[]{:S(2)}, u32[]{:S(2)}) collective-permute-start(bf16[1040,128]{1,0:T(8,128)(2,1)} %collective-permute-done.17.refs_6_), channel_id=1, source_target_pairs={{0,1},{1,0},{2,3},{3,2},{4,5},{5,4},{6,7},{7,6},{8,9},{9,8},{10,11... | collective-permute-start | bytes 798728 | tf_op jit(solution)/shard_map/ppermute | solution.py:174
  70.6 1.9 %collective-permute-start.25 = (bf16[912,128]{1,0:T(8,128)(2,1)S(1)}, bf16[912,128]{1,0:T(8,128)(2,1)S(1)}, u32[]{:S(2)}, u32[]{:S(2)}) collective-permute-start(bf16[912,128]{1,0:T(8,128)(2,1)S(1)} %collective-permute-done.18.refs_9_), channel_id=1, source_target_pairs={{0,1},{1,0},{2,3},{3,2},{4,5},{5,4},{6,7},{7,6},{8,9},{9,8},{10,11... | collective-permute-start | bytes 700424 | tf_op jit(solution)/shard_map/ppermute | solution.py:174
  79.3 1.6 %collective-permute-start.26 = (bf16[1040,128]{1,0:T(8,128)(2,1)S(1)}, bf16[1040,128]{1,0:T(8,128)(2,1)S(1)}, u32[]{:S(2)}, u32[]{:S(2)}) collective-permute-start(bf16[1040,128]{1,0:T(8,128)(2,1)S(1)} %collective-permute-done.21.refs_10_), channel_id=1, source_target_pairs={{0,1},{1,0},{2,3},{3,2},{4,5},{5,4},{6,7},{7,6},{8,9},{9,8},{10,11... | collective-permute-start | bytes 798728 | tf_op jit(solution)/shard_map/ppermute | solution.py:174
  87.2 8.4 %collective-permute-start.27 = (f32[4,128,128]{2,1,0:T(8,128)}, f32[4,128,128]{2,1,0:T(8,128)S(1)}, u32[]{:S(2)}, u32[]{:S(2)}) collective-permute-start(f32[4,128,128]{2,1,0:T(8,128)} %get-tuple-element.70), channel_id=1, source_target_pairs={{0,1},{1,0},{2,3},{3,2},{4,5},{5,4},{6,7},{7,6},{8,9},{9,8},{10,11... | collective-permute-start | bytes 786440 | tf_op jit(solution)/shard_map/ppermute | solution.py:174
  87.3 4.9 %collective-permute-start.28 = (bf16[4,128,128]{2,1,0:T(8,128)(2,1)}, bf16[4,128,128]{2,1,0:T(8,128)(2,1)S(1)}, u32[]{:S(2)}, u32[]{:S(2)}) collective-permute-start(bf16[4,128,128]{2,1,0:T(8,128)(2,1)} %get-tuple-element.71), channel_id=1, source_target_pairs={{0,2},{1,3},{2,0},{3,1},{4,6},{5,7},{6,4},{7,5},{8,10},{9,11},{10,... | collective-permute-start | bytes 393224 | tf_op jit(solution)/shard_map/ppermute | solution.py:174
  88.3 7.2 %collective-permute-start.29 = (bf16[4,128,128]{2,1,0:T(8,128)(2,1)}, bf16[4,128,128]{2,1,0:T(8,128)(2,1)S(1)}, u32[]{:S(2)}, u32[]{:S(2)}) collective-permute-start(bf16[4,128,128]{2,1,0:T(8,128)(2,1)} %get-tuple-element.72), channel_id=1, source_target_pairs={{0,3},{1,2},{2,1},{3,0},{4,7},{5,6},{6,5},{7,4},{8,11},{9,10},{10,... | collective-permute-start | bytes 393224 | tf_op jit(solution)/shard_map/ppermute | solution.py:174
  (25 other events, 135.5 us)
